TPU v7x, 32 devices: a whole 2x2x4 slice. The times are simulated.
32 devices in a mesh: group: 2 (over y), ctx: 4 (over z), tp: 4 (over x, core).
Axes of the slice: x: 2, y: 2, z: 4, core: 2. Of those that a mesh axis runs over, the one named last changes fastest.
Arguments:
- queries: bfloat16 [1024, 4096], P(('group', 'ctx'), 'tp'), parts along dimension 0, as said below
- key_rows: bfloat16 [1024, 1024], P(('group', 'ctx'), 'tp'), parts along dimension 0, as said below
- value_rows: bfloat16 [1024, 1024], P(('group', 'ctx'), 'tp'), parts along dimension 0, may hold values from -6 to 6
- doc_start: int32 [1024], P(('group', 'ctx')), parts along dimension 0, may hold values from 0 to 511, as said below
- doc_end: int32 [1024], P(('group', 'ctx')), parts along dimension 0, may hold values from 1 to 512, as said below
- block_target: int32 [16], P(('group', 'ctx')), parts along dimension 0, may hold values from 0 to 7, as said below
- out_weight: bfloat16 [4096, 2048], P('tp', 'ctx'), may hold values from -0.09375 to 0.09375
Outputs:
- balanced_out: bfloat16 [1024, 2048], P(('group', 'ctx', 'tp')), parts along dimension 0
There are 2 independent parts, one for each index of `group`. A program takes and returns all parts, laid end to end along the dimension named above; an argument that names none is the same for every part. Nothing has to cross between parts.
Inputs may be any that keep to these rules, and one draw needn't show every extreme that they name: Documents are consecutive runs of rows; row i's document begins at row doc_start[i] <= i; each document has 1 to 128 rows and one has exactly 128. Row i's document ends just before row doc_end[i] > i; doc_start and doc_end describe the same documents. A permutation of the 8 row blocks of 64 rows: block b goes to index block_target[b] // 2 of ctx at position block_target[b] % 2; the 2 blocks of one index of ctx go to 2 different indices. `queries`: entries lie within -6 to 6. `key_rows`: entries lie within -6 to 6.
All inputs are finite; a program needn't handle non-finite values.
Results may differ from a plain program's by a relative error of at most 0.012.
Values may be sent and summed in bfloat16 or wider, within the bound.
No kernel may reach another device: no remote copies, remote signals or barrier semaphores. Data moves between devices by JAX's collectives and lax.ppermute only.
A program may use at most 64 MiB of HBM per device.

v0:
```python
import math

import jax
import jax.numpy as jnp
from jax import lax
from jax.sharding import PartitionSpec as P

HEAD_DIM = 128


neg_large = -1e30


def attend_block(
    soft_state, query_grid, query_pos, query_start, key_block, value_block, key_end, key_pos
):
    running_max, weight_sum, weighted = soft_state
    scores = jnp.einsum(
        "rkgd,nkd->rkgn", query_grid, key_block, preferred_element_type=jnp.float32
    ) * HEAD_DIM ** (-0.5)
    visible = (
        (key_pos[None, :] <= query_pos[:, None])
        & (key_pos[None, :] >= query_start[:, None])
        & (key_end[None, :] > query_pos[:, None])
    )
    visible = visible[:, None, None, :]
    new_max = jnp.maximum(running_max, jnp.max(jnp.where(visible, scores, neg_large), axis=-1))
    weights = jnp.where(visible, jnp.exp(scores - new_max[..., None]), 0.0)
    fading = jnp.exp(running_max - new_max)
    weight_sum = weight_sum * fading + jnp.sum(weights, axis=-1)
    weighted = weighted * fading[..., None] + jnp.einsum(
        "rkgn,nkd->rkgd",
        weights.astype(jnp.bfloat16),
        value_block,
        preferred_element_type=jnp.float32,
    )
    return (new_max, weight_sum, weighted)


def fold_keys(soft_state, query_grid, query_pos, query_start, key_part, value_part, end_part):
    key_count = key_part.shape[0]
    kv_here = key_part.shape[1] // HEAD_DIM
    block_len = math.gcd(key_count, 512)
    block_count = key_count // block_len
    key_blocks = key_part.reshape(block_count, block_len, kv_here, HEAD_DIM)
    value_blocks = value_part.reshape(block_count, block_len, kv_here, HEAD_DIM)
    end_blocks = end_part.reshape(block_count, block_len)
    pos_blocks = jnp.arange(key_count, dtype=jnp.int32).reshape(block_count, block_len)

    def one_block(carry_state, block_items):
        return (
            attend_block(
                carry_state,
                query_grid,
                query_pos,
                query_start,
                block_items[0],
                block_items[1],
                block_items[2],
                block_items[3],
            ),
            None,
        )

    soft_state, unused_out = lax.scan(
        one_block, soft_state, (key_blocks, value_blocks, end_blocks, pos_blocks)
    )
    return soft_state


def finish_rows(soft_state, row_count):
    running_max, weight_sum, weighted = soft_state
    return (weighted / weight_sum[..., None]).astype(jnp.bfloat16).reshape(row_count, -1)


def shards(queries, key_rows, value_rows, doc_start, doc_end, block_target, out_weight):
    row_count = queries.shape[0]
    ctx_count = lax.axis_size("ctx")
    ctx_pos = lax.axis_index("ctx")
    per_device = block_target.shape[0]
    block_rows = row_count // per_device
    heads_here = queries.shape[1] // HEAD_DIM
    kv_here = key_rows.shape[1] // HEAD_DIM
    group_size = heads_here // kv_here
    dest_device = block_target // per_device
    dest_slot = block_target % per_device
    peer_ids = jnp.arange(ctx_count, dtype=jnp.int32)
    sending = dest_device[None, :] == peer_ids[:, None]
    sending_low = sending.astype(jnp.bfloat16)
    slot_sent = jnp.sum(jnp.where(sending, dest_slot[None, :] + 1, 0), axis=1) - 1
    slot_ids = jnp.arange(per_device, dtype=jnp.int32)
    start_state = (
        jnp.full((row_count, kv_here, group_size), neg_large, jnp.float32),
        jnp.zeros((row_count, kv_here, group_size), jnp.float32),
        jnp.zeros((row_count, kv_here, group_size, HEAD_DIM), jnp.float32),
    )
    query_blocks = queries.reshape(per_device, block_rows, -1)
    send_rows = jnp.einsum(
        "pb,bqc->pqc", sending_low, query_blocks, preferred_element_type=jnp.float32
    ).astype(jnp.bfloat16)
    first_rows = (ctx_pos * per_device + slot_ids) * block_rows
    row_sent = jnp.sum(jnp.where(sending, first_rows[None, :], 0), axis=1)
    send_info = jnp.stack([slot_sent, row_sent], axis=1)
    start_blocks = doc_start.reshape(per_device, block_rows)
    send_start = jnp.sum(jnp.where(sending[:, :, None], start_blocks[None, :, :], 0), axis=1)
    got_rows, got_info, got_start = (
        lax.all_to_all(send_rows, "ctx", split_axis=0, concat_axis=0, tiled=True),
        lax.all_to_all(send_info, "ctx", split_axis=0, concat_axis=0, tiled=True),
        lax.all_to_all(send_start, "ctx", split_axis=0, concat_axis=0, tiled=True),
    )
    placing = got_info[:, 0][None, :] == slot_ids[:, None]
    placed_rows = jnp.einsum(
        "bp,pqc->bqc", placing.astype(jnp.bfloat16), got_rows, preferred_element_type=jnp.float32
    ).astype(jnp.bfloat16)
    query_first = jnp.sum(jnp.where(placing, got_info[:, 1][None, :], 0), axis=1).astype(jnp.int32)
    query_pos = (query_first[:, None] + jnp.arange(block_rows, dtype=jnp.int32)[None, :]).reshape(
        row_count
    )
    query_start = (
        jnp.sum(jnp.where(placing[:, :, None], got_start[None, :, :], 0), axis=1)
        .astype(jnp.int32)
        .reshape(row_count)
    )
    query_grid = placed_rows.reshape(row_count, kv_here, group_size, HEAD_DIM)
    final_state = fold_keys(
        start_state,
        query_grid,
        query_pos,
        query_start,
        lax.all_gather(key_rows, "ctx", axis=0, tiled=True),
        lax.all_gather(value_rows, "ctx", axis=0, tiled=True),
        lax.all_gather(doc_end, "ctx", axis=0, tiled=True),
    )
    attended = finish_rows(final_state, row_count)
    partial_out = jnp.dot(
        attended,
        lax.all_gather(out_weight, "ctx", axis=1, tiled=True),
        preferred_element_type=jnp.float32,
    )
    return lax.psum_scatter(partial_out.astype(jnp.bfloat16), "tp", scatter_dimension=0, tiled=True)


def solution(mesh):
    in_specs = (
        P(("group", "ctx"), "tp"),
        P(("group", "ctx"), "tp"),
        P(("group", "ctx"), "tp"),
        P(("group", "ctx")),
        P(("group", "ctx")),
        P(("group", "ctx")),
        P("tp", "ctx"),
    )
    out_specs = P(("group", "ctx", "tp"), None)
    return jax.shard_map(shards, mesh=mesh, in_specs=in_specs, out_specs=out_specs, check_vma=False)
```

profile of v0, /device:TPU:0, one launch (start us, length us, event | category | flops | bytes accessed | tf_op | source)
XLA Modules:
  0.0 142.2 jit_solution(14230935683547552493)
XLA Ops:
  6.6 0.7 all-gather.3.cloned.1.call-update
  7.3 0.7 fusion.21
  8.1 0.6 copy.25
  8.7 6.3 %all-to-all-start = ((s32[4,1,2]{2,1,0:T(1,128)}), s32[4,1,2]{2,1,0:T(1,128)S(1)}, u32[]{:S(2)}, u32[]{:S(2)}) async-start(s32[4,1,2]{2,1,0:T(1,128)} %copy.25), calls=%async_computation | async-start | bytes 4096 | tf_op jit(solution)/shard_map/all_to_all | solution.py:108
  15.0 0.7 broadcast_in_dim.136
  15.8 0.6 convolution_convert_fusion.1
  16.4 1.0 copy.29
  17.4 18.4 %all_gather.14 = bf16[512,256]{1,0:T(8,128)(2,1)S(1)} all-gather(bf16[128,256]{1,0:T(8,128)(2,1)S(1)} %copy-done.1), channel_id=1, replica_groups=mesh['group'=2,'ctx'=4,'tp'=4] {'ctx'}, dimensions={0}, use_global_device_ids=true | all-gather | bytes 327680 | tf_op jit(solution)/shard_map/all_gather | solution.py:131
  36.0 11.4 %all-gather = s32[4,1,128]{2,1,0:T(1,128)S(1)} all-gather(s32[1,1,128]{2,1,0:T(1,128)S(1)} %bitcast.68), channel_id=1, replica_groups=mesh['group'=2,'ctx'=4,'tp'=4] {'ctx'}, dimensions={0}, use_global_device_ids=true | all-gather | bytes 2560 | tf_op jit(solution)/shard_map/all_gather | solution.py:132
  47.4 16.5 %all_gather.13 = bf16[512,256]{0,1:T(8,128)(2,1)S(1)} all-gather(bf16[128,256]{0,1:T(8,128)(2,1)S(1)} %copy.32), channel_id=1, replica_groups=mesh['group'=2,'ctx'=4,'tp'=4] {'ctx'}, dimensions={0}, use_global_device_ids=true | all-gather | bytes 327680 | tf_op jit(solution)/shard_map/all_gather | solution.py:130
  64.0 0.7 select_reduce_fusion.1
  64.7 4.5 %all-to-all-start.1 = ((s32[4,1,64]{2,1,0:T(1,128)}), s32[4,1,64]{2,1,0:T(1,128)S(1)}, u32[]{:S(2)}, u32[]{:S(2)}) async-start(s32[4,1,64]{2,1,0:T(1,128)} %bitcast.7), calls=%async_computation.1 | async-start | bytes 4096 | tf_op jit(solution)/shard_map/all_to_all | solution.py:109
  69.4 5.4 %all-to-all-done.1 = s32[4,1,64]{2,1,0:T(1,128)S(1)} async-done(((s32[4,1,64]{2,1,0:T(1,128)}), s32[4,1,64]{2,1,0:T(1,128)S(1)}, u32[]{:S(2)}, u32[]{:S(2)}) %all-to-all-start.1) | async-done | bytes 1056 | tf_op jit(solution)/shard_map/all_to_all | solution.py:109
  74.8 3.5 %all-to-all-start.2 = ((bf16[4,64,1024]{2,1,0:T(8,128)(2,1)}), bf16[4,64,1024]{2,1,0:T(8,128)(2,1)S(1)}, u32[]{:S(2)}, u32[]{:S(2)}) async-start(bf16[4,64,1024]{2,1,0:T(8,128)(2,1)} %copy.29), calls=%async_computation.2 | async-start | bytes 1048576 | tf_op jit(solution)/shard_map/all_to_all | solution.py:107
  78.7 0.2 fusion.18
  78.8 23.5 %all-to-all-done.2 = bf16[4,64,1024]{2,1,0:T(8,128)(2,1)S(1)} async-done(((bf16[4,64,1024]{2,1,0:T(8,128)(2,1)}), bf16[4,64,1024]{2,1,0:T(8,128)(2,1)S(1)}, u32[]{:S(2)}, u32[]{:S(2)}) %all-to-all-start.2) | async-done | bytes 524320 | tf_op jit(solution)/shard_map/all_to_all | solution.py:107
  102.3 0.5 convolution_convert_fusion.2
  102.8 0.2 reshape.168
  103.0 0.6 fusion
  103.6 0.7 fusion.3
  104.3 0.7 fusion.7
  105.0 5.7 %all-gather.3.cloned.1.call-done = bf16[1024,2048]{1,0:T(8,128)(2,1)} async-done(((bf16[1024,512]{1,0:T(8,128)(2,1)}), bf16[1024,2048]{1,0:T(8,128)(2,1)}) %all-gather.3.cloned.1.call-update) | async-done | bytes 4194320 | tf_op jit(solution)/shard_map/all_gather | solution.py:137
  110.7 3.7 %convolution_convert_fusion = bf16[128,2048]{1,0:T(8,128)(2,1)} fusion(bf16[128,1024]{0,1:T(8,128)(2,1)S(1)} %bitcast.62, bf16[1024,2048]{1,0:T(8,128)(2,1)} %all-gather.3.cloned.1.call-done), kind=kOutput, calls=%fused_computation | convolution fusion | flops 537133056 | bytes 4980736 | tf_op jit(solution)/shard_map/dot_general | solution.py:135
  114.5 20.9 %reduce-scatter.2.cloned.1.call-done = bf16[32,2048]{1,0:T(8,128)(2,1)} async-done(((bf16[128,2048]{1,0:T(8,128)(2,1)}), bf16[32,2048]{1,0:T(8,128)(2,1)}) %reduce-scatter.2.cloned.1.call-update) | async-done | bytes 131088 | tf_op jit(solution)/shard_map/reduce_scatter | solution.py:140
  (29 shorter events, 1.2 us)
Async XLA Ops:
  6.5 9.2 %copy-start = (bf16[128,1024]{1,0:T(8,128)(2,1)S(1)}, bf16[128,1024]{1,0:T(8,128)(2,1)}, u32[]{:S(2)}) copy-start(bf16[128,1024]{1,0:T(8,128)(2,1)} %param.7) | copy-start | bytes 786436
  6.5 10.8 %copy-start.2 = (bf16[128,256]{1,0:T(8,128)(2,1)S(1)}, bf16[128,256]{1,0:T(8,128)(2,1)}, u32[]{:S(2)}) copy-start(bf16[128,256]{1,0:T(8,128)(2,1)} %param.8) | copy-start | bytes 196612
  6.5 10.9 %copy-start.1 = (bf16[128,256]{1,0:T(8,128)(2,1)S(1)}, bf16[128,256]{1,0:T(8,128)(2,1)}, u32[]{:S(2)}) copy-start(bf16[128,256]{1,0:T(8,128)(2,1)} %param.9) | copy-start | bytes 196612
  6.5 29.5 %copy-start.3 = (s32[128]{0:T(128)S(1)}, s32[128]{0:T(128)}, u32[]{:S(2)}) copy-start(s32[128]{0:T(128)} %param.11) | copy-start | bytes 1540
  6.5 104.2 %all-gather.3.cloned.1.call-start = ((), (), s32[]{:S(2)}) async-start(), calls=%async_computation.4 | async-start | bytes 5242880 | tf_op jit(solution)/shard_map/all_gather | solution.py:137
  8.7 55.9 %all-to-all-start = ((s32[4,1,2]{2,1,0:T(1,128)}), s32[4,1,2]{2,1,0:T(1,128)S(1)}, u32[]{:S(2)}, u32[]{:S(2)}) async-start(s32[4,1,2]{2,1,0:T(1,128)} %copy.25), calls=%async_computation | async-start | bytes 4096 | tf_op jit(solution)/shard_map/all_to_all | solution.py:108
  64.7 10.1 %all-to-all-start.1 = ((s32[4,1,64]{2,1,0:T(1,128)}), s32[4,1,64]{2,1,0:T(1,128)S(1)}, u32[]{:S(2)}, u32[]{:S(2)}) async-start(s32[4,1,64]{2,1,0:T(1,128)} %bitcast.7), calls=%async_computation.1 | async-start | bytes 4096 | tf_op jit(solution)/shard_map/all_to_all | solution.py:109
  74.8 27.5 %all-to-all-start.2 = ((bf16[4,64,1024]{2,1,0:T(8,128)(2,1)}), bf16[4,64,1024]{2,1,0:T(8,128)(2,1)S(1)}, u32[]{:S(2)}, u32[]{:S(2)}) async-start(bf16[4,64,1024]{2,1,0:T(8,128)(2,1)} %copy.29), calls=%async_computation.2 | async-start | bytes 1048576 | tf_op jit(solution)/shard_map/all_to_all | solution.py:107
  78.3 57.1 %reduce-scatter.2.cloned.1.call-start = ((), (), s32[]{:S(2)}) async-start(), calls=%async_computation.5 | async-start | bytes 655360 | tf_op jit(solution)/shard_map/reduce_scatter | solution.py:140
Sparse Core Ops, SparseCore 0:
  8.9 101.7 all-gather.2
  114.6 20.7 reduce-scatter.1
where the time goes:
time: 143 us; the launch traced here: 142 us
  waiting for transfers between devices  56.2 us (39%)
  blocking collectives  46.3 us (32%)
  starting transfers between devices  14.4 us (10%)
  between operations  13.5 us (9%)
  matrix products  6.07 us (4%)
  local copies, waits for them, and re-layouts  3.09 us (2%)
  other arithmetic  2.63 us (2%)
    all_to_all x1, waiting for transfers between devices, shards(): lax.all_to_all(send_rows, 'ctx', split_axis=0, concat_axis=0, tiled=True)  23.5 us
    reduce_scatter x1, waiting for transfers between devices, shards(): lax.psum_scatter(partial_out.astype(jnp.bfloat16), 'tp', scatter_dimensio...  20.9 us
    all_gather x1, blocking collectives, shards(): lax.all_gather(value_rows, 'ctx', axis=0, tiled=True)  18.4 us
    all_gather x1, blocking collectives, shards(): lax.all_gather(key_rows, 'ctx', axis=0, tiled=True)  16.5 us
    all_gather x1, blocking collectives, shards(): lax.all_gather(doc_end, 'ctx', axis=0, tiled=True)  11.4 us
    all_to_all x1, starting transfers between devices, shards(): lax.all_to_all(send_info, 'ctx', split_axis=0, concat_axis=0, tiled=True)  6.32 us
    all_gather x1, waiting for transfers between devices, shards(): lax.all_gather(out_weight, 'ctx', axis=1, tiled=True)  5.74 us
    all_to_all x1, waiting for transfers between devices, shards(): lax.all_to_all(send_start, 'ctx', split_axis=0, concat_axis=0, tiled=True)  5.37 us
  transfers between devices with their start and end apart: 5, of which 4 were waited for; matrix products, arithmetic and copies ran while one was open for 6% of the time, Pallas kernels for 0%

commit v1 on v0

v1 whole, which is shorter than its diff:
```python
import functools
import math

import jax
import jax.numpy as jnp
from jax import lax
from jax.experimental import pallas as pl
from jax.experimental.pallas import tpu as pltpu
from jax.sharding import PartitionSpec as P

HEAD_DIM = 128
NEG_LARGE = -1e30


def vmem(count):
    return [pl.BlockSpec(memory_space=pltpu.VMEM)] * count


def smem(count):
    return [pl.BlockSpec(memory_space=pltpu.SMEM)] * count


def params():
    return pltpu.CompilerParams(vmem_limit_bytes=16 * 1024 * 1024)


def cost(flops, moved):
    return pl.CostEstimate(flops=int(flops), bytes_accessed=int(moved), transcendentals=0)


def column(row):
    size = row.shape[1]
    return jnp.transpose(jnp.broadcast_to(row, (size, size)))


def attend_kernel(blocks, q_ref, kh_ref, ko_ref, vh_ref, vo_ref, st_ref, eh_ref, eo_ref, out_ref):
    rows = q_ref.shape[0]
    kv_here = ko_ref.shape[1] // HEAD_DIM
    group = q_ref.shape[1] // HEAD_DIM // kv_here
    core = lax.axis_index("tp") % 2
    base = lax.axis_index("ctx") * rows
    half = rows // blocks // 2
    query_pos = base + lax.broadcasted_iota(jnp.int32, (rows, rows), 0)
    query_start = column(st_ref[...])
    masks = []
    for shift, end_ref in ((rows, eh_ref), (0, eo_ref)):
        key_pos = base - shift + lax.broadcasted_iota(jnp.int32, (rows, rows), 1)
        masks.append(
            (key_pos <= query_pos) & (key_pos >= query_start) & (end_ref[...] > query_pos)
        )
    visible = jnp.concatenate(masks, axis=1)
    visible = jnp.concatenate([visible] * group, axis=0)
    for kv in range(kv_here):
        lanes = pl.ds(kv * HEAD_DIM, HEAD_DIM)
        keys = jnp.concatenate([kh_ref[:, lanes], ko_ref[:, lanes]], axis=0)
        values = jnp.concatenate([vh_ref[:, lanes], vo_ref[:, lanes]], axis=0)
        query = jnp.concatenate(
            [q_ref[:, pl.ds((kv * group + g) * HEAD_DIM, HEAD_DIM)] for g in range(group)], axis=0
        )
        scores = (
            lax.dot_general(
                query, keys, (((1,), (1,)), ((), ())), preferred_element_type=jnp.float32
            )
            * HEAD_DIM**-0.5
        )
        row_max = jnp.max(jnp.where(visible, scores, NEG_LARGE), axis=1, keepdims=True)
        weights = jnp.where(visible, jnp.exp(scores - row_max), 0.0)
        weight_sum = jnp.sum(weights, axis=1, keepdims=True)
        summed = jnp.dot(
            weights.astype(jnp.bfloat16), values, preferred_element_type=jnp.float32
        )
        attended = (summed / weight_sum).astype(jnp.bfloat16)
        for g in range(group):
            for p in range(blocks):
                for h in range(2):
                    first = g * rows + (p * 2 + h) * half
                    place = pl.multiple_of((h ^ core) * (blocks * half) + p * half, half)
                    out_ref[pl.ds(place, half), pl.ds((kv * group + g) * HEAD_DIM, HEAD_DIM)] = (
                        attended[first : first + half]
                    )


def attend(blocks, queries, key_halo, key_own, value_halo, value_own, start, end_halo, end_own):
    rows = queries.shape[0]
    return pl.pallas_call(
        functools.partial(attend_kernel, blocks),
        out_shape=jax.ShapeDtypeStruct(queries.shape, jnp.bfloat16),
        in_specs=vmem(8),
        out_specs=pl.BlockSpec(memory_space=pltpu.VMEM),
        compiler_params=params(),
        cost_estimate=cost(8 * rows * rows * queries.shape[1], 6 * queries.size),
    )(queries, key_halo, key_own, value_halo, value_own, start, end_halo, end_own)


def project_kernel(chunk_count, *refs):
    chunks, weight_ref, mine_ref, other_ref = refs[:-3], refs[-3], refs[-2], refs[-1]
    rows = chunks[0].shape[0]
    half = rows // 2
    if chunk_count == 1 and len(chunks) == 2:
        place = lax.axis_index("ctx")
        inner = (place == 1) | (place == 2)
        stacked = jnp.where(inner, chunks[0][...], chunks[1][...])
    else:
        stacked = jnp.concatenate([c[...] for c in chunks], axis=0)
    share = jnp.dot(stacked, weight_ref[...], preferred_element_type=jnp.float32).astype(
        jnp.bfloat16
    )
    for n in range(chunk_count):
        mine_ref[pl.ds(n * half, half), :] = share[n * rows : n * rows + half]
        other_ref[pl.ds(n * half, half), :] = share[n * rows + half : (n + 1) * rows]


def project(chunk_count, chunks, weight):
    rows = chunks[0].shape[0] * chunk_count // 2
    out = jax.ShapeDtypeStruct((rows, weight.shape[1]), jnp.bfloat16)
    return pl.pallas_call(
        functools.partial(project_kernel, chunk_count),
        out_shape=(out, out),
        in_specs=vmem(len(chunks) + 1),
        out_specs=(pl.BlockSpec(memory_space=pltpu.VMEM),) * 2,
        compiler_params=params(),
        cost_estimate=cost(4 * rows * weight.size, 2 * weight.size),
    )(*chunks, weight)


def total_kernel(*refs):
    terms, out_ref = refs[:-1], refs[-1]
    out_ref[...] = sum(t[...].astype(jnp.float32) for t in terms).astype(out_ref.dtype)


def total(terms):
    return pl.pallas_call(
        total_kernel,
        out_shape=jax.ShapeDtypeStruct(terms[0].shape, jnp.bfloat16),
        in_specs=vmem(len(terms)),
        out_specs=pl.BlockSpec(memory_space=pltpu.VMEM),
        compiler_params=params(),
        cost_estimate=cost(4 * terms[0].size, 10 * terms[0].size),
    )(*terms)


def pick_kernel(blocks, *refs):
    targets, refs = refs[:4], refs[4:]
    own_ref, pair_ref, late_refs, outs, held = refs[0], refs[1], refs[2:6], refs[6:10], refs[10]
    half = own_ref.shape[0] // blocks
    x = lax.axis_index("tp") // 2
    c = lax.axis_index("ctx")
    late = sum(t[...].astype(jnp.float32) for t in late_refs).astype(jnp.bfloat16)
    held[pl.ds(0, blocks * half), :] = own_ref[...]
    held[pl.ds(blocks * half, blocks * half), :] = pair_ref[pl.ds(blocks * half, blocks * half), :]
    held[pl.ds(2 * blocks * half, blocks * half), :] = late
    held[pl.ds(3 * blocks * half, blocks * half), :] = pair_ref[pl.ds(0, blocks * half), :]
    for k in range(4):
        wanted = (c ^ k) * blocks + x
        where = jnp.int32(0)
        for d in range(4):
            for p in range(blocks):
                where = jnp.where(targets[d][p] == wanted, d * blocks + p, where)
        outs[k][...] = held[pl.ds(pl.multiple_of(where * half, half), half), :]


def pick(blocks, targets, own, pair, late):
    rows, cols = own.shape
    out = jax.ShapeDtypeStruct((rows // blocks, cols), jnp.bfloat16)
    return pl.pallas_call(
        functools.partial(pick_kernel, blocks),
        out_shape=(out,) * 4,
        in_specs=smem(4) + vmem(6),
        out_specs=(pl.BlockSpec(memory_space=pltpu.VMEM),) * 4,
        scratch_shapes=[pltpu.VMEM((4 * rows, cols), jnp.bfloat16)],
        compiler_params=params(),
        cost_estimate=cost(4 * own.size, 20 * own.size),
    )(*targets, own, pair, *late)


def join_kernel(*refs):
    pieces, out_ref = refs[:-1], refs[-1]
    cols = pieces[0].shape[1]
    c = lax.axis_index("ctx")
    for k in range(4):
        out_ref[:, pl.ds(pl.multiple_of((c ^ k) * cols, cols), cols)] = pieces[k][...]


def join(pieces):
    rows, cols = pieces[0].shape
    return pl.pallas_call(
        join_kernel,
        out_shape=jax.ShapeDtypeStruct((rows, 4 * cols), jnp.bfloat16),
        in_specs=vmem(4),
        out_specs=pl.BlockSpec(memory_space=pltpu.VMEM),
        compiler_params=params(),
        cost_estimate=cost(0, 16 * pieces[0].size),
    )(*pieces)


def flip(array, axis, bits, members=(0, 1, 2, 3)):
    return lax.ppermute(array, axis, [(i, i ^ bits) for i in members])


def tp_total(mine, other):
    return mine, flip(other, "tp", 1), flip(mine, "tp", 2), flip(other, "tp", 3)


def small_ring(queries, key_rows, value_rows, doc_start, doc_end, block_target, out_weight):
    rows = queries.shape[0]
    blocks = block_target.shape[0]
    following = [(0, 1), (1, 2), (2, 3)]
    ends = doc_end.reshape(1, rows)
    key_halo = lax.ppermute(key_rows, "ctx", following)
    value_halo = lax.ppermute(value_rows, "ctx", following)
    end_halo = lax.ppermute(ends, "ctx", following)
    attended = attend(
        blocks,
        queries,
        key_halo,
        key_rows,
        value_halo,
        value_rows,
        doc_start.reshape(1, rows),
        end_halo,
        ends,
    )
    got_3 = flip(attended, "ctx", 3)
    got_1 = flip(attended, "ctx", 1)
    got_2_inner = lax.ppermute(attended, "ctx", [(0, 2), (3, 1)])
    got_2_outer = lax.ppermute(got_3, "ctx", [(1, 0), (2, 3)])
    targets = [block_target] + [flip(block_target, "ctx", d) for d in (1, 2, 3)]
    own = total(tp_total(*project(1, (attended,), out_weight)))
    pair = total(tp_total(*project(2, (got_3, got_1), out_weight)))
    late = tp_total(*project(1, (got_2_inner, got_2_outer), out_weight))
    kept, *sent = pick(blocks, targets, own, pair, late)
    return join([kept] + [flip(sent[k - 1], "ctx", k) for k in (1, 2, 3)])


def attend_block(soft_state, query_grid, query_pos, query_start, key_block, value_block, key_end, key_pos):
    running_max, weight_sum, weighted = soft_state
    scores = jnp.einsum(
        "rkgd,nkd->rkgn", query_grid, key_block, preferred_element_type=jnp.float32
    ) * HEAD_DIM ** (-0.5)
    visible = (
        (key_pos[None, :] <= query_pos[:, None])
        & (key_pos[None, :] >= query_start[:, None])
        & (key_end[None, :] > query_pos[:, None])
    )
    visible = visible[:, None, None, :]
    new_max = jnp.maximum(running_max, jnp.max(jnp.where(visible, scores, NEG_LARGE), axis=-1))
    weights = jnp.where(visible, jnp.exp(scores - new_max[..., None]), 0.0)
    fading = jnp.exp(running_max - new_max)
    weight_sum = weight_sum * fading + jnp.sum(weights, axis=-1)
    weighted = weighted * fading[..., None] + jnp.einsum(
        "rkgn,nkd->rkgd",
        weights.astype(jnp.bfloat16),
        value_block,
        preferred_element_type=jnp.float32,
    )
    return (new_max, weight_sum, weighted)


def attend_all(queries, query_pos, query_start, key_part, value_part, end_part):
    rows = queries.shape[0]
    key_count = key_part.shape[0]
    kv_here = key_part.shape[1] // HEAD_DIM
    query_grid = queries.reshape(rows, kv_here, -1, HEAD_DIM)
    block_len = math.gcd(key_count, 512)
    block_count = key_count // block_len
    items = (
        key_part.reshape(block_count, block_len, kv_here, HEAD_DIM),
        value_part.reshape(block_count, block_len, kv_here, HEAD_DIM),
        end_part.reshape(block_count, block_len),
        jnp.arange(key_count, dtype=jnp.int32).reshape(block_count, block_len),
    )
    start_state = (
        jnp.full(query_grid.shape[:3], NEG_LARGE, jnp.float32),
        jnp.zeros(query_grid.shape[:3], jnp.float32),
        jnp.zeros(query_grid.shape, jnp.float32),
    )

    def one_block(state, item):
        return attend_block(state, query_grid, query_pos, query_start, *item), None

    (_, weight_sum, weighted), _ = lax.scan(one_block, start_state, items)
    return (weighted / weight_sum[..., None]).astype(jnp.bfloat16).reshape(rows, -1)


def any_ring(queries, key_rows, value_rows, doc_start, doc_end, block_target, out_weight):
    rows = queries.shape[0]
    blocks = block_target.shape[0]
    block_rows = rows // blocks
    ctx_count = lax.axis_size("ctx")
    tp_count = lax.axis_size("tp")
    gather = functools.partial(lax.all_gather, axis_name="ctx", axis=0, tiled=True)
    query_pos = lax.axis_index("ctx") * rows + jnp.arange(rows, dtype=jnp.int32)
    attended = attend_all(
        queries, query_pos, doc_start, gather(key_rows), gather(value_rows), gather(doc_end)
    )
    targets = gather(block_target)
    source = jnp.zeros_like(targets).at[targets].set(jnp.arange(targets.size, dtype=jnp.int32))
    source_rows = (source[:, None] * block_rows + jnp.arange(block_rows, dtype=jnp.int32)).reshape(-1)
    balanced = jnp.take(gather(attended), source_rows, axis=0)
    share = jnp.dot(balanced, out_weight, preferred_element_type=jnp.float32).astype(jnp.bfloat16)
    share = share.reshape(ctx_count, tp_count, rows // tp_count, -1)
    summed = lax.psum_scatter(share, "tp", scatter_dimension=1, tiled=True)
    pieces = lax.all_to_all(summed[:, 0], "ctx", split_axis=0, concat_axis=0, tiled=True)
    return jnp.swapaxes(pieces, 0, 1).reshape(rows // tp_count, -1)


def shards(queries, key_rows, value_rows, doc_start, doc_end, block_target, out_weight):
    ctx_count, tp_count = lax.axis_size("ctx"), lax.axis_size("tp")
    rows, blocks = queries.shape[0], block_target.shape[0]
    longest = rows * ctx_count // 2 - rows
    near = longest <= rows and ctx_count == 4 and tp_count == 4 and blocks == 2
    plan = small_ring if near and rows % (4 * blocks * 2) == 0 else any_ring
    return plan(queries, key_rows, value_rows, doc_start, doc_end, block_target, out_weight)


def solution(mesh):
    in_specs = (
        P(("group", "ctx"), "tp"),
        P(("group", "ctx"), "tp"),
        P(("group", "ctx"), "tp"),
        P(("group", "ctx")),
        P(("group", "ctx")),
        P(("group", "ctx")),
        P("tp", "ctx"),
    )
    out_specs = P(("group", "ctx", "tp"), None)
    return jax.shard_map(shards, mesh=mesh, in_specs=in_specs, out_specs=out_specs, check_vma=False)
```

time: 143 us -> 66.1 us (0.46)
  blocking collectives: 46.3 us -> 0 us
  waiting for transfers between devices: 56.2 us -> 23.1 us
  starting transfers between devices: 14.4 us -> 34.7 us
  between operations: 13.5 us -> 0.19 us
  matrix products: 6.07 us -> 0 us
  Pallas kernels: 0 us -> 3.11 us
  other arithmetic: 2.63 us -> 0 us
  local copies, waits for them, and re-layouts: 3.09 us -> 4.67 us
    all_gather x3 -> x0, blocking collectives: 46.3 us -> none  [the longest x1 18.4 us: shards(): lax.all_gather(value_rows, 'ctx', axis=0, tiled=True)]
    ppermute x0 -> x22, starting transfers between devices: none -> 34.7 us  [the longest x17 17.4 us: flip(): return lax.ppermute(array, axis, [(i, i ^ bits) for i in members])]
    all_to_all x3 -> x0, waiting for transfers between devices: 28.8 us -> none  [the longest x1 23.5 us: shards(): lax.all_to_all(send_rows, 'ctx', split_axis=0, concat_axis=0, tiled=True)]
    ppermute x0 -> x22, waiting for transfers between devices: none -> 23.1 us  [the longest x17 17.5 us: flip(): return lax.ppermute(array, axis, [(i, i ^ bits) for i in members])]
    reduce_scatter x1 -> x0, waiting for transfers between devices: 20.9 us -> none  [shards(): lax.psum_scatter(partial_out.astype(jnp.bfloat16), 'tp', scatter_dimensio...]
    all_to_all x3 -> x0, starting transfers between devices: 14.3 us -> none  [the longest x1 6.32 us: shards(): lax.all_to_all(send_info, 'ctx', split_axis=0, concat_axis=0, tiled=True)]
    dot_general x5 -> x0, matrix products: 6.07 us -> none  [the longest x1 3.73 us: shards(): jnp.dot(attended, lax.all_gather(out_weight, 'ctx', axis=1, tiled=True),...]
    all_gather x1 -> x0, waiting for transfers between devices: 5.74 us -> none  [shards(): lax.all_gather(out_weight, 'ctx', axis=1, tiled=True)]
  transfers between devices with their start and end apart: 5 -> 22, of which waited for: 4 -> 10; matrix products, arithmetic and copies ran while one was open for 6% -> 0% of each run, Pallas kernels for 0% -> 2%
where the time goes in v1:
time: 66.1 us; the launch traced here: 65.7 us
  starting transfers between devices  34.7 us (52%)
  waiting for transfers between devices  23.1 us (35%)
  local copies, waits for them, and re-layouts  4.67 us (7%)
  Pallas kernels  3.11 us (5%)
    ppermute x17, waiting for transfers between devices, flip(): return lax.ppermute(array, axis, [(i, i ^ bits) for i in members])  17.5 us
    ppermute x17, starting transfers between devices, flip(): return lax.ppermute(array, axis, [(i, i ^ bits) for i in members])  17.4 us
    ppermute x1, starting transfers between devices, small_ring(): key_halo = lax.ppermute(key_rows, 'ctx', following)  5.05 us
    unnamed x16, local copies, waits for them, and re-layouts  4.67 us
    ppermute x1, waiting for transfers between devices, small_ring(): got_2_outer = lax.ppermute(got_3, 'ctx', [(1, 0), (2, 3)])  4.31 us
    ppermute x1, starting transfers between devices, small_ring(): got_2_inner = lax.ppermute(attended, 'ctx', [(0, 2), (3, 1)])  3.97 us
    ppermute x1, starting transfers between devices, small_ring(): value_halo = lax.ppermute(value_rows, 'ctx', following)  3.48 us
    ppermute x1, starting transfers between devices, small_ring(): end_halo = lax.ppermute(ends, 'ctx', following)  3.48 us
  transfers between devices with their start and end apart: 22, of which 10 were waited for; matrix products, arithmetic and copies ran while one was open for 0% of the time, Pallas kernels for 2%

profile of v1, /device:TPU:0, one launch (start us, length us, event | category | flops | bytes accessed | tf_op | source)
XLA Modules:
  0.0 65.7 jit_solution(2570126584126383348)
XLA Ops:
  0.0 5.0 %collective-permute-start.3 = (bf16[128,256]{1,0:T(8,128)(2,1)}, bf16[128,256]{1,0:T(8,128)(2,1)S(1)}, u32[]{:S(2)}, u32[]{:S(2)}) collective-permute-start(bf16[128,256]{1,0:T(8,128)(2,1)} %ko_ref.1), channel_id=1, source_target_pairs={{0,4},{4,8},{8,12},{1,5},{5,9},{9,13},{2,6},{6,10},{10,14},{3,7},{... | collective-permute-start | bytes 196616 | tf_op jit(solution)/shard_map/ppermute | solution.py:209
  5.1 3.5 %collective-permute-start.4 = (bf16[128,256]{1,0:T(8,128)(2,1)}, bf16[128,256]{1,0:T(8,128)(2,1)S(1)}, u32[]{:S(2)}, u32[]{:S(2)}) collective-permute-start(bf16[128,256]{1,0:T(8,128)(2,1)} %vo_ref.1), channel_id=1, source_target_pairs={{0,4},{4,8},{8,12},{1,5},{5,9},{9,13},{2,6},{6,10},{10,14},{3,7},{... | collective-permute-start | bytes 196616 | tf_op jit(solution)/shard_map/ppermute | solution.py:210
  8.6 3.5 %collective-permute-start.5 = (s32[1,128]{1,0:T(1,128)S(1)}, s32[1,128]{1,0:T(1,128)S(1)}, u32[]{:S(2)}, u32[]{:S(2)}) collective-permute-start(s32[1,128]{1,0:T(1,128)S(1)} %bitcast.3), channel_id=1, source_target_pairs={{0,4},{4,8},{8,12},{1,5},{5,9},{9,13},{2,6},{6,10},{10,14},{3,7},{... | collective-permute-start | bytes 1544 | tf_op jit(solution)/shard_map/ppermute | solution.py:211
  12.1 1.3 %collective-permute-done.5.eh_ref = s32[1,128]{1,0:T(1,128)S(1)} collective-permute-done((s32[1,128]{1,0:T(1,128)S(1)}, s32[1,128]{1,0:T(1,128)S(1)}, u32[]{:S(2)}, u32[]{:S(2)}) %collective-permute-start.5) | collective-permute-done | bytes 544 | tf_op jit(solution)/shard_map/ppermute | solution.py:211
  16.7 1.2 %collective-permute-start.9 = (bf16[128,1024]{1,0:T(8,128)(2,1)S(1)}, bf16[128,1024]{1,0:T(8,128)(2,1)S(1)}, u32[]{:S(2)}, u32[]{:S(2)}) collective-permute-start(bf16[128,1024]{1,0:T(8,128)(2,1)S(1)} %shard_map.73.refs_0_), channel_id=1, source_target_pairs={{0,12},{4,8},{8,4},{12,0},{1,13},{5,9},{9,5},{13,1},{2,14},{6,10},... | collective-permute-start | bytes 786440 | tf_op jit(solution)/shard_map/ppermute | solution.py:197
  17.9 1.2 %collective-permute-start.10 = (bf16[128,1024]{1,0:T(8,128)(2,1)S(1)}, bf16[128,1024]{1,0:T(8,128)(2,1)S(1)}, u32[]{:S(2)}, u32[]{:S(2)}) collective-permute-start(bf16[128,1024]{1,0:T(8,128)(2,1)S(1)} %shard_map.73.refs_0_), channel_id=1, source_target_pairs={{0,4},{4,0},{8,12},{12,8},{1,5},{5,1},{9,13},{13,9},{2,6},{6,2},{1... | collective-permute-start | bytes 786440 | tf_op jit(solution)/shard_map/ppermute | solution.py:197
  19.1 4.0 %collective-permute-start.14 = (bf16[128,1024]{1,0:T(8,128)(2,1)S(1)}, bf16[128,1024]{1,0:T(8,128)(2,1)S(1)}, u32[]{:S(2)}, u32[]{:S(2)}) collective-permute-start(bf16[128,1024]{1,0:T(8,128)(2,1)S(1)} %shard_map.73.refs_0_), channel_id=1, source_target_pairs={{0,8},{12,4},{1,9},{13,5},{2,10},{14,6},{3,11},{15,7},{16,24},{28,... | collective-permute-start | bytes 786440 | tf_op jit(solution)/shard_map/ppermute | solution.py:225
  23.0 4.7 %collective-permute-done.9.refs_0_ = bf16[128,1024]{1,0:T(8,128)(2,1)S(1)} collective-permute-done((bf16[128,1024]{1,0:T(8,128)(2,1)S(1)}, bf16[128,1024]{1,0:T(8,128)(2,1)S(1)}, u32[]{:S(2)}, u32[]{:S(2)}) %collective-permute-start.9) | collective-permute-done | bytes 262176 | tf_op jit(solution)/shard_map/ppermute | solution.py:197
  27.8 1.3 %collective-permute-start.15 = (bf16[128,1024]{1,0:T(8,128)(2,1)S(1)}, bf16[128,1024]{1,0:T(8,128)(2,1)S(1)}, u32[]{:S(2)}, u32[]{:S(2)}) collective-permute-start(bf16[128,1024]{1,0:T(8,128)(2,1)S(1)} %collective-permute-done.9.refs_0_), channel_id=1, source_target_pairs={{4,0},{8,12},{5,1},{9,13},{6,2},{10,14},{7,3},{11,15},{20,16},{24,... | collective-permute-start | bytes 786440 | tf_op jit(solution)/shard_map/ppermute | solution.py:226
  29.1 1.2 %copy-done = bf16[1024,512]{1,0:T(8,128)(2,1)S(1)} copy-done((bf16[1024,512]{1,0:T(8,128)(2,1)S(1)}, bf16[1024,512]{1,0:T(8,128)(2,1)}, u32[]{:S(2)}) %copy-start) | copy-done | bytes 1048600
  32.0 1.6 %collective-permute-start.12 = (bf16[128,512]{1,0:T(8,128)(2,1)S(1)}, bf16[128,512]{1,0:T(8,128)(2,1)S(1)}, u32[]{:S(2)}, u32[]{:S(2)}) collective-permute-start(bf16[128,512]{1,0:T(8,128)(2,1)S(1)} %get-tuple-element.17.refs_0_), channel_id=1, source_target_pairs={{0,2},{1,3},{2,0},{3,1},{4,6},{5,7},{6,4},{7,5},{8,10},{9,11},{10,... | collective-permute-start | bytes 393224 | tf_op jit(solution)/shard_map/ppermute | solution.py:197
  33.9 1.5 %collective-permute-start.7 = (bf16[64,512]{1,0:T(8,128)(2,1)S(1)}, bf16[64,512]{1,0:T(8,128)(2,1)S(1)}, u32[]{:S(2)}, u32[]{:S(2)}) collective-permute-start(bf16[64,512]{1,0:T(8,128)(2,1)S(1)} %get-tuple-element.15.refs_0_), channel_id=1, source_target_pairs={{0,2},{1,3},{2,0},{3,1},{4,6},{5,7},{6,4},{7,5},{8,10},{9,11},{10,... | collective-permute-start | bytes 196616 | tf_op jit(solution)/shard_map/ppermute | solution.py:197
  35.4 4.3 %collective-permute-done.15.refs_1_ = bf16[128,1024]{1,0:T(8,128)(2,1)S(1)} collective-permute-done((bf16[128,1024]{1,0:T(8,128)(2,1)S(1)}, bf16[128,1024]{1,0:T(8,128)(2,1)S(1)}, u32[]{:S(2)}, u32[]{:S(2)}) %collective-permute-start.15) | collective-permute-done | bytes 262176 | tf_op jit(solution)/shard_map/ppermute | solution.py:226
  40.0 2.1 %collective-permute-done.7.refs_2_ = bf16[64,512]{1,0:T(8,128)(2,1)S(1)} collective-permute-done((bf16[64,512]{1,0:T(8,128)(2,1)S(1)}, bf16[64,512]{1,0:T(8,128)(2,1)S(1)}, u32[]{:S(2)}, u32[]{:S(2)}) %collective-permute-start.7) | collective-permute-done | bytes 65568 | tf_op jit(solution)/shard_map/ppermute | solution.py:197
  42.2 1.9 %collective-permute-done.8.refs_3_ = bf16[64,512]{1,0:T(8,128)(2,1)S(1)} collective-permute-done((bf16[64,512]{1,0:T(8,128)(2,1)S(1)}, bf16[64,512]{1,0:T(8,128)(2,1)S(1)}, u32[]{:S(2)}, u32[]{:S(2)}) %collective-permute-start.8) | collective-permute-done | bytes 65568 | tf_op jit(solution)/shard_map/ppermute | solution.py:197
  44.1 1.0 %collective-permute-start.17 = (bf16[64,512]{1,0:T(8,128)(2,1)S(1)}, bf16[64,512]{1,0:T(8,128)(2,1)S(1)}, u32[]{:S(2)}, u32[]{:S(2)}) collective-permute-start(bf16[64,512]{1,0:T(8,128)(2,1)S(1)} %get-tuple-element.19.refs_6_), channel_id=1, source_target_pairs={{0,2},{1,3},{2,0},{3,1},{4,6},{5,7},{6,4},{7,5},{8,10},{9,11},{10,... | collective-permute-start | bytes 196616 | tf_op jit(solution)/shard_map/ppermute | solution.py:197
  45.6 4.5 %collective-permute-start = (s32[2]{0:T(128)S(1)}, s32[2]{0:T(128)S(1)}, u32[]{:S(2)}, u32[]{:S(2)}) collective-permute-start(s32[2]{0:T(128)S(1)} %copy-done.5), channel_id=1, source_target_pairs={{0,4},{4,0},{8,12},{12,8},{1,5},{5,1},{9,13},{13,9},{2,6},{6,2},{1... | collective-permute-start | bytes 32 | tf_op jit(solution)/shard_map/ppermute | solution.py:197
  50.2 1.4 %collective-permute-done.refs_1_ = s32[2]{0:T(128)S(1)} collective-permute-done((s32[2]{0:T(128)S(1)}, s32[2]{0:T(128)S(1)}, u32[]{:S(2)}, u32[]{:S(2)}) %collective-permute-start) | collective-permute-done | bytes 40 | tf_op jit(solution)/shard_map/ppermute | solution.py:197
  51.7 1.1 %collective-permute-start.2 = (s32[2]{0:T(128)S(1)}, s32[2]{0:T(128)S(1)}, u32[]{:S(2)}, u32[]{:S(2)}) collective-permute-start(s32[2]{0:T(128)S(1)} %copy-done.5), channel_id=1, source_target_pairs={{0,12},{4,8},{8,4},{12,0},{1,13},{5,9},{9,5},{13,1},{2,14},{6,10},... | collective-permute-start | bytes 32 | tf_op jit(solution)/shard_map/ppermute | solution.py:197
  52.7 1.8 %collective-permute-done.1.refs_2_ = s32[2]{0:T(128)S(1)} collective-permute-done((s32[2]{0:T(128)S(1)}, s32[2]{0:T(128)S(1)}, u32[]{:S(2)}, u32[]{:S(2)}) %collective-permute-start.1) | collective-permute-done | bytes 40 | tf_op jit(solution)/shard_map/ppermute | solution.py:197
  54.6 2.4 %collective-permute-done.2.refs_3_ = s32[2]{0:T(128)S(1)} collective-permute-done((s32[2]{0:T(128)S(1)}, s32[2]{0:T(128)S(1)}, u32[]{:S(2)}, u32[]{:S(2)}) %collective-permute-start.2) | collective-permute-done | bytes 40 | tf_op jit(solution)/shard_map/ppermute | solution.py:197
  57.9 1.4 %collective-permute-start.20 = (bf16[32,512]{1,0:T(8,128)(2,1)S(1)}, bf16[32,512]{1,0:T(8,128)(2,1)S(1)}, u32[]{:S(2)}, u32[]{:S(2)}) collective-permute-start(bf16[32,512]{1,0:T(8,128)(2,1)S(1)} %get-tuple-element.23), channel_id=1, source_target_pairs={{0,8},{4,12},{8,0},{12,4},{1,9},{5,13},{9,1},{13,5},{2,10},{6,14},... | collective-permute-start | bytes 98312 | tf_op jit(solution)/shard_map/ppermute | solution.py:197
  59.3 2.7 %collective-permute-start.21 = (bf16[32,512]{1,0:T(8,128)(2,1)S(1)}, bf16[32,512]{1,0:T(8,128)(2,1)S(1)}, u32[]{:S(2)}, u32[]{:S(2)}) collective-permute-start(bf16[32,512]{1,0:T(8,128)(2,1)S(1)} %get-tuple-element.24), channel_id=1, source_target_pairs={{0,12},{4,8},{8,4},{12,0},{1,13},{5,9},{9,5},{13,1},{2,14},{6,10},... | collective-permute-start | bytes 98312 | tf_op jit(solution)/shard_map/ppermute | solution.py:197
  63.0 2.1 %collective-permute-done.21.refs_3_ = bf16[32,512]{1,0:T(8,128)(2,1)S(1)} collective-permute-done((bf16[32,512]{1,0:T(8,128)(2,1)S(1)}, bf16[32,512]{1,0:T(8,128)(2,1)S(1)}, u32[]{:S(2)}, u32[]{:S(2)}) %collective-permute-start.21) | collective-permute-done | bytes 32800 | tf_op jit(solution)/shard_map/ppermute | solution.py:197
  (44 shorter events, 8.7 us)
Async XLA Ops:
  0.0 8.6 %copy-start.7 = (s32[128]{0:T(128)S(1)}, s32[128]{0:T(128)}, u32[]{:S(2)}) copy-start(s32[128]{0:T(128)} %param.11) | copy-start | bytes 1540
  0.0 13.3 %collective-permute-start.3 = (bf16[128,256]{1,0:T(8,128)(2,1)}, bf16[128,256]{1,0:T(8,128)(2,1)S(1)}, u32[]{:S(2)}, u32[]{:S(2)}) collective-permute-start(bf16[128,256]{1,0:T(8,128)(2,1)} %ko_ref.1), channel_id=1, source_target_pairs={{0,4},{4,8},{8,12},{1,5},{5,9},{9,13},{2,6},{6,10},{10,14},{3,7},{... | collective-permute-start | bytes 196616 | tf_op jit(solution)/shard_map/ppermute | solution.py:209
  5.1 8.3 %collective-permute-start.4 = (bf16[128,256]{1,0:T(8,128)(2,1)}, bf16[128,256]{1,0:T(8,128)(2,1)S(1)}, u32[]{:S(2)}, u32[]{:S(2)}) collective-permute-start(bf16[128,256]{1,0:T(8,128)(2,1)} %vo_ref.1), channel_id=1, source_target_pairs={{0,4},{4,8},{8,12},{1,5},{5,9},{9,13},{2,6},{6,10},{10,14},{3,7},{... | collective-permute-start | bytes 196616 | tf_op jit(solution)/shard_map/ppermute | solution.py:210
  8.6 4.8 %copy-start.6 = (s32[128]{0:T(128)S(1)}, s32[128]{0:T(128)}, u32[]{:S(2)}) copy-start(s32[128]{0:T(128)} %param.10) | copy-start | bytes 1540
  8.6 4.8 %collective-permute-start.5 = (s32[1,128]{1,0:T(1,128)S(1)}, s32[1,128]{1,0:T(1,128)S(1)}, u32[]{:S(2)}, u32[]{:S(2)}) collective-permute-start(s32[1,128]{1,0:T(1,128)S(1)} %bitcast.3), channel_id=1, source_target_pairs={{0,4},{4,8},{8,12},{1,5},{5,9},{9,13},{2,6},{6,10},{10,14},{3,7},{... | collective-permute-start | bytes 1544 | tf_op jit(solution)/shard_map/ppermute | solution.py:211
  16.7 11.1 %collective-permute-start.9 = (bf16[128,1024]{1,0:T(8,128)(2,1)S(1)}, bf16[128,1024]{1,0:T(8,128)(2,1)S(1)}, u32[]{:S(2)}, u32[]{:S(2)}) collective-permute-start(bf16[128,1024]{1,0:T(8,128)(2,1)S(1)} %shard_map.73.refs_0_), channel_id=1, source_target_pairs={{0,12},{4,8},{8,4},{12,0},{1,13},{5,9},{9,5},{13,1},{2,14},{6,10},... | collective-permute-start | bytes 786440 | tf_op jit(solution)/shard_map/ppermute | solution.py:197
  17.9 12.8 %collective-permute-start.10 = (bf16[128,1024]{1,0:T(8,128)(2,1)S(1)}, bf16[128,1024]{1,0:T(8,128)(2,1)S(1)}, u32[]{:S(2)}, u32[]{:S(2)}) collective-permute-start(bf16[128,1024]{1,0:T(8,128)(2,1)S(1)} %shard_map.73.refs_0_), channel_id=1, source_target_pairs={{0,4},{4,0},{8,12},{12,8},{1,5},{5,1},{9,13},{13,9},{2,6},{6,2},{1... | collective-permute-start | bytes 786440 | tf_op jit(solution)/shard_map/ppermute | solution.py:197
  19.1 14.9 %collective-permute-start.14 = (bf16[128,1024]{1,0:T(8,128)(2,1)S(1)}, bf16[128,1024]{1,0:T(8,128)(2,1)S(1)}, u32[]{:S(2)}, u32[]{:S(2)}) collective-permute-start(bf16[128,1024]{1,0:T(8,128)(2,1)S(1)} %shard_map.73.refs_0_), channel_id=1, source_target_pairs={{0,8},{12,4},{1,9},{13,5},{2,10},{14,6},{3,11},{15,7},{16,24},{28,... | collective-permute-start | bytes 786440 | tf_op jit(solution)/shard_map/ppermute | solution.py:225
  27.8 11.9 %collective-permute-start.15 = (bf16[128,1024]{1,0:T(8,128)(2,1)S(1)}, bf16[128,1024]{1,0:T(8,128)(2,1)S(1)}, u32[]{:S(2)}, u32[]{:S(2)}) collective-permute-start(bf16[128,1024]{1,0:T(8,128)(2,1)S(1)} %collective-permute-done.9.refs_0_), channel_id=1, source_target_pairs={{4,0},{8,12},{5,1},{9,13},{6,2},{10,14},{7,3},{11,15},{20,16},{24,... | collective-permute-start | bytes 786440 | tf_op jit(solution)/shard_map/ppermute | solution.py:226
  30.6 3.0 %collective-permute-start.6 = (bf16[64,512]{1,0:T(8,128)(2,1)S(1)}, bf16[64,512]{1,0:T(8,128)(2,1)S(1)}, u32[]{:S(2)}, u32[]{:S(2)}) collective-permute-start(bf16[64,512]{1,0:T(8,128)(2,1)S(1)} %get-tuple-element.16), channel_id=1, source_target_pairs={{0,1},{1,0},{2,3},{3,2},{4,5},{5,4},{6,7},{7,6},{8,9},{9,8},{10,11... | collective-permute-start | bytes 196616 | tf_op jit(solution)/shard_map/ppermute | solution.py:197
  32.0 13.1 %collective-permute-start.11 = (bf16[128,512]{1,0:T(8,128)(2,1)S(1)}, bf16[128,512]{1,0:T(8,128)(2,1)S(1)}, u32[]{:S(2)}, u32[]{:S(2)}) collective-permute-start(bf16[128,512]{1,0:T(8,128)(2,1)S(1)} %get-tuple-element.18), channel_id=1, source_target_pairs={{0,1},{1,0},{2,3},{3,2},{4,5},{5,4},{6,7},{7,6},{8,9},{9,8},{10,11... | collective-permute-start | bytes 393224 | tf_op jit(solution)/shard_map/ppermute | solution.py:197
  32.0 13.5 %collective-permute-start.12 = (bf16[128,512]{1,0:T(8,128)(2,1)S(1)}, bf16[128,512]{1,0:T(8,128)(2,1)S(1)}, u32[]{:S(2)}, u32[]{:S(2)}) collective-permute-start(bf16[128,512]{1,0:T(8,128)(2,1)S(1)} %get-tuple-element.17.refs_0_), channel_id=1, source_target_pairs={{0,2},{1,3},{2,0},{3,1},{4,6},{5,7},{6,4},{7,5},{8,10},{9,11},{10,... | collective-permute-start | bytes 393224 | tf_op jit(solution)/shard_map/ppermute | solution.py:197
  33.6 16.5 %collective-permute-start.13 = (bf16[128,512]{1,0:T(8,128)(2,1)S(1)}, bf16[128,512]{1,0:T(8,128)(2,1)S(1)}, u32[]{:S(2)}, u32[]{:S(2)}) collective-permute-start(bf16[128,512]{1,0:T(8,128)(2,1)S(1)} %get-tuple-element.18), channel_id=1, source_target_pairs={{0,3},{1,2},{2,1},{3,0},{4,7},{5,6},{6,5},{7,4},{8,11},{9,10},{10,... | collective-permute-start | bytes 393224 | tf_op jit(solution)/shard_map/ppermute | solution.py:197
  33.9 8.2 %collective-permute-start.7 = (bf16[64,512]{1,0:T(8,128)(2,1)S(1)}, bf16[64,512]{1,0:T(8,128)(2,1)S(1)}, u32[]{:S(2)}, u32[]{:S(2)}) collective-permute-start(bf16[64,512]{1,0:T(8,128)(2,1)S(1)} %get-tuple-element.15.refs_0_), channel_id=1, source_target_pairs={{0,2},{1,3},{2,0},{3,1},{4,6},{5,7},{6,4},{7,5},{8,10},{9,11},{10,... | collective-permute-start | bytes 196616 | tf_op jit(solution)/shard_map/ppermute | solution.py:197
  39.7 4.3 %collective-permute-start.8 = (bf16[64,512]{1,0:T(8,128)(2,1)S(1)}, bf16[64,512]{1,0:T(8,128)(2,1)S(1)}, u32[]{:S(2)}, u32[]{:S(2)}) collective-permute-start(bf16[64,512]{1,0:T(8,128)(2,1)S(1)} %get-tuple-element.16), channel_id=1, source_target_pairs={{0,3},{1,2},{2,1},{3,0},{4,7},{5,6},{6,5},{7,4},{8,11},{9,10},{10,... | collective-permute-start | bytes 196616 | tf_op jit(solution)/shard_map/ppermute | solution.py:197
  42.2 14.8 %collective-permute-start.16 = (bf16[64,512]{1,0:T(8,128)(2,1)S(1)}, bf16[64,512]{1,0:T(8,128)(2,1)S(1)}, u32[]{:S(2)}, u32[]{:S(2)}) collective-permute-start(bf16[64,512]{1,0:T(8,128)(2,1)S(1)} %get-tuple-element.20), channel_id=1, source_target_pairs={{0,1},{1,0},{2,3},{3,2},{4,5},{5,4},{6,7},{7,6},{8,9},{9,8},{10,11... | collective-permute-start | bytes 196616 | tf_op jit(solution)/shard_map/ppermute | solution.py:197
  44.1 12.9 %collective-permute-start.17 = (bf16[64,512]{1,0:T(8,128)(2,1)S(1)}, bf16[64,512]{1,0:T(8,128)(2,1)S(1)}, u32[]{:S(2)}, u32[]{:S(2)}) collective-permute-start(bf16[64,512]{1,0:T(8,128)(2,1)S(1)} %get-tuple-element.19.refs_6_), channel_id=1, source_target_pairs={{0,2},{1,3},{2,0},{3,1},{4,6},{5,7},{6,4},{7,5},{8,10},{9,11},{10,... | collective-permute-start | bytes 196616 | tf_op jit(solution)/shard_map/ppermute | solution.py:197
  45.1 11.9 %collective-permute-start.18 = (bf16[64,512]{1,0:T(8,128)(2,1)S(1)}, bf16[64,512]{1,0:T(8,128)(2,1)S(1)}, u32[]{:S(2)}, u32[]{:S(2)}) collective-permute-start(bf16[64,512]{1,0:T(8,128)(2,1)S(1)} %get-tuple-element.20), channel_id=1, source_target_pairs={{0,3},{1,2},{2,1},{3,0},{4,7},{5,6},{6,5},{7,4},{8,11},{9,10},{10,... | collective-permute-start | bytes 196616 | tf_op jit(solution)/shard_map/ppermute | solution.py:197
  45.6 6.1 %collective-permute-start = (s32[2]{0:T(128)S(1)}, s32[2]{0:T(128)S(1)}, u32[]{:S(2)}, u32[]{:S(2)}) collective-permute-start(s32[2]{0:T(128)S(1)} %copy-done.5), channel_id=1, source_target_pairs={{0,4},{4,0},{8,12},{12,8},{1,5},{5,1},{9,13},{13,9},{2,6},{6,2},{1... | collective-permute-start | bytes 32 | tf_op jit(solution)/shard_map/ppermute | solution.py:197
  50.1 4.4 %collective-permute-start.1 = (s32[2]{0:T(128)S(1)}, s32[2]{0:T(128)S(1)}, u32[]{:S(2)}, u32[]{:S(2)}) collective-permute-start(s32[2]{0:T(128)S(1)} %copy-done.5), channel_id=1, source_target_pairs={{0,8},{4,12},{8,0},{12,4},{1,9},{5,13},{9,1},{13,5},{2,10},{6,14},... | collective-permute-start | bytes 32 | tf_op jit(solution)/shard_map/ppermute | solution.py:197
  51.7 5.3 %collective-permute-start.2 = (s32[2]{0:T(128)S(1)}, s32[2]{0:T(128)S(1)}, u32[]{:S(2)}, u32[]{:S(2)}) collective-permute-start(s32[2]{0:T(128)S(1)} %copy-done.5), channel_id=1, source_target_pairs={{0,12},{4,8},{8,4},{12,0},{1,13},{5,9},{9,5},{13,1},{2,14},{6,10},... | collective-permute-start | bytes 32 | tf_op jit(solution)/shard_map/ppermute | solution.py:197
  57.6 4.5 %collective-permute-start.19 = (bf16[32,512]{1,0:T(8,128)(2,1)S(1)}, bf16[32,512]{1,0:T(8,128)(2,1)S(1)}, u32[]{:S(2)}, u32[]{:S(2)}) collective-permute-start(bf16[32,512]{1,0:T(8,128)(2,1)S(1)} %get-tuple-element.22), channel_id=1, source_target_pairs={{0,4},{4,0},{8,12},{12,8},{1,5},{5,1},{9,13},{13,9},{2,6},{6,2},{1... | collective-permute-start | bytes 98312 | tf_op jit(solution)/shard_map/ppermute | solution.py:197
  57.9 5.0 %collective-permute-start.20 = (bf16[32,512]{1,0:T(8,128)(2,1)S(1)}, bf16[32,512]{1,0:T(8,128)(2,1)S(1)}, u32[]{:S(2)}, u32[]{:S(2)}) collective-permute-start(bf16[32,512]{1,0:T(8,128)(2,1)S(1)} %get-tuple-element.23), channel_id=1, source_target_pairs={{0,8},{4,12},{8,0},{12,4},{1,9},{5,13},{9,1},{13,5},{2,10},{6,14},... | collective-permute-start | bytes 98312 | tf_op jit(solution)/shard_map/ppermute | solution.py:197
  59.3 5.7 %collective-permute-start.21 = (bf16[32,512]{1,0:T(8,128)(2,1)S(1)}, bf16[32,512]{1,0:T(8,128)(2,1)S(1)}, u32[]{:S(2)}, u32[]{:S(2)}) collective-permute-start(bf16[32,512]{1,0:T(8,128)(2,1)S(1)} %get-tuple-element.24), channel_id=1, source_target_pairs={{0,12},{4,8},{8,4},{12,0},{1,13},{5,9},{9,5},{13,1},{2,14},{6,10},... | collective-permute-start | bytes 98312 | tf_op jit(solution)/shard_map/ppermute | solution.py:197
  (6 other events, 6.6 us)

commit v2 on v1

--- a/solution.py
+++ b/solution.py
@@ -10,6 +10,7 @@
 
 HEAD_DIM = 128
 NEG_LARGE = -1e30
+END_PART = 128
 
 
 def vmem(count):
@@ -33,27 +34,58 @@
     return jnp.transpose(jnp.broadcast_to(row, (size, size)))
 
 
-def attend_kernel(blocks, q_ref, kh_ref, ko_ref, vh_ref, vo_ref, st_ref, eh_ref, eo_ref, out_ref):
+def pack_kernel(k_ref, v_ref, end_ref, message_ref):
+    rows, width = k_ref.shape
+    message_ref[pl.ds(0, rows), pl.ds(0, width)] = k_ref[...]
+    message_ref[pl.ds(0, rows), pl.ds(width, width)] = v_ref[...]
+    extra = message_ref.shape[0] - rows
+    line = lax.broadcasted_iota(jnp.int32, (extra, rows), 0)
+    ends = jnp.broadcast_to(end_ref[...], (extra, rows))
+    parts = jnp.where(line == 0, ends // END_PART, jnp.where(line == 1, ends % END_PART, 0))
+    message_ref[pl.ds(rows, extra), :] = jnp.zeros((extra, 2 * width), jnp.bfloat16)
+    message_ref[pl.ds(rows, extra), pl.ds(0, rows)] = parts.astype(jnp.float32).astype(jnp.bfloat16)
+
+
+def pack(key_rows, value_rows, ends):
+    rows, width = key_rows.shape
+    return pl.pallas_call(
+        pack_kernel,
+        out_shape=jax.ShapeDtypeStruct((rows + 16, 2 * width), jnp.bfloat16),
+        in_specs=vmem(3),
+        out_specs=pl.BlockSpec(memory_space=pltpu.VMEM),
+        cost_estimate=cost(10**9, 8 * key_rows.size),
+    )(key_rows, value_rows, ends)
+
+
+def attend_kernel(blocks, q_ref, halo_ref, k_ref, v_ref, end_ref, st_ref, *refs):
+    whole_ref, *out_refs = refs
     rows = q_ref.shape[0]
-    kv_here = ko_ref.shape[1] // HEAD_DIM
+    width = k_ref.shape[1]
+    kv_here = width // HEAD_DIM
     group = q_ref.shape[1] // HEAD_DIM // kv_here
     core = lax.axis_index("tp") % 2
     base = lax.axis_index("ctx") * rows
     half = rows // blocks // 2
     query_pos = base + lax.broadcasted_iota(jnp.int32, (rows, rows), 0)
     query_start = column(st_ref[...])
+    parts = halo_ref[pl.ds(rows, 16), pl.ds(0, rows)].astype(jnp.float32).astype(jnp.int32)
     masks = []
-    for shift, end_ref in ((rows, eh_ref), (0, eo_ref)):
+    for shift, key_end in ((rows, parts[0:1] * END_PART + parts[1:2]), (0, end_ref[...])):
         key_pos = base - shift + lax.broadcasted_iota(jnp.int32, (rows, rows), 1)
-        masks.append(
-            (key_pos <= query_pos) & (key_pos >= query_start) & (end_ref[...] > query_pos)
-        )
+        masks.append((key_pos <= query_pos) & (key_pos >= query_start) & (key_end > query_pos))
     visible = jnp.concatenate(masks, axis=1)
     visible = jnp.concatenate([visible] * group, axis=0)
     for kv in range(kv_here):
-        lanes = pl.ds(kv * HEAD_DIM, HEAD_DIM)
-        keys = jnp.concatenate([kh_ref[:, lanes], ko_ref[:, lanes]], axis=0)
-        values = jnp.concatenate([vh_ref[:, lanes], vo_ref[:, lanes]], axis=0)
+        keys, values = (
+            jnp.concatenate(
+                [
+                    halo_ref[pl.ds(0, rows), pl.ds(first + kv * HEAD_DIM, HEAD_DIM)],
+                    ref[:, pl.ds(kv * HEAD_DIM, HEAD_DIM)],
+                ],
+                axis=0,
+            )
+            for first, ref in ((0, k_ref), (width, v_ref))
+        )
         query = jnp.concatenate(
             [q_ref[:, pl.ds((kv * group + g) * HEAD_DIM, HEAD_DIM)] for g in range(group)], axis=0
         )
@@ -74,52 +106,53 @@
             for p in range(blocks):
                 for h in range(2):
                     first = g * rows + (p * 2 + h) * half
-                    place = pl.multiple_of((h ^ core) * (blocks * half) + p * half, half)
-                    out_ref[pl.ds(place, half), pl.ds((kv * group + g) * HEAD_DIM, HEAD_DIM)] = (
+                    place = pl.multiple_of((h ^ core) * half, half)
+                    lanes = pl.ds((kv * group + g) * HEAD_DIM, HEAD_DIM)
+                    out_refs[p][pl.ds(place, half), lanes] = attended[first : first + half]
+                    whole_ref[pl.ds(p * 2 * half + place, half), lanes] = (
                         attended[first : first + half]
                     )
 
 
-def attend(blocks, queries, key_halo, key_own, value_halo, value_own, start, end_halo, end_own):
-    rows = queries.shape[0]
+def attend(blocks, queries, halo, keys, values, end, start):
+    rows, features = queries.shape
+    out = jax.ShapeDtypeStruct((rows // blocks, features), jnp.bfloat16)
     return pl.pallas_call(
         functools.partial(attend_kernel, blocks),
-        out_shape=jax.ShapeDtypeStruct(queries.shape, jnp.bfloat16),
-        in_specs=vmem(8),
-        out_specs=pl.BlockSpec(memory_space=pltpu.VMEM),
-        compiler_params=params(),
-        cost_estimate=cost(8 * rows * rows * queries.shape[1], 6 * queries.size),
-    )(queries, key_halo, key_own, value_halo, value_own, start, end_halo, end_own)
-
-
-def project_kernel(chunk_count, *refs):
+        out_shape=(
+            jax.ShapeDtypeStruct(queries.shape, jnp.bfloat16),
+        )
+        + (out,) * blocks,
+        in_specs=vmem(6),
+        out_specs=tuple(vmem(1 + blocks)),
+        compiler_params=params(),
+        cost_estimate=cost(8 * rows * rows * features, 6 * queries.size),
+    )(queries, halo, keys, values, end, start)
+
+
+def project_kernel(block_rows, *refs):
     chunks, weight_ref, mine_ref, other_ref = refs[:-3], refs[-3], refs[-2], refs[-1]
-    rows = chunks[0].shape[0]
-    half = rows // 2
-    if chunk_count == 1 and len(chunks) == 2:
-        place = lax.axis_index("ctx")
-        inner = (place == 1) | (place == 2)
-        stacked = jnp.where(inner, chunks[0][...], chunks[1][...])
-    else:
-        stacked = jnp.concatenate([c[...] for c in chunks], axis=0)
+    half = block_rows // 2
+    stacked = jnp.concatenate([c[...] for c in chunks], axis=0)
     share = jnp.dot(stacked, weight_ref[...], preferred_element_type=jnp.float32).astype(
         jnp.bfloat16
     )
-    for n in range(chunk_count):
-        mine_ref[pl.ds(n * half, half), :] = share[n * rows : n * rows + half]
-        other_ref[pl.ds(n * half, half), :] = share[n * rows + half : (n + 1) * rows]
-
-
-def project(chunk_count, chunks, weight):
-    rows = chunks[0].shape[0] * chunk_count // 2
-    out = jax.ShapeDtypeStruct((rows, weight.shape[1]), jnp.bfloat16)
-    return pl.pallas_call(
-        functools.partial(project_kernel, chunk_count),
+    for n in range(share.shape[0] // block_rows):
+        first = n * block_rows
+        mine_ref[pl.ds(n * half, half), :] = share[first : first + half]
+        other_ref[pl.ds(n * half, half), :] = share[first + half : first + block_rows]
+
+
+def project(block_rows, chunks, weight):
+    rows = sum(c.shape[0] for c in chunks)
+    out = jax.ShapeDtypeStruct((rows // 2, weight.shape[1]), jnp.bfloat16)
+    return pl.pallas_call(
+        functools.partial(project_kernel, block_rows),
         out_shape=(out, out),
         in_specs=vmem(len(chunks) + 1),
-        out_specs=(pl.BlockSpec(memory_space=pltpu.VMEM),) * 2,
-        compiler_params=params(),
-        cost_estimate=cost(4 * rows * weight.size, 2 * weight.size),
+        out_specs=tuple(vmem(2)),
+        compiler_params=params(),
+        cost_estimate=cost(2 * rows * weight.size, 2 * weight.size),
     )(*chunks, weight)
 
 
@@ -139,38 +172,40 @@
     )(*terms)
 
 
-def pick_kernel(blocks, *refs):
-    targets, refs = refs[:4], refs[4:]
-    own_ref, pair_ref, late_refs, outs, held = refs[0], refs[1], refs[2:6], refs[6:10], refs[10]
-    half = own_ref.shape[0] // blocks
+def pick_kernel(blocks, sums, late, half, *refs):
+    (at_0, at_2, at_13), refs = refs[:3], refs[3:]
+    done_refs, late_refs, outs, held = refs[:sums], refs[sums : sums + late], refs[-5:-1], refs[-1]
     x = lax.axis_index("tp") // 2
     c = lax.axis_index("ctx")
-    late = sum(t[...].astype(jnp.float32) for t in late_refs).astype(jnp.bfloat16)
-    held[pl.ds(0, blocks * half), :] = own_ref[...]
-    held[pl.ds(blocks * half, blocks * half), :] = pair_ref[pl.ds(blocks * half, blocks * half), :]
-    held[pl.ds(2 * blocks * half, blocks * half), :] = late
-    held[pl.ds(3 * blocks * half, blocks * half), :] = pair_ref[pl.ds(0, blocks * half), :]
+    first = 0
+    for ref in done_refs:
+        held[pl.ds(first, ref.shape[0]), :] = ref[...]
+        first += ref.shape[0]
+    total_late = sum(t[...].astype(jnp.float32) for t in late_refs)
+    held[pl.ds(first, late_refs[0].shape[0]), :] = total_late.astype(held.dtype)
     for k in range(4):
         wanted = (c ^ k) * blocks + x
         where = jnp.int32(0)
-        for d in range(4):
-            for p in range(blocks):
-                where = jnp.where(targets[d][p] == wanted, d * blocks + p, where)
+        for p in range(blocks):
+            for d, target in enumerate((at_0[p], at_13[p], at_2[p], at_13[blocks + p])):
+                where = jnp.where(target == wanted, d * blocks + p, where)
         outs[k][...] = held[pl.ds(pl.multiple_of(where * half, half), half), :]
 
 
-def pick(blocks, targets, own, pair, late):
-    rows, cols = own.shape
-    out = jax.ShapeDtypeStruct((rows // blocks, cols), jnp.bfloat16)
-    return pl.pallas_call(
-        functools.partial(pick_kernel, blocks),
+def pick(blocks, targets, sums, late):
+    cols = late[0].shape[1]
+    rows = sum(s.shape[0] for s in sums) + late[0].shape[0]
+    half = rows // (4 * blocks)
+    out = jax.ShapeDtypeStruct((half, cols), jnp.bfloat16)
+    return pl.pallas_call(
+        functools.partial(pick_kernel, blocks, len(sums), len(late), half),
         out_shape=(out,) * 4,
-        in_specs=smem(4) + vmem(6),
-        out_specs=(pl.BlockSpec(memory_space=pltpu.VMEM),) * 4,
-        scratch_shapes=[pltpu.VMEM((4 * rows, cols), jnp.bfloat16)],
-        compiler_params=params(),
-        cost_estimate=cost(4 * own.size, 20 * own.size),
-    )(*targets, own, pair, *late)
+        in_specs=smem(3) + vmem(len(sums) + len(late)),
+        out_specs=tuple(vmem(4)),
+        scratch_shapes=[pltpu.VMEM((rows, cols), jnp.bfloat16)],
+        compiler_params=params(),
+        cost_estimate=cost(4 * rows * cols, 8 * rows * cols),
+    )(*targets, *sums, *late)
 
 
 def join_kernel(*refs):
@@ -193,42 +228,42 @@
     )(*pieces)
 
 
-def flip(array, axis, bits, members=(0, 1, 2, 3)):
-    return lax.ppermute(array, axis, [(i, i ^ bits) for i in members])
-
-
-def tp_total(mine, other):
+def flip(array, axis, bits):
+    return lax.ppermute(array, axis, [(i, i ^ bits) for i in range(4)])
+
+
+def tp_terms(mine, other):
     return mine, flip(other, "tp", 1), flip(mine, "tp", 2), flip(other, "tp", 3)
+
+
+def after(value, *others):
+    return lax.optimization_barrier((value, *others))[0]
 
 
 def small_ring(queries, key_rows, value_rows, doc_start, doc_end, block_target, out_weight):
     rows = queries.shape[0]
     blocks = block_target.shape[0]
-    following = [(0, 1), (1, 2), (2, 3)]
-    ends = doc_end.reshape(1, rows)
-    key_halo = lax.ppermute(key_rows, "ctx", following)
-    value_halo = lax.ppermute(value_rows, "ctx", following)
-    end_halo = lax.ppermute(ends, "ctx", following)
-    attended = attend(
-        blocks,
-        queries,
-        key_halo,
-        key_rows,
-        value_halo,
-        value_rows,
-        doc_start.reshape(1, rows),
-        end_halo,
-        ends,
-    )
-    got_3 = flip(attended, "ctx", 3)
-    got_1 = flip(attended, "ctx", 1)
-    got_2_inner = lax.ppermute(attended, "ctx", [(0, 2), (3, 1)])
-    got_2_outer = lax.ppermute(got_3, "ctx", [(1, 0), (2, 3)])
-    targets = [block_target] + [flip(block_target, "ctx", d) for d in (1, 2, 3)]
-    own = total(tp_total(*project(1, (attended,), out_weight)))
-    pair = total(tp_total(*project(2, (got_3, got_1), out_weight)))
-    late = tp_total(*project(1, (got_2_inner, got_2_outer), out_weight))
-    kept, *sent = pick(blocks, targets, own, pair, late)
+    block_rows = rows // blocks
+    end, start = doc_end.reshape(1, rows), doc_start.reshape(1, rows)
+    message = pack(key_rows, value_rows, end)
+    halo = lax.ppermute(message, "ctx", [(0, 1), (1, 2), (2, 3)])
+    whole, first, second = attend(blocks, queries, halo, key_rows, value_rows, end, start)
+    first_2, second_2 = flip(first, "ctx", 2), flip(second, "ctx", 2)
+    whole_1 = flip(whole, "ctx", 1)
+    first_3, second_3 = flip(first_2, "ctx", 1), flip(second_2, "ctx", 1)
+    terms_a = tp_terms(*project(block_rows, (whole,), out_weight))
+    target_2 = flip(after(block_target, terms_a[0]), "ctx", 2)
+    target_13 = flip(jnp.concatenate([block_target, target_2]), "ctx", 1)
+    terms_b = tp_terms(*project(block_rows, (whole_1, first_2), out_weight))
+    sum_a = total(terms_a)
+    second_2 = after(second_2, sum_a, target_13, terms_b[0])
+    terms_c = tp_terms(*project(block_rows, (second_2, first_3), out_weight))
+    sum_b = total(terms_b)
+    second_3 = after(second_3, sum_b, terms_c[0])
+    terms_d = tp_terms(*project(block_rows, (second_3,), out_weight))
+    sum_c = total(terms_c)
+    targets = (block_target, target_2, target_13)
+    kept, *sent = pick(blocks, targets, (sum_a, sum_b, sum_c), terms_d)
     return join([kept] + [flip(sent[k - 1], "ctx", k) for k in (1, 2, 3)])
 
 

time: 66.1 us -> 56.1 us (0.85)
  waiting for transfers between devices: 23.1 us -> 18.8 us
  local copies, waits for them, and re-layouts: 4.67 us -> 0.67 us
  starting transfers between devices: 34.7 us -> 31.1 us
  Pallas kernels: 3.11 us -> 5.05 us
    ppermute x22 -> x23, waiting for transfers between devices: 23.1 us -> 18.8 us  [the longest x22 15.4 us: flip(): return lax.ppermute(array, axis, [(i, i ^ bits) for i in range(4)])]
    unnamed x16 -> x14, local copies, waits for them, and re-layouts: 4.67 us -> 0.67 us
    ppermute x22 -> x23, starting transfers between devices: 34.7 us -> 31.1 us  [the longest x22 26.1 us: flip(): return lax.ppermute(array, axis, [(i, i ^ bits) for i in range(4)])]
    pallas_call x5 -> x7, Pallas kernels: 2.34 us -> 4.25 us  [the longest x1 1.65 us: pack(): pl.pallas_call(pack_kernel, out_shape=jax.ShapeDtypeStruct((rows + 16, 2...]
  transfers between devices with their start and end apart: 22 -> 23, of which waited for: 10 -> 10; matrix products, arithmetic and copies ran while one was open for 0% -> 0% of each run, Pallas kernels for 2% -> 3%
where the time goes in v2:
time: 56.1 us; the launch traced here: 55.9 us
  starting transfers between devices  31.1 us (55%)
  waiting for transfers between devices  18.8 us (34%)
  Pallas kernels  5.05 us (9%)
  local copies, waits for them, and re-layouts  0.67 us (1%)
    ppermute x22, starting transfers between devices, flip(): return lax.ppermute(array, axis, [(i, i ^ bits) for i in range(4)])  26.1 us
    ppermute x22, waiting for transfers between devices, flip(): return lax.ppermute(array, axis, [(i, i ^ bits) for i in range(4)])  15.4 us
    ppermute x1, starting transfers between devices, small_ring(): halo = lax.ppermute(message, 'ctx', [(0, 1), (1, 2), (2, 3)])  5.07 us
    ppermute x1, waiting for transfers between devices, small_ring(): halo = lax.ppermute(message, 'ctx', [(0, 1), (1, 2), (2, 3)])  3.4 us
    pallas_call x1, Pallas kernels, pack(): pl.pallas_call(pack_kernel, out_shape=jax.ShapeDtypeStruct((rows + 16, 2...  1.65 us
    pallas_call x4, Pallas kernels, project(): pl.pallas_call(functools.partial(project_kernel, block_rows), out_shape=(...  1.31 us
  transfers between devices with their start and end apart: 23, of which 10 were waited for; matrix products, arithmetic and copies ran while one was open for 0% of the time, Pallas kernels for 3%

profile of v2, /device:TPU:0, one launch (start us, length us, event | category | flops | bytes accessed | tf_op | source)
XLA Modules:
  0.0 55.9 jit_solution(6886622948708525378)
XLA Ops:
  0.0 1.7 %shard_map.73 = bf16[144,512]{1,0:T(8,128)(2,1)} custom-call(bf16[128,256]{1,0:T(8,128)(2,1)} %k_ref.3, bf16[128,256]{1,0:T(8,128)(2,1)} %v_ref.3, s32[1,128]{1,0:T(1,128)} %bitcast.2), custom_call_target="tpu_custom_call" | custom-call | flops 1000000000 | bytes 262144 | tf_op jit(solution)/shard_map/pallas_call | solution.py:51
  1.7 5.1 %collective-permute-start = (bf16[144,512]{1,0:T(8,128)(2,1)}, bf16[144,512]{1,0:T(8,128)(2,1)S(1)}, u32[]{:S(2)}, u32[]{:S(2)}) collective-permute-start(bf16[144,512]{1,0:T(8,128)(2,1)} %shard_map.73), channel_id=1, source_target_pairs={{0,4},{4,8},{8,12},{1,5},{5,9},{9,13},{2,6},{6,10},{10,14},{3,7},{... | collective-permute-start | bytes 442376 | tf_op jit(solution)/shard_map/ppermute | solution.py:249
  6.7 3.4 %collective-permute-done.halo_ref = bf16[144,512]{1,0:T(8,128)(2,1)S(1)} collective-permute-done((bf16[144,512]{1,0:T(8,128)(2,1)}, bf16[144,512]{1,0:T(8,128)(2,1)S(1)}, u32[]{:S(2)}, u32[]{:S(2)}) %collective-permute-start) | collective-permute-done | bytes 147488 | tf_op jit(solution)/shard_map/ppermute | solution.py:249
  10.2 0.7 %shard_map.74 = (bf16[128,1024]{1,0:T(8,128)(2,1)S(1)}, bf16[64,1024]{1,0:T(8,128)(2,1)S(1)}, bf16[64,1024]{1,0:T(8,128)(2,1)S(1)}) custom-call(bf16[128,1024]{1,0:T(8,128)(2,1)S(1)} %copy-done.1, bf16[144,512]{1,0:T(8,128)(2,1)S(1)} %collective-permute-done.halo_ref, bf16[128,256]{1,0:T(8,128)(2,1)S(1)} %copy-done.2, bf16[128,256]{1,0:T(8,128)(2,1)S(1)} %copy-done.3, ...), custom_call_target="tpu_custom_call" | custom-call | flops 134217728 | bytes 786432 | tf_op jit(solution)/shard_map/pallas_call | solution.py:120
  10.9 3.5 %collective-permute-start.7 = (bf16[64,1024]{1,0:T(8,128)(2,1)S(1)}, bf16[64,1024]{1,0:T(8,128)(2,1)S(1)}, u32[]{:S(2)}, u32[]{:S(2)}) collective-permute-start(bf16[64,1024]{1,0:T(8,128)(2,1)S(1)} %get-tuple-element.27), channel_id=1, source_target_pairs={{0,8},{4,12},{8,0},{12,4},{1,9},{5,13},{9,1},{13,5},{2,10},{6,14},... | collective-permute-start | bytes 393224 | tf_op jit(solution)/shard_map/ppermute | solution.py:232
  14.3 1.6 %collective-permute-start.6 = (bf16[128,1024]{1,0:T(8,128)(2,1)S(1)}, bf16[128,1024]{1,0:T(8,128)(2,1)S(1)}, u32[]{:S(2)}, u32[]{:S(2)}) collective-permute-start(bf16[128,1024]{1,0:T(8,128)(2,1)S(1)} %get-tuple-element.23.refs_0_), channel_id=1, source_target_pairs={{0,4},{4,0},{8,12},{12,8},{1,5},{5,1},{9,13},{13,9},{2,6},{6,2},{1... | collective-permute-start | bytes 786440 | tf_op jit(solution)/shard_map/ppermute | solution.py:232
  17.2 2.6 %collective-permute-start.11 = (bf16[64,1024]{1,0:T(8,128)(2,1)S(1)}, bf16[64,1024]{1,0:T(8,128)(2,1)S(1)}, u32[]{:S(2)}, u32[]{:S(2)}) collective-permute-start(bf16[64,1024]{1,0:T(8,128)(2,1)S(1)} %get-tuple-element.30), channel_id=1, source_target_pairs={{0,8},{4,12},{8,0},{12,4},{1,9},{5,13},{9,1},{13,5},{2,10},{6,14},... | collective-permute-start | bytes 393224 | tf_op jit(solution)/shard_map/ppermute | solution.py:232
  19.8 0.8 %collective-permute-start.12 = (bf16[64,1024]{1,0:T(8,128)(2,1)S(1)}, bf16[64,1024]{1,0:T(8,128)(2,1)S(1)}, u32[]{:S(2)}, u32[]{:S(2)}) collective-permute-start(bf16[64,1024]{1,0:T(8,128)(2,1)S(1)} %collective-permute-done.7.refs_1_), channel_id=1, source_target_pairs={{0,4},{4,0},{8,12},{12,8},{1,5},{5,1},{9,13},{13,9},{2,6},{6,2},{1... | collective-permute-start | bytes 393224 | tf_op jit(solution)/shard_map/ppermute | solution.py:232
  20.6 2.6 %collective-permute-done.1.refs_1_ = s32[2]{0:T(128)S(1)} collective-permute-done((s32[2]{0:T(128)S(1)}, s32[2]{0:T(128)S(1)}, u32[]{:S(2)}, u32[]{:S(2)}) %collective-permute-start.1) | collective-permute-done | bytes 40 | tf_op jit(solution)/shard_map/ppermute | solution.py:232
  23.3 3.0 %collective-permute-start.2 = (s32[4]{0:T(128)S(1)}, s32[4]{0:T(128)S(1)}, u32[]{:S(2)}, u32[]{:S(2)}) collective-permute-start(s32[4]{0:T(128)S(1)} %pad_add_fusion), channel_id=1, source_target_pairs={{0,4},{4,0},{8,12},{12,8},{1,5},{5,1},{9,13},{13,9},{2,6},{6,2},{1... | collective-permute-start | bytes 56 | tf_op jit(solution)/shard_map/ppermute | solution.py:232
  26.3 2.2 %collective-permute-done.2.refs_2_ = s32[4]{0:T(128)S(1)} collective-permute-done((s32[4]{0:T(128)S(1)}, s32[4]{0:T(128)S(1)}, u32[]{:S(2)}, u32[]{:S(2)}) %collective-permute-start.2) | collective-permute-done | bytes 48 | tf_op jit(solution)/shard_map/ppermute | solution.py:232
  28.6 1.5 %collective-permute-start.4 = (bf16[64,512]{1,0:T(8,128)(2,1)S(1)}, bf16[64,512]{1,0:T(8,128)(2,1)S(1)}, u32[]{:S(2)}, u32[]{:S(2)}) collective-permute-start(bf16[64,512]{1,0:T(8,128)(2,1)S(1)} %get-tuple-element.24.refs_0_), channel_id=1, source_target_pairs={{0,2},{1,3},{2,0},{3,1},{4,6},{5,7},{6,4},{7,5},{8,10},{9,11},{10,... | collective-permute-start | bytes 196616 | tf_op jit(solution)/shard_map/ppermute | solution.py:232
  30.1 1.5 %collective-permute-start.16 = (bf16[64,1024]{1,0:T(8,128)(2,1)S(1)}, bf16[64,1024]{1,0:T(8,128)(2,1)S(1)}, u32[]{:S(2)}, u32[]{:S(2)}) collective-permute-start(bf16[64,1024]{1,0:T(8,128)(2,1)S(1)} %collective-permute-done.11.refs_0_), channel_id=1, source_target_pairs={{0,4},{4,0},{8,12},{12,8},{1,5},{5,1},{9,13},{13,9},{2,6},{6,2},{1... | collective-permute-start | bytes 393224 | tf_op jit(solution)/shard_map/ppermute | solution.py:232
  32.8 2.2 %collective-permute-start.9 = (bf16[96,512]{1,0:T(8,128)(2,1)S(1)}, bf16[96,512]{1,0:T(8,128)(2,1)S(1)}, u32[]{:S(2)}, u32[]{:S(2)}) collective-permute-start(bf16[96,512]{1,0:T(8,128)(2,1)S(1)} %get-tuple-element.28.refs_0_), channel_id=1, source_target_pairs={{0,2},{1,3},{2,0},{3,1},{4,6},{5,7},{6,4},{7,5},{8,10},{9,11},{10,... | collective-permute-start | bytes 294920 | tf_op jit(solution)/shard_map/ppermute | solution.py:232
  35.9 1.7 %collective-permute-start.14 = (bf16[64,512]{1,0:T(8,128)(2,1)S(1)}, bf16[64,512]{1,0:T(8,128)(2,1)S(1)}, u32[]{:S(2)}, u32[]{:S(2)}) collective-permute-start(bf16[64,512]{1,0:T(8,128)(2,1)S(1)} %get-tuple-element.32.refs_0_), channel_id=1, source_target_pairs={{0,2},{1,3},{2,0},{3,1},{4,6},{5,7},{6,4},{7,5},{8,10},{9,11},{10,... | collective-permute-start | bytes 196616 | tf_op jit(solution)/shard_map/ppermute | solution.py:232
  37.7 2.1 %collective-permute-done.10.refs_3_ = bf16[96,512]{1,0:T(8,128)(2,1)S(1)} collective-permute-done((bf16[96,512]{1,0:T(8,128)(2,1)S(1)}, bf16[96,512]{1,0:T(8,128)(2,1)S(1)}, u32[]{:S(2)}, u32[]{:S(2)}) %collective-permute-start.10) | collective-permute-done | bytes 98336 | tf_op jit(solution)/shard_map/ppermute | solution.py:232
  40.7 1.5 %collective-permute-start.18 = (bf16[32,512]{1,0:T(8,128)(2,1)S(1)}, bf16[32,512]{1,0:T(8,128)(2,1)S(1)}, u32[]{:S(2)}, u32[]{:S(2)}) collective-permute-start(bf16[32,512]{1,0:T(8,128)(2,1)S(1)} %get-tuple-element.35.refs_6_), channel_id=1, source_target_pairs={{0,2},{1,3},{2,0},{3,1},{4,6},{5,7},{6,4},{7,5},{8,10},{9,11},{10,... | collective-permute-start | bytes 98312 | tf_op jit(solution)/shard_map/ppermute | solution.py:232
  42.2 2.4 %collective-permute-done.18.refs_8_ = bf16[32,512]{1,0:T(8,128)(2,1)S(1)} collective-permute-done((bf16[32,512]{1,0:T(8,128)(2,1)S(1)}, bf16[32,512]{1,0:T(8,128)(2,1)S(1)}, u32[]{:S(2)}, u32[]{:S(2)}) %collective-permute-start.18) | collective-permute-done | bytes 32800 | tf_op jit(solution)/shard_map/ppermute | solution.py:232
  44.6 1.2 %collective-permute-done.19.refs_9_ = bf16[32,512]{1,0:T(8,128)(2,1)S(1)} collective-permute-done((bf16[32,512]{1,0:T(8,128)(2,1)S(1)}, bf16[32,512]{1,0:T(8,128)(2,1)S(1)}, u32[]{:S(2)}, u32[]{:S(2)}) %collective-permute-start.19) | collective-permute-done | bytes 32800 | tf_op jit(solution)/shard_map/ppermute | solution.py:232
  46.4 1.5 %collective-permute-start.20 = (bf16[32,512]{1,0:T(8,128)(2,1)S(1)}, bf16[32,512]{1,0:T(8,128)(2,1)S(1)}, u32[]{:S(2)}, u32[]{:S(2)}) collective-permute-start(bf16[32,512]{1,0:T(8,128)(2,1)S(1)} %get-tuple-element.38), channel_id=1, source_target_pairs={{0,4},{4,0},{8,12},{12,8},{1,5},{5,1},{9,13},{13,9},{2,6},{6,2},{1... | collective-permute-start | bytes 98312 | tf_op jit(solution)/shard_map/ppermute | solution.py:232
  47.9 1.7 %collective-permute-start.21 = (bf16[32,512]{1,0:T(8,128)(2,1)S(1)}, bf16[32,512]{1,0:T(8,128)(2,1)S(1)}, u32[]{:S(2)}, u32[]{:S(2)}) collective-permute-start(bf16[32,512]{1,0:T(8,128)(2,1)S(1)} %get-tuple-element.39), channel_id=1, source_target_pairs={{0,8},{4,12},{8,0},{12,4},{1,9},{5,13},{9,1},{13,5},{2,10},{6,14},... | collective-permute-start | bytes 98312 | tf_op jit(solution)/shard_map/ppermute | solution.py:232
  49.6 1.3 %collective-permute-start.22 = (bf16[32,512]{1,0:T(8,128)(2,1)S(1)}, bf16[32,512]{1,0:T(8,128)(2,1)S(1)}, u32[]{:S(2)}, u32[]{:S(2)}) collective-permute-start(bf16[32,512]{1,0:T(8,128)(2,1)S(1)} %get-tuple-element.40), channel_id=1, source_target_pairs={{0,12},{4,8},{8,4},{12,0},{1,13},{5,9},{9,5},{13,1},{2,14},{6,10},... | collective-permute-start | bytes 98312 | tf_op jit(solution)/shard_map/ppermute | solution.py:232
  50.9 2.2 %collective-permute-done.21.refs_2_ = bf16[32,512]{1,0:T(8,128)(2,1)S(1)} collective-permute-done((bf16[32,512]{1,0:T(8,128)(2,1)S(1)}, bf16[32,512]{1,0:T(8,128)(2,1)S(1)}, u32[]{:S(2)}, u32[]{:S(2)}) %collective-permute-start.21) | collective-permute-done | bytes 32800 | tf_op jit(solution)/shard_map/ppermute | solution.py:232
  53.1 2.2 %collective-permute-done.22.refs_3_ = bf16[32,512]{1,0:T(8,128)(2,1)S(1)} collective-permute-done((bf16[32,512]{1,0:T(8,128)(2,1)S(1)}, bf16[32,512]{1,0:T(8,128)(2,1)S(1)}, u32[]{:S(2)}, u32[]{:S(2)}) %collective-permute-start.22) | collective-permute-done | bytes 32800 | tf_op jit(solution)/shard_map/ppermute | solution.py:232
  (48 shorter events, 5.8 us)
Async XLA Ops:
  0.0 15.9 %copy-start = (bf16[1024,512]{1,0:T(8,128)(2,1)S(1)}, bf16[1024,512]{1,0:T(8,128)(2,1)}, u32[]{:S(2)}) copy-start(bf16[1024,512]{1,0:T(8,128)(2,1)} %refs_1_.3) | copy-start | bytes 3145732
  1.7 8.5 %collective-permute-start = (bf16[144,512]{1,0:T(8,128)(2,1)}, bf16[144,512]{1,0:T(8,128)(2,1)S(1)}, u32[]{:S(2)}, u32[]{:S(2)}) collective-permute-start(bf16[144,512]{1,0:T(8,128)(2,1)} %shard_map.73), channel_id=1, source_target_pairs={{0,4},{4,8},{8,12},{1,5},{5,9},{9,13},{2,6},{6,10},{10,14},{3,7},{... | collective-permute-start | bytes 442376 | tf_op jit(solution)/shard_map/ppermute | solution.py:249
  10.9 9.0 %collective-permute-start.7 = (bf16[64,1024]{1,0:T(8,128)(2,1)S(1)}, bf16[64,1024]{1,0:T(8,128)(2,1)S(1)}, u32[]{:S(2)}, u32[]{:S(2)}) collective-permute-start(bf16[64,1024]{1,0:T(8,128)(2,1)S(1)} %get-tuple-element.27), channel_id=1, source_target_pairs={{0,8},{4,12},{8,0},{12,4},{1,9},{5,13},{9,1},{13,5},{2,10},{6,14},... | collective-permute-start | bytes 393224 | tf_op jit(solution)/shard_map/ppermute | solution.py:232
  14.3 15.7 %collective-permute-start.6 = (bf16[128,1024]{1,0:T(8,128)(2,1)S(1)}, bf16[128,1024]{1,0:T(8,128)(2,1)S(1)}, u32[]{:S(2)}, u32[]{:S(2)}) collective-permute-start(bf16[128,1024]{1,0:T(8,128)(2,1)S(1)} %get-tuple-element.23.refs_0_), channel_id=1, source_target_pairs={{0,4},{4,0},{8,12},{12,8},{1,5},{5,1},{9,13},{13,9},{2,6},{6,2},{1... | collective-permute-start | bytes 786440 | tf_op jit(solution)/shard_map/ppermute | solution.py:232
  16.9 6.3 %collective-permute-start.1 = (s32[2]{0:T(128)S(1)}, s32[2]{0:T(128)S(1)}, u32[]{:S(2)}, u32[]{:S(2)}) collective-permute-start(s32[2]{0:T(128)S(1)} %copy-done.4), channel_id=1, source_target_pairs={{0,8},{4,12},{8,0},{12,4},{1,9},{5,13},{9,1},{13,5},{2,10},{6,14},... | collective-permute-start | bytes 32 | tf_op jit(solution)/shard_map/ppermute | solution.py:232
  17.2 14.7 %collective-permute-start.3 = (bf16[64,512]{1,0:T(8,128)(2,1)S(1)}, bf16[64,512]{1,0:T(8,128)(2,1)S(1)}, u32[]{:S(2)}, u32[]{:S(2)}) collective-permute-start(bf16[64,512]{1,0:T(8,128)(2,1)S(1)} %get-tuple-element.26), channel_id=1, source_target_pairs={{0,1},{1,0},{2,3},{3,2},{4,5},{5,4},{6,7},{7,6},{8,9},{9,8},{10,11... | collective-permute-start | bytes 196616 | tf_op jit(solution)/shard_map/ppermute | solution.py:232
  17.2 12.8 %collective-permute-start.11 = (bf16[64,1024]{1,0:T(8,128)(2,1)S(1)}, bf16[64,1024]{1,0:T(8,128)(2,1)S(1)}, u32[]{:S(2)}, u32[]{:S(2)}) collective-permute-start(bf16[64,1024]{1,0:T(8,128)(2,1)S(1)} %get-tuple-element.30), channel_id=1, source_target_pairs={{0,8},{4,12},{8,0},{12,4},{1,9},{5,13},{9,1},{13,5},{2,10},{6,14},... | collective-permute-start | bytes 393224 | tf_op jit(solution)/shard_map/ppermute | solution.py:232
  19.8 15.6 %collective-permute-start.12 = (bf16[64,1024]{1,0:T(8,128)(2,1)S(1)}, bf16[64,1024]{1,0:T(8,128)(2,1)S(1)}, u32[]{:S(2)}, u32[]{:S(2)}) collective-permute-start(bf16[64,1024]{1,0:T(8,128)(2,1)S(1)} %collective-permute-done.7.refs_1_), channel_id=1, source_target_pairs={{0,4},{4,0},{8,12},{12,8},{1,5},{5,1},{9,13},{13,9},{2,6},{6,2},{1... | collective-permute-start | bytes 393224 | tf_op jit(solution)/shard_map/ppermute | solution.py:232
  23.3 5.3 %collective-permute-start.2 = (s32[4]{0:T(128)S(1)}, s32[4]{0:T(128)S(1)}, u32[]{:S(2)}, u32[]{:S(2)}) collective-permute-start(s32[4]{0:T(128)S(1)} %pad_add_fusion), channel_id=1, source_target_pairs={{0,4},{4,0},{8,12},{12,8},{1,5},{5,1},{9,13},{13,9},{2,6},{6,2},{1... | collective-permute-start | bytes 56 | tf_op jit(solution)/shard_map/ppermute | solution.py:232
  28.6 4.3 %collective-permute-start.4 = (bf16[64,512]{1,0:T(8,128)(2,1)S(1)}, bf16[64,512]{1,0:T(8,128)(2,1)S(1)}, u32[]{:S(2)}, u32[]{:S(2)}) collective-permute-start(bf16[64,512]{1,0:T(8,128)(2,1)S(1)} %get-tuple-element.24.refs_0_), channel_id=1, source_target_pairs={{0,2},{1,3},{2,0},{3,1},{4,6},{5,7},{6,4},{7,5},{8,10},{9,11},{10,... | collective-permute-start | bytes 196616 | tf_op jit(solution)/shard_map/ppermute | solution.py:232
  30.1 4.9 %collective-permute-start.5 = (bf16[64,512]{1,0:T(8,128)(2,1)S(1)}, bf16[64,512]{1,0:T(8,128)(2,1)S(1)}, u32[]{:S(2)}, u32[]{:S(2)}) collective-permute-start(bf16[64,512]{1,0:T(8,128)(2,1)S(1)} %get-tuple-element.26), channel_id=1, source_target_pairs={{0,3},{1,2},{2,1},{3,0},{4,7},{5,6},{6,5},{7,4},{8,11},{9,10},{10,... | collective-permute-start | bytes 196616 | tf_op jit(solution)/shard_map/ppermute | solution.py:232
  30.1 9.8 %collective-permute-start.16 = (bf16[64,1024]{1,0:T(8,128)(2,1)S(1)}, bf16[64,1024]{1,0:T(8,128)(2,1)S(1)}, u32[]{:S(2)}, u32[]{:S(2)}) collective-permute-start(bf16[64,1024]{1,0:T(8,128)(2,1)S(1)} %collective-permute-done.11.refs_0_), channel_id=1, source_target_pairs={{0,4},{4,0},{8,12},{12,8},{1,5},{5,1},{9,13},{13,9},{2,6},{6,2},{1... | collective-permute-start | bytes 393224 | tf_op jit(solution)/shard_map/ppermute | solution.py:232
  32.0 3.9 %collective-permute-start.8 = (bf16[96,512]{1,0:T(8,128)(2,1)S(1)}, bf16[96,512]{1,0:T(8,128)(2,1)S(1)}, u32[]{:S(2)}, u32[]{:S(2)}) collective-permute-start(bf16[96,512]{1,0:T(8,128)(2,1)S(1)} %get-tuple-element.29), channel_id=1, source_target_pairs={{0,1},{1,0},{2,3},{3,2},{4,5},{5,4},{6,7},{7,6},{8,9},{9,8},{10,11... | collective-permute-start | bytes 294920 | tf_op jit(solution)/shard_map/ppermute | solution.py:232
  32.8 4.8 %collective-permute-start.9 = (bf16[96,512]{1,0:T(8,128)(2,1)S(1)}, bf16[96,512]{1,0:T(8,128)(2,1)S(1)}, u32[]{:S(2)}, u32[]{:S(2)}) collective-permute-start(bf16[96,512]{1,0:T(8,128)(2,1)S(1)} %get-tuple-element.28.refs_0_), channel_id=1, source_target_pairs={{0,2},{1,3},{2,0},{3,1},{4,6},{5,7},{6,4},{7,5},{8,10},{9,11},{10,... | collective-permute-start | bytes 294920 | tf_op jit(solution)/shard_map/ppermute | solution.py:232
  35.0 4.8 %collective-permute-start.10 = (bf16[96,512]{1,0:T(8,128)(2,1)S(1)}, bf16[96,512]{1,0:T(8,128)(2,1)S(1)}, u32[]{:S(2)}, u32[]{:S(2)}) collective-permute-start(bf16[96,512]{1,0:T(8,128)(2,1)S(1)} %get-tuple-element.29), channel_id=1, source_target_pairs={{0,3},{1,2},{2,1},{3,0},{4,7},{5,6},{6,5},{7,4},{8,11},{9,10},{10,... | collective-permute-start | bytes 294920 | tf_op jit(solution)/shard_map/ppermute | solution.py:232
  35.8 6.4 %collective-permute-start.13 = (bf16[64,512]{1,0:T(8,128)(2,1)S(1)}, bf16[64,512]{1,0:T(8,128)(2,1)S(1)}, u32[]{:S(2)}, u32[]{:S(2)}) collective-permute-start(bf16[64,512]{1,0:T(8,128)(2,1)S(1)} %get-tuple-element.33), channel_id=1, source_target_pairs={{0,1},{1,0},{2,3},{3,2},{4,5},{5,4},{6,7},{7,6},{8,9},{9,8},{10,11... | collective-permute-start | bytes 196616 | tf_op jit(solution)/shard_map/ppermute | solution.py:232
  35.9 6.3 %collective-permute-start.14 = (bf16[64,512]{1,0:T(8,128)(2,1)S(1)}, bf16[64,512]{1,0:T(8,128)(2,1)S(1)}, u32[]{:S(2)}, u32[]{:S(2)}) collective-permute-start(bf16[64,512]{1,0:T(8,128)(2,1)S(1)} %get-tuple-element.32.refs_0_), channel_id=1, source_target_pairs={{0,2},{1,3},{2,0},{3,1},{4,6},{5,7},{6,4},{7,5},{8,10},{9,11},{10,... | collective-permute-start | bytes 196616 | tf_op jit(solution)/shard_map/ppermute | solution.py:232
  37.6 4.5 %collective-permute-start.15 = (bf16[64,512]{1,0:T(8,128)(2,1)S(1)}, bf16[64,512]{1,0:T(8,128)(2,1)S(1)}, u32[]{:S(2)}, u32[]{:S(2)}) collective-permute-start(bf16[64,512]{1,0:T(8,128)(2,1)S(1)} %get-tuple-element.33), channel_id=1, source_target_pairs={{0,3},{1,2},{2,1},{3,0},{4,7},{5,6},{6,5},{7,4},{8,11},{9,10},{10,... | collective-permute-start | bytes 196616 | tf_op jit(solution)/shard_map/ppermute | solution.py:232
  40.2 2.0 %collective-permute-start.17 = (bf16[32,512]{1,0:T(8,128)(2,1)S(1)}, bf16[32,512]{1,0:T(8,128)(2,1)S(1)}, u32[]{:S(2)}, u32[]{:S(2)}) collective-permute-start(bf16[32,512]{1,0:T(8,128)(2,1)S(1)} %get-tuple-element.36), channel_id=1, source_target_pairs={{0,1},{1,0},{2,3},{3,2},{4,5},{5,4},{6,7},{7,6},{8,9},{9,8},{10,11... | collective-permute-start | bytes 98312 | tf_op jit(solution)/shard_map/ppermute | solution.py:232
  40.7 3.9 %collective-permute-start.18 = (bf16[32,512]{1,0:T(8,128)(2,1)S(1)}, bf16[32,512]{1,0:T(8,128)(2,1)S(1)}, u32[]{:S(2)}, u32[]{:S(2)}) collective-permute-start(bf16[32,512]{1,0:T(8,128)(2,1)S(1)} %get-tuple-element.35.refs_6_), channel_id=1, source_target_pairs={{0,2},{1,3},{2,0},{3,1},{4,6},{5,7},{6,4},{7,5},{8,10},{9,11},{10,... | collective-permute-start | bytes 98312 | tf_op jit(solution)/shard_map/ppermute | solution.py:232
  42.1 3.7 %collective-permute-start.19 = (bf16[32,512]{1,0:T(8,128)(2,1)S(1)}, bf16[32,512]{1,0:T(8,128)(2,1)S(1)}, u32[]{:S(2)}, u32[]{:S(2)}) collective-permute-start(bf16[32,512]{1,0:T(8,128)(2,1)S(1)} %get-tuple-element.36), channel_id=1, source_target_pairs={{0,3},{1,2},{2,1},{3,0},{4,7},{5,6},{6,5},{7,4},{8,11},{9,10},{10,... | collective-permute-start | bytes 98312 | tf_op jit(solution)/shard_map/ppermute | solution.py:232
  46.4 4.5 %collective-permute-start.20 = (bf16[32,512]{1,0:T(8,128)(2,1)S(1)}, bf16[32,512]{1,0:T(8,128)(2,1)S(1)}, u32[]{:S(2)}, u32[]{:S(2)}) collective-permute-start(bf16[32,512]{1,0:T(8,128)(2,1)S(1)} %get-tuple-element.38), channel_id=1, source_target_pairs={{0,4},{4,0},{8,12},{12,8},{1,5},{5,1},{9,13},{13,9},{2,6},{6,2},{1... | collective-permute-start | bytes 98312 | tf_op jit(solution)/shard_map/ppermute | solution.py:232
  47.9 5.2 %collective-permute-start.21 = (bf16[32,512]{1,0:T(8,128)(2,1)S(1)}, bf16[32,512]{1,0:T(8,128)(2,1)S(1)}, u32[]{:S(2)}, u32[]{:S(2)}) collective-permute-start(bf16[32,512]{1,0:T(8,128)(2,1)S(1)} %get-tuple-element.39), channel_id=1, source_target_pairs={{0,8},{4,12},{8,0},{12,4},{1,9},{5,13},{9,1},{13,5},{2,10},{6,14},... | collective-permute-start | bytes 98312 | tf_op jit(solution)/shard_map/ppermute | solution.py:232
  49.6 5.7 %collective-permute-start.22 = (bf16[32,512]{1,0:T(8,128)(2,1)S(1)}, bf16[32,512]{1,0:T(8,128)(2,1)S(1)}, u32[]{:S(2)}, u32[]{:S(2)}) collective-permute-start(bf16[32,512]{1,0:T(8,128)(2,1)S(1)} %get-tuple-element.40), channel_id=1, source_target_pairs={{0,12},{4,8},{8,4},{12,0},{1,13},{5,9},{9,5},{13,1},{2,14},{6,10},... | collective-permute-start | bytes 98312 | tf_op jit(solution)/shard_map/ppermute | solution.py:232
  (6 other events, 48.0 us)

commit v3 on v2

--- a/solution.py
+++ b/solution.py
@@ -172,40 +172,35 @@
     )(*terms)
 
 
-def pick_kernel(blocks, sums, late, half, *refs):
-    (at_0, at_2, at_13), refs = refs[:3], refs[3:]
-    done_refs, late_refs, outs, held = refs[:sums], refs[sums : sums + late], refs[-5:-1], refs[-1]
+def pick_kernel(blocks, half, own_ref, far_ref, *refs):
+    sums, outs = refs[:-4], refs[-4:]
     x = lax.axis_index("tp") // 2
     c = lax.axis_index("ctx")
-    first = 0
-    for ref in done_refs:
-        held[pl.ds(first, ref.shape[0]), :] = ref[...]
-        first += ref.shape[0]
-    total_late = sum(t[...].astype(jnp.float32) for t in late_refs)
-    held[pl.ds(first, late_refs[0].shape[0]), :] = total_late.astype(held.dtype)
+    order = (0, 1, 2, 3, 4, 6, 5, 7)
+    pieces = [r[pl.ds(n, half), :] for r in sums for n in range(0, r.shape[0], half)]
+    targets = jnp.concatenate([own_ref[...], far_ref[...]], axis=1)
     for k in range(4):
         wanted = (c ^ k) * blocks + x
-        where = jnp.int32(0)
-        for p in range(blocks):
-            for d, target in enumerate((at_0[p], at_13[p], at_2[p], at_13[blocks + p])):
-                where = jnp.where(target == wanted, d * blocks + p, where)
-        outs[k][...] = held[pl.ds(pl.multiple_of(where * half, half), half), :]
-
-
-def pick(blocks, targets, sums, late):
-    cols = late[0].shape[1]
-    rows = sum(s.shape[0] for s in sums) + late[0].shape[0]
+        piece = pieces[0]
+        for n in range(1, len(pieces)):
+            column_of = order[n]
+            here = jnp.broadcast_to(targets[:, column_of : column_of + 1] == wanted, piece.shape)
+            piece = jnp.where(here, pieces[n], piece)
+        outs[k][...] = piece
+
+
+def pick(blocks, own_targets, far_targets, sums):
+    rows, cols = sum(s.shape[0] for s in sums), sums[0].shape[1]
     half = rows // (4 * blocks)
     out = jax.ShapeDtypeStruct((half, cols), jnp.bfloat16)
     return pl.pallas_call(
-        functools.partial(pick_kernel, blocks, len(sums), len(late), half),
+        functools.partial(pick_kernel, blocks, half),
         out_shape=(out,) * 4,
-        in_specs=smem(3) + vmem(len(sums) + len(late)),
+        in_specs=vmem(2 + len(sums)),
         out_specs=tuple(vmem(4)),
-        scratch_shapes=[pltpu.VMEM((rows, cols), jnp.bfloat16)],
         compiler_params=params(),
         cost_estimate=cost(4 * rows * cols, 8 * rows * cols),
-    )(*targets, *sums, *late)
+    )(own_targets, far_targets, *sums)
 
 
 def join_kernel(*refs):
@@ -232,8 +227,12 @@
     return lax.ppermute(array, axis, [(i, i ^ bits) for i in range(4)])
 
 
-def tp_terms(mine, other):
-    return mine, flip(other, "tp", 1), flip(mine, "tp", 2), flip(other, "tp", 3)
+def core_total(mine, other):
+    return total((mine, flip(other, "tp", 1)))
+
+
+def chip_total(share):
+    return total((share, flip(share, "tp", 2)))
 
 
 def after(value, *others):
@@ -250,21 +249,22 @@
     whole, first, second = attend(blocks, queries, halo, key_rows, value_rows, end, start)
     first_2, second_2 = flip(first, "ctx", 2), flip(second, "ctx", 2)
     whole_1 = flip(whole, "ctx", 1)
+    target_1 = flip(after(block_target, whole), "ctx", 1)
+    own_targets = jnp.concatenate([block_target, target_1]).reshape(1, 2 * blocks)
+    share_a = core_total(*project(block_rows, (whole,), out_weight))
+    first_2 = after(first_2, share_a, own_targets)
     first_3, second_3 = flip(first_2, "ctx", 1), flip(second_2, "ctx", 1)
-    terms_a = tp_terms(*project(block_rows, (whole,), out_weight))
-    target_2 = flip(after(block_target, terms_a[0]), "ctx", 2)
-    target_13 = flip(jnp.concatenate([block_target, target_2]), "ctx", 1)
-    terms_b = tp_terms(*project(block_rows, (whole_1, first_2), out_weight))
-    sum_a = total(terms_a)
-    second_2 = after(second_2, sum_a, target_13, terms_b[0])
-    terms_c = tp_terms(*project(block_rows, (second_2, first_3), out_weight))
-    sum_b = total(terms_b)
-    second_3 = after(second_3, sum_b, terms_c[0])
-    terms_d = tp_terms(*project(block_rows, (second_3,), out_weight))
-    sum_c = total(terms_c)
-    targets = (block_target, target_2, target_13)
-    kept, *sent = pick(blocks, targets, (sum_a, sum_b, sum_c), terms_d)
-    return join([kept] + [flip(sent[k - 1], "ctx", k) for k in (1, 2, 3)])
+    sum_a = chip_total(share_a)
+    second_2 = after(second_2, sum_a)
+    share_b = core_total(*project(block_rows, (whole_1, first_2, first_3, second_2), out_weight))
+    far_targets = flip(own_targets, "ctx", 2)
+    second_3 = after(second_3, share_b, far_targets)
+    share_c = core_total(*project(block_rows, (second_3,), out_weight))
+    sum_b = chip_total(share_b)
+    sum_c = chip_total(share_c)
+    kept, *sent = pick(blocks, own_targets, far_targets, (sum_a, sum_b, sum_c))
+    got = [flip(sent[k - 1], "ctx", k) for k in (3, 2, 1)]
+    return join([kept] + got[::-1])
 
 
 def attend_block(soft_state, query_grid, query_pos, query_start, key_block, value_block, key_end, key_pos):

time: 56.1 us -> 55.1 us (0.982)
  waiting for transfers between devices: 18.8 us -> 26.3 us
  starting transfers between devices: 31.1 us -> 23.7 us
    ppermute x22 -> x16, waiting for transfers between devices: 15.4 us -> 22.9 us  [flip(): return lax.ppermute(array, axis, [(i, i ^ bits) for i in range(4)])]
    ppermute x22 -> x16, starting transfers between devices: 26.1 us -> 18.6 us  [flip(): return lax.ppermute(array, axis, [(i, i ^ bits) for i in range(4)])]
    pallas_call x4 -> x3, Pallas kernels: 1.31 us -> 1.12 us  [project(): pl.pallas_call(functools.partial(project_kernel, block_rows), out_shape=(...]
  transfers between devices with their start and end apart: 23 -> 17, of which waited for: 10 -> 9; matrix products, arithmetic and copies ran while one was open for 0% -> 0% of each run, Pallas kernels for 3% -> 1%
where the time goes in v3:
time: 55.1 us; the launch traced here: 54.9 us
  waiting for transfers between devices  26.3 us (48%)
  starting transfers between devices  23.7 us (43%)
  Pallas kernels  4.51 us (8%)
    ppermute x16, waiting for transfers between devices, flip(): return lax.ppermute(array, axis, [(i, i ^ bits) for i in range(4)])  22.9 us
    ppermute x16, starting transfers between devices, flip(): return lax.ppermute(array, axis, [(i, i ^ bits) for i in range(4)])  18.6 us
    ppermute x1, starting transfers between devices, small_ring(): halo = lax.ppermute(message, 'ctx', [(0, 1), (1, 2), (2, 3)])  5.07 us
    ppermute x1, waiting for transfers between devices, small_ring(): halo = lax.ppermute(message, 'ctx', [(0, 1), (1, 2), (2, 3)])  3.4 us
    pallas_call x1, Pallas kernels, pack(): pl.pallas_call(pack_kernel, out_shape=jax.ShapeDtypeStruct((rows + 16, 2...  1.67 us
    pallas_call x3, Pallas kernels, project(): pl.pallas_call(functools.partial(project_kernel, block_rows), out_shape=(...  1.12 us
  transfers between devices with their start and end apart: 17, of which 9 were waited for; matrix products, arithmetic and copies ran while one was open for 0% of the time, Pallas kernels for 1%

profile of v3, /device:TPU:0, one launch (start us, length us, event | category | flops | bytes accessed | tf_op | source)
XLA Modules:
  0.0 54.9 jit_solution(6670059457624318071)
XLA Ops:
  0.0 1.7 %shard_map.73 = bf16[144,512]{1,0:T(8,128)(2,1)} custom-call(bf16[128,256]{1,0:T(8,128)(2,1)} %k_ref.3, bf16[128,256]{1,0:T(8,128)(2,1)} %v_ref.3, s32[1,128]{1,0:T(1,128)} %bitcast.4), custom_call_target="tpu_custom_call" | custom-call | flops 1000000000 | bytes 262144 | tf_op jit(solution)/shard_map/pallas_call | solution.py:51
  1.7 5.1 %collective-permute-start = (bf16[144,512]{1,0:T(8,128)(2,1)}, bf16[144,512]{1,0:T(8,128)(2,1)S(1)}, u32[]{:S(2)}, u32[]{:S(2)}) collective-permute-start(bf16[144,512]{1,0:T(8,128)(2,1)} %shard_map.73), channel_id=1, source_target_pairs={{0,4},{4,8},{8,12},{1,5},{5,9},{9,13},{2,6},{6,10},{10,14},{3,7},{... | collective-permute-start | bytes 442376 | tf_op jit(solution)/shard_map/ppermute | solution.py:248
  6.8 3.4 %collective-permute-done.halo_ref = bf16[144,512]{1,0:T(8,128)(2,1)S(1)} collective-permute-done((bf16[144,512]{1,0:T(8,128)(2,1)}, bf16[144,512]{1,0:T(8,128)(2,1)S(1)}, u32[]{:S(2)}, u32[]{:S(2)}) %collective-permute-start) | collective-permute-done | bytes 147488 | tf_op jit(solution)/shard_map/ppermute | solution.py:248
  10.2 0.7 %shard_map.74 = (bf16[128,1024]{1,0:T(8,128)(2,1)S(1)}, bf16[64,1024]{1,0:T(8,128)(2,1)S(1)}, bf16[64,1024]{1,0:T(8,128)(2,1)S(1)}) custom-call(bf16[128,1024]{1,0:T(8,128)(2,1)S(1)} %copy-done.1, bf16[144,512]{1,0:T(8,128)(2,1)S(1)} %collective-permute-done.halo_ref, bf16[128,256]{1,0:T(8,128)(2,1)S(1)} %copy-done.2, bf16[128,256]{1,0:T(8,128)(2,1)S(1)} %copy-done.3, ...), custom_call_target="tpu_custom_call" | custom-call | flops 134217728 | bytes 786432 | tf_op jit(solution)/shard_map/pallas_call | solution.py:120
  10.9 3.5 %collective-permute-start.6 = (bf16[64,1024]{1,0:T(8,128)(2,1)S(1)}, bf16[64,1024]{1,0:T(8,128)(2,1)S(1)}, u32[]{:S(2)}, u32[]{:S(2)}) collective-permute-start(bf16[64,1024]{1,0:T(8,128)(2,1)S(1)} %get-tuple-element.26), channel_id=1, source_target_pairs={{0,8},{4,12},{8,0},{12,4},{1,9},{5,13},{9,1},{13,5},{2,10},{6,14},... | collective-permute-start | bytes 393224 | tf_op jit(solution)/shard_map/ppermute | solution.py:227
  14.3 1.6 %collective-permute-start.5 = (bf16[128,1024]{1,0:T(8,128)(2,1)S(1)}, bf16[128,1024]{1,0:T(8,128)(2,1)S(1)}, u32[]{:S(2)}, u32[]{:S(2)}) collective-permute-start(bf16[128,1024]{1,0:T(8,128)(2,1)S(1)} %get-tuple-element.22.refs_0_), channel_id=1, source_target_pairs={{0,4},{4,0},{8,12},{12,8},{1,5},{5,1},{9,13},{13,9},{2,6},{6,2},{1... | collective-permute-start | bytes 786440 | tf_op jit(solution)/shard_map/ppermute | solution.py:227
  17.3 8.4 %collective-permute-done.1 = s32[2]{0:T(128)S(1)} collective-permute-done((s32[2]{0:T(128)S(1)}, s32[2]{0:T(128)S(1)}, u32[]{:S(2)}, u32[]{:S(2)}) %collective-permute-start.1) | collective-permute-done | bytes 40 | tf_op jit(solution)/shard_map/ppermute | solution.py:227
  25.9 1.4 %collective-permute-start.7 = (bf16[64,1024]{1,0:T(8,128)(2,1)S(1)}, bf16[64,1024]{1,0:T(8,128)(2,1)S(1)}, u32[]{:S(2)}, u32[]{:S(2)}) collective-permute-start(bf16[64,1024]{1,0:T(8,128)(2,1)S(1)} %collective-permute-done.6.refs_1_), channel_id=1, source_target_pairs={{0,4},{4,0},{8,12},{12,8},{1,5},{5,1},{9,13},{13,9},{2,6},{6,2},{1... | collective-permute-start | bytes 393224 | tf_op jit(solution)/shard_map/ppermute | solution.py:227
  27.3 1.5 %collective-permute-start.4 = (bf16[64,512]{1,0:T(8,128)(2,1)S(1)}, bf16[64,512]{1,0:T(8,128)(2,1)S(1)}, u32[]{:S(2)}, u32[]{:S(2)}) collective-permute-start(bf16[64,512]{1,0:T(8,128)(2,1)S(1)} %shard_map.76.refs_0_), channel_id=1, source_target_pairs={{0,2},{1,3},{2,0},{3,1},{4,6},{5,7},{6,4},{7,5},{8,10},{9,11},{10,... | collective-permute-start | bytes 196616 | tf_op jit(solution)/shard_map/ppermute | solution.py:227
  28.8 2.8 %collective-permute-done.4.refs_1_ = bf16[64,512]{1,0:T(8,128)(2,1)S(1)} collective-permute-done((bf16[64,512]{1,0:T(8,128)(2,1)S(1)}, bf16[64,512]{1,0:T(8,128)(2,1)S(1)}, u32[]{:S(2)}, u32[]{:S(2)}) %collective-permute-start.4) | collective-permute-done | bytes 65568 | tf_op jit(solution)/shard_map/ppermute | solution.py:227
  32.2 0.7 %collective-permute-start.11 = (bf16[64,1024]{1,0:T(8,128)(2,1)S(1)}, bf16[64,1024]{1,0:T(8,128)(2,1)S(1)}, u32[]{:S(2)}, u32[]{:S(2)}) collective-permute-start(bf16[64,1024]{1,0:T(8,128)(2,1)S(1)} %collective-permute-done.8.refs_3_), channel_id=1, source_target_pairs={{0,4},{4,0},{8,12},{12,8},{1,5},{5,1},{9,13},{13,9},{2,6},{6,2},{1... | collective-permute-start | bytes 393224 | tf_op jit(solution)/shard_map/ppermute | solution.py:227
  32.9 0.6 %collective-permute-done.9.refs_1_ = bf16[160,512]{1,0:T(8,128)(2,1)S(1)} collective-permute-done((bf16[160,512]{1,0:T(8,128)(2,1)S(1)}, bf16[160,512]{1,0:T(8,128)(2,1)S(1)}, u32[]{:S(2)}, u32[]{:S(2)}) %collective-permute-start.9) | collective-permute-done | bytes 163872 | tf_op jit(solution)/shard_map/ppermute | solution.py:227
  33.6 1.6 %collective-permute-start.10 = (bf16[160,512]{1,0:T(8,128)(2,1)S(1)}, bf16[160,512]{1,0:T(8,128)(2,1)S(1)}, u32[]{:S(2)}, u32[]{:S(2)}) collective-permute-start(bf16[160,512]{1,0:T(8,128)(2,1)S(1)} %shard_map.79.refs_0_), channel_id=1, source_target_pairs={{0,2},{1,3},{2,0},{3,1},{4,6},{5,7},{6,4},{7,5},{8,10},{9,11},{10,... | collective-permute-start | bytes 491528 | tf_op jit(solution)/shard_map/ppermute | solution.py:227
  35.2 2.3 %collective-permute-start.2 = (s32[1,4]{1,0:T(1,128)S(1)}, s32[1,4]{1,0:T(1,128)S(1)}, u32[]{:S(2)}, u32[]{:S(2)}) collective-permute-start(s32[1,4]{1,0:T(1,128)S(1)} %add_bitcast_fusion.own_ref), channel_id=1, source_target_pairs={{0,8},{4,12},{8,0},{12,4},{1,9},{5,13},{9,1},{13,5},{2,10},{6,14},... | collective-permute-start | bytes 56 | tf_op jit(solution)/shard_map/ppermute | solution.py:227
  37.5 2.2 %collective-permute-done.2.far_ref = s32[1,4]{1,0:T(1,128)S(1)} collective-permute-done((s32[1,4]{1,0:T(1,128)S(1)}, s32[1,4]{1,0:T(1,128)S(1)}, u32[]{:S(2)}, u32[]{:S(2)}) %collective-permute-start.2) | collective-permute-done | bytes 48 | tf_op jit(solution)/shard_map/ppermute | solution.py:227
  40.0 1.2 %collective-permute-done.12.refs_1_ = bf16[32,512]{1,0:T(8,128)(2,1)S(1)} collective-permute-done((bf16[32,512]{1,0:T(8,128)(2,1)S(1)}, bf16[32,512]{1,0:T(8,128)(2,1)S(1)}, u32[]{:S(2)}, u32[]{:S(2)}) %collective-permute-start.12) | collective-permute-done | bytes 32800 | tf_op jit(solution)/shard_map/ppermute | solution.py:227
  41.2 0.6 %collective-permute-start.13 = (bf16[32,512]{1,0:T(8,128)(2,1)S(1)}, bf16[32,512]{1,0:T(8,128)(2,1)S(1)}, u32[]{:S(2)}, u32[]{:S(2)}) collective-permute-start(bf16[32,512]{1,0:T(8,128)(2,1)S(1)} %shard_map.82.refs_0_), channel_id=1, source_target_pairs={{0,2},{1,3},{2,0},{3,1},{4,6},{5,7},{6,4},{7,5},{8,10},{9,11},{10,... | collective-permute-start | bytes 98312 | tf_op jit(solution)/shard_map/ppermute | solution.py:227
  41.8 3.4 %collective-permute-done.13.refs_1_ = bf16[32,512]{1,0:T(8,128)(2,1)S(1)} collective-permute-done((bf16[32,512]{1,0:T(8,128)(2,1)S(1)}, bf16[32,512]{1,0:T(8,128)(2,1)S(1)}, u32[]{:S(2)}, u32[]{:S(2)}) %collective-permute-start.13) | collective-permute-done | bytes 32800 | tf_op jit(solution)/shard_map/ppermute | solution.py:227
  45.5 0.8 %collective-permute-start.14 = (bf16[32,512]{1,0:T(8,128)(2,1)S(1)}, bf16[32,512]{1,0:T(8,128)(2,1)S(1)}, u32[]{:S(2)}, u32[]{:S(2)}) collective-permute-start(bf16[32,512]{1,0:T(8,128)(2,1)S(1)} %get-tuple-element.36), channel_id=1, source_target_pairs={{0,4},{4,0},{8,12},{12,8},{1,5},{5,1},{9,13},{13,9},{2,6},{6,2},{1... | collective-permute-start | bytes 98312 | tf_op jit(solution)/shard_map/ppermute | solution.py:227
  46.3 2.2 %collective-permute-start.15 = (bf16[32,512]{1,0:T(8,128)(2,1)S(1)}, bf16[32,512]{1,0:T(8,128)(2,1)S(1)}, u32[]{:S(2)}, u32[]{:S(2)}) collective-permute-start(bf16[32,512]{1,0:T(8,128)(2,1)S(1)} %get-tuple-element.37), channel_id=1, source_target_pairs={{0,8},{4,12},{8,0},{12,4},{1,9},{5,13},{9,1},{13,5},{2,10},{6,14},... | collective-permute-start | bytes 98312 | tf_op jit(solution)/shard_map/ppermute | solution.py:227
  48.6 1.4 %collective-permute-start.16 = (bf16[32,512]{1,0:T(8,128)(2,1)S(1)}, bf16[32,512]{1,0:T(8,128)(2,1)S(1)}, u32[]{:S(2)}, u32[]{:S(2)}) collective-permute-start(bf16[32,512]{1,0:T(8,128)(2,1)S(1)} %get-tuple-element.38), channel_id=1, source_target_pairs={{0,12},{4,8},{8,4},{12,0},{1,13},{5,9},{9,5},{13,1},{2,14},{6,10},... | collective-permute-start | bytes 98312 | tf_op jit(solution)/shard_map/ppermute | solution.py:227
  50.0 1.2 %collective-permute-done.15.refs_2_ = bf16[32,512]{1,0:T(8,128)(2,1)S(1)} collective-permute-done((bf16[32,512]{1,0:T(8,128)(2,1)S(1)}, bf16[32,512]{1,0:T(8,128)(2,1)S(1)}, u32[]{:S(2)}, u32[]{:S(2)}) %collective-permute-start.15) | collective-permute-done | bytes 32800 | tf_op jit(solution)/shard_map/ppermute | solution.py:227
  51.1 3.1 %collective-permute-done.16.refs_3_ = bf16[32,512]{1,0:T(8,128)(2,1)S(1)} collective-permute-done((bf16[32,512]{1,0:T(8,128)(2,1)S(1)}, bf16[32,512]{1,0:T(8,128)(2,1)S(1)}, u32[]{:S(2)}, u32[]{:S(2)}) %collective-permute-start.16) | collective-permute-done | bytes 32800 | tf_op jit(solution)/shard_map/ppermute | solution.py:227
  54.3 0.7 %shard_map.85 = bf16[32,2048]{1,0:T(8,128)(2,1)} custom-call(bf16[32,512]{1,0:T(8,128)(2,1)S(1)} %get-tuple-element.35.refs_0_, bf16[32,512]{1,0:T(8,128)(2,1)S(1)} %collective-permute-done.14.refs_1_, bf16[32,512]{1,0:T(8,128)(2,1)S(1)} %collective-permute-done.15.refs_2_, bf16[32,512]{1,0:T(8,128)(2,1)S(1)} %collective-permute-done.16.refs_3_), custom_call_target="tpu_custom_call" | custom-call | bytes 262144 | tf_op jit(solution)/shard_map/pallas_call | solution.py:216
  (38 shorter events, 2.8 us)
Async XLA Ops:
  0.0 10.2 %copy-start.1 = (bf16[128,1024]{1,0:T(8,128)(2,1)S(1)}, bf16[128,1024]{1,0:T(8,128)(2,1)}, u32[]{:S(2)}) copy-start(bf16[128,1024]{1,0:T(8,128)(2,1)} %q_ref.1) | copy-start | bytes 786436
  0.0 10.2 %copy-start.2 = (bf16[128,256]{1,0:T(8,128)(2,1)S(1)}, bf16[128,256]{1,0:T(8,128)(2,1)}, u32[]{:S(2)}) copy-start(bf16[128,256]{1,0:T(8,128)(2,1)} %k_ref.3) | copy-start | bytes 196612
  0.0 10.2 %copy-start.3 = (bf16[128,256]{1,0:T(8,128)(2,1)S(1)}, bf16[128,256]{1,0:T(8,128)(2,1)}, u32[]{:S(2)}) copy-start(bf16[128,256]{1,0:T(8,128)(2,1)} %v_ref.3) | copy-start | bytes 196612
  0.0 15.9 %copy-start = (bf16[1024,512]{1,0:T(8,128)(2,1)S(1)}, bf16[1024,512]{1,0:T(8,128)(2,1)}, u32[]{:S(2)}) copy-start(bf16[1024,512]{1,0:T(8,128)(2,1)} %refs_1_.3) | copy-start | bytes 3145732
  1.7 8.5 %copy-start.4 = (s32[128]{0:T(128)S(1)}, s32[128]{0:T(128)}, u32[]{:S(2)}) copy-start(s32[128]{0:T(128)} %param.11) | copy-start | bytes 1540
  1.7 8.5 %copy-start.5 = (s32[128]{0:T(128)S(1)}, s32[128]{0:T(128)}, u32[]{:S(2)}) copy-start(s32[128]{0:T(128)} %param.10) | copy-start | bytes 1540
  1.7 8.5 %collective-permute-start = (bf16[144,512]{1,0:T(8,128)(2,1)}, bf16[144,512]{1,0:T(8,128)(2,1)S(1)}, u32[]{:S(2)}, u32[]{:S(2)}) collective-permute-start(bf16[144,512]{1,0:T(8,128)(2,1)} %shard_map.73), channel_id=1, source_target_pairs={{0,4},{4,8},{8,12},{1,5},{5,9},{9,13},{2,6},{6,10},{10,14},{3,7},{... | collective-permute-start | bytes 442376 | tf_op jit(solution)/shard_map/ppermute | solution.py:248
  10.9 15.0 %collective-permute-start.6 = (bf16[64,1024]{1,0:T(8,128)(2,1)S(1)}, bf16[64,1024]{1,0:T(8,128)(2,1)S(1)}, u32[]{:S(2)}, u32[]{:S(2)}) collective-permute-start(bf16[64,1024]{1,0:T(8,128)(2,1)S(1)} %get-tuple-element.26), channel_id=1, source_target_pairs={{0,8},{4,12},{8,0},{12,4},{1,9},{5,13},{9,1},{13,5},{2,10},{6,14},... | collective-permute-start | bytes 393224 | tf_op jit(solution)/shard_map/ppermute | solution.py:227
  14.3 17.3 %collective-permute-start.5 = (bf16[128,1024]{1,0:T(8,128)(2,1)S(1)}, bf16[128,1024]{1,0:T(8,128)(2,1)S(1)}, u32[]{:S(2)}, u32[]{:S(2)}) collective-permute-start(bf16[128,1024]{1,0:T(8,128)(2,1)S(1)} %get-tuple-element.22.refs_0_), channel_id=1, source_target_pairs={{0,4},{4,0},{8,12},{12,8},{1,5},{5,1},{9,13},{13,9},{2,6},{6,2},{1... | collective-permute-start | bytes 786440 | tf_op jit(solution)/shard_map/ppermute | solution.py:227
  16.2 0.7 %copy-start.6 = (s32[2]{0:T(128)S(1)}, s32[2]{0:T(128)}, u32[]{:S(2)}) copy-start(s32[2]{0:T(128)} %param.12) | copy-start | bytes 28
  16.2 9.6 %collective-permute-start.3 = (bf16[64,512]{1,0:T(8,128)(2,1)S(1)}, bf16[64,512]{1,0:T(8,128)(2,1)S(1)}, u32[]{:S(2)}, u32[]{:S(2)}) collective-permute-start(bf16[64,512]{1,0:T(8,128)(2,1)S(1)} %get-tuple-element.25), channel_id=1, source_target_pairs={{0,1},{1,0},{2,3},{3,2},{4,5},{5,4},{6,7},{7,6},{8,9},{9,8},{10,11... | collective-permute-start | bytes 196616 | tf_op jit(solution)/shard_map/ppermute | solution.py:227
  16.3 15.3 %collective-permute-start.8 = (bf16[64,1024]{1,0:T(8,128)(2,1)S(1)}, bf16[64,1024]{1,0:T(8,128)(2,1)S(1)}, u32[]{:S(2)}, u32[]{:S(2)}) collective-permute-start(bf16[64,1024]{1,0:T(8,128)(2,1)S(1)} %get-tuple-element.28), channel_id=1, source_target_pairs={{0,8},{4,12},{8,0},{12,4},{1,9},{5,13},{9,1},{13,5},{2,10},{6,14},... | collective-permute-start | bytes 393224 | tf_op jit(solution)/shard_map/ppermute | solution.py:227
  16.9 8.9 %collective-permute-start.1 = (s32[2]{0:T(128)S(1)}, s32[2]{0:T(128)S(1)}, u32[]{:S(2)}, u32[]{:S(2)}) collective-permute-start(s32[2]{0:T(128)S(1)} %copy-done.6), channel_id=1, source_target_pairs={{0,4},{4,0},{8,12},{12,8},{1,5},{5,1},{9,13},{13,9},{2,6},{6,2},{1... | collective-permute-start | bytes 32 | tf_op jit(solution)/shard_map/ppermute | solution.py:227
  25.9 5.7 %collective-permute-start.7 = (bf16[64,1024]{1,0:T(8,128)(2,1)S(1)}, bf16[64,1024]{1,0:T(8,128)(2,1)S(1)}, u32[]{:S(2)}, u32[]{:S(2)}) collective-permute-start(bf16[64,1024]{1,0:T(8,128)(2,1)S(1)} %collective-permute-done.6.refs_1_), channel_id=1, source_target_pairs={{0,4},{4,0},{8,12},{12,8},{1,5},{5,1},{9,13},{13,9},{2,6},{6,2},{1... | collective-permute-start | bytes 393224 | tf_op jit(solution)/shard_map/ppermute | solution.py:227
  27.3 4.3 %collective-permute-start.4 = (bf16[64,512]{1,0:T(8,128)(2,1)S(1)}, bf16[64,512]{1,0:T(8,128)(2,1)S(1)}, u32[]{:S(2)}, u32[]{:S(2)}) collective-permute-start(bf16[64,512]{1,0:T(8,128)(2,1)S(1)} %shard_map.76.refs_0_), channel_id=1, source_target_pairs={{0,2},{1,3},{2,0},{3,1},{4,6},{5,7},{6,4},{7,5},{8,10},{9,11},{10,... | collective-permute-start | bytes 196616 | tf_op jit(solution)/shard_map/ppermute | solution.py:227
  32.1 1.5 %collective-permute-start.9 = (bf16[160,512]{1,0:T(8,128)(2,1)S(1)}, bf16[160,512]{1,0:T(8,128)(2,1)S(1)}, u32[]{:S(2)}, u32[]{:S(2)}) collective-permute-start(bf16[160,512]{1,0:T(8,128)(2,1)S(1)} %get-tuple-element.31), channel_id=1, source_target_pairs={{0,1},{1,0},{2,3},{3,2},{4,5},{5,4},{6,7},{7,6},{8,9},{9,8},{10,11... | collective-permute-start | bytes 491528 | tf_op jit(solution)/shard_map/ppermute | solution.py:227
  32.2 7.4 %collective-permute-start.11 = (bf16[64,1024]{1,0:T(8,128)(2,1)S(1)}, bf16[64,1024]{1,0:T(8,128)(2,1)S(1)}, u32[]{:S(2)}, u32[]{:S(2)}) collective-permute-start(bf16[64,1024]{1,0:T(8,128)(2,1)S(1)} %collective-permute-done.8.refs_3_), channel_id=1, source_target_pairs={{0,4},{4,0},{8,12},{12,8},{1,5},{5,1},{9,13},{13,9},{2,6},{6,2},{1... | collective-permute-start | bytes 393224 | tf_op jit(solution)/shard_map/ppermute | solution.py:227
  33.6 11.6 %collective-permute-start.10 = (bf16[160,512]{1,0:T(8,128)(2,1)S(1)}, bf16[160,512]{1,0:T(8,128)(2,1)S(1)}, u32[]{:S(2)}, u32[]{:S(2)}) collective-permute-start(bf16[160,512]{1,0:T(8,128)(2,1)S(1)} %shard_map.79.refs_0_), channel_id=1, source_target_pairs={{0,2},{1,3},{2,0},{3,1},{4,6},{5,7},{6,4},{7,5},{8,10},{9,11},{10,... | collective-permute-start | bytes 491528 | tf_op jit(solution)/shard_map/ppermute | solution.py:227
  35.2 4.4 %collective-permute-start.2 = (s32[1,4]{1,0:T(1,128)S(1)}, s32[1,4]{1,0:T(1,128)S(1)}, u32[]{:S(2)}, u32[]{:S(2)}) collective-permute-start(s32[1,4]{1,0:T(1,128)S(1)} %add_bitcast_fusion.own_ref), channel_id=1, source_target_pairs={{0,8},{4,12},{8,0},{12,4},{1,9},{5,13},{9,1},{13,5},{2,10},{6,14},... | collective-permute-start | bytes 56 | tf_op jit(solution)/shard_map/ppermute | solution.py:227
  39.9 1.3 %collective-permute-start.12 = (bf16[32,512]{1,0:T(8,128)(2,1)S(1)}, bf16[32,512]{1,0:T(8,128)(2,1)S(1)}, u32[]{:S(2)}, u32[]{:S(2)}) collective-permute-start(bf16[32,512]{1,0:T(8,128)(2,1)S(1)} %get-tuple-element.34), channel_id=1, source_target_pairs={{0,1},{1,0},{2,3},{3,2},{4,5},{5,4},{6,7},{7,6},{8,9},{9,8},{10,11... | collective-permute-start | bytes 98312 | tf_op jit(solution)/shard_map/ppermute | solution.py:227
  41.2 4.0 %collective-permute-start.13 = (bf16[32,512]{1,0:T(8,128)(2,1)S(1)}, bf16[32,512]{1,0:T(8,128)(2,1)S(1)}, u32[]{:S(2)}, u32[]{:S(2)}) collective-permute-start(bf16[32,512]{1,0:T(8,128)(2,1)S(1)} %shard_map.82.refs_0_), channel_id=1, source_target_pairs={{0,2},{1,3},{2,0},{3,1},{4,6},{5,7},{6,4},{7,5},{8,10},{9,11},{10,... | collective-permute-start | bytes 98312 | tf_op jit(solution)/shard_map/ppermute | solution.py:227
  45.5 4.5 %collective-permute-start.14 = (bf16[32,512]{1,0:T(8,128)(2,1)S(1)}, bf16[32,512]{1,0:T(8,128)(2,1)S(1)}, u32[]{:S(2)}, u32[]{:S(2)}) collective-permute-start(bf16[32,512]{1,0:T(8,128)(2,1)S(1)} %get-tuple-element.36), channel_id=1, source_target_pairs={{0,4},{4,0},{8,12},{12,8},{1,5},{5,1},{9,13},{13,9},{2,6},{6,2},{1... | collective-permute-start | bytes 98312 | tf_op jit(solution)/shard_map/ppermute | solution.py:227
  46.3 4.8 %collective-permute-start.15 = (bf16[32,512]{1,0:T(8,128)(2,1)S(1)}, bf16[32,512]{1,0:T(8,128)(2,1)S(1)}, u32[]{:S(2)}, u32[]{:S(2)}) collective-permute-start(bf16[32,512]{1,0:T(8,128)(2,1)S(1)} %get-tuple-element.37), channel_id=1, source_target_pairs={{0,8},{4,12},{8,0},{12,4},{1,9},{5,13},{9,1},{13,5},{2,10},{6,14},... | collective-permute-start | bytes 98312 | tf_op jit(solution)/shard_map/ppermute | solution.py:227
  48.6 5.7 %collective-permute-start.16 = (bf16[32,512]{1,0:T(8,128)(2,1)S(1)}, bf16[32,512]{1,0:T(8,128)(2,1)S(1)}, u32[]{:S(2)}, u32[]{:S(2)}) collective-permute-start(bf16[32,512]{1,0:T(8,128)(2,1)S(1)} %get-tuple-element.38), channel_id=1, source_target_pairs={{0,12},{4,8},{8,4},{12,0},{1,13},{5,9},{9,5},{13,1},{2,14},{6,10},... | collective-permute-start | bytes 98312 | tf_op jit(solution)/shard_map/ppermute | solution.py:227

commit v4 on v3

--- a/solution.py
+++ b/solution.py
@@ -246,19 +246,20 @@
     end, start = doc_end.reshape(1, rows), doc_start.reshape(1, rows)
     message = pack(key_rows, value_rows, end)
     halo = lax.ppermute(message, "ctx", [(0, 1), (1, 2), (2, 3)])
+    target_1 = flip(after(block_target, message), "ctx", 1)
+    own_targets = jnp.concatenate([block_target, target_1]).reshape(1, 2 * blocks)
+    start = after(start, own_targets)
     whole, first, second = attend(blocks, queries, halo, key_rows, value_rows, end, start)
     first_2, second_2 = flip(first, "ctx", 2), flip(second, "ctx", 2)
     whole_1 = flip(whole, "ctx", 1)
-    target_1 = flip(after(block_target, whole), "ctx", 1)
-    own_targets = jnp.concatenate([block_target, target_1]).reshape(1, 2 * blocks)
+    far_targets = flip(own_targets, "ctx", 2)
     share_a = core_total(*project(block_rows, (whole,), out_weight))
-    first_2 = after(first_2, share_a, own_targets)
+    first_2 = after(first_2, share_a)
     first_3, second_3 = flip(first_2, "ctx", 1), flip(second_2, "ctx", 1)
     sum_a = chip_total(share_a)
-    second_2 = after(second_2, sum_a)
+    second_2 = after(second_2, sum_a, far_targets)
     share_b = core_total(*project(block_rows, (whole_1, first_2, first_3, second_2), out_weight))
-    far_targets = flip(own_targets, "ctx", 2)
-    second_3 = after(second_3, share_b, far_targets)
+    second_3 = after(second_3, share_b)
     share_c = core_total(*project(block_rows, (second_3,), out_weight))
     sum_b = chip_total(share_b)
     sum_c = chip_total(share_c)

time: 55.1 us -> 51.2 us (0.929)
  waiting for transfers between devices: 26.3 us -> 17 us
  starting transfers between devices: 23.7 us -> 28.6 us
    ppermute x16, waiting for transfers between devices: 22.9 us -> 17 us  [flip(): return lax.ppermute(array, axis, [(i, i ^ bits) for i in range(4)])]
    ppermute x16, starting transfers between devices: 18.6 us -> 23.7 us  [flip(): return lax.ppermute(array, axis, [(i, i ^ bits) for i in range(4)])]
    ppermute x1, waiting for transfers between devices: 3.4 us -> 0.01 us  [small_ring(): halo = lax.ppermute(message, 'ctx', [(0, 1), (1, 2), (2, 3)])]
  transfers between devices with their start and end apart: 17 -> 17, of which waited for: 9 -> 10; matrix products, arithmetic and copies ran while one was open for 0% -> 0% of each run, Pallas kernels for 1% -> 1%
where the time goes in v4:
time: 51.2 us; the launch traced here: 51 us
  starting transfers between devices  28.6 us (56%)
  waiting for transfers between devices  17 us (33%)
  Pallas kernels  4.53 us (9%)
  local copies, waits for them, and re-layouts  0.66 us (1%)
    ppermute x16, starting transfers between devices, flip(): return lax.ppermute(array, axis, [(i, i ^ bits) for i in range(4)])  23.7 us
    ppermute x16, waiting for transfers between devices, flip(): return lax.ppermute(array, axis, [(i, i ^ bits) for i in range(4)])  17 us
    ppermute x1, starting transfers between devices, small_ring(): halo = lax.ppermute(message, 'ctx', [(0, 1), (1, 2), (2, 3)])  4.94 us
    pallas_call x1, Pallas kernels, pack(): pl.pallas_call(pack_kernel, out_shape=jax.ShapeDtypeStruct((rows + 16, 2...  1.67 us
    pallas_call x3, Pallas kernels, project(): pl.pallas_call(functools.partial(project_kernel, block_rows), out_shape=(...  1.13 us
  transfers between devices with their start and end apart: 17, of which 10 were waited for; matrix products, arithmetic and copies ran while one was open for 0% of the time, Pallas kernels for 1%

profile of v4, /device:TPU:0, one launch (start us, length us, event | category | flops | bytes accessed | tf_op | source)
XLA Modules:
  0.0 51.0 jit_solution(12278048553537508088)
XLA Ops:
  0.0 1.7 %shard_map.73 = bf16[144,512]{1,0:T(8,128)(2,1)} custom-call(bf16[128,256]{1,0:T(8,128)(2,1)} %k_ref.3, bf16[128,256]{1,0:T(8,128)(2,1)} %v_ref.3, s32[1,128]{1,0:T(1,128)} %bitcast.4), custom_call_target="tpu_custom_call" | custom-call | flops 1000000000 | bytes 262144 | tf_op jit(solution)/shard_map/pallas_call | solution.py:51
  1.7 4.9 %collective-permute-start.2 = (bf16[144,512]{1,0:T(8,128)(2,1)}, bf16[144,512]{1,0:T(8,128)(2,1)S(1)}, u32[]{:S(2)}, u32[]{:S(2)}) collective-permute-start(bf16[144,512]{1,0:T(8,128)(2,1)} %shard_map.73), channel_id=1, source_target_pairs={{0,4},{4,8},{8,12},{1,5},{5,9},{9,13},{2,6},{6,10},{10,14},{3,7},{... | collective-permute-start | bytes 442376 | tf_op jit(solution)/shard_map/ppermute | solution.py:248
  6.6 1.6 %collective-permute-start = (s32[2]{0:T(128)S(1)}, s32[2]{0:T(128)S(1)}, u32[]{:S(2)}, u32[]{:S(2)}) collective-permute-start(s32[2]{0:T(128)S(1)} %copy-done.6), channel_id=1, source_target_pairs={{0,4},{4,0},{8,12},{12,8},{1,5},{5,1},{9,13},{13,9},{2,6},{6,2},{1... | collective-permute-start | bytes 32 | tf_op jit(solution)/shard_map/ppermute | solution.py:227
  8.3 2.0 %collective-permute-done = s32[2]{0:T(128)S(1)} collective-permute-done((s32[2]{0:T(128)S(1)}, s32[2]{0:T(128)S(1)}, u32[]{:S(2)}, u32[]{:S(2)}) %collective-permute-start) | collective-permute-done | bytes 40 | tf_op jit(solution)/shard_map/ppermute | solution.py:227
  11.0 0.7 %shard_map.74 = (bf16[128,1024]{1,0:T(8,128)(2,1)S(1)}, bf16[64,1024]{1,0:T(8,128)(2,1)S(1)}, bf16[64,1024]{1,0:T(8,128)(2,1)S(1)}) custom-call(bf16[128,1024]{1,0:T(8,128)(2,1)S(1)} %copy-done.1, bf16[144,512]{1,0:T(8,128)(2,1)S(1)} %collective-permute-done.2.halo_ref, bf16[128,256]{1,0:T(8,128)(2,1)S(1)} %copy-done.2, bf16[128,256]{1,0:T(8,128)(2,1)S(1)} %copy-done.3, ...), custom_call_target="tpu_custom_call" | custom-call | flops 134217728 | bytes 786432 | tf_op jit(solution)/shard_map/pallas_call | solution.py:120
  11.7 2.7 %collective-permute-start.6 = (bf16[64,1024]{1,0:T(8,128)(2,1)S(1)}, bf16[64,1024]{1,0:T(8,128)(2,1)S(1)}, u32[]{:S(2)}, u32[]{:S(2)}) collective-permute-start(bf16[64,1024]{1,0:T(8,128)(2,1)S(1)} %get-tuple-element.28), channel_id=1, source_target_pairs={{0,8},{4,12},{8,0},{12,4},{1,9},{5,13},{9,1},{13,5},{2,10},{6,14},... | collective-permute-start | bytes 393224 | tf_op jit(solution)/shard_map/ppermute | solution.py:227
  14.3 2.2 %collective-permute-start.5 = (bf16[128,1024]{1,0:T(8,128)(2,1)S(1)}, bf16[128,1024]{1,0:T(8,128)(2,1)S(1)}, u32[]{:S(2)}, u32[]{:S(2)}) collective-permute-start(bf16[128,1024]{1,0:T(8,128)(2,1)S(1)} %get-tuple-element.25.refs_0_), channel_id=1, source_target_pairs={{0,4},{4,0},{8,12},{12,8},{1,5},{5,1},{9,13},{13,9},{2,6},{6,2},{1... | collective-permute-start | bytes 786440 | tf_op jit(solution)/shard_map/ppermute | solution.py:227
  17.4 0.8 %collective-permute-done.3.refs_1_ = bf16[64,512]{1,0:T(8,128)(2,1)S(1)} collective-permute-done((bf16[64,512]{1,0:T(8,128)(2,1)S(1)}, bf16[64,512]{1,0:T(8,128)(2,1)S(1)}, u32[]{:S(2)}, u32[]{:S(2)}) %collective-permute-start.3) | collective-permute-done | bytes 65568 | tf_op jit(solution)/shard_map/ppermute | solution.py:227
  18.2 1.0 %collective-permute-done.6.refs_1_ = bf16[64,1024]{1,0:T(8,128)(2,1)S(1)} collective-permute-done((bf16[64,1024]{1,0:T(8,128)(2,1)S(1)}, bf16[64,1024]{1,0:T(8,128)(2,1)S(1)}, u32[]{:S(2)}, u32[]{:S(2)}) %collective-permute-start.6) | collective-permute-done | bytes 131104 | tf_op jit(solution)/shard_map/ppermute | solution.py:227
  19.3 2.3 %collective-permute-start.7 = (bf16[64,1024]{1,0:T(8,128)(2,1)S(1)}, bf16[64,1024]{1,0:T(8,128)(2,1)S(1)}, u32[]{:S(2)}, u32[]{:S(2)}) collective-permute-start(bf16[64,1024]{1,0:T(8,128)(2,1)S(1)} %collective-permute-done.6.refs_1_), channel_id=1, source_target_pairs={{0,4},{4,0},{8,12},{12,8},{1,5},{5,1},{9,13},{13,9},{2,6},{6,2},{1... | collective-permute-start | bytes 393224 | tf_op jit(solution)/shard_map/ppermute | solution.py:227
  21.6 1.5 %collective-permute-start.4 = (bf16[64,512]{1,0:T(8,128)(2,1)S(1)}, bf16[64,512]{1,0:T(8,128)(2,1)S(1)}, u32[]{:S(2)}, u32[]{:S(2)}) collective-permute-start(bf16[64,512]{1,0:T(8,128)(2,1)S(1)} %shard_map.76.refs_0_), channel_id=1, source_target_pairs={{0,2},{1,3},{2,0},{3,1},{4,6},{5,7},{6,4},{7,5},{8,10},{9,11},{10,... | collective-permute-start | bytes 196616 | tf_op jit(solution)/shard_map/ppermute | solution.py:227
  23.0 3.4 %collective-permute-start.1 = (s32[1,4]{1,0:T(1,128)S(1)}, s32[1,4]{1,0:T(1,128)S(1)}, u32[]{:S(2)}, u32[]{:S(2)}) collective-permute-start(s32[1,4]{1,0:T(1,128)S(1)} %add_bitcast_fusion.own_ref), channel_id=1, source_target_pairs={{0,8},{4,12},{8,0},{12,4},{1,9},{5,13},{9,1},{13,5},{2,10},{6,14},... | collective-permute-start | bytes 56 | tf_op jit(solution)/shard_map/ppermute | solution.py:227
  26.5 1.6 %collective-permute-done.1.far_ref = s32[1,4]{1,0:T(1,128)S(1)} collective-permute-done((s32[1,4]{1,0:T(1,128)S(1)}, s32[1,4]{1,0:T(1,128)S(1)}, u32[]{:S(2)}, u32[]{:S(2)}) %collective-permute-start.1) | collective-permute-done | bytes 48 | tf_op jit(solution)/shard_map/ppermute | solution.py:227
  29.3 1.8 %collective-permute-start.11 = (bf16[64,1024]{1,0:T(8,128)(2,1)S(1)}, bf16[64,1024]{1,0:T(8,128)(2,1)S(1)}, u32[]{:S(2)}, u32[]{:S(2)}) collective-permute-start(bf16[64,1024]{1,0:T(8,128)(2,1)S(1)} %collective-permute-done.8.refs_3_), channel_id=1, source_target_pairs={{0,4},{4,0},{8,12},{12,8},{1,5},{5,1},{9,13},{13,9},{2,6},{6,2},{1... | collective-permute-start | bytes 393224 | tf_op jit(solution)/shard_map/ppermute | solution.py:227
  31.1 1.6 %collective-permute-start.10 = (bf16[160,512]{1,0:T(8,128)(2,1)S(1)}, bf16[160,512]{1,0:T(8,128)(2,1)S(1)}, u32[]{:S(2)}, u32[]{:S(2)}) collective-permute-start(bf16[160,512]{1,0:T(8,128)(2,1)S(1)} %shard_map.79.refs_0_), channel_id=1, source_target_pairs={{0,2},{1,3},{2,0},{3,1},{4,6},{5,7},{6,4},{7,5},{8,10},{9,11},{10,... | collective-permute-start | bytes 491528 | tf_op jit(solution)/shard_map/ppermute | solution.py:227
  32.7 2.5 %collective-permute-done.11.refs_0_ = bf16[64,1024]{1,0:T(8,128)(2,1)S(1)} collective-permute-done((bf16[64,1024]{1,0:T(8,128)(2,1)S(1)}, bf16[64,1024]{1,0:T(8,128)(2,1)S(1)}, u32[]{:S(2)}, u32[]{:S(2)}) %collective-permute-start.11) | collective-permute-done | bytes 131104 | tf_op jit(solution)/shard_map/ppermute | solution.py:227
  35.6 1.2 %collective-permute-done.12.refs_1_ = bf16[32,512]{1,0:T(8,128)(2,1)S(1)} collective-permute-done((bf16[32,512]{1,0:T(8,128)(2,1)S(1)}, bf16[32,512]{1,0:T(8,128)(2,1)S(1)}, u32[]{:S(2)}, u32[]{:S(2)}) %collective-permute-start.12) | collective-permute-done | bytes 32800 | tf_op jit(solution)/shard_map/ppermute | solution.py:227
  36.8 1.6 %collective-permute-start.13 = (bf16[32,512]{1,0:T(8,128)(2,1)S(1)}, bf16[32,512]{1,0:T(8,128)(2,1)S(1)}, u32[]{:S(2)}, u32[]{:S(2)}) collective-permute-start(bf16[32,512]{1,0:T(8,128)(2,1)S(1)} %shard_map.82.refs_0_), channel_id=1, source_target_pairs={{0,2},{1,3},{2,0},{3,1},{4,6},{5,7},{6,4},{7,5},{8,10},{9,11},{10,... | collective-permute-start | bytes 98312 | tf_op jit(solution)/shard_map/ppermute | solution.py:227
  38.4 2.4 %collective-permute-done.13.refs_1_ = bf16[32,512]{1,0:T(8,128)(2,1)S(1)} collective-permute-done((bf16[32,512]{1,0:T(8,128)(2,1)S(1)}, bf16[32,512]{1,0:T(8,128)(2,1)S(1)}, u32[]{:S(2)}, u32[]{:S(2)}) %collective-permute-start.13) | collective-permute-done | bytes 32800 | tf_op jit(solution)/shard_map/ppermute | solution.py:227
  41.1 1.8 %collective-permute-start.14 = (bf16[32,512]{1,0:T(8,128)(2,1)S(1)}, bf16[32,512]{1,0:T(8,128)(2,1)S(1)}, u32[]{:S(2)}, u32[]{:S(2)}) collective-permute-start(bf16[32,512]{1,0:T(8,128)(2,1)S(1)} %get-tuple-element.38), channel_id=1, source_target_pairs={{0,4},{4,0},{8,12},{12,8},{1,5},{5,1},{9,13},{13,9},{2,6},{6,2},{1... | collective-permute-start | bytes 98312 | tf_op jit(solution)/shard_map/ppermute | solution.py:227
  42.9 1.8 %collective-permute-start.15 = (bf16[32,512]{1,0:T(8,128)(2,1)S(1)}, bf16[32,512]{1,0:T(8,128)(2,1)S(1)}, u32[]{:S(2)}, u32[]{:S(2)}) collective-permute-start(bf16[32,512]{1,0:T(8,128)(2,1)S(1)} %get-tuple-element.39), channel_id=1, source_target_pairs={{0,8},{4,12},{8,0},{12,4},{1,9},{5,13},{9,1},{13,5},{2,10},{6,14},... | collective-permute-start | bytes 98312 | tf_op jit(solution)/shard_map/ppermute | solution.py:227
  44.7 0.9 %collective-permute-start.16 = (bf16[32,512]{1,0:T(8,128)(2,1)S(1)}, bf16[32,512]{1,0:T(8,128)(2,1)S(1)}, u32[]{:S(2)}, u32[]{:S(2)}) collective-permute-start(bf16[32,512]{1,0:T(8,128)(2,1)S(1)} %get-tuple-element.40), channel_id=1, source_target_pairs={{0,12},{4,8},{8,4},{12,0},{1,13},{5,9},{9,5},{13,1},{2,14},{6,10},... | collective-permute-start | bytes 98312 | tf_op jit(solution)/shard_map/ppermute | solution.py:227
  45.5 2.6 %collective-permute-done.15.refs_2_ = bf16[32,512]{1,0:T(8,128)(2,1)S(1)} collective-permute-done((bf16[32,512]{1,0:T(8,128)(2,1)S(1)}, bf16[32,512]{1,0:T(8,128)(2,1)S(1)}, u32[]{:S(2)}, u32[]{:S(2)}) %collective-permute-start.15) | collective-permute-done | bytes 32800 | tf_op jit(solution)/shard_map/ppermute | solution.py:227
  48.2 2.2 %collective-permute-done.16.refs_3_ = bf16[32,512]{1,0:T(8,128)(2,1)S(1)} collective-permute-done((bf16[32,512]{1,0:T(8,128)(2,1)S(1)}, bf16[32,512]{1,0:T(8,128)(2,1)S(1)}, u32[]{:S(2)}, u32[]{:S(2)}) %collective-permute-start.16) | collective-permute-done | bytes 32800 | tf_op jit(solution)/shard_map/ppermute | solution.py:227
  (38 shorter events, 4.2 us)
Async XLA Ops:
  0.0 6.6 %copy-start.6 = (s32[2]{0:T(128)S(1)}, s32[2]{0:T(128)}, u32[]{:S(2)}) copy-start(s32[2]{0:T(128)} %param.12) | copy-start | bytes 28
  0.0 10.3 %copy-start.1 = (bf16[128,1024]{1,0:T(8,128)(2,1)S(1)}, bf16[128,1024]{1,0:T(8,128)(2,1)}, u32[]{:S(2)}) copy-start(bf16[128,1024]{1,0:T(8,128)(2,1)} %q_ref.1) | copy-start | bytes 786436
  0.0 10.3 %copy-start.2 = (bf16[128,256]{1,0:T(8,128)(2,1)S(1)}, bf16[128,256]{1,0:T(8,128)(2,1)}, u32[]{:S(2)}) copy-start(bf16[128,256]{1,0:T(8,128)(2,1)} %k_ref.3) | copy-start | bytes 196612
  0.0 10.3 %copy-start.3 = (bf16[128,256]{1,0:T(8,128)(2,1)S(1)}, bf16[128,256]{1,0:T(8,128)(2,1)}, u32[]{:S(2)}) copy-start(bf16[128,256]{1,0:T(8,128)(2,1)} %v_ref.3) | copy-start | bytes 196612
  0.0 16.6 %copy-start = (bf16[1024,512]{1,0:T(8,128)(2,1)S(1)}, bf16[1024,512]{1,0:T(8,128)(2,1)}, u32[]{:S(2)}) copy-start(bf16[1024,512]{1,0:T(8,128)(2,1)} %refs_1_.3) | copy-start | bytes 3145732
  1.7 8.6 %collective-permute-start.2 = (bf16[144,512]{1,0:T(8,128)(2,1)}, bf16[144,512]{1,0:T(8,128)(2,1)S(1)}, u32[]{:S(2)}, u32[]{:S(2)}) collective-permute-start(bf16[144,512]{1,0:T(8,128)(2,1)} %shard_map.73), channel_id=1, source_target_pairs={{0,4},{4,8},{8,12},{1,5},{5,9},{9,13},{2,6},{6,10},{10,14},{3,7},{... | collective-permute-start | bytes 442376 | tf_op jit(solution)/shard_map/ppermute | solution.py:248
  6.6 3.6 %collective-permute-start = (s32[2]{0:T(128)S(1)}, s32[2]{0:T(128)S(1)}, u32[]{:S(2)}, u32[]{:S(2)}) collective-permute-start(s32[2]{0:T(128)S(1)} %copy-done.6), channel_id=1, source_target_pairs={{0,4},{4,0},{8,12},{12,8},{1,5},{5,1},{9,13},{13,9},{2,6},{6,2},{1... | collective-permute-start | bytes 32 | tf_op jit(solution)/shard_map/ppermute | solution.py:227
  10.3 0.7 %copy-start.4 = (s32[128]{0:T(128)S(1)}, s32[128]{0:T(128)}, u32[]{:S(2)}) copy-start(s32[128]{0:T(128)} %param.11) | copy-start | bytes 1540
  10.3 0.7 %copy-start.5 = (s32[128]{0:T(128)S(1)}, s32[128]{0:T(128)}, u32[]{:S(2)}) copy-start(s32[128]{0:T(128)} %param.10) | copy-start | bytes 1540
  11.7 7.6 %collective-permute-start.6 = (bf16[64,1024]{1,0:T(8,128)(2,1)S(1)}, bf16[64,1024]{1,0:T(8,128)(2,1)S(1)}, u32[]{:S(2)}, u32[]{:S(2)}) collective-permute-start(bf16[64,1024]{1,0:T(8,128)(2,1)S(1)} %get-tuple-element.28), channel_id=1, source_target_pairs={{0,8},{4,12},{8,0},{12,4},{1,9},{5,13},{9,1},{13,5},{2,10},{6,14},... | collective-permute-start | bytes 393224 | tf_op jit(solution)/shard_map/ppermute | solution.py:227
  14.3 14.3 %collective-permute-start.5 = (bf16[128,1024]{1,0:T(8,128)(2,1)S(1)}, bf16[128,1024]{1,0:T(8,128)(2,1)S(1)}, u32[]{:S(2)}, u32[]{:S(2)}) collective-permute-start(bf16[128,1024]{1,0:T(8,128)(2,1)S(1)} %get-tuple-element.25.refs_0_), channel_id=1, source_target_pairs={{0,4},{4,0},{8,12},{12,8},{1,5},{5,1},{9,13},{13,9},{2,6},{6,2},{1... | collective-permute-start | bytes 786440 | tf_op jit(solution)/shard_map/ppermute | solution.py:227
  16.9 1.3 %collective-permute-start.3 = (bf16[64,512]{1,0:T(8,128)(2,1)S(1)}, bf16[64,512]{1,0:T(8,128)(2,1)S(1)}, u32[]{:S(2)}, u32[]{:S(2)}) collective-permute-start(bf16[64,512]{1,0:T(8,128)(2,1)S(1)} %get-tuple-element.27), channel_id=1, source_target_pairs={{0,1},{1,0},{2,3},{3,2},{4,5},{5,4},{6,7},{7,6},{8,9},{9,8},{10,11... | collective-permute-start | bytes 196616 | tf_op jit(solution)/shard_map/ppermute | solution.py:227
  17.0 11.1 %collective-permute-start.8 = (bf16[64,1024]{1,0:T(8,128)(2,1)S(1)}, bf16[64,1024]{1,0:T(8,128)(2,1)S(1)}, u32[]{:S(2)}, u32[]{:S(2)}) collective-permute-start(bf16[64,1024]{1,0:T(8,128)(2,1)S(1)} %get-tuple-element.30), channel_id=1, source_target_pairs={{0,8},{4,12},{8,0},{12,4},{1,9},{5,13},{9,1},{13,5},{2,10},{6,14},... | collective-permute-start | bytes 393224 | tf_op jit(solution)/shard_map/ppermute | solution.py:227
  19.3 9.4 %collective-permute-start.7 = (bf16[64,1024]{1,0:T(8,128)(2,1)S(1)}, bf16[64,1024]{1,0:T(8,128)(2,1)S(1)}, u32[]{:S(2)}, u32[]{:S(2)}) collective-permute-start(bf16[64,1024]{1,0:T(8,128)(2,1)S(1)} %collective-permute-done.6.refs_1_), channel_id=1, source_target_pairs={{0,4},{4,0},{8,12},{12,8},{1,5},{5,1},{9,13},{13,9},{2,6},{6,2},{1... | collective-permute-start | bytes 393224 | tf_op jit(solution)/shard_map/ppermute | solution.py:227
  21.6 4.9 %collective-permute-start.4 = (bf16[64,512]{1,0:T(8,128)(2,1)S(1)}, bf16[64,512]{1,0:T(8,128)(2,1)S(1)}, u32[]{:S(2)}, u32[]{:S(2)}) collective-permute-start(bf16[64,512]{1,0:T(8,128)(2,1)S(1)} %shard_map.76.refs_0_), channel_id=1, source_target_pairs={{0,2},{1,3},{2,0},{3,1},{4,6},{5,7},{6,4},{7,5},{8,10},{9,11},{10,... | collective-permute-start | bytes 196616 | tf_op jit(solution)/shard_map/ppermute | solution.py:227
  23.0 5.0 %collective-permute-start.1 = (s32[1,4]{1,0:T(1,128)S(1)}, s32[1,4]{1,0:T(1,128)S(1)}, u32[]{:S(2)}, u32[]{:S(2)}) collective-permute-start(s32[1,4]{1,0:T(1,128)S(1)} %add_bitcast_fusion.own_ref), channel_id=1, source_target_pairs={{0,8},{4,12},{8,0},{12,4},{1,9},{5,13},{9,1},{13,5},{2,10},{6,14},... | collective-permute-start | bytes 56 | tf_op jit(solution)/shard_map/ppermute | solution.py:227
  29.2 1.9 %collective-permute-start.9 = (bf16[160,512]{1,0:T(8,128)(2,1)S(1)}, bf16[160,512]{1,0:T(8,128)(2,1)S(1)}, u32[]{:S(2)}, u32[]{:S(2)}) collective-permute-start(bf16[160,512]{1,0:T(8,128)(2,1)S(1)} %get-tuple-element.33), channel_id=1, source_target_pairs={{0,1},{1,0},{2,3},{3,2},{4,5},{5,4},{6,7},{7,6},{8,9},{9,8},{10,11... | collective-permute-start | bytes 491528 | tf_op jit(solution)/shard_map/ppermute | solution.py:227
  29.3 5.9 %collective-permute-start.11 = (bf16[64,1024]{1,0:T(8,128)(2,1)S(1)}, bf16[64,1024]{1,0:T(8,128)(2,1)S(1)}, u32[]{:S(2)}, u32[]{:S(2)}) collective-permute-start(bf16[64,1024]{1,0:T(8,128)(2,1)S(1)} %collective-permute-done.8.refs_3_), channel_id=1, source_target_pairs={{0,4},{4,0},{8,12},{12,8},{1,5},{5,1},{9,13},{13,9},{2,6},{6,2},{1... | collective-permute-start | bytes 393224 | tf_op jit(solution)/shard_map/ppermute | solution.py:227
  31.1 9.6 %collective-permute-start.10 = (bf16[160,512]{1,0:T(8,128)(2,1)S(1)}, bf16[160,512]{1,0:T(8,128)(2,1)S(1)}, u32[]{:S(2)}, u32[]{:S(2)}) collective-permute-start(bf16[160,512]{1,0:T(8,128)(2,1)S(1)} %shard_map.79.refs_0_), channel_id=1, source_target_pairs={{0,2},{1,3},{2,0},{3,1},{4,6},{5,7},{6,4},{7,5},{8,10},{9,11},{10,... | collective-permute-start | bytes 491528 | tf_op jit(solution)/shard_map/ppermute | solution.py:227
  35.5 1.3 %collective-permute-start.12 = (bf16[32,512]{1,0:T(8,128)(2,1)S(1)}, bf16[32,512]{1,0:T(8,128)(2,1)S(1)}, u32[]{:S(2)}, u32[]{:S(2)}) collective-permute-start(bf16[32,512]{1,0:T(8,128)(2,1)S(1)} %get-tuple-element.36), channel_id=1, source_target_pairs={{0,1},{1,0},{2,3},{3,2},{4,5},{5,4},{6,7},{7,6},{8,9},{9,8},{10,11... | collective-permute-start | bytes 98312 | tf_op jit(solution)/shard_map/ppermute | solution.py:227
  36.8 4.0 %collective-permute-start.13 = (bf16[32,512]{1,0:T(8,128)(2,1)S(1)}, bf16[32,512]{1,0:T(8,128)(2,1)S(1)}, u32[]{:S(2)}, u32[]{:S(2)}) collective-permute-start(bf16[32,512]{1,0:T(8,128)(2,1)S(1)} %shard_map.82.refs_0_), channel_id=1, source_target_pairs={{0,2},{1,3},{2,0},{3,1},{4,6},{5,7},{6,4},{7,5},{8,10},{9,11},{10,... | collective-permute-start | bytes 98312 | tf_op jit(solution)/shard_map/ppermute | solution.py:227
  41.1 4.5 %collective-permute-start.14 = (bf16[32,512]{1,0:T(8,128)(2,1)S(1)}, bf16[32,512]{1,0:T(8,128)(2,1)S(1)}, u32[]{:S(2)}, u32[]{:S(2)}) collective-permute-start(bf16[32,512]{1,0:T(8,128)(2,1)S(1)} %get-tuple-element.38), channel_id=1, source_target_pairs={{0,4},{4,0},{8,12},{12,8},{1,5},{5,1},{9,13},{13,9},{2,6},{6,2},{1... | collective-permute-start | bytes 98312 | tf_op jit(solution)/shard_map/ppermute | solution.py:227
  42.9 5.3 %collective-permute-start.15 = (bf16[32,512]{1,0:T(8,128)(2,1)S(1)}, bf16[32,512]{1,0:T(8,128)(2,1)S(1)}, u32[]{:S(2)}, u32[]{:S(2)}) collective-permute-start(bf16[32,512]{1,0:T(8,128)(2,1)S(1)} %get-tuple-element.39), channel_id=1, source_target_pairs={{0,8},{4,12},{8,0},{12,4},{1,9},{5,13},{9,1},{13,5},{2,10},{6,14},... | collective-permute-start | bytes 98312 | tf_op jit(solution)/shard_map/ppermute | solution.py:227
  44.7 5.7 %collective-permute-start.16 = (bf16[32,512]{1,0:T(8,128)(2,1)S(1)}, bf16[32,512]{1,0:T(8,128)(2,1)S(1)}, u32[]{:S(2)}, u32[]{:S(2)}) collective-permute-start(bf16[32,512]{1,0:T(8,128)(2,1)S(1)} %get-tuple-element.40), channel_id=1, source_target_pairs={{0,12},{4,8},{8,4},{12,0},{1,13},{5,9},{9,5},{13,1},{2,14},{6,10},... | collective-permute-start | bytes 98312 | tf_op jit(solution)/shard_map/ppermute | solution.py:227

commit v5 on v4

--- a/solution.py
+++ b/solution.py
@@ -246,13 +246,15 @@
     end, start = doc_end.reshape(1, rows), doc_start.reshape(1, rows)
     message = pack(key_rows, value_rows, end)
     halo = lax.ppermute(message, "ctx", [(0, 1), (1, 2), (2, 3)])
-    target_1 = flip(after(block_target, message), "ctx", 1)
+    early = after(block_target, message)
+    target_1, target_2 = flip(early, "ctx", 1), flip(early, "ctx", 2)
     own_targets = jnp.concatenate([block_target, target_1]).reshape(1, 2 * blocks)
     start = after(start, own_targets)
     whole, first, second = attend(blocks, queries, halo, key_rows, value_rows, end, start)
     first_2, second_2 = flip(first, "ctx", 2), flip(second, "ctx", 2)
     whole_1 = flip(whole, "ctx", 1)
-    far_targets = flip(own_targets, "ctx", 2)
+    target_3 = flip(after(target_2, whole), "ctx", 1)
+    far_targets = jnp.concatenate([target_2, target_3]).reshape(1, 2 * blocks)
     share_a = core_total(*project(block_rows, (whole,), out_weight))
     first_2 = after(first_2, share_a)
     first_3, second_3 = flip(first_2, "ctx", 1), flip(second_2, "ctx", 1)

time: 51.2 us -> 56.6 us (1.11)
  waiting for transfers between devices: 17 us -> 21.7 us
  starting transfers between devices: 28.6 us -> 29.3 us
    ppermute x16 -> x17, waiting for transfers between devices: 17 us -> 21.7 us  [flip(): return lax.ppermute(array, axis, [(i, i ^ bits) for i in range(4)])]
    ppermute x16 -> x17, starting transfers between devices: 23.7 us -> 24.4 us  [flip(): return lax.ppermute(array, axis, [(i, i ^ bits) for i in range(4)])]
  transfers between devices with their start and end apart: 17 -> 18, of which waited for: 10 -> 11; matrix products, arithmetic and copies ran while one was open for 0% -> 0% of each run, Pallas kernels for 1% -> 1%
where the time goes in v5:
time: 56.6 us; the launch traced here: 56.5 us
  starting transfers between devices  29.3 us (52%)
  waiting for transfers between devices  21.7 us (38%)
  Pallas kernels  4.52 us (8%)
  local copies, waits for them, and re-layouts  0.66 us (1%)
    ppermute x17, starting transfers between devices, flip(): return lax.ppermute(array, axis, [(i, i ^ bits) for i in range(4)])  24.4 us
    ppermute x17, waiting for transfers between devices, flip(): return lax.ppermute(array, axis, [(i, i ^ bits) for i in range(4)])  21.7 us
    ppermute x1, starting transfers between devices, small_ring(): halo = lax.ppermute(message, 'ctx', [(0, 1), (1, 2), (2, 3)])  4.94 us
    pallas_call x1, Pallas kernels, pack(): pl.pallas_call(pack_kernel, out_shape=jax.ShapeDtypeStruct((rows + 16, 2...  1.67 us
  transfers between devices with their start and end apart: 18, of which 11 were waited for; matrix products, arithmetic and copies ran while one was open for 0% of the time, Pallas kernels for 1%

profile of v5, /device:TPU:0, one launch (start us, length us, event | category | flops | bytes accessed | tf_op | source)
XLA Modules:
  0.0 56.5 jit_solution(5900004656065134192)
XLA Ops:
  0.0 1.7 %shard_map.73 = bf16[144,512]{1,0:T(8,128)(2,1)} custom-call(bf16[128,256]{1,0:T(8,128)(2,1)} %k_ref.3, bf16[128,256]{1,0:T(8,128)(2,1)} %v_ref.3, s32[1,128]{1,0:T(1,128)} %bitcast.6), custom_call_target="tpu_custom_call" | custom-call | flops 1000000000 | bytes 262144 | tf_op jit(solution)/shard_map/pallas_call | solution.py:51
  1.7 4.9 %collective-permute-start.2 = (bf16[144,512]{1,0:T(8,128)(2,1)}, bf16[144,512]{1,0:T(8,128)(2,1)S(1)}, u32[]{:S(2)}, u32[]{:S(2)}) collective-permute-start(bf16[144,512]{1,0:T(8,128)(2,1)} %shard_map.73), channel_id=1, source_target_pairs={{0,4},{4,8},{8,12},{1,5},{5,9},{9,13},{2,6},{6,10},{10,14},{3,7},{... | collective-permute-start | bytes 442376 | tf_op jit(solution)/shard_map/ppermute | solution.py:248
  6.6 1.6 %collective-permute-start = (s32[2]{0:T(128)S(1)}, s32[2]{0:T(128)S(1)}, u32[]{:S(2)}, u32[]{:S(2)}) collective-permute-start(s32[2]{0:T(128)S(1)} %copy-done.6), channel_id=1, source_target_pairs={{0,4},{4,0},{8,12},{12,8},{1,5},{5,1},{9,13},{13,9},{2,6},{6,2},{1... | collective-permute-start | bytes 32 | tf_op jit(solution)/shard_map/ppermute | solution.py:227
  8.3 2.0 %collective-permute-done = s32[2]{0:T(128)S(1)} collective-permute-done((s32[2]{0:T(128)S(1)}, s32[2]{0:T(128)S(1)}, u32[]{:S(2)}, u32[]{:S(2)}) %collective-permute-start) | collective-permute-done | bytes 40 | tf_op jit(solution)/shard_map/ppermute | solution.py:227
  11.0 0.7 %shard_map.74 = (bf16[128,1024]{1,0:T(8,128)(2,1)S(1)}, bf16[64,1024]{1,0:T(8,128)(2,1)S(1)}, bf16[64,1024]{1,0:T(8,128)(2,1)S(1)}) custom-call(bf16[128,1024]{1,0:T(8,128)(2,1)S(1)} %copy-done.1, bf16[144,512]{1,0:T(8,128)(2,1)S(1)} %collective-permute-done.2.halo_ref, bf16[128,256]{1,0:T(8,128)(2,1)S(1)} %copy-done.2, bf16[128,256]{1,0:T(8,128)(2,1)S(1)} %copy-done.3, ...), custom_call_target="tpu_custom_call" | custom-call | flops 134217728 | bytes 786432 | tf_op jit(solution)/shard_map/pallas_call | solution.py:120
  11.7 2.6 %collective-permute-start.7 = (bf16[64,1024]{1,0:T(8,128)(2,1)S(1)}, bf16[64,1024]{1,0:T(8,128)(2,1)S(1)}, u32[]{:S(2)}, u32[]{:S(2)}) collective-permute-start(bf16[64,1024]{1,0:T(8,128)(2,1)S(1)} %get-tuple-element.30), channel_id=1, source_target_pairs={{0,8},{4,12},{8,0},{12,4},{1,9},{5,13},{9,1},{13,5},{2,10},{6,14},... | collective-permute-start | bytes 393224 | tf_op jit(solution)/shard_map/ppermute | solution.py:227
  14.3 2.2 %collective-permute-start.6 = (bf16[128,1024]{1,0:T(8,128)(2,1)S(1)}, bf16[128,1024]{1,0:T(8,128)(2,1)S(1)}, u32[]{:S(2)}, u32[]{:S(2)}) collective-permute-start(bf16[128,1024]{1,0:T(8,128)(2,1)S(1)} %get-tuple-element.26.refs_0_), channel_id=1, source_target_pairs={{0,4},{4,0},{8,12},{12,8},{1,5},{5,1},{9,13},{13,9},{2,6},{6,2},{1... | collective-permute-start | bytes 786440 | tf_op jit(solution)/shard_map/ppermute | solution.py:227
  17.4 0.8 %collective-permute-done.4.refs_1_ = bf16[64,512]{1,0:T(8,128)(2,1)S(1)} collective-permute-done((bf16[64,512]{1,0:T(8,128)(2,1)S(1)}, bf16[64,512]{1,0:T(8,128)(2,1)S(1)}, u32[]{:S(2)}, u32[]{:S(2)}) %collective-permute-start.4) | collective-permute-done | bytes 65568 | tf_op jit(solution)/shard_map/ppermute | solution.py:227
  18.2 1.0 %collective-permute-done.7.refs_1_ = bf16[64,1024]{1,0:T(8,128)(2,1)S(1)} collective-permute-done((bf16[64,1024]{1,0:T(8,128)(2,1)S(1)}, bf16[64,1024]{1,0:T(8,128)(2,1)S(1)}, u32[]{:S(2)}, u32[]{:S(2)}) %collective-permute-start.7) | collective-permute-done | bytes 131104 | tf_op jit(solution)/shard_map/ppermute | solution.py:227
  19.3 2.3 %collective-permute-start.8 = (bf16[64,1024]{1,0:T(8,128)(2,1)S(1)}, bf16[64,1024]{1,0:T(8,128)(2,1)S(1)}, u32[]{:S(2)}, u32[]{:S(2)}) collective-permute-start(bf16[64,1024]{1,0:T(8,128)(2,1)S(1)} %collective-permute-done.7.refs_1_), channel_id=1, source_target_pairs={{0,4},{4,0},{8,12},{12,8},{1,5},{5,1},{9,13},{13,9},{2,6},{6,2},{1... | collective-permute-start | bytes 393224 | tf_op jit(solution)/shard_map/ppermute | solution.py:227
  21.5 3.4 %collective-permute-start.1 = (s32[2]{0:T(128)S(1)}, s32[2]{0:T(128)S(1)}, u32[]{:S(2)}, u32[]{:S(2)}) collective-permute-start(s32[2]{0:T(128)S(1)} %copy-done.6), channel_id=1, source_target_pairs={{0,8},{4,12},{8,0},{12,4},{1,9},{5,13},{9,1},{13,5},{2,10},{6,14},... | collective-permute-start | bytes 32 | tf_op jit(solution)/shard_map/ppermute | solution.py:227
  25.0 3.0 %collective-permute-done.1 = s32[2]{0:T(128)S(1)} collective-permute-done((s32[2]{0:T(128)S(1)}, s32[2]{0:T(128)S(1)}, u32[]{:S(2)}, u32[]{:S(2)}) %collective-permute-start.1) | collective-permute-done | bytes 40 | tf_op jit(solution)/shard_map/ppermute | solution.py:227
  28.0 2.4 %collective-permute-start.3 = (s32[2]{0:T(128)S(1)}, s32[2]{0:T(128)S(1)}, u32[]{:S(2)}, u32[]{:S(2)}) collective-permute-start(s32[2]{0:T(128)S(1)} %collective-permute-done.1), channel_id=1, source_target_pairs={{0,4},{4,0},{8,12},{12,8},{1,5},{5,1},{9,13},{13,9},{2,6},{6,2},{1... | collective-permute-start | bytes 32 | tf_op jit(solution)/shard_map/ppermute | solution.py:227
  30.4 1.5 %collective-permute-start.5 = (bf16[64,512]{1,0:T(8,128)(2,1)S(1)}, bf16[64,512]{1,0:T(8,128)(2,1)S(1)}, u32[]{:S(2)}, u32[]{:S(2)}) collective-permute-start(bf16[64,512]{1,0:T(8,128)(2,1)S(1)} %shard_map.76.refs_0_), channel_id=1, source_target_pairs={{0,2},{1,3},{2,0},{3,1},{4,6},{5,7},{6,4},{7,5},{8,10},{9,11},{10,... | collective-permute-start | bytes 196616 | tf_op jit(solution)/shard_map/ppermute | solution.py:227
  32.0 2.7 %collective-permute-done.5.refs_1_ = bf16[64,512]{1,0:T(8,128)(2,1)S(1)} collective-permute-done((bf16[64,512]{1,0:T(8,128)(2,1)S(1)}, bf16[64,512]{1,0:T(8,128)(2,1)S(1)}, u32[]{:S(2)}, u32[]{:S(2)}) %collective-permute-start.5) | collective-permute-done | bytes 65568 | tf_op jit(solution)/shard_map/ppermute | solution.py:227
  35.4 1.3 %collective-permute-done.10.refs_1_ = bf16[160,512]{1,0:T(8,128)(2,1)S(1)} collective-permute-done((bf16[160,512]{1,0:T(8,128)(2,1)S(1)}, bf16[160,512]{1,0:T(8,128)(2,1)S(1)}, u32[]{:S(2)}, u32[]{:S(2)}) %collective-permute-start.10) | collective-permute-done | bytes 163872 | tf_op jit(solution)/shard_map/ppermute | solution.py:227
  36.7 1.6 %collective-permute-start.11 = (bf16[160,512]{1,0:T(8,128)(2,1)S(1)}, bf16[160,512]{1,0:T(8,128)(2,1)S(1)}, u32[]{:S(2)}, u32[]{:S(2)}) collective-permute-start(bf16[160,512]{1,0:T(8,128)(2,1)S(1)} %shard_map.79.refs_0_), channel_id=1, source_target_pairs={{0,2},{1,3},{2,0},{3,1},{4,6},{5,7},{6,4},{7,5},{8,10},{9,11},{10,... | collective-permute-start | bytes 491528 | tf_op jit(solution)/shard_map/ppermute | solution.py:227
  38.3 2.9 %collective-permute-done.12.refs_0_ = bf16[64,1024]{1,0:T(8,128)(2,1)S(1)} collective-permute-done((bf16[64,1024]{1,0:T(8,128)(2,1)S(1)}, bf16[64,1024]{1,0:T(8,128)(2,1)S(1)}, u32[]{:S(2)}, u32[]{:S(2)}) %collective-permute-start.12) | collective-permute-done | bytes 131104 | tf_op jit(solution)/shard_map/ppermute | solution.py:227
  41.6 1.2 %collective-permute-done.13.refs_1_ = bf16[32,512]{1,0:T(8,128)(2,1)S(1)} collective-permute-done((bf16[32,512]{1,0:T(8,128)(2,1)S(1)}, bf16[32,512]{1,0:T(8,128)(2,1)S(1)}, u32[]{:S(2)}, u32[]{:S(2)}) %collective-permute-start.13) | collective-permute-done | bytes 32800 | tf_op jit(solution)/shard_map/ppermute | solution.py:227
  42.8 1.6 %collective-permute-start.14 = (bf16[32,512]{1,0:T(8,128)(2,1)S(1)}, bf16[32,512]{1,0:T(8,128)(2,1)S(1)}, u32[]{:S(2)}, u32[]{:S(2)}) collective-permute-start(bf16[32,512]{1,0:T(8,128)(2,1)S(1)} %shard_map.82.refs_0_), channel_id=1, source_target_pairs={{0,2},{1,3},{2,0},{3,1},{4,6},{5,7},{6,4},{7,5},{8,10},{9,11},{10,... | collective-permute-start | bytes 98312 | tf_op jit(solution)/shard_map/ppermute | solution.py:227
  44.4 2.4 %collective-permute-done.14.refs_1_ = bf16[32,512]{1,0:T(8,128)(2,1)S(1)} collective-permute-done((bf16[32,512]{1,0:T(8,128)(2,1)S(1)}, bf16[32,512]{1,0:T(8,128)(2,1)S(1)}, u32[]{:S(2)}, u32[]{:S(2)}) %collective-permute-start.14) | collective-permute-done | bytes 32800 | tf_op jit(solution)/shard_map/ppermute | solution.py:227
  47.4 2.7 %collective-permute-start.16 = (bf16[32,512]{1,0:T(8,128)(2,1)S(1)}, bf16[32,512]{1,0:T(8,128)(2,1)S(1)}, u32[]{:S(2)}, u32[]{:S(2)}) collective-permute-start(bf16[32,512]{1,0:T(8,128)(2,1)S(1)} %get-tuple-element.41), channel_id=1, source_target_pairs={{0,8},{4,12},{8,0},{12,4},{1,9},{5,13},{9,1},{13,5},{2,10},{6,14},... | collective-permute-start | bytes 98312 | tf_op jit(solution)/shard_map/ppermute | solution.py:227
  50.1 1.5 %collective-permute-start.17 = (bf16[32,512]{1,0:T(8,128)(2,1)S(1)}, bf16[32,512]{1,0:T(8,128)(2,1)S(1)}, u32[]{:S(2)}, u32[]{:S(2)}) collective-permute-start(bf16[32,512]{1,0:T(8,128)(2,1)S(1)} %get-tuple-element.42), channel_id=1, source_target_pairs={{0,12},{4,8},{8,4},{12,0},{1,13},{5,9},{9,5},{13,1},{2,14},{6,10},... | collective-permute-start | bytes 98312 | tf_op jit(solution)/shard_map/ppermute | solution.py:227
  52.3 3.6 %collective-permute-done.17.refs_3_ = bf16[32,512]{1,0:T(8,128)(2,1)S(1)} collective-permute-done((bf16[32,512]{1,0:T(8,128)(2,1)S(1)}, bf16[32,512]{1,0:T(8,128)(2,1)S(1)}, u32[]{:S(2)}, u32[]{:S(2)}) %collective-permute-start.17) | collective-permute-done | bytes 32800 | tf_op jit(solution)/shard_map/ppermute | solution.py:227
  (41 shorter events, 4.7 us)
Async XLA Ops:
  0.0 6.6 %copy-start.6 = (s32[2]{0:T(128)S(1)}, s32[2]{0:T(128)}, u32[]{:S(2)}) copy-start(s32[2]{0:T(128)} %param.12) | copy-start | bytes 28
  0.0 10.3 %copy-start.1 = (bf16[128,1024]{1,0:T(8,128)(2,1)S(1)}, bf16[128,1024]{1,0:T(8,128)(2,1)}, u32[]{:S(2)}) copy-start(bf16[128,1024]{1,0:T(8,128)(2,1)} %q_ref.1) | copy-start | bytes 786436
  0.0 10.3 %copy-start.2 = (bf16[128,256]{1,0:T(8,128)(2,1)S(1)}, bf16[128,256]{1,0:T(8,128)(2,1)}, u32[]{:S(2)}) copy-start(bf16[128,256]{1,0:T(8,128)(2,1)} %k_ref.3) | copy-start | bytes 196612
  0.0 10.3 %copy-start.3 = (bf16[128,256]{1,0:T(8,128)(2,1)S(1)}, bf16[128,256]{1,0:T(8,128)(2,1)}, u32[]{:S(2)}) copy-start(bf16[128,256]{1,0:T(8,128)(2,1)} %v_ref.3) | copy-start | bytes 196612
  0.0 16.6 %copy-start = (bf16[1024,512]{1,0:T(8,128)(2,1)S(1)}, bf16[1024,512]{1,0:T(8,128)(2,1)}, u32[]{:S(2)}) copy-start(bf16[1024,512]{1,0:T(8,128)(2,1)} %refs_1_.3) | copy-start | bytes 3145732
  1.7 8.6 %collective-permute-start.2 = (bf16[144,512]{1,0:T(8,128)(2,1)}, bf16[144,512]{1,0:T(8,128)(2,1)S(1)}, u32[]{:S(2)}, u32[]{:S(2)}) collective-permute-start(bf16[144,512]{1,0:T(8,128)(2,1)} %shard_map.73), channel_id=1, source_target_pairs={{0,4},{4,8},{8,12},{1,5},{5,9},{9,13},{2,6},{6,10},{10,14},{3,7},{... | collective-permute-start | bytes 442376 | tf_op jit(solution)/shard_map/ppermute | solution.py:248
  6.6 3.6 %collective-permute-start = (s32[2]{0:T(128)S(1)}, s32[2]{0:T(128)S(1)}, u32[]{:S(2)}, u32[]{:S(2)}) collective-permute-start(s32[2]{0:T(128)S(1)} %copy-done.6), channel_id=1, source_target_pairs={{0,4},{4,0},{8,12},{12,8},{1,5},{5,1},{9,13},{13,9},{2,6},{6,2},{1... | collective-permute-start | bytes 32 | tf_op jit(solution)/shard_map/ppermute | solution.py:227
  10.3 0.7 %copy-start.5 = (s32[128]{0:T(128)S(1)}, s32[128]{0:T(128)}, u32[]{:S(2)}) copy-start(s32[128]{0:T(128)} %param.10) | copy-start | bytes 1540
  11.7 7.6 %collective-permute-start.7 = (bf16[64,1024]{1,0:T(8,128)(2,1)S(1)}, bf16[64,1024]{1,0:T(8,128)(2,1)S(1)}, u32[]{:S(2)}, u32[]{:S(2)}) collective-permute-start(bf16[64,1024]{1,0:T(8,128)(2,1)S(1)} %get-tuple-element.30), channel_id=1, source_target_pairs={{0,8},{4,12},{8,0},{12,4},{1,9},{5,13},{9,1},{13,5},{2,10},{6,14},... | collective-permute-start | bytes 393224 | tf_op jit(solution)/shard_map/ppermute | solution.py:227
  14.3 20.4 %collective-permute-start.6 = (bf16[128,1024]{1,0:T(8,128)(2,1)S(1)}, bf16[128,1024]{1,0:T(8,128)(2,1)S(1)}, u32[]{:S(2)}, u32[]{:S(2)}) collective-permute-start(bf16[128,1024]{1,0:T(8,128)(2,1)S(1)} %get-tuple-element.26.refs_0_), channel_id=1, source_target_pairs={{0,4},{4,0},{8,12},{12,8},{1,5},{5,1},{9,13},{13,9},{2,6},{6,2},{1... | collective-permute-start | bytes 786440 | tf_op jit(solution)/shard_map/ppermute | solution.py:227
  16.9 1.3 %collective-permute-start.4 = (bf16[64,512]{1,0:T(8,128)(2,1)S(1)}, bf16[64,512]{1,0:T(8,128)(2,1)S(1)}, u32[]{:S(2)}, u32[]{:S(2)}) collective-permute-start(bf16[64,512]{1,0:T(8,128)(2,1)S(1)} %get-tuple-element.29), channel_id=1, source_target_pairs={{0,1},{1,0},{2,3},{3,2},{4,5},{5,4},{6,7},{7,6},{8,9},{9,8},{10,11... | collective-permute-start | bytes 196616 | tf_op jit(solution)/shard_map/ppermute | solution.py:227
  17.0 17.7 %collective-permute-start.9 = (bf16[64,1024]{1,0:T(8,128)(2,1)S(1)}, bf16[64,1024]{1,0:T(8,128)(2,1)S(1)}, u32[]{:S(2)}, u32[]{:S(2)}) collective-permute-start(bf16[64,1024]{1,0:T(8,128)(2,1)S(1)} %get-tuple-element.32), channel_id=1, source_target_pairs={{0,8},{4,12},{8,0},{12,4},{1,9},{5,13},{9,1},{13,5},{2,10},{6,14},... | collective-permute-start | bytes 393224 | tf_op jit(solution)/shard_map/ppermute | solution.py:227
  19.3 15.4 %collective-permute-start.8 = (bf16[64,1024]{1,0:T(8,128)(2,1)S(1)}, bf16[64,1024]{1,0:T(8,128)(2,1)S(1)}, u32[]{:S(2)}, u32[]{:S(2)}) collective-permute-start(bf16[64,1024]{1,0:T(8,128)(2,1)S(1)} %collective-permute-done.7.refs_1_), channel_id=1, source_target_pairs={{0,4},{4,0},{8,12},{12,8},{1,5},{5,1},{9,13},{13,9},{2,6},{6,2},{1... | collective-permute-start | bytes 393224 | tf_op jit(solution)/shard_map/ppermute | solution.py:227
  21.5 6.4 %collective-permute-start.1 = (s32[2]{0:T(128)S(1)}, s32[2]{0:T(128)S(1)}, u32[]{:S(2)}, u32[]{:S(2)}) collective-permute-start(s32[2]{0:T(128)S(1)} %copy-done.6), channel_id=1, source_target_pairs={{0,8},{4,12},{8,0},{12,4},{1,9},{5,13},{9,1},{13,5},{2,10},{6,14},... | collective-permute-start | bytes 32 | tf_op jit(solution)/shard_map/ppermute | solution.py:227
  28.0 3.9 %collective-permute-start.3 = (s32[2]{0:T(128)S(1)}, s32[2]{0:T(128)S(1)}, u32[]{:S(2)}, u32[]{:S(2)}) collective-permute-start(s32[2]{0:T(128)S(1)} %collective-permute-done.1), channel_id=1, source_target_pairs={{0,4},{4,0},{8,12},{12,8},{1,5},{5,1},{9,13},{13,9},{2,6},{6,2},{1... | collective-permute-start | bytes 32 | tf_op jit(solution)/shard_map/ppermute | solution.py:227
  30.4 4.3 %collective-permute-start.5 = (bf16[64,512]{1,0:T(8,128)(2,1)S(1)}, bf16[64,512]{1,0:T(8,128)(2,1)S(1)}, u32[]{:S(2)}, u32[]{:S(2)}) collective-permute-start(bf16[64,512]{1,0:T(8,128)(2,1)S(1)} %shard_map.76.refs_0_), channel_id=1, source_target_pairs={{0,2},{1,3},{2,0},{3,1},{4,6},{5,7},{6,4},{7,5},{8,10},{9,11},{10,... | collective-permute-start | bytes 196616 | tf_op jit(solution)/shard_map/ppermute | solution.py:227
  35.2 1.5 %collective-permute-start.10 = (bf16[160,512]{1,0:T(8,128)(2,1)S(1)}, bf16[160,512]{1,0:T(8,128)(2,1)S(1)}, u32[]{:S(2)}, u32[]{:S(2)}) collective-permute-start(bf16[160,512]{1,0:T(8,128)(2,1)S(1)} %get-tuple-element.35), channel_id=1, source_target_pairs={{0,1},{1,0},{2,3},{3,2},{4,5},{5,4},{6,7},{7,6},{8,9},{9,8},{10,11... | collective-permute-start | bytes 491528 | tf_op jit(solution)/shard_map/ppermute | solution.py:227
  35.3 5.9 %collective-permute-start.12 = (bf16[64,1024]{1,0:T(8,128)(2,1)S(1)}, bf16[64,1024]{1,0:T(8,128)(2,1)S(1)}, u32[]{:S(2)}, u32[]{:S(2)}) collective-permute-start(bf16[64,1024]{1,0:T(8,128)(2,1)S(1)} %collective-permute-done.9.refs_3_), channel_id=1, source_target_pairs={{0,4},{4,0},{8,12},{12,8},{1,5},{5,1},{9,13},{13,9},{2,6},{6,2},{1... | collective-permute-start | bytes 393224 | tf_op jit(solution)/shard_map/ppermute | solution.py:227
  36.7 10.1 %collective-permute-start.11 = (bf16[160,512]{1,0:T(8,128)(2,1)S(1)}, bf16[160,512]{1,0:T(8,128)(2,1)S(1)}, u32[]{:S(2)}, u32[]{:S(2)}) collective-permute-start(bf16[160,512]{1,0:T(8,128)(2,1)S(1)} %shard_map.79.refs_0_), channel_id=1, source_target_pairs={{0,2},{1,3},{2,0},{3,1},{4,6},{5,7},{6,4},{7,5},{8,10},{9,11},{10,... | collective-permute-start | bytes 491528 | tf_op jit(solution)/shard_map/ppermute | solution.py:227
  41.5 1.3 %collective-permute-start.13 = (bf16[32,512]{1,0:T(8,128)(2,1)S(1)}, bf16[32,512]{1,0:T(8,128)(2,1)S(1)}, u32[]{:S(2)}, u32[]{:S(2)}) collective-permute-start(bf16[32,512]{1,0:T(8,128)(2,1)S(1)} %get-tuple-element.38), channel_id=1, source_target_pairs={{0,1},{1,0},{2,3},{3,2},{4,5},{5,4},{6,7},{7,6},{8,9},{9,8},{10,11... | collective-permute-start | bytes 98312 | tf_op jit(solution)/shard_map/ppermute | solution.py:227
  42.8 4.0 %collective-permute-start.14 = (bf16[32,512]{1,0:T(8,128)(2,1)S(1)}, bf16[32,512]{1,0:T(8,128)(2,1)S(1)}, u32[]{:S(2)}, u32[]{:S(2)}) collective-permute-start(bf16[32,512]{1,0:T(8,128)(2,1)S(1)} %shard_map.82.refs_0_), channel_id=1, source_target_pairs={{0,2},{1,3},{2,0},{3,1},{4,6},{5,7},{6,4},{7,5},{8,10},{9,11},{10,... | collective-permute-start | bytes 98312 | tf_op jit(solution)/shard_map/ppermute | solution.py:227
  47.1 4.5 %collective-permute-start.15 = (bf16[32,512]{1,0:T(8,128)(2,1)S(1)}, bf16[32,512]{1,0:T(8,128)(2,1)S(1)}, u32[]{:S(2)}, u32[]{:S(2)}) collective-permute-start(bf16[32,512]{1,0:T(8,128)(2,1)S(1)} %get-tuple-element.40), channel_id=1, source_target_pairs={{0,4},{4,0},{8,12},{12,8},{1,5},{5,1},{9,13},{13,9},{2,6},{6,2},{1... | collective-permute-start | bytes 98312 | tf_op jit(solution)/shard_map/ppermute | solution.py:227
  47.4 4.8 %collective-permute-start.16 = (bf16[32,512]{1,0:T(8,128)(2,1)S(1)}, bf16[32,512]{1,0:T(8,128)(2,1)S(1)}, u32[]{:S(2)}, u32[]{:S(2)}) collective-permute-start(bf16[32,512]{1,0:T(8,128)(2,1)S(1)} %get-tuple-element.41), channel_id=1, source_target_pairs={{0,8},{4,12},{8,0},{12,4},{1,9},{5,13},{9,1},{13,5},{2,10},{6,14},... | collective-permute-start | bytes 98312 | tf_op jit(solution)/shard_map/ppermute | solution.py:227
  50.1 5.7 %collective-permute-start.17 = (bf16[32,512]{1,0:T(8,128)(2,1)S(1)}, bf16[32,512]{1,0:T(8,128)(2,1)S(1)}, u32[]{:S(2)}, u32[]{:S(2)}) collective-permute-start(bf16[32,512]{1,0:T(8,128)(2,1)S(1)} %get-tuple-element.42), channel_id=1, source_target_pairs={{0,12},{4,8},{8,4},{12,0},{1,13},{5,9},{9,5},{13,1},{2,14},{6,10},... | collective-permute-start | bytes 98312 | tf_op jit(solution)/shard_map/ppermute | solution.py:227
  (1 other events, 0.7 us)

commit v6 on v4

--- a/solution.py
+++ b/solution.py
@@ -172,13 +172,13 @@
     )(*terms)
 
 
-def pick_kernel(blocks, half, own_ref, far_ref, *refs):
+def pick_kernel(blocks, half, even_ref, odd_ref, *refs):
     sums, outs = refs[:-4], refs[-4:]
     x = lax.axis_index("tp") // 2
     c = lax.axis_index("ctx")
-    order = (0, 1, 2, 3, 4, 6, 5, 7)
+    order = (0, 1, 4, 5, 2, 6, 3, 7)
     pieces = [r[pl.ds(n, half), :] for r in sums for n in range(0, r.shape[0], half)]
-    targets = jnp.concatenate([own_ref[...], far_ref[...]], axis=1)
+    targets = jnp.concatenate([even_ref[...], odd_ref[...]], axis=1)
     for k in range(4):
         wanted = (c ^ k) * blocks + x
         piece = pieces[0]
@@ -189,7 +189,7 @@
         outs[k][...] = piece
 
 
-def pick(blocks, own_targets, far_targets, sums):
+def pick(blocks, even_targets, odd_targets, sums):
     rows, cols = sum(s.shape[0] for s in sums), sums[0].shape[1]
     half = rows // (4 * blocks)
     out = jax.ShapeDtypeStruct((half, cols), jnp.bfloat16)
@@ -200,7 +200,7 @@
         out_specs=tuple(vmem(4)),
         compiler_params=params(),
         cost_estimate=cost(4 * rows * cols, 8 * rows * cols),
-    )(own_targets, far_targets, *sums)
+    )(even_targets, odd_targets, *sums)
 
 
 def join_kernel(*refs):
@@ -246,24 +246,23 @@
     end, start = doc_end.reshape(1, rows), doc_start.reshape(1, rows)
     message = pack(key_rows, value_rows, end)
     halo = lax.ppermute(message, "ctx", [(0, 1), (1, 2), (2, 3)])
-    target_1 = flip(after(block_target, message), "ctx", 1)
-    own_targets = jnp.concatenate([block_target, target_1]).reshape(1, 2 * blocks)
-    start = after(start, own_targets)
+    target_2 = flip(after(block_target, message), "ctx", 2)
+    even_targets = jnp.concatenate([block_target, target_2]).reshape(1, 2 * blocks)
+    halo = after(halo, target_2)
     whole, first, second = attend(blocks, queries, halo, key_rows, value_rows, end, start)
+    whole_1 = flip(whole, "ctx", 1)
     first_2, second_2 = flip(first, "ctx", 2), flip(second, "ctx", 2)
-    whole_1 = flip(whole, "ctx", 1)
-    far_targets = flip(own_targets, "ctx", 2)
-    share_a = core_total(*project(block_rows, (whole,), out_weight))
-    first_2 = after(first_2, share_a)
+    odd_targets = flip(even_targets, "ctx", 1)
+    share_a = core_total(*project(block_rows, (whole, whole_1), out_weight))
     first_3, second_3 = flip(first_2, "ctx", 1), flip(second_2, "ctx", 1)
     sum_a = chip_total(share_a)
-    second_2 = after(second_2, sum_a, far_targets)
-    share_b = core_total(*project(block_rows, (whole_1, first_2, first_3, second_2), out_weight))
+    second_2 = after(second_2, share_a, odd_targets)
+    share_b = core_total(*project(block_rows, (first_2, first_3, second_2), out_weight))
     second_3 = after(second_3, share_b)
     share_c = core_total(*project(block_rows, (second_3,), out_weight))
     sum_b = chip_total(share_b)
     sum_c = chip_total(share_c)
-    kept, *sent = pick(blocks, own_targets, far_targets, (sum_a, sum_b, sum_c))
+    kept, *sent = pick(blocks, even_targets, odd_targets, (sum_a, sum_b, sum_c))
     got = [flip(sent[k - 1], "ctx", k) for k in (3, 2, 1)]
     return join([kept] + got[::-1])
 

time: 51.2 us -> 50.5 us (0.986)
  starting transfers between devices: 28.6 us -> 23 us
  waiting for transfers between devices: 17 us -> 22.6 us
  local copies, waits for them, and re-layouts: 0.66 us -> 0.03 us
    ppermute x16, starting transfers between devices: 23.7 us -> 17.9 us  [flip(): return lax.ppermute(array, axis, [(i, i ^ bits) for i in range(4)])]
    ppermute x16, waiting for transfers between devices: 17 us -> 22.6 us  [flip(): return lax.ppermute(array, axis, [(i, i ^ bits) for i in range(4)])]
    unnamed x14, local copies, waits for them, and re-layouts: 0.66 us -> 0.03 us
  transfers between devices with their start and end apart: 17 -> 17, of which waited for: 10 -> 9; matrix products, arithmetic and copies ran while one was open for 0% -> 0% of each run, Pallas kernels for 1% -> 2%
where the time goes in v6:
time: 50.5 us; the launch traced here: 50.4 us
  starting transfers between devices  23 us (46%)
  waiting for transfers between devices  22.6 us (45%)
  Pallas kernels  4.5 us (9%)
    ppermute x16, waiting for transfers between devices, flip(): return lax.ppermute(array, axis, [(i, i ^ bits) for i in range(4)])  22.6 us
    ppermute x16, starting transfers between devices, flip(): return lax.ppermute(array, axis, [(i, i ^ bits) for i in range(4)])  17.9 us
    ppermute x1, starting transfers between devices, small_ring(): halo = lax.ppermute(message, 'ctx', [(0, 1), (1, 2), (2, 3)])  5.07 us
    pallas_call x1, Pallas kernels, pack(): pl.pallas_call(pack_kernel, out_shape=jax.ShapeDtypeStruct((rows + 16, 2...  1.67 us
    pallas_call x3, Pallas kernels, project(): pl.pallas_call(functools.partial(project_kernel, block_rows), out_shape=(...  1.1 us
  transfers between devices with their start and end apart: 17, of which 9 were waited for; matrix products, arithmetic and copies ran while one was open for 0% of the time, Pallas kernels for 2%

profile of v6, /device:TPU:0, one launch (start us, length us, event | category | flops | bytes accessed | tf_op | source)
XLA Modules:
  0.0 50.4 jit_solution(7200854780832303123)
XLA Ops:
  0.0 1.7 %shard_map.73 = bf16[144,512]{1,0:T(8,128)(2,1)} custom-call(bf16[128,256]{1,0:T(8,128)(2,1)} %k_ref.3, bf16[128,256]{1,0:T(8,128)(2,1)} %v_ref.3, s32[1,128]{1,0:T(1,128)} %bitcast.4), custom_call_target="tpu_custom_call" | custom-call | flops 1000000000 | bytes 262144 | tf_op jit(solution)/shard_map/pallas_call | solution.py:51
  1.7 5.1 %collective-permute-start.2 = (bf16[144,512]{1,0:T(8,128)(2,1)}, bf16[144,512]{1,0:T(8,128)(2,1)S(1)}, u32[]{:S(2)}, u32[]{:S(2)}) collective-permute-start(bf16[144,512]{1,0:T(8,128)(2,1)} %shard_map.73), channel_id=1, source_target_pairs={{0,4},{4,8},{8,12},{1,5},{5,9},{9,13},{2,6},{6,10},{10,14},{3,7},{... | collective-permute-start | bytes 442376 | tf_op jit(solution)/shard_map/ppermute | solution.py:248
  6.8 2.6 %collective-permute-start = (s32[2]{0:T(128)S(1)}, s32[2]{0:T(128)S(1)}, u32[]{:S(2)}, u32[]{:S(2)}) collective-permute-start(s32[2]{0:T(128)S(1)} %copy-done.6), channel_id=1, source_target_pairs={{0,8},{4,12},{8,0},{12,4},{1,9},{5,13},{9,1},{13,5},{2,10},{6,14},... | collective-permute-start | bytes 32 | tf_op jit(solution)/shard_map/ppermute | solution.py:227
  9.4 1.9 %collective-permute-done = s32[2]{0:T(128)S(1)} collective-permute-done((s32[2]{0:T(128)S(1)}, s32[2]{0:T(128)S(1)}, u32[]{:S(2)}, u32[]{:S(2)}) %collective-permute-start) | collective-permute-done | bytes 40 | tf_op jit(solution)/shard_map/ppermute | solution.py:227
  11.3 0.7 %shard_map.74 = (bf16[128,1024]{1,0:T(8,128)(2,1)S(1)}, bf16[64,1024]{1,0:T(8,128)(2,1)S(1)}, bf16[64,1024]{1,0:T(8,128)(2,1)S(1)}) custom-call(bf16[128,1024]{1,0:T(8,128)(2,1)S(1)} %copy-done.1, bf16[144,512]{1,0:T(8,128)(2,1)S(1)} %collective-permute-done.2.halo_ref, bf16[128,256]{1,0:T(8,128)(2,1)S(1)} %copy-done.2, bf16[128,256]{1,0:T(8,128)(2,1)S(1)} %copy-done.3, ...), custom_call_target="tpu_custom_call" | custom-call | flops 134217728 | bytes 786432 | tf_op jit(solution)/shard_map/pallas_call | solution.py:120
  12.0 1.6 %collective-permute-start.3 = (bf16[128,1024]{1,0:T(8,128)(2,1)S(1)}, bf16[128,1024]{1,0:T(8,128)(2,1)S(1)}, u32[]{:S(2)}, u32[]{:S(2)}) collective-permute-start(bf16[128,1024]{1,0:T(8,128)(2,1)S(1)} %get-tuple-element.24.refs_0_), channel_id=1, source_target_pairs={{0,4},{4,0},{8,12},{12,8},{1,5},{5,1},{9,13},{13,9},{2,6},{6,2},{1... | collective-permute-start | bytes 786440 | tf_op jit(solution)/shard_map/ppermute | solution.py:227
  13.7 2.3 %collective-permute-start.6 = (bf16[64,1024]{1,0:T(8,128)(2,1)S(1)}, bf16[64,1024]{1,0:T(8,128)(2,1)S(1)}, u32[]{:S(2)}, u32[]{:S(2)}) collective-permute-start(bf16[64,1024]{1,0:T(8,128)(2,1)S(1)} %get-tuple-element.27), channel_id=1, source_target_pairs={{0,8},{4,12},{8,0},{12,4},{1,9},{5,13},{9,1},{13,5},{2,10},{6,14},... | collective-permute-start | bytes 393224 | tf_op jit(solution)/shard_map/ppermute | solution.py:227
  15.9 0.7 %collective-permute-start.8 = (bf16[64,1024]{1,0:T(8,128)(2,1)S(1)}, bf16[64,1024]{1,0:T(8,128)(2,1)S(1)}, u32[]{:S(2)}, u32[]{:S(2)}) collective-permute-start(bf16[64,1024]{1,0:T(8,128)(2,1)S(1)} %get-tuple-element.28), channel_id=1, source_target_pairs={{0,8},{4,12},{8,0},{12,4},{1,9},{5,13},{9,1},{13,5},{2,10},{6,14},... | collective-permute-start | bytes 393224 | tf_op jit(solution)/shard_map/ppermute | solution.py:227
  16.6 6.7 %collective-permute-done.3.refs_1_ = bf16[128,1024]{1,0:T(8,128)(2,1)S(1)} collective-permute-done((bf16[128,1024]{1,0:T(8,128)(2,1)S(1)}, bf16[128,1024]{1,0:T(8,128)(2,1)S(1)}, u32[]{:S(2)}, u32[]{:S(2)}) %collective-permute-start.3) | collective-permute-done | bytes 262176 | tf_op jit(solution)/shard_map/ppermute | solution.py:227
  23.8 2.1 %collective-permute-start.7 = (bf16[64,1024]{1,0:T(8,128)(2,1)S(1)}, bf16[64,1024]{1,0:T(8,128)(2,1)S(1)}, u32[]{:S(2)}, u32[]{:S(2)}) collective-permute-start(bf16[64,1024]{1,0:T(8,128)(2,1)S(1)} %collective-permute-done.6.refs_0_), channel_id=1, source_target_pairs={{0,4},{4,0},{8,12},{12,8},{1,5},{5,1},{9,13},{13,9},{2,6},{6,2},{1... | collective-permute-start | bytes 393224 | tf_op jit(solution)/shard_map/ppermute | solution.py:227
  25.9 1.8 %collective-permute-done.8.refs_2_ = bf16[64,1024]{1,0:T(8,128)(2,1)S(1)} collective-permute-done((bf16[64,1024]{1,0:T(8,128)(2,1)S(1)}, bf16[64,1024]{1,0:T(8,128)(2,1)S(1)}, u32[]{:S(2)}, u32[]{:S(2)}) %collective-permute-start.8) | collective-permute-done | bytes 131104 | tf_op jit(solution)/shard_map/ppermute | solution.py:227
  28.0 2.6 %collective-permute-done.1.odd_ref = s32[1,4]{1,0:T(1,128)S(1)} collective-permute-done((s32[1,4]{1,0:T(1,128)S(1)}, s32[1,4]{1,0:T(1,128)S(1)}, u32[]{:S(2)}, u32[]{:S(2)}) %collective-permute-start.1) | collective-permute-done | bytes 48 | tf_op jit(solution)/shard_map/ppermute | solution.py:227
  31.0 1.6 %collective-permute-start.5 = (bf16[128,512]{1,0:T(8,128)(2,1)S(1)}, bf16[128,512]{1,0:T(8,128)(2,1)S(1)}, u32[]{:S(2)}, u32[]{:S(2)}) collective-permute-start(bf16[128,512]{1,0:T(8,128)(2,1)S(1)} %shard_map.76.refs_0_), channel_id=1, source_target_pairs={{0,2},{1,3},{2,0},{3,1},{4,6},{5,7},{6,4},{7,5},{8,10},{9,11},{10,... | collective-permute-start | bytes 393224 | tf_op jit(solution)/shard_map/ppermute | solution.py:227
  32.6 1.3 %collective-permute-start.10 = (bf16[96,512]{1,0:T(8,128)(2,1)S(1)}, bf16[96,512]{1,0:T(8,128)(2,1)S(1)}, u32[]{:S(2)}, u32[]{:S(2)}) collective-permute-start(bf16[96,512]{1,0:T(8,128)(2,1)S(1)} %shard_map.79.refs_0_), channel_id=1, source_target_pairs={{0,2},{1,3},{2,0},{3,1},{4,6},{5,7},{6,4},{7,5},{8,10},{9,11},{10,... | collective-permute-start | bytes 294920 | tf_op jit(solution)/shard_map/ppermute | solution.py:227
  34.3 1.2 %collective-permute-done.12.refs_1_ = bf16[32,512]{1,0:T(8,128)(2,1)S(1)} collective-permute-done((bf16[32,512]{1,0:T(8,128)(2,1)S(1)}, bf16[32,512]{1,0:T(8,128)(2,1)S(1)}, u32[]{:S(2)}, u32[]{:S(2)}) %collective-permute-start.12) | collective-permute-done | bytes 32800 | tf_op jit(solution)/shard_map/ppermute | solution.py:227
  35.5 0.9 %collective-permute-start.13 = (bf16[32,512]{1,0:T(8,128)(2,1)S(1)}, bf16[32,512]{1,0:T(8,128)(2,1)S(1)}, u32[]{:S(2)}, u32[]{:S(2)}) collective-permute-start(bf16[32,512]{1,0:T(8,128)(2,1)S(1)} %shard_map.82.refs_0_), channel_id=1, source_target_pairs={{0,2},{1,3},{2,0},{3,1},{4,6},{5,7},{6,4},{7,5},{8,10},{9,11},{10,... | collective-permute-start | bytes 98312 | tf_op jit(solution)/shard_map/ppermute | solution.py:227
  36.4 1.0 %collective-permute-done.5.refs_1_ = bf16[128,512]{1,0:T(8,128)(2,1)S(1)} collective-permute-done((bf16[128,512]{1,0:T(8,128)(2,1)S(1)}, bf16[128,512]{1,0:T(8,128)(2,1)S(1)}, u32[]{:S(2)}, u32[]{:S(2)}) %collective-permute-start.5) | collective-permute-done | bytes 131104 | tf_op jit(solution)/shard_map/ppermute | solution.py:227
  37.4 2.3 %collective-permute-done.13.refs_1_ = bf16[32,512]{1,0:T(8,128)(2,1)S(1)} collective-permute-done((bf16[32,512]{1,0:T(8,128)(2,1)S(1)}, bf16[32,512]{1,0:T(8,128)(2,1)S(1)}, u32[]{:S(2)}, u32[]{:S(2)}) %collective-permute-start.13) | collective-permute-done | bytes 32800 | tf_op jit(solution)/shard_map/ppermute | solution.py:227
  40.1 1.1 %collective-permute-start.14 = (bf16[32,512]{1,0:T(8,128)(2,1)S(1)}, bf16[32,512]{1,0:T(8,128)(2,1)S(1)}, u32[]{:S(2)}, u32[]{:S(2)}) collective-permute-start(bf16[32,512]{1,0:T(8,128)(2,1)S(1)} %get-tuple-element.36), channel_id=1, source_target_pairs={{0,4},{4,0},{8,12},{12,8},{1,5},{5,1},{9,13},{13,9},{2,6},{6,2},{1... | collective-permute-start | bytes 98312 | tf_op jit(solution)/shard_map/ppermute | solution.py:227
  41.2 2.8 %collective-permute-start.15 = (bf16[32,512]{1,0:T(8,128)(2,1)S(1)}, bf16[32,512]{1,0:T(8,128)(2,1)S(1)}, u32[]{:S(2)}, u32[]{:S(2)}) collective-permute-start(bf16[32,512]{1,0:T(8,128)(2,1)S(1)} %get-tuple-element.37), channel_id=1, source_target_pairs={{0,8},{4,12},{8,0},{12,4},{1,9},{5,13},{9,1},{13,5},{2,10},{6,14},... | collective-permute-start | bytes 98312 | tf_op jit(solution)/shard_map/ppermute | solution.py:227
  44.0 0.5 %collective-permute-start.16 = (bf16[32,512]{1,0:T(8,128)(2,1)S(1)}, bf16[32,512]{1,0:T(8,128)(2,1)S(1)}, u32[]{:S(2)}, u32[]{:S(2)}) collective-permute-start(bf16[32,512]{1,0:T(8,128)(2,1)S(1)} %get-tuple-element.38), channel_id=1, source_target_pairs={{0,12},{4,8},{8,4},{12,0},{1,13},{5,9},{9,5},{13,1},{2,14},{6,10},... | collective-permute-start | bytes 98312 | tf_op jit(solution)/shard_map/ppermute | solution.py:227
  44.5 2.0 %collective-permute-done.15.refs_2_ = bf16[32,512]{1,0:T(8,128)(2,1)S(1)} collective-permute-done((bf16[32,512]{1,0:T(8,128)(2,1)S(1)}, bf16[32,512]{1,0:T(8,128)(2,1)S(1)}, u32[]{:S(2)}, u32[]{:S(2)}) %collective-permute-start.15) | collective-permute-done | bytes 32800 | tf_op jit(solution)/shard_map/ppermute | solution.py:227
  46.5 3.2 %collective-permute-done.16.refs_3_ = bf16[32,512]{1,0:T(8,128)(2,1)S(1)} collective-permute-done((bf16[32,512]{1,0:T(8,128)(2,1)S(1)}, bf16[32,512]{1,0:T(8,128)(2,1)S(1)}, u32[]{:S(2)}, u32[]{:S(2)}) %collective-permute-start.16) | collective-permute-done | bytes 32800 | tf_op jit(solution)/shard_map/ppermute | solution.py:227
  49.7 0.7 %shard_map.85 = bf16[32,2048]{1,0:T(8,128)(2,1)} custom-call(bf16[32,512]{1,0:T(8,128)(2,1)S(1)} %get-tuple-element.35.refs_0_, bf16[32,512]{1,0:T(8,128)(2,1)S(1)} %collective-permute-done.14.refs_1_, bf16[32,512]{1,0:T(8,128)(2,1)S(1)} %collective-permute-done.15.refs_2_, bf16[32,512]{1,0:T(8,128)(2,1)S(1)} %collective-permute-done.16.refs_3_), custom_call_target="tpu_custom_call" | custom-call | bytes 262144 | tf_op jit(solution)/shard_map/pallas_call | solution.py:216
  (38 shorter events, 2.0 us)
Async XLA Ops:
  0.0 6.8 %copy-start.6 = (s32[2]{0:T(128)S(1)}, s32[2]{0:T(128)}, u32[]{:S(2)}) copy-start(s32[2]{0:T(128)} %param.12) | copy-start | bytes 28
  0.0 11.3 %copy-start.1 = (bf16[128,1024]{1,0:T(8,128)(2,1)S(1)}, bf16[128,1024]{1,0:T(8,128)(2,1)}, u32[]{:S(2)}) copy-start(bf16[128,1024]{1,0:T(8,128)(2,1)} %q_ref.1) | copy-start | bytes 786436
  0.0 11.3 %copy-start.2 = (bf16[128,256]{1,0:T(8,128)(2,1)S(1)}, bf16[128,256]{1,0:T(8,128)(2,1)}, u32[]{:S(2)}) copy-start(bf16[128,256]{1,0:T(8,128)(2,1)} %k_ref.3) | copy-start | bytes 196612
  0.0 11.3 %copy-start.3 = (bf16[128,256]{1,0:T(8,128)(2,1)S(1)}, bf16[128,256]{1,0:T(8,128)(2,1)}, u32[]{:S(2)}) copy-start(bf16[128,256]{1,0:T(8,128)(2,1)} %v_ref.3) | copy-start | bytes 196612
  0.0 23.2 %copy-start = (bf16[1024,512]{1,0:T(8,128)(2,1)S(1)}, bf16[1024,512]{1,0:T(8,128)(2,1)}, u32[]{:S(2)}) copy-start(bf16[1024,512]{1,0:T(8,128)(2,1)} %refs_1_.1) | copy-start | bytes 3145732
  1.7 9.6 %copy-start.4 = (s32[128]{0:T(128)S(1)}, s32[128]{0:T(128)}, u32[]{:S(2)}) copy-start(s32[128]{0:T(128)} %param.11) | copy-start | bytes 1540
  1.7 9.6 %copy-start.5 = (s32[128]{0:T(128)S(1)}, s32[128]{0:T(128)}, u32[]{:S(2)}) copy-start(s32[128]{0:T(128)} %param.10) | copy-start | bytes 1540
  1.7 9.6 %collective-permute-start.2 = (bf16[144,512]{1,0:T(8,128)(2,1)}, bf16[144,512]{1,0:T(8,128)(2,1)S(1)}, u32[]{:S(2)}, u32[]{:S(2)}) collective-permute-start(bf16[144,512]{1,0:T(8,128)(2,1)} %shard_map.73), channel_id=1, source_target_pairs={{0,4},{4,8},{8,12},{1,5},{5,9},{9,13},{2,6},{6,10},{10,14},{3,7},{... | collective-permute-start | bytes 442376 | tf_op jit(solution)/shard_map/ppermute | solution.py:248
  6.8 4.5 %collective-permute-start = (s32[2]{0:T(128)S(1)}, s32[2]{0:T(128)S(1)}, u32[]{:S(2)}, u32[]{:S(2)}) collective-permute-start(s32[2]{0:T(128)S(1)} %copy-done.6), channel_id=1, source_target_pairs={{0,8},{4,12},{8,0},{12,4},{1,9},{5,13},{9,1},{13,5},{2,10},{6,14},... | collective-permute-start | bytes 32 | tf_op jit(solution)/shard_map/ppermute | solution.py:227
  12.0 11.2 %collective-permute-start.3 = (bf16[128,1024]{1,0:T(8,128)(2,1)S(1)}, bf16[128,1024]{1,0:T(8,128)(2,1)S(1)}, u32[]{:S(2)}, u32[]{:S(2)}) collective-permute-start(bf16[128,1024]{1,0:T(8,128)(2,1)S(1)} %get-tuple-element.24.refs_0_), channel_id=1, source_target_pairs={{0,4},{4,0},{8,12},{12,8},{1,5},{5,1},{9,13},{13,9},{2,6},{6,2},{1... | collective-permute-start | bytes 786440 | tf_op jit(solution)/shard_map/ppermute | solution.py:227
  13.7 10.1 %collective-permute-start.6 = (bf16[64,1024]{1,0:T(8,128)(2,1)S(1)}, bf16[64,1024]{1,0:T(8,128)(2,1)S(1)}, u32[]{:S(2)}, u32[]{:S(2)}) collective-permute-start(bf16[64,1024]{1,0:T(8,128)(2,1)S(1)} %get-tuple-element.27), channel_id=1, source_target_pairs={{0,8},{4,12},{8,0},{12,4},{1,9},{5,13},{9,1},{13,5},{2,10},{6,14},... | collective-permute-start | bytes 393224 | tf_op jit(solution)/shard_map/ppermute | solution.py:227
  15.9 11.8 %collective-permute-start.8 = (bf16[64,1024]{1,0:T(8,128)(2,1)S(1)}, bf16[64,1024]{1,0:T(8,128)(2,1)S(1)}, u32[]{:S(2)}, u32[]{:S(2)}) collective-permute-start(bf16[64,1024]{1,0:T(8,128)(2,1)S(1)} %get-tuple-element.28), channel_id=1, source_target_pairs={{0,8},{4,12},{8,0},{12,4},{1,9},{5,13},{9,1},{13,5},{2,10},{6,14},... | collective-permute-start | bytes 393224 | tf_op jit(solution)/shard_map/ppermute | solution.py:227
  23.7 4.3 %collective-permute-start.4 = (bf16[128,512]{1,0:T(8,128)(2,1)S(1)}, bf16[128,512]{1,0:T(8,128)(2,1)S(1)}, u32[]{:S(2)}, u32[]{:S(2)}) collective-permute-start(bf16[128,512]{1,0:T(8,128)(2,1)S(1)} %get-tuple-element.26), channel_id=1, source_target_pairs={{0,1},{1,0},{2,3},{3,2},{4,5},{5,4},{6,7},{7,6},{8,9},{9,8},{10,11... | collective-permute-start | bytes 393224 | tf_op jit(solution)/shard_map/ppermute | solution.py:227
  23.8 6.8 %collective-permute-start.7 = (bf16[64,1024]{1,0:T(8,128)(2,1)S(1)}, bf16[64,1024]{1,0:T(8,128)(2,1)S(1)}, u32[]{:S(2)}, u32[]{:S(2)}) collective-permute-start(bf16[64,1024]{1,0:T(8,128)(2,1)S(1)} %collective-permute-done.6.refs_0_), channel_id=1, source_target_pairs={{0,4},{4,0},{8,12},{12,8},{1,5},{5,1},{9,13},{13,9},{2,6},{6,2},{1... | collective-permute-start | bytes 393224 | tf_op jit(solution)/shard_map/ppermute | solution.py:227
  25.9 4.7 %collective-permute-start.1 = (s32[1,4]{1,0:T(1,128)S(1)}, s32[1,4]{1,0:T(1,128)S(1)}, u32[]{:S(2)}, u32[]{:S(2)}) collective-permute-start(s32[1,4]{1,0:T(1,128)S(1)} %add_bitcast_fusion.even_ref), channel_id=1, source_target_pairs={{0,4},{4,0},{8,12},{12,8},{1,5},{5,1},{9,13},{13,9},{2,6},{6,2},{1... | collective-permute-start | bytes 56 | tf_op jit(solution)/shard_map/ppermute | solution.py:227
  27.7 6.2 %collective-permute-start.11 = (bf16[64,1024]{1,0:T(8,128)(2,1)S(1)}, bf16[64,1024]{1,0:T(8,128)(2,1)S(1)}, u32[]{:S(2)}, u32[]{:S(2)}) collective-permute-start(bf16[64,1024]{1,0:T(8,128)(2,1)S(1)} %collective-permute-done.8.refs_2_), channel_id=1, source_target_pairs={{0,4},{4,0},{8,12},{12,8},{1,5},{5,1},{9,13},{13,9},{2,6},{6,2},{1... | collective-permute-start | bytes 393224 | tf_op jit(solution)/shard_map/ppermute | solution.py:227
  31.0 1.6 %collective-permute-start.9 = (bf16[96,512]{1,0:T(8,128)(2,1)S(1)}, bf16[96,512]{1,0:T(8,128)(2,1)S(1)}, u32[]{:S(2)}, u32[]{:S(2)}) collective-permute-start(bf16[96,512]{1,0:T(8,128)(2,1)S(1)} %get-tuple-element.31), channel_id=1, source_target_pairs={{0,1},{1,0},{2,3},{3,2},{4,5},{5,4},{6,7},{7,6},{8,9},{9,8},{10,11... | collective-permute-start | bytes 294920 | tf_op jit(solution)/shard_map/ppermute | solution.py:227
  31.0 6.4 %collective-permute-start.5 = (bf16[128,512]{1,0:T(8,128)(2,1)S(1)}, bf16[128,512]{1,0:T(8,128)(2,1)S(1)}, u32[]{:S(2)}, u32[]{:S(2)}) collective-permute-start(bf16[128,512]{1,0:T(8,128)(2,1)S(1)} %shard_map.76.refs_0_), channel_id=1, source_target_pairs={{0,2},{1,3},{2,0},{3,1},{4,6},{5,7},{6,4},{7,5},{8,10},{9,11},{10,... | collective-permute-start | bytes 393224 | tf_op jit(solution)/shard_map/ppermute | solution.py:227
  32.6 7.2 %collective-permute-start.10 = (bf16[96,512]{1,0:T(8,128)(2,1)S(1)}, bf16[96,512]{1,0:T(8,128)(2,1)S(1)}, u32[]{:S(2)}, u32[]{:S(2)}) collective-permute-start(bf16[96,512]{1,0:T(8,128)(2,1)S(1)} %shard_map.79.refs_0_), channel_id=1, source_target_pairs={{0,2},{1,3},{2,0},{3,1},{4,6},{5,7},{6,4},{7,5},{8,10},{9,11},{10,... | collective-permute-start | bytes 294920 | tf_op jit(solution)/shard_map/ppermute | solution.py:227
  34.2 1.3 %collective-permute-start.12 = (bf16[32,512]{1,0:T(8,128)(2,1)S(1)}, bf16[32,512]{1,0:T(8,128)(2,1)S(1)}, u32[]{:S(2)}, u32[]{:S(2)}) collective-permute-start(bf16[32,512]{1,0:T(8,128)(2,1)S(1)} %get-tuple-element.34), channel_id=1, source_target_pairs={{0,1},{1,0},{2,3},{3,2},{4,5},{5,4},{6,7},{7,6},{8,9},{9,8},{10,11... | collective-permute-start | bytes 98312 | tf_op jit(solution)/shard_map/ppermute | solution.py:227
  35.5 4.3 %collective-permute-start.13 = (bf16[32,512]{1,0:T(8,128)(2,1)S(1)}, bf16[32,512]{1,0:T(8,128)(2,1)S(1)}, u32[]{:S(2)}, u32[]{:S(2)}) collective-permute-start(bf16[32,512]{1,0:T(8,128)(2,1)S(1)} %shard_map.82.refs_0_), channel_id=1, source_target_pairs={{0,2},{1,3},{2,0},{3,1},{4,6},{5,7},{6,4},{7,5},{8,10},{9,11},{10,... | collective-permute-start | bytes 98312 | tf_op jit(solution)/shard_map/ppermute | solution.py:227
  40.1 4.5 %collective-permute-start.14 = (bf16[32,512]{1,0:T(8,128)(2,1)S(1)}, bf16[32,512]{1,0:T(8,128)(2,1)S(1)}, u32[]{:S(2)}, u32[]{:S(2)}) collective-permute-start(bf16[32,512]{1,0:T(8,128)(2,1)S(1)} %get-tuple-element.36), channel_id=1, source_target_pairs={{0,4},{4,0},{8,12},{12,8},{1,5},{5,1},{9,13},{13,9},{2,6},{6,2},{1... | collective-permute-start | bytes 98312 | tf_op jit(solution)/shard_map/ppermute | solution.py:227
  41.2 5.3 %collective-permute-start.15 = (bf16[32,512]{1,0:T(8,128)(2,1)S(1)}, bf16[32,512]{1,0:T(8,128)(2,1)S(1)}, u32[]{:S(2)}, u32[]{:S(2)}) collective-permute-start(bf16[32,512]{1,0:T(8,128)(2,1)S(1)} %get-tuple-element.37), channel_id=1, source_target_pairs={{0,8},{4,12},{8,0},{12,4},{1,9},{5,13},{9,1},{13,5},{2,10},{6,14},... | collective-permute-start | bytes 98312 | tf_op jit(solution)/shard_map/ppermute | solution.py:227
  44.0 5.7 %collective-permute-start.16 = (bf16[32,512]{1,0:T(8,128)(2,1)S(1)}, bf16[32,512]{1,0:T(8,128)(2,1)S(1)}, u32[]{:S(2)}, u32[]{:S(2)}) collective-permute-start(bf16[32,512]{1,0:T(8,128)(2,1)S(1)} %get-tuple-element.38), channel_id=1, source_target_pairs={{0,12},{4,8},{8,4},{12,0},{1,13},{5,9},{9,5},{13,1},{2,14},{6,10},... | collective-permute-start | bytes 98312 | tf_op jit(solution)/shard_map/ppermute | solution.py:227

commit v7 on v6

--- a/solution.py
+++ b/solution.py
@@ -203,24 +203,42 @@
     )(even_targets, odd_targets, *sums)
 
 
-def join_kernel(*refs):
-    pieces, out_ref = refs[:-1], refs[-1]
-    cols = pieces[0].shape[1]
+def hold_kernel(near_ref, far_ref, out_ref):
+    cols = near_ref.shape[1]
+    out_ref[:, pl.ds(0, cols)] = near_ref[...]
+    out_ref[:, pl.ds(cols, cols)] = far_ref[...]
+
+
+def hold(near, far):
+    rows, cols = near.shape
+    return pl.pallas_call(
+        hold_kernel,
+        out_shape=jax.ShapeDtypeStruct((rows, 2 * cols), near.dtype),
+        in_specs=vmem(2),
+        out_specs=pl.BlockSpec(memory_space=pltpu.VMEM),
+        compiler_params=params(),
+        cost_estimate=cost(0, 8 * near.size),
+    )(near, far)
+
+
+def join_kernel(held_ref, two_ref, one_ref, out_ref):
+    cols = one_ref.shape[1]
     c = lax.axis_index("ctx")
+    pieces = (held_ref[:, pl.ds(0, cols)], one_ref[...], two_ref[...], held_ref[:, pl.ds(cols, cols)])
     for k in range(4):
-        out_ref[:, pl.ds(pl.multiple_of((c ^ k) * cols, cols), cols)] = pieces[k][...]
-
-
-def join(pieces):
-    rows, cols = pieces[0].shape
+        out_ref[:, pl.ds(pl.multiple_of((c ^ k) * cols, cols), cols)] = pieces[k]
+
+
+def join(held, two, one):
+    rows, cols = one.shape
     return pl.pallas_call(
         join_kernel,
         out_shape=jax.ShapeDtypeStruct((rows, 4 * cols), jnp.bfloat16),
-        in_specs=vmem(4),
+        in_specs=vmem(3),
         out_specs=pl.BlockSpec(memory_space=pltpu.VMEM),
         compiler_params=params(),
-        cost_estimate=cost(0, 16 * pieces[0].size),
-    )(*pieces)
+        cost_estimate=cost(0, 16 * one.size),
+    )(held, two, one)
 
 
 def flip(array, axis, bits):
@@ -253,18 +271,19 @@
     whole_1 = flip(whole, "ctx", 1)
     first_2, second_2 = flip(first, "ctx", 2), flip(second, "ctx", 2)
     odd_targets = flip(even_targets, "ctx", 1)
+    whole_1 = after(whole_1, odd_targets)
     share_a = core_total(*project(block_rows, (whole, whole_1), out_weight))
     first_3, second_3 = flip(first_2, "ctx", 1), flip(second_2, "ctx", 1)
     sum_a = chip_total(share_a)
-    second_2 = after(second_2, share_a, odd_targets)
+    second_2 = after(second_2, share_a)
     share_b = core_total(*project(block_rows, (first_2, first_3, second_2), out_weight))
     second_3 = after(second_3, share_b)
     share_c = core_total(*project(block_rows, (second_3,), out_weight))
     sum_b = chip_total(share_b)
     sum_c = chip_total(share_c)
     kept, *sent = pick(blocks, even_targets, odd_targets, (sum_a, sum_b, sum_c))
-    got = [flip(sent[k - 1], "ctx", k) for k in (3, 2, 1)]
-    return join([kept] + got[::-1])
+    got_3, got_2, got_1 = (flip(sent[k - 1], "ctx", k) for k in (3, 2, 1))
+    return join(hold(kept, got_3), got_2, got_1)
 
 
 def attend_block(soft_state, query_grid, query_pos, query_start, key_block, value_block, key_end, key_pos):

time: 50.5 us -> 49.1 us (0.972)
  waiting for transfers between devices: 22.6 us -> 20.6 us
  starting transfers between devices: 23 us -> 23.6 us
    ppermute x16, waiting for transfers between devices: 22.6 us -> 20.6 us  [flip(): return lax.ppermute(array, axis, [(i, i ^ bits) for i in range(4)])]
    ppermute x16, starting transfers between devices: 17.9 us -> 18.5 us  [flip(): return lax.ppermute(array, axis, [(i, i ^ bits) for i in range(4)])]
where the time goes in v7:
time: 49.1 us; the launch traced here: 48.9 us
  starting transfers between devices  23.6 us (48%)
  waiting for transfers between devices  20.6 us (42%)
  Pallas kernels  4.5 us (9%)
    ppermute x16, waiting for transfers between devices, flip(): return lax.ppermute(array, axis, [(i, i ^ bits) for i in range(4)])  20.6 us
    ppermute x16, starting transfers between devices, flip(): return lax.ppermute(array, axis, [(i, i ^ bits) for i in range(4)])  18.5 us
    ppermute x1, starting transfers between devices, small_ring(): halo = lax.ppermute(message, 'ctx', [(0, 1), (1, 2), (2, 3)])  5.07 us
    pallas_call x1, Pallas kernels, pack(): pl.pallas_call(pack_kernel, out_shape=jax.ShapeDtypeStruct((rows + 16, 2...  1.67 us
    pallas_call x3, Pallas kernels, project(): pl.pallas_call(functools.partial(project_kernel, block_rows), out_shape=(...  1.1 us
  transfers between devices with their start and end apart: 17, of which 9 were waited for; matrix products, arithmetic and copies ran while one was open for 0% of the time, Pallas kernels for 2%

profile of v7, /device:TPU:0, one launch (start us, length us, event | category | flops | bytes accessed | tf_op | source)
XLA Modules:
  0.0 48.9 jit_solution(3956664886955932150)
XLA Ops:
  0.0 1.7 %shard_map.73 = bf16[144,512]{1,0:T(8,128)(2,1)} custom-call(bf16[128,256]{1,0:T(8,128)(2,1)} %k_ref.3, bf16[128,256]{1,0:T(8,128)(2,1)} %v_ref.3, s32[1,128]{1,0:T(1,128)} %bitcast.4), custom_call_target="tpu_custom_call" | custom-call | flops 1000000000 | bytes 262144 | tf_op jit(solution)/shard_map/pallas_call | solution.py:51
  1.7 5.1 %collective-permute-start.2 = (bf16[144,512]{1,0:T(8,128)(2,1)}, bf16[144,512]{1,0:T(8,128)(2,1)S(1)}, u32[]{:S(2)}, u32[]{:S(2)}) collective-permute-start(bf16[144,512]{1,0:T(8,128)(2,1)} %shard_map.73), channel_id=1, source_target_pairs={{0,4},{4,8},{8,12},{1,5},{5,9},{9,13},{2,6},{6,10},{10,14},{3,7},{... | collective-permute-start | bytes 442376 | tf_op jit(solution)/shard_map/ppermute | solution.py:266
  6.8 2.6 %collective-permute-start = (s32[2]{0:T(128)S(1)}, s32[2]{0:T(128)S(1)}, u32[]{:S(2)}, u32[]{:S(2)}) collective-permute-start(s32[2]{0:T(128)S(1)} %copy-done.6), channel_id=1, source_target_pairs={{0,8},{4,12},{8,0},{12,4},{1,9},{5,13},{9,1},{13,5},{2,10},{6,14},... | collective-permute-start | bytes 32 | tf_op jit(solution)/shard_map/ppermute | solution.py:245
  9.4 1.9 %collective-permute-done = s32[2]{0:T(128)S(1)} collective-permute-done((s32[2]{0:T(128)S(1)}, s32[2]{0:T(128)S(1)}, u32[]{:S(2)}, u32[]{:S(2)}) %collective-permute-start) | collective-permute-done | bytes 40 | tf_op jit(solution)/shard_map/ppermute | solution.py:245
  11.3 0.7 %shard_map.74 = (bf16[128,1024]{1,0:T(8,128)(2,1)S(1)}, bf16[64,1024]{1,0:T(8,128)(2,1)S(1)}, bf16[64,1024]{1,0:T(8,128)(2,1)S(1)}) custom-call(bf16[128,1024]{1,0:T(8,128)(2,1)S(1)} %copy-done.1, bf16[144,512]{1,0:T(8,128)(2,1)S(1)} %collective-permute-done.2.halo_ref, bf16[128,256]{1,0:T(8,128)(2,1)S(1)} %copy-done.2, bf16[128,256]{1,0:T(8,128)(2,1)S(1)} %copy-done.3, ...), custom_call_target="tpu_custom_call" | custom-call | flops 134217728 | bytes 786432 | tf_op jit(solution)/shard_map/pallas_call | solution.py:120
  12.0 1.6 %collective-permute-start.3 = (bf16[128,1024]{1,0:T(8,128)(2,1)S(1)}, bf16[128,1024]{1,0:T(8,128)(2,1)S(1)}, u32[]{:S(2)}, u32[]{:S(2)}) collective-permute-start(bf16[128,1024]{1,0:T(8,128)(2,1)S(1)} %get-tuple-element.25.refs_0_), channel_id=1, source_target_pairs={{0,4},{4,0},{8,12},{12,8},{1,5},{5,1},{9,13},{13,9},{2,6},{6,2},{1... | collective-permute-start | bytes 786440 | tf_op jit(solution)/shard_map/ppermute | solution.py:245
  13.7 2.3 %collective-permute-start.6 = (bf16[64,1024]{1,0:T(8,128)(2,1)S(1)}, bf16[64,1024]{1,0:T(8,128)(2,1)S(1)}, u32[]{:S(2)}, u32[]{:S(2)}) collective-permute-start(bf16[64,1024]{1,0:T(8,128)(2,1)S(1)} %get-tuple-element.29), channel_id=1, source_target_pairs={{0,8},{4,12},{8,0},{12,4},{1,9},{5,13},{9,1},{13,5},{2,10},{6,14},... | collective-permute-start | bytes 393224 | tf_op jit(solution)/shard_map/ppermute | solution.py:245
  16.0 0.8 %collective-permute-start.1 = (s32[1,4]{1,0:T(1,128)S(1)}, s32[1,4]{1,0:T(1,128)S(1)}, u32[]{:S(2)}, u32[]{:S(2)}) collective-permute-start(s32[1,4]{1,0:T(1,128)S(1)} %add_bitcast_fusion.even_ref), channel_id=1, source_target_pairs={{0,4},{4,0},{8,12},{12,8},{1,5},{5,1},{9,13},{13,9},{2,6},{6,2},{1... | collective-permute-start | bytes 56 | tf_op jit(solution)/shard_map/ppermute | solution.py:245
  17.1 5.7 %collective-permute-done.1.odd_ref = s32[1,4]{1,0:T(1,128)S(1)} collective-permute-done((s32[1,4]{1,0:T(1,128)S(1)}, s32[1,4]{1,0:T(1,128)S(1)}, u32[]{:S(2)}, u32[]{:S(2)}) %collective-permute-start.1) | collective-permute-done | bytes 48 | tf_op jit(solution)/shard_map/ppermute | solution.py:245
  22.9 0.4 shard_map.75
  23.4 2.4 %collective-permute-start.7 = (bf16[64,1024]{1,0:T(8,128)(2,1)S(1)}, bf16[64,1024]{1,0:T(8,128)(2,1)S(1)}, u32[]{:S(2)}, u32[]{:S(2)}) collective-permute-start(bf16[64,1024]{1,0:T(8,128)(2,1)S(1)} %collective-permute-done.6.refs_0_), channel_id=1, source_target_pairs={{0,4},{4,0},{8,12},{12,8},{1,5},{5,1},{9,13},{13,9},{2,6},{6,2},{1... | collective-permute-start | bytes 393224 | tf_op jit(solution)/shard_map/ppermute | solution.py:245
  25.8 2.2 %collective-permute-done.8.refs_2_ = bf16[64,1024]{1,0:T(8,128)(2,1)S(1)} collective-permute-done((bf16[64,1024]{1,0:T(8,128)(2,1)S(1)}, bf16[64,1024]{1,0:T(8,128)(2,1)S(1)}, u32[]{:S(2)}, u32[]{:S(2)}) %collective-permute-start.8) | collective-permute-done | bytes 131104 | tf_op jit(solution)/shard_map/ppermute | solution.py:245
  28.1 2.8 %collective-permute-done.7.refs_1_ = bf16[64,1024]{1,0:T(8,128)(2,1)S(1)} collective-permute-done((bf16[64,1024]{1,0:T(8,128)(2,1)S(1)}, bf16[64,1024]{1,0:T(8,128)(2,1)S(1)}, u32[]{:S(2)}, u32[]{:S(2)}) %collective-permute-start.7) | collective-permute-done | bytes 131104 | tf_op jit(solution)/shard_map/ppermute | solution.py:245
  31.3 1.6 %collective-permute-start.5 = (bf16[128,512]{1,0:T(8,128)(2,1)S(1)}, bf16[128,512]{1,0:T(8,128)(2,1)S(1)}, u32[]{:S(2)}, u32[]{:S(2)}) collective-permute-start(bf16[128,512]{1,0:T(8,128)(2,1)S(1)} %shard_map.76.refs_0_), channel_id=1, source_target_pairs={{0,2},{1,3},{2,0},{3,1},{4,6},{5,7},{6,4},{7,5},{8,10},{9,11},{10,... | collective-permute-start | bytes 393224 | tf_op jit(solution)/shard_map/ppermute | solution.py:245
  32.9 1.3 %collective-permute-start.10 = (bf16[96,512]{1,0:T(8,128)(2,1)S(1)}, bf16[96,512]{1,0:T(8,128)(2,1)S(1)}, u32[]{:S(2)}, u32[]{:S(2)}) collective-permute-start(bf16[96,512]{1,0:T(8,128)(2,1)S(1)} %shard_map.79.refs_0_), channel_id=1, source_target_pairs={{0,2},{1,3},{2,0},{3,1},{4,6},{5,7},{6,4},{7,5},{8,10},{9,11},{10,... | collective-permute-start | bytes 294920 | tf_op jit(solution)/shard_map/ppermute | solution.py:245
  34.5 1.2 %collective-permute-done.12.refs_1_ = bf16[32,512]{1,0:T(8,128)(2,1)S(1)} collective-permute-done((bf16[32,512]{1,0:T(8,128)(2,1)S(1)}, bf16[32,512]{1,0:T(8,128)(2,1)S(1)}, u32[]{:S(2)}, u32[]{:S(2)}) %collective-permute-start.12) | collective-permute-done | bytes 32800 | tf_op jit(solution)/shard_map/ppermute | solution.py:245
  35.7 0.9 %collective-permute-start.13 = (bf16[32,512]{1,0:T(8,128)(2,1)S(1)}, bf16[32,512]{1,0:T(8,128)(2,1)S(1)}, u32[]{:S(2)}, u32[]{:S(2)}) collective-permute-start(bf16[32,512]{1,0:T(8,128)(2,1)S(1)} %shard_map.82.refs_0_), channel_id=1, source_target_pairs={{0,2},{1,3},{2,0},{3,1},{4,6},{5,7},{6,4},{7,5},{8,10},{9,11},{10,... | collective-permute-start | bytes 98312 | tf_op jit(solution)/shard_map/ppermute | solution.py:245
  36.6 1.0 %collective-permute-done.5.refs_1_ = bf16[128,512]{1,0:T(8,128)(2,1)S(1)} collective-permute-done((bf16[128,512]{1,0:T(8,128)(2,1)S(1)}, bf16[128,512]{1,0:T(8,128)(2,1)S(1)}, u32[]{:S(2)}, u32[]{:S(2)}) %collective-permute-start.5) | collective-permute-done | bytes 131104 | tf_op jit(solution)/shard_map/ppermute | solution.py:245
  37.7 2.3 %collective-permute-done.13.refs_1_ = bf16[32,512]{1,0:T(8,128)(2,1)S(1)} collective-permute-done((bf16[32,512]{1,0:T(8,128)(2,1)S(1)}, bf16[32,512]{1,0:T(8,128)(2,1)S(1)}, u32[]{:S(2)}, u32[]{:S(2)}) %collective-permute-start.13) | collective-permute-done | bytes 32800 | tf_op jit(solution)/shard_map/ppermute | solution.py:245
  40.3 3.2 %collective-permute-start.14 = (bf16[32,512]{1,0:T(8,128)(2,1)S(1)}, bf16[32,512]{1,0:T(8,128)(2,1)S(1)}, u32[]{:S(2)}, u32[]{:S(2)}) collective-permute-start(bf16[32,512]{1,0:T(8,128)(2,1)S(1)} %get-tuple-element.38), channel_id=1, source_target_pairs={{0,12},{4,8},{8,4},{12,0},{1,13},{5,9},{9,5},{13,1},{2,14},{6,10},... | collective-permute-start | bytes 98312 | tf_op jit(solution)/shard_map/ppermute | solution.py:245
  43.4 1.3 %collective-permute-start.16 = (bf16[32,512]{1,0:T(8,128)(2,1)S(1)}, bf16[32,512]{1,0:T(8,128)(2,1)S(1)}, u32[]{:S(2)}, u32[]{:S(2)}) collective-permute-start(bf16[32,512]{1,0:T(8,128)(2,1)S(1)} %get-tuple-element.40), channel_id=1, source_target_pairs={{0,4},{4,0},{8,12},{12,8},{1,5},{5,1},{9,13},{13,9},{2,6},{6,2},{1... | collective-permute-start | bytes 98312 | tf_op jit(solution)/shard_map/ppermute | solution.py:245
  44.7 1.4 %collective-permute-done.14.far_ref = bf16[32,512]{1,0:T(8,128)(2,1)S(1)} collective-permute-done((bf16[32,512]{1,0:T(8,128)(2,1)S(1)}, bf16[32,512]{1,0:T(8,128)(2,1)S(1)}, u32[]{:S(2)}, u32[]{:S(2)}) %collective-permute-start.14) | collective-permute-done | bytes 32800 | tf_op jit(solution)/shard_map/ppermute | solution.py:245
  46.1 2.1 %collective-permute-done.15.two_ref = bf16[32,512]{1,0:T(8,128)(2,1)S(1)} collective-permute-done((bf16[32,512]{1,0:T(8,128)(2,1)S(1)}, bf16[32,512]{1,0:T(8,128)(2,1)S(1)}, u32[]{:S(2)}, u32[]{:S(2)}) %collective-permute-start.15) | collective-permute-done | bytes 32800 | tf_op jit(solution)/shard_map/ppermute | solution.py:245
  48.2 0.7 %shard_map.86 = bf16[32,2048]{1,0:T(8,128)(2,1)} custom-call(bf16[32,1024]{1,0:T(8,128)(2,1)S(1)} %shard_map.85.held_ref, bf16[32,512]{1,0:T(8,128)(2,1)S(1)} %collective-permute-done.15.two_ref, bf16[32,512]{1,0:T(8,128)(2,1)S(1)} %collective-permute-done.16.one_ref), custom_call_target="tpu_custom_call" | custom-call | bytes 262144 | tf_op jit(solution)/shard_map/pallas_call | solution.py:234
  (39 shorter events, 1.7 us)
Async XLA Ops:
  0.0 6.8 %copy-start.6 = (s32[2]{0:T(128)S(1)}, s32[2]{0:T(128)}, u32[]{:S(2)}) copy-start(s32[2]{0:T(128)} %param.12) | copy-start | bytes 28
  0.0 11.3 %copy-start.1 = (bf16[128,1024]{1,0:T(8,128)(2,1)S(1)}, bf16[128,1024]{1,0:T(8,128)(2,1)}, u32[]{:S(2)}) copy-start(bf16[128,1024]{1,0:T(8,128)(2,1)} %q_ref.1) | copy-start | bytes 786436
  0.0 11.3 %copy-start.2 = (bf16[128,256]{1,0:T(8,128)(2,1)S(1)}, bf16[128,256]{1,0:T(8,128)(2,1)}, u32[]{:S(2)}) copy-start(bf16[128,256]{1,0:T(8,128)(2,1)} %k_ref.3) | copy-start | bytes 196612
  0.0 11.3 %copy-start.3 = (bf16[128,256]{1,0:T(8,128)(2,1)S(1)}, bf16[128,256]{1,0:T(8,128)(2,1)}, u32[]{:S(2)}) copy-start(bf16[128,256]{1,0:T(8,128)(2,1)} %v_ref.3) | copy-start | bytes 196612
  0.0 22.9 %copy-start = (bf16[1024,512]{1,0:T(8,128)(2,1)S(1)}, bf16[1024,512]{1,0:T(8,128)(2,1)}, u32[]{:S(2)}) copy-start(bf16[1024,512]{1,0:T(8,128)(2,1)} %refs_1_.1) | copy-start | bytes 3145732
  1.7 9.6 %copy-start.4 = (s32[128]{0:T(128)S(1)}, s32[128]{0:T(128)}, u32[]{:S(2)}) copy-start(s32[128]{0:T(128)} %param.11) | copy-start | bytes 1540
  1.7 9.6 %copy-start.5 = (s32[128]{0:T(128)S(1)}, s32[128]{0:T(128)}, u32[]{:S(2)}) copy-start(s32[128]{0:T(128)} %param.10) | copy-start | bytes 1540
  1.7 9.6 %collective-permute-start.2 = (bf16[144,512]{1,0:T(8,128)(2,1)}, bf16[144,512]{1,0:T(8,128)(2,1)S(1)}, u32[]{:S(2)}, u32[]{:S(2)}) collective-permute-start(bf16[144,512]{1,0:T(8,128)(2,1)} %shard_map.73), channel_id=1, source_target_pairs={{0,4},{4,8},{8,12},{1,5},{5,9},{9,13},{2,6},{6,10},{10,14},{3,7},{... | collective-permute-start | bytes 442376 | tf_op jit(solution)/shard_map/ppermute | solution.py:266
  6.8 4.5 %collective-permute-start = (s32[2]{0:T(128)S(1)}, s32[2]{0:T(128)S(1)}, u32[]{:S(2)}, u32[]{:S(2)}) collective-permute-start(s32[2]{0:T(128)S(1)} %copy-done.6), channel_id=1, source_target_pairs={{0,8},{4,12},{8,0},{12,4},{1,9},{5,13},{9,1},{13,5},{2,10},{6,14},... | collective-permute-start | bytes 32 | tf_op jit(solution)/shard_map/ppermute | solution.py:245
  12.0 10.8 %collective-permute-start.3 = (bf16[128,1024]{1,0:T(8,128)(2,1)S(1)}, bf16[128,1024]{1,0:T(8,128)(2,1)S(1)}, u32[]{:S(2)}, u32[]{:S(2)}) collective-permute-start(bf16[128,1024]{1,0:T(8,128)(2,1)S(1)} %get-tuple-element.25.refs_0_), channel_id=1, source_target_pairs={{0,4},{4,0},{8,12},{12,8},{1,5},{5,1},{9,13},{13,9},{2,6},{6,2},{1... | collective-permute-start | bytes 786440 | tf_op jit(solution)/shard_map/ppermute | solution.py:245
  13.7 9.7 %collective-permute-start.6 = (bf16[64,1024]{1,0:T(8,128)(2,1)S(1)}, bf16[64,1024]{1,0:T(8,128)(2,1)S(1)}, u32[]{:S(2)}, u32[]{:S(2)}) collective-permute-start(bf16[64,1024]{1,0:T(8,128)(2,1)S(1)} %get-tuple-element.29), channel_id=1, source_target_pairs={{0,8},{4,12},{8,0},{12,4},{1,9},{5,13},{9,1},{13,5},{2,10},{6,14},... | collective-permute-start | bytes 393224 | tf_op jit(solution)/shard_map/ppermute | solution.py:245
  16.0 6.9 %collective-permute-start.1 = (s32[1,4]{1,0:T(1,128)S(1)}, s32[1,4]{1,0:T(1,128)S(1)}, u32[]{:S(2)}, u32[]{:S(2)}) collective-permute-start(s32[1,4]{1,0:T(1,128)S(1)} %add_bitcast_fusion.even_ref), channel_id=1, source_target_pairs={{0,4},{4,0},{8,12},{12,8},{1,5},{5,1},{9,13},{13,9},{2,6},{6,2},{1... | collective-permute-start | bytes 56 | tf_op jit(solution)/shard_map/ppermute | solution.py:245
  16.8 11.2 %collective-permute-start.8 = (bf16[64,1024]{1,0:T(8,128)(2,1)S(1)}, bf16[64,1024]{1,0:T(8,128)(2,1)S(1)}, u32[]{:S(2)}, u32[]{:S(2)}) collective-permute-start(bf16[64,1024]{1,0:T(8,128)(2,1)S(1)} %get-tuple-element.30), channel_id=1, source_target_pairs={{0,8},{4,12},{8,0},{12,4},{1,9},{5,13},{9,1},{13,5},{2,10},{6,14},... | collective-permute-start | bytes 393224 | tf_op jit(solution)/shard_map/ppermute | solution.py:245
  23.3 4.7 %collective-permute-start.4 = (bf16[128,512]{1,0:T(8,128)(2,1)S(1)}, bf16[128,512]{1,0:T(8,128)(2,1)S(1)}, u32[]{:S(2)}, u32[]{:S(2)}) collective-permute-start(bf16[128,512]{1,0:T(8,128)(2,1)S(1)} %get-tuple-element.28), channel_id=1, source_target_pairs={{0,1},{1,0},{2,3},{3,2},{4,5},{5,4},{6,7},{7,6},{8,9},{9,8},{10,11... | collective-permute-start | bytes 393224 | tf_op jit(solution)/shard_map/ppermute | solution.py:245
  23.4 7.4 %collective-permute-start.7 = (bf16[64,1024]{1,0:T(8,128)(2,1)S(1)}, bf16[64,1024]{1,0:T(8,128)(2,1)S(1)}, u32[]{:S(2)}, u32[]{:S(2)}) collective-permute-start(bf16[64,1024]{1,0:T(8,128)(2,1)S(1)} %collective-permute-done.6.refs_0_), channel_id=1, source_target_pairs={{0,4},{4,0},{8,12},{12,8},{1,5},{5,1},{9,13},{13,9},{2,6},{6,2},{1... | collective-permute-start | bytes 393224 | tf_op jit(solution)/shard_map/ppermute | solution.py:245
  28.0 6.1 %collective-permute-start.11 = (bf16[64,1024]{1,0:T(8,128)(2,1)S(1)}, bf16[64,1024]{1,0:T(8,128)(2,1)S(1)}, u32[]{:S(2)}, u32[]{:S(2)}) collective-permute-start(bf16[64,1024]{1,0:T(8,128)(2,1)S(1)} %collective-permute-done.8.refs_2_), channel_id=1, source_target_pairs={{0,4},{4,0},{8,12},{12,8},{1,5},{5,1},{9,13},{13,9},{2,6},{6,2},{1... | collective-permute-start | bytes 393224 | tf_op jit(solution)/shard_map/ppermute | solution.py:245
  31.2 1.6 %collective-permute-start.9 = (bf16[96,512]{1,0:T(8,128)(2,1)S(1)}, bf16[96,512]{1,0:T(8,128)(2,1)S(1)}, u32[]{:S(2)}, u32[]{:S(2)}) collective-permute-start(bf16[96,512]{1,0:T(8,128)(2,1)S(1)} %get-tuple-element.33), channel_id=1, source_target_pairs={{0,1},{1,0},{2,3},{3,2},{4,5},{5,4},{6,7},{7,6},{8,9},{9,8},{10,11... | collective-permute-start | bytes 294920 | tf_op jit(solution)/shard_map/ppermute | solution.py:245
  31.3 6.4 %collective-permute-start.5 = (bf16[128,512]{1,0:T(8,128)(2,1)S(1)}, bf16[128,512]{1,0:T(8,128)(2,1)S(1)}, u32[]{:S(2)}, u32[]{:S(2)}) collective-permute-start(bf16[128,512]{1,0:T(8,128)(2,1)S(1)} %shard_map.76.refs_0_), channel_id=1, source_target_pairs={{0,2},{1,3},{2,0},{3,1},{4,6},{5,7},{6,4},{7,5},{8,10},{9,11},{10,... | collective-permute-start | bytes 393224 | tf_op jit(solution)/shard_map/ppermute | solution.py:245
  32.9 7.1 %collective-permute-start.10 = (bf16[96,512]{1,0:T(8,128)(2,1)S(1)}, bf16[96,512]{1,0:T(8,128)(2,1)S(1)}, u32[]{:S(2)}, u32[]{:S(2)}) collective-permute-start(bf16[96,512]{1,0:T(8,128)(2,1)S(1)} %shard_map.79.refs_0_), channel_id=1, source_target_pairs={{0,2},{1,3},{2,0},{3,1},{4,6},{5,7},{6,4},{7,5},{8,10},{9,11},{10,... | collective-permute-start | bytes 294920 | tf_op jit(solution)/shard_map/ppermute | solution.py:245
  34.4 1.3 %collective-permute-start.12 = (bf16[32,512]{1,0:T(8,128)(2,1)S(1)}, bf16[32,512]{1,0:T(8,128)(2,1)S(1)}, u32[]{:S(2)}, u32[]{:S(2)}) collective-permute-start(bf16[32,512]{1,0:T(8,128)(2,1)S(1)} %get-tuple-element.36), channel_id=1, source_target_pairs={{0,1},{1,0},{2,3},{3,2},{4,5},{5,4},{6,7},{7,6},{8,9},{9,8},{10,11... | collective-permute-start | bytes 98312 | tf_op jit(solution)/shard_map/ppermute | solution.py:245
  35.7 4.3 %collective-permute-start.13 = (bf16[32,512]{1,0:T(8,128)(2,1)S(1)}, bf16[32,512]{1,0:T(8,128)(2,1)S(1)}, u32[]{:S(2)}, u32[]{:S(2)}) collective-permute-start(bf16[32,512]{1,0:T(8,128)(2,1)S(1)} %shard_map.82.refs_0_), channel_id=1, source_target_pairs={{0,2},{1,3},{2,0},{3,1},{4,6},{5,7},{6,4},{7,5},{8,10},{9,11},{10,... | collective-permute-start | bytes 98312 | tf_op jit(solution)/shard_map/ppermute | solution.py:245
  40.3 5.8 %collective-permute-start.14 = (bf16[32,512]{1,0:T(8,128)(2,1)S(1)}, bf16[32,512]{1,0:T(8,128)(2,1)S(1)}, u32[]{:S(2)}, u32[]{:S(2)}) collective-permute-start(bf16[32,512]{1,0:T(8,128)(2,1)S(1)} %get-tuple-element.38), channel_id=1, source_target_pairs={{0,12},{4,8},{8,4},{12,0},{1,13},{5,9},{9,5},{13,1},{2,14},{6,10},... | collective-permute-start | bytes 98312 | tf_op jit(solution)/shard_map/ppermute | solution.py:245
  43.4 4.8 %collective-permute-start.15 = (bf16[32,512]{1,0:T(8,128)(2,1)S(1)}, bf16[32,512]{1,0:T(8,128)(2,1)S(1)}, u32[]{:S(2)}, u32[]{:S(2)}) collective-permute-start(bf16[32,512]{1,0:T(8,128)(2,1)S(1)} %get-tuple-element.39), channel_id=1, source_target_pairs={{0,8},{4,12},{8,0},{12,4},{1,9},{5,13},{9,1},{13,5},{2,10},{6,14},... | collective-permute-start | bytes 98312 | tf_op jit(solution)/shard_map/ppermute | solution.py:245
  43.4 4.8 %collective-permute-start.16 = (bf16[32,512]{1,0:T(8,128)(2,1)S(1)}, bf16[32,512]{1,0:T(8,128)(2,1)S(1)}, u32[]{:S(2)}, u32[]{:S(2)}) collective-permute-start(bf16[32,512]{1,0:T(8,128)(2,1)S(1)} %get-tuple-element.40), channel_id=1, source_target_pairs={{0,4},{4,0},{8,12},{12,8},{1,5},{5,1},{9,13},{13,9},{2,6},{6,2},{1... | collective-permute-start | bytes 98312 | tf_op jit(solution)/shard_map/ppermute | solution.py:245

commit v8 on v7

--- a/solution.py
+++ b/solution.py
@@ -57,8 +57,12 @@
     )(key_rows, value_rows, ends)
 
 
-def attend_kernel(blocks, q_ref, halo_ref, k_ref, v_ref, end_ref, st_ref, *refs):
+def attend_kernel(blocks, q_ref, halo_ref, k_ref, v_ref, end_ref, st_ref, targets_ref, *refs):
     whole_ref, *out_refs = refs
+    count = targets_ref.shape[1]
+    targets = jnp.broadcast_to(targets_ref[...].astype(jnp.float32), (8, count)).astype(jnp.bfloat16)
+    whole_ref[pl.ds(q_ref.shape[0], 8), :] = jnp.zeros((8, q_ref.shape[1]), jnp.bfloat16)
+    whole_ref[pl.ds(q_ref.shape[0], 8), pl.ds(0, count)] = targets
     rows = q_ref.shape[0]
     width = k_ref.shape[1]
     kv_here = width // HEAD_DIM
@@ -114,26 +118,27 @@
                     )
 
 
-def attend(blocks, queries, halo, keys, values, end, start):
+def attend(blocks, queries, halo, keys, values, end, start, targets):
     rows, features = queries.shape
     out = jax.ShapeDtypeStruct((rows // blocks, features), jnp.bfloat16)
     return pl.pallas_call(
         functools.partial(attend_kernel, blocks),
         out_shape=(
-            jax.ShapeDtypeStruct(queries.shape, jnp.bfloat16),
+            jax.ShapeDtypeStruct((rows + 8, features), jnp.bfloat16),
         )
         + (out,) * blocks,
-        in_specs=vmem(6),
+        in_specs=vmem(7),
         out_specs=tuple(vmem(1 + blocks)),
         compiler_params=params(),
         cost_estimate=cost(8 * rows * rows * features, 6 * queries.size),
-    )(queries, halo, keys, values, end, start)
+    )(queries, halo, keys, values, end, start, targets)
 
 
 def project_kernel(block_rows, *refs):
     chunks, weight_ref, mine_ref, other_ref = refs[:-3], refs[-3], refs[-2], refs[-1]
     half = block_rows // 2
-    stacked = jnp.concatenate([c[...] for c in chunks], axis=0)
+    whole = [c.shape[0] // block_rows * block_rows for c in chunks]
+    stacked = jnp.concatenate([c[pl.ds(0, n), :] for c, n in zip(chunks, whole)], axis=0)
     share = jnp.dot(stacked, weight_ref[...], preferred_element_type=jnp.float32).astype(
         jnp.bfloat16
     )
@@ -143,8 +148,8 @@
         other_ref[pl.ds(n * half, half), :] = share[first + half : first + block_rows]
 
 
-def project(block_rows, chunks, weight):
-    rows = sum(c.shape[0] for c in chunks)
+def project(block_rows, chunks, weight, estimate=None):
+    rows = sum(c.shape[0] // block_rows * block_rows for c in chunks)
     out = jax.ShapeDtypeStruct((rows // 2, weight.shape[1]), jnp.bfloat16)
     return pl.pallas_call(
         functools.partial(project_kernel, block_rows),
@@ -152,7 +157,7 @@
         in_specs=vmem(len(chunks) + 1),
         out_specs=tuple(vmem(2)),
         compiler_params=params(),
-        cost_estimate=cost(2 * rows * weight.size, 2 * weight.size),
+        cost_estimate=estimate or cost(2 * rows * weight.size, 2 * weight.size),
     )(*chunks, weight)
 
 
@@ -172,13 +177,15 @@
     )(*terms)
 
 
-def pick_kernel(blocks, half, even_ref, odd_ref, *refs):
+def pick_kernel(blocks, half, even_ref, whole_ref, *refs):
     sums, outs = refs[:-4], refs[-4:]
     x = lax.axis_index("tp") // 2
     c = lax.axis_index("ctx")
     order = (0, 1, 4, 5, 2, 6, 3, 7)
     pieces = [r[pl.ds(n, half), :] for r in sums for n in range(0, r.shape[0], half)]
-    targets = jnp.concatenate([even_ref[...], odd_ref[...]], axis=1)
+    tail = whole_ref[pl.ds(whole_ref.shape[0] - 8, 8), pl.ds(0, HEAD_DIM)].astype(jnp.float32)
+    odd = tail[0:1, 0 : 2 * blocks].astype(jnp.int32)
+    targets = jnp.concatenate([even_ref[...], odd], axis=1)
     for k in range(4):
         wanted = (c ^ k) * blocks + x
         piece = pieces[0]
@@ -189,7 +196,7 @@
         outs[k][...] = piece
 
 
-def pick(blocks, even_targets, odd_targets, sums):
+def pick(blocks, even_targets, whole_1, sums):
     rows, cols = sum(s.shape[0] for s in sums), sums[0].shape[1]
     half = rows // (4 * blocks)
     out = jax.ShapeDtypeStruct((half, cols), jnp.bfloat16)
@@ -200,7 +207,7 @@
         out_specs=tuple(vmem(4)),
         compiler_params=params(),
         cost_estimate=cost(4 * rows * cols, 8 * rows * cols),
-    )(even_targets, odd_targets, *sums)
+    )(even_targets, whole_1, *sums)
 
 
 def hold_kernel(near_ref, far_ref, out_ref):
@@ -247,6 +254,25 @@
 
 def core_total(mine, other):
     return total((mine, flip(other, "tp", 1)))
+
+
+def stack_kernel(done_ref, mine_ref, got_ref, out_ref):
+    rows = done_ref.shape[0]
+    out_ref[pl.ds(0, rows), :] = done_ref[...]
+    both = mine_ref[...].astype(jnp.float32) + got_ref[...].astype(jnp.float32)
+    out_ref[pl.ds(rows, mine_ref.shape[0]), :] = both.astype(out_ref.dtype)
+
+
+def stack_core_total(done, mine, other):
+    rows = done.shape[0] + mine.shape[0]
+    return pl.pallas_call(
+        stack_kernel,
+        out_shape=jax.ShapeDtypeStruct((rows, mine.shape[1]), jnp.bfloat16),
+        in_specs=vmem(3),
+        out_specs=pl.BlockSpec(memory_space=pltpu.VMEM),
+        compiler_params=params(),
+        cost_estimate=cost(mine.size, 8 * mine.size),
+    )(done, mine, flip(other, "tp", 1))
 
 
 def chip_total(share):
@@ -267,21 +293,19 @@
     target_2 = flip(after(block_target, message), "ctx", 2)
     even_targets = jnp.concatenate([block_target, target_2]).reshape(1, 2 * blocks)
     halo = after(halo, target_2)
-    whole, first, second = attend(blocks, queries, halo, key_rows, value_rows, end, start)
+    whole, first, second = attend(
+        blocks, queries, halo, key_rows, value_rows, end, start, even_targets
+    )
     whole_1 = flip(whole, "ctx", 1)
     first_2, second_2 = flip(first, "ctx", 2), flip(second, "ctx", 2)
-    odd_targets = flip(even_targets, "ctx", 1)
-    whole_1 = after(whole_1, odd_targets)
+    first_3, second_3 = flip(first_2, "ctx", 1), flip(second_2, "ctx", 1)
     share_a = core_total(*project(block_rows, (whole, whole_1), out_weight))
-    first_3, second_3 = flip(first_2, "ctx", 1), flip(second_2, "ctx", 1)
-    sum_a = chip_total(share_a)
-    second_2 = after(second_2, share_a)
-    share_b = core_total(*project(block_rows, (first_2, first_3, second_2), out_weight))
-    second_3 = after(second_3, share_b)
-    share_c = core_total(*project(block_rows, (second_3,), out_weight))
-    sum_b = chip_total(share_b)
-    sum_c = chip_total(share_c)
-    kept, *sent = pick(blocks, even_targets, odd_targets, (sum_a, sum_b, sum_c))
+    share_ab = stack_core_total(
+        share_a, *project(block_rows, (first_2, first_3, second_2), out_weight, cost(3 * 10**9, 0))
+    )
+    share_c = core_total(*project(block_rows, (second_3,), out_weight, cost(10**10, 0)))
+    sums = (chip_total(share_ab), chip_total(share_c))
+    kept, *sent = pick(blocks, even_targets, whole_1, sums)
     got_3, got_2, got_1 = (flip(sent[k - 1], "ctx", k) for k in (3, 2, 1))
     return join(hold(kept, got_3), got_2, got_1)
 

time: 49.1 us -> 49.7 us (1.012)
  starting transfers between devices: 23.6 us -> 26.5 us
  waiting for transfers between devices: 20.6 us -> 17.8 us
  local copies, waits for them, and re-layouts: 0.03 us -> 0.66 us
    ppermute x16 -> x14, starting transfers between devices: 18.5 us -> 21.5 us  [flip(): return lax.ppermute(array, axis, [(i, i ^ bits) for i in range(4)])]
    ppermute x16 -> x14, waiting for transfers between devices: 20.6 us -> 17.8 us  [flip(): return lax.ppermute(array, axis, [(i, i ^ bits) for i in range(4)])]
    unnamed x14, local copies, waits for them, and re-layouts: 0.03 us -> 0.66 us
  transfers between devices with their start and end apart: 17 -> 15, of which waited for: 9 -> 9; matrix products, arithmetic and copies ran while one was open for 0% -> 0% of each run, Pallas kernels for 2% -> 2%
where the time goes in v8:
time: 49.7 us; the launch traced here: 49.6 us
  starting transfers between devices  26.5 us (53%)
  waiting for transfers between devices  17.8 us (36%)
  Pallas kernels  4.49 us (9%)
  local copies, waits for them, and re-layouts  0.66 us (1%)
    ppermute x14, starting transfers between devices, flip(): return lax.ppermute(array, axis, [(i, i ^ bits) for i in range(4)])  21.5 us
    ppermute x14, waiting for transfers between devices, flip(): return lax.ppermute(array, axis, [(i, i ^ bits) for i in range(4)])  17.8 us
    ppermute x1, starting transfers between devices, small_ring(): halo = lax.ppermute(message, 'ctx', [(0, 1), (1, 2), (2, 3)])  4.94 us
    pallas_call x1, Pallas kernels, pack(): pl.pallas_call(pack_kernel, out_shape=jax.ShapeDtypeStruct((rows + 16, 2...  1.66 us
    pallas_call x3, Pallas kernels, project(): pl.pallas_call(functools.partial(project_kernel, block_rows), out_shape=(...  1.1 us
  transfers between devices with their start and end apart: 15, of which 9 were waited for; matrix products, arithmetic and copies ran while one was open for 0% of the time, Pallas kernels for 2%

profile of v8, /device:TPU:0, one launch (start us, length us, event | category | flops | bytes accessed | tf_op | source)
XLA Modules:
  0.0 49.6 jit_solution(15295017395547302126)
XLA Ops:
  0.0 1.7 %shard_map.73 = bf16[144,512]{1,0:T(8,128)(2,1)} custom-call(bf16[128,256]{1,0:T(8,128)(2,1)} %k_ref.3, bf16[128,256]{1,0:T(8,128)(2,1)} %v_ref.3, s32[1,128]{1,0:T(1,128)} %bitcast.4), custom_call_target="tpu_custom_call" | custom-call | flops 1000000000 | bytes 262144 | tf_op jit(solution)/shard_map/pallas_call | solution.py:51
  1.7 4.9 %collective-permute-start.1 = (bf16[144,512]{1,0:T(8,128)(2,1)}, bf16[144,512]{1,0:T(8,128)(2,1)S(1)}, u32[]{:S(2)}, u32[]{:S(2)}) collective-permute-start(bf16[144,512]{1,0:T(8,128)(2,1)} %shard_map.73), channel_id=1, source_target_pairs={{0,4},{4,8},{8,12},{1,5},{5,9},{9,13},{2,6},{6,10},{10,14},{3,7},{... | collective-permute-start | bytes 442376 | tf_op jit(solution)/shard_map/ppermute | solution.py:292
  6.6 2.6 %collective-permute-start = (s32[2]{0:T(128)S(1)}, s32[2]{0:T(128)S(1)}, u32[]{:S(2)}, u32[]{:S(2)}) collective-permute-start(s32[2]{0:T(128)S(1)} %copy-done.6), channel_id=1, source_target_pairs={{0,8},{4,12},{8,0},{12,4},{1,9},{5,13},{9,1},{13,5},{2,10},{6,14},... | collective-permute-start | bytes 32 | tf_op jit(solution)/shard_map/ppermute | solution.py:252
  9.3 1.9 %collective-permute-done = s32[2]{0:T(128)S(1)} collective-permute-done((s32[2]{0:T(128)S(1)}, s32[2]{0:T(128)S(1)}, u32[]{:S(2)}, u32[]{:S(2)}) %collective-permute-start) | collective-permute-done | bytes 40 | tf_op jit(solution)/shard_map/ppermute | solution.py:252
  11.2 0.6 %copy-done.4 = s32[128]{0:T(128)S(1)} copy-done((s32[128]{0:T(128)S(1)}, s32[128]{0:T(128)}, u32[]{:S(2)}) %copy-start.4) | copy-done | bytes 536
  11.9 0.7 %shard_map.74 = (bf16[136,1024]{1,0:T(8,128)(2,1)S(1)}, bf16[64,1024]{1,0:T(8,128)(2,1)S(1)}, bf16[64,1024]{1,0:T(8,128)(2,1)S(1)}) custom-call(bf16[128,1024]{1,0:T(8,128)(2,1)S(1)} %copy-done.1, bf16[144,512]{1,0:T(8,128)(2,1)S(1)} %collective-permute-done.1.halo_ref, bf16[128,256]{1,0:T(8,128)(2,1)S(1)} %copy-done.2, bf16[128,256]{1,0:T(8,128)(2,1)S(1)} %copy-done.3, ...), custom_call_target="tpu_custom_call" | custom-call | flops 134217728 | bytes 786432 | tf_op jit(solution)/shard_map/pallas_call | solution.py:124
  12.6 1.6 %collective-permute-start.2 = (bf16[136,1024]{1,0:T(8,128)(2,1)S(1)}, bf16[136,1024]{1,0:T(8,128)(2,1)S(1)}, u32[]{:S(2)}, u32[]{:S(2)}) collective-permute-start(bf16[136,1024]{1,0:T(8,128)(2,1)S(1)} %get-tuple-element.22.refs_0_), channel_id=1, source_target_pairs={{0,4},{4,0},{8,12},{12,8},{1,5},{5,1},{9,13},{13,9},{2,6},{6,2},{1... | collective-permute-start | bytes 835592 | tf_op jit(solution)/shard_map/ppermute | solution.py:252
  14.2 2.2 %collective-permute-start.4 = (bf16[64,1024]{1,0:T(8,128)(2,1)S(1)}, bf16[64,1024]{1,0:T(8,128)(2,1)S(1)}, u32[]{:S(2)}, u32[]{:S(2)}) collective-permute-start(bf16[64,1024]{1,0:T(8,128)(2,1)S(1)} %get-tuple-element.25), channel_id=1, source_target_pairs={{0,8},{4,12},{8,0},{12,4},{1,9},{5,13},{9,1},{13,5},{2,10},{6,14},... | collective-permute-start | bytes 393224 | tf_op jit(solution)/shard_map/ppermute | solution.py:252
  16.4 0.8 %collective-permute-start.6 = (bf16[64,1024]{1,0:T(8,128)(2,1)S(1)}, bf16[64,1024]{1,0:T(8,128)(2,1)S(1)}, u32[]{:S(2)}, u32[]{:S(2)}) collective-permute-start(bf16[64,1024]{1,0:T(8,128)(2,1)S(1)} %get-tuple-element.26), channel_id=1, source_target_pairs={{0,8},{4,12},{8,0},{12,4},{1,9},{5,13},{9,1},{13,5},{2,10},{6,14},... | collective-permute-start | bytes 393224 | tf_op jit(solution)/shard_map/ppermute | solution.py:252
  17.1 6.4 %collective-permute-done.4.refs_0_ = bf16[64,1024]{1,0:T(8,128)(2,1)S(1)} collective-permute-done((bf16[64,1024]{1,0:T(8,128)(2,1)S(1)}, bf16[64,1024]{1,0:T(8,128)(2,1)S(1)}, u32[]{:S(2)}, u32[]{:S(2)}) %collective-permute-start.4) | collective-permute-done | bytes 131104 | tf_op jit(solution)/shard_map/ppermute | solution.py:252
  23.5 4.1 %collective-permute-start.5 = (bf16[64,1024]{1,0:T(8,128)(2,1)S(1)}, bf16[64,1024]{1,0:T(8,128)(2,1)S(1)}, u32[]{:S(2)}, u32[]{:S(2)}) collective-permute-start(bf16[64,1024]{1,0:T(8,128)(2,1)S(1)} %collective-permute-done.4.refs_0_), channel_id=1, source_target_pairs={{0,4},{4,0},{8,12},{12,8},{1,5},{5,1},{9,13},{13,9},{2,6},{6,2},{1... | collective-permute-start | bytes 393224 | tf_op jit(solution)/shard_map/ppermute | solution.py:252
  27.6 2.8 %collective-permute-start.9 = (bf16[64,1024]{1,0:T(8,128)(2,1)S(1)}, bf16[64,1024]{1,0:T(8,128)(2,1)S(1)}, u32[]{:S(2)}, u32[]{:S(2)}) collective-permute-start(bf16[64,1024]{1,0:T(8,128)(2,1)S(1)} %collective-permute-done.6.refs_2_), channel_id=1, source_target_pairs={{0,4},{4,0},{8,12},{12,8},{1,5},{5,1},{9,13},{13,9},{2,6},{6,2},{1... | collective-permute-start | bytes 393224 | tf_op jit(solution)/shard_map/ppermute | solution.py:252
  31.4 0.6 %collective-permute-start.7 = (bf16[96,512]{1,0:T(8,128)(2,1)S(1)}, bf16[96,512]{1,0:T(8,128)(2,1)S(1)}, u32[]{:S(2)}, u32[]{:S(2)}) collective-permute-start(bf16[96,512]{1,0:T(8,128)(2,1)S(1)} %get-tuple-element.28), channel_id=1, source_target_pairs={{0,1},{1,0},{2,3},{3,2},{4,5},{5,4},{6,7},{7,6},{8,9},{9,8},{10,11... | collective-permute-start | bytes 294920 | tf_op jit(solution)/shard_map/ppermute | solution.py:252
  32.3 0.5 %collective-permute-done.7.got_ref = bf16[96,512]{1,0:T(8,128)(2,1)S(1)} collective-permute-done((bf16[96,512]{1,0:T(8,128)(2,1)S(1)}, bf16[96,512]{1,0:T(8,128)(2,1)S(1)}, u32[]{:S(2)}, u32[]{:S(2)}) %collective-permute-start.7) | collective-permute-done | bytes 98336 | tf_op jit(solution)/shard_map/ppermute | solution.py:252
  32.9 1.6 %collective-permute-start.8 = (bf16[224,512]{1,0:T(8,128)(2,1)S(1)}, bf16[224,512]{1,0:T(8,128)(2,1)S(1)}, u32[]{:S(2)}, u32[]{:S(2)}) collective-permute-start(bf16[224,512]{1,0:T(8,128)(2,1)S(1)} %shard_map.78.refs_0_), channel_id=1, source_target_pairs={{0,2},{1,3},{2,0},{3,1},{4,6},{5,7},{6,4},{7,5},{8,10},{9,11},{10,... | collective-permute-start | bytes 688136 | tf_op jit(solution)/shard_map/ppermute | solution.py:252
  34.9 1.1 %collective-permute-done.10.refs_1_ = bf16[32,512]{1,0:T(8,128)(2,1)S(1)} collective-permute-done((bf16[32,512]{1,0:T(8,128)(2,1)S(1)}, bf16[32,512]{1,0:T(8,128)(2,1)S(1)}, u32[]{:S(2)}, u32[]{:S(2)}) %collective-permute-start.10) | collective-permute-done | bytes 32800 | tf_op jit(solution)/shard_map/ppermute | solution.py:252
  36.1 0.6 %collective-permute-start.11 = (bf16[32,512]{1,0:T(8,128)(2,1)S(1)}, bf16[32,512]{1,0:T(8,128)(2,1)S(1)}, u32[]{:S(2)}, u32[]{:S(2)}) collective-permute-start(bf16[32,512]{1,0:T(8,128)(2,1)S(1)} %shard_map.81.refs_0_), channel_id=1, source_target_pairs={{0,2},{1,3},{2,0},{3,1},{4,6},{5,7},{6,4},{7,5},{8,10},{9,11},{10,... | collective-permute-start | bytes 98312 | tf_op jit(solution)/shard_map/ppermute | solution.py:252
  36.7 4.9 %collective-permute-done.11.refs_1_ = bf16[32,512]{1,0:T(8,128)(2,1)S(1)} collective-permute-done((bf16[32,512]{1,0:T(8,128)(2,1)S(1)}, bf16[32,512]{1,0:T(8,128)(2,1)S(1)}, u32[]{:S(2)}, u32[]{:S(2)}) %collective-permute-start.11) | collective-permute-done | bytes 32800 | tf_op jit(solution)/shard_map/ppermute | solution.py:252
  41.9 1.6 %collective-permute-start.12 = (bf16[32,512]{1,0:T(8,128)(2,1)S(1)}, bf16[32,512]{1,0:T(8,128)(2,1)S(1)}, u32[]{:S(2)}, u32[]{:S(2)}) collective-permute-start(bf16[32,512]{1,0:T(8,128)(2,1)S(1)} %get-tuple-element.32), channel_id=1, source_target_pairs={{0,12},{4,8},{8,4},{12,0},{1,13},{5,9},{9,5},{13,1},{2,14},{6,10},... | collective-permute-start | bytes 98312 | tf_op jit(solution)/shard_map/ppermute | solution.py:252
  43.5 1.2 %collective-permute-start.13 = (bf16[32,512]{1,0:T(8,128)(2,1)S(1)}, bf16[32,512]{1,0:T(8,128)(2,1)S(1)}, u32[]{:S(2)}, u32[]{:S(2)}) collective-permute-start(bf16[32,512]{1,0:T(8,128)(2,1)S(1)} %get-tuple-element.33), channel_id=1, source_target_pairs={{0,8},{4,12},{8,0},{12,4},{1,9},{5,13},{9,1},{13,5},{2,10},{6,14},... | collective-permute-start | bytes 98312 | tf_op jit(solution)/shard_map/ppermute | solution.py:252
  44.7 1.6 %collective-permute-start.14 = (bf16[32,512]{1,0:T(8,128)(2,1)S(1)}, bf16[32,512]{1,0:T(8,128)(2,1)S(1)}, u32[]{:S(2)}, u32[]{:S(2)}) collective-permute-start(bf16[32,512]{1,0:T(8,128)(2,1)S(1)} %get-tuple-element.34), channel_id=1, source_target_pairs={{0,4},{4,0},{8,12},{12,8},{1,5},{5,1},{9,13},{13,9},{2,6},{6,2},{1... | collective-permute-start | bytes 98312 | tf_op jit(solution)/shard_map/ppermute | solution.py:252
  46.3 1.6 %collective-permute-done.12.far_ref = bf16[32,512]{1,0:T(8,128)(2,1)S(1)} collective-permute-done((bf16[32,512]{1,0:T(8,128)(2,1)S(1)}, bf16[32,512]{1,0:T(8,128)(2,1)S(1)}, u32[]{:S(2)}, u32[]{:S(2)}) %collective-permute-start.12) | collective-permute-done | bytes 32800 | tf_op jit(solution)/shard_map/ppermute | solution.py:252
  47.9 0.7 %collective-permute-done.13.two_ref = bf16[32,512]{1,0:T(8,128)(2,1)S(1)} collective-permute-done((bf16[32,512]{1,0:T(8,128)(2,1)S(1)}, bf16[32,512]{1,0:T(8,128)(2,1)S(1)}, u32[]{:S(2)}, u32[]{:S(2)}) %collective-permute-start.13) | collective-permute-done | bytes 32800 | tf_op jit(solution)/shard_map/ppermute | solution.py:252
  48.9 0.7 %shard_map.85 = bf16[32,2048]{1,0:T(8,128)(2,1)} custom-call(bf16[32,1024]{1,0:T(8,128)(2,1)S(1)} %shard_map.84.held_ref, bf16[32,512]{1,0:T(8,128)(2,1)S(1)} %collective-permute-done.13.two_ref, bf16[32,512]{1,0:T(8,128)(2,1)S(1)} %collective-permute-done.14.one_ref), custom_call_target="tpu_custom_call" | custom-call | bytes 262144 | tf_op jit(solution)/shard_map/pallas_call | solution.py:241
  (34 shorter events, 2.5 us)
Async XLA Ops:
  0.0 6.6 %copy-start.6 = (s32[2]{0:T(128)S(1)}, s32[2]{0:T(128)}, u32[]{:S(2)}) copy-start(s32[2]{0:T(128)} %param.12) | copy-start | bytes 28
  0.0 11.2 %copy-start.1 = (bf16[128,1024]{1,0:T(8,128)(2,1)S(1)}, bf16[128,1024]{1,0:T(8,128)(2,1)}, u32[]{:S(2)}) copy-start(bf16[128,1024]{1,0:T(8,128)(2,1)} %q_ref.1) | copy-start | bytes 786436
  0.0 11.2 %copy-start.2 = (bf16[128,256]{1,0:T(8,128)(2,1)S(1)}, bf16[128,256]{1,0:T(8,128)(2,1)}, u32[]{:S(2)}) copy-start(bf16[128,256]{1,0:T(8,128)(2,1)} %k_ref.3) | copy-start | bytes 196612
  0.0 11.2 %copy-start.3 = (bf16[128,256]{1,0:T(8,128)(2,1)S(1)}, bf16[128,256]{1,0:T(8,128)(2,1)}, u32[]{:S(2)}) copy-start(bf16[128,256]{1,0:T(8,128)(2,1)} %v_ref.3) | copy-start | bytes 196612
  0.0 30.4 %copy-start = (bf16[1024,512]{1,0:T(8,128)(2,1)S(1)}, bf16[1024,512]{1,0:T(8,128)(2,1)}, u32[]{:S(2)}) copy-start(bf16[1024,512]{1,0:T(8,128)(2,1)} %refs_1_.1) | copy-start | bytes 3145732
  1.7 9.5 %collective-permute-start.1 = (bf16[144,512]{1,0:T(8,128)(2,1)}, bf16[144,512]{1,0:T(8,128)(2,1)S(1)}, u32[]{:S(2)}, u32[]{:S(2)}) collective-permute-start(bf16[144,512]{1,0:T(8,128)(2,1)} %shard_map.73), channel_id=1, source_target_pairs={{0,4},{4,8},{8,12},{1,5},{5,9},{9,13},{2,6},{6,10},{10,14},{3,7},{... | collective-permute-start | bytes 442376 | tf_op jit(solution)/shard_map/ppermute | solution.py:292
  6.6 4.5 %collective-permute-start = (s32[2]{0:T(128)S(1)}, s32[2]{0:T(128)S(1)}, u32[]{:S(2)}, u32[]{:S(2)}) collective-permute-start(s32[2]{0:T(128)S(1)} %copy-done.6), channel_id=1, source_target_pairs={{0,8},{4,12},{8,0},{12,4},{1,9},{5,13},{9,1},{13,5},{2,10},{6,14},... | collective-permute-start | bytes 32 | tf_op jit(solution)/shard_map/ppermute | solution.py:252
  11.2 0.7 %copy-start.4 = (s32[128]{0:T(128)S(1)}, s32[128]{0:T(128)}, u32[]{:S(2)}) copy-start(s32[128]{0:T(128)} %param.11) | copy-start | bytes 1540
  11.2 0.7 %copy-start.5 = (s32[128]{0:T(128)S(1)}, s32[128]{0:T(128)}, u32[]{:S(2)}) copy-start(s32[128]{0:T(128)} %param.10) | copy-start | bytes 1540
  12.6 17.9 %collective-permute-start.2 = (bf16[136,1024]{1,0:T(8,128)(2,1)S(1)}, bf16[136,1024]{1,0:T(8,128)(2,1)S(1)}, u32[]{:S(2)}, u32[]{:S(2)}) collective-permute-start(bf16[136,1024]{1,0:T(8,128)(2,1)S(1)} %get-tuple-element.22.refs_0_), channel_id=1, source_target_pairs={{0,4},{4,0},{8,12},{12,8},{1,5},{5,1},{9,13},{13,9},{2,6},{6,2},{1... | collective-permute-start | bytes 835592 | tf_op jit(solution)/shard_map/ppermute | solution.py:252
  14.2 9.3 %collective-permute-start.4 = (bf16[64,1024]{1,0:T(8,128)(2,1)S(1)}, bf16[64,1024]{1,0:T(8,128)(2,1)S(1)}, u32[]{:S(2)}, u32[]{:S(2)}) collective-permute-start(bf16[64,1024]{1,0:T(8,128)(2,1)S(1)} %get-tuple-element.25), channel_id=1, source_target_pairs={{0,8},{4,12},{8,0},{12,4},{1,9},{5,13},{9,1},{13,5},{2,10},{6,14},... | collective-permute-start | bytes 393224 | tf_op jit(solution)/shard_map/ppermute | solution.py:252
  16.4 11.3 %collective-permute-start.6 = (bf16[64,1024]{1,0:T(8,128)(2,1)S(1)}, bf16[64,1024]{1,0:T(8,128)(2,1)S(1)}, u32[]{:S(2)}, u32[]{:S(2)}) collective-permute-start(bf16[64,1024]{1,0:T(8,128)(2,1)S(1)} %get-tuple-element.26), channel_id=1, source_target_pairs={{0,8},{4,12},{8,0},{12,4},{1,9},{5,13},{9,1},{13,5},{2,10},{6,14},... | collective-permute-start | bytes 393224 | tf_op jit(solution)/shard_map/ppermute | solution.py:252
  23.5 7.5 %collective-permute-start.5 = (bf16[64,1024]{1,0:T(8,128)(2,1)S(1)}, bf16[64,1024]{1,0:T(8,128)(2,1)S(1)}, u32[]{:S(2)}, u32[]{:S(2)}) collective-permute-start(bf16[64,1024]{1,0:T(8,128)(2,1)S(1)} %collective-permute-done.4.refs_0_), channel_id=1, source_target_pairs={{0,4},{4,0},{8,12},{12,8},{1,5},{5,1},{9,13},{13,9},{2,6},{6,2},{1... | collective-permute-start | bytes 393224 | tf_op jit(solution)/shard_map/ppermute | solution.py:252
  27.6 6.8 %collective-permute-start.9 = (bf16[64,1024]{1,0:T(8,128)(2,1)S(1)}, bf16[64,1024]{1,0:T(8,128)(2,1)S(1)}, u32[]{:S(2)}, u32[]{:S(2)}) collective-permute-start(bf16[64,1024]{1,0:T(8,128)(2,1)S(1)} %collective-permute-done.6.refs_2_), channel_id=1, source_target_pairs={{0,4},{4,0},{8,12},{12,8},{1,5},{5,1},{9,13},{13,9},{2,6},{6,2},{1... | collective-permute-start | bytes 393224 | tf_op jit(solution)/shard_map/ppermute | solution.py:252
  30.9 1.4 %collective-permute-start.3 = (bf16[128,512]{1,0:T(8,128)(2,1)S(1)}, bf16[128,512]{1,0:T(8,128)(2,1)S(1)}, u32[]{:S(2)}, u32[]{:S(2)}) collective-permute-start(bf16[128,512]{1,0:T(8,128)(2,1)S(1)} %get-tuple-element.24), channel_id=1, source_target_pairs={{0,1},{1,0},{2,3},{3,2},{4,5},{5,4},{6,7},{7,6},{8,9},{9,8},{10,11... | collective-permute-start | bytes 393224 | tf_op jit(solution)/shard_map/ppermute | solution.py:252
  31.4 1.5 %collective-permute-start.7 = (bf16[96,512]{1,0:T(8,128)(2,1)S(1)}, bf16[96,512]{1,0:T(8,128)(2,1)S(1)}, u32[]{:S(2)}, u32[]{:S(2)}) collective-permute-start(bf16[96,512]{1,0:T(8,128)(2,1)S(1)} %get-tuple-element.28), channel_id=1, source_target_pairs={{0,1},{1,0},{2,3},{3,2},{4,5},{5,4},{6,7},{7,6},{8,9},{9,8},{10,11... | collective-permute-start | bytes 294920 | tf_op jit(solution)/shard_map/ppermute | solution.py:252
  32.9 8.7 %collective-permute-start.8 = (bf16[224,512]{1,0:T(8,128)(2,1)S(1)}, bf16[224,512]{1,0:T(8,128)(2,1)S(1)}, u32[]{:S(2)}, u32[]{:S(2)}) collective-permute-start(bf16[224,512]{1,0:T(8,128)(2,1)S(1)} %shard_map.78.refs_0_), channel_id=1, source_target_pairs={{0,2},{1,3},{2,0},{3,1},{4,6},{5,7},{6,4},{7,5},{8,10},{9,11},{10,... | collective-permute-start | bytes 688136 | tf_op jit(solution)/shard_map/ppermute | solution.py:252
  34.8 1.3 %collective-permute-start.10 = (bf16[32,512]{1,0:T(8,128)(2,1)S(1)}, bf16[32,512]{1,0:T(8,128)(2,1)S(1)}, u32[]{:S(2)}, u32[]{:S(2)}) collective-permute-start(bf16[32,512]{1,0:T(8,128)(2,1)S(1)} %get-tuple-element.30), channel_id=1, source_target_pairs={{0,1},{1,0},{2,3},{3,2},{4,5},{5,4},{6,7},{7,6},{8,9},{9,8},{10,11... | collective-permute-start | bytes 98312 | tf_op jit(solution)/shard_map/ppermute | solution.py:252
  36.1 5.5 %collective-permute-start.11 = (bf16[32,512]{1,0:T(8,128)(2,1)S(1)}, bf16[32,512]{1,0:T(8,128)(2,1)S(1)}, u32[]{:S(2)}, u32[]{:S(2)}) collective-permute-start(bf16[32,512]{1,0:T(8,128)(2,1)S(1)} %shard_map.81.refs_0_), channel_id=1, source_target_pairs={{0,2},{1,3},{2,0},{3,1},{4,6},{5,7},{6,4},{7,5},{8,10},{9,11},{10,... | collective-permute-start | bytes 98312 | tf_op jit(solution)/shard_map/ppermute | solution.py:252
  41.9 6.0 %collective-permute-start.12 = (bf16[32,512]{1,0:T(8,128)(2,1)S(1)}, bf16[32,512]{1,0:T(8,128)(2,1)S(1)}, u32[]{:S(2)}, u32[]{:S(2)}) collective-permute-start(bf16[32,512]{1,0:T(8,128)(2,1)S(1)} %get-tuple-element.32), channel_id=1, source_target_pairs={{0,12},{4,8},{8,4},{12,0},{1,13},{5,9},{9,5},{13,1},{2,14},{6,10},... | collective-permute-start | bytes 98312 | tf_op jit(solution)/shard_map/ppermute | solution.py:252
  43.5 5.2 %collective-permute-start.13 = (bf16[32,512]{1,0:T(8,128)(2,1)S(1)}, bf16[32,512]{1,0:T(8,128)(2,1)S(1)}, u32[]{:S(2)}, u32[]{:S(2)}) collective-permute-start(bf16[32,512]{1,0:T(8,128)(2,1)S(1)} %get-tuple-element.33), channel_id=1, source_target_pairs={{0,8},{4,12},{8,0},{12,4},{1,9},{5,13},{9,1},{13,5},{2,10},{6,14},... | collective-permute-start | bytes 98312 | tf_op jit(solution)/shard_map/ppermute | solution.py:252
  44.7 4.2 %collective-permute-start.14 = (bf16[32,512]{1,0:T(8,128)(2,1)S(1)}, bf16[32,512]{1,0:T(8,128)(2,1)S(1)}, u32[]{:S(2)}, u32[]{:S(2)}) collective-permute-start(bf16[32,512]{1,0:T(8,128)(2,1)S(1)} %get-tuple-element.34), channel_id=1, source_target_pairs={{0,4},{4,0},{8,12},{12,8},{1,5},{5,1},{9,13},{13,9},{2,6},{6,2},{1... | collective-permute-start | bytes 98312 | tf_op jit(solution)/shard_map/ppermute | solution.py:252

commit v9 on v8

--- a/solution.py
+++ b/solution.py
@@ -57,12 +57,14 @@
     )(key_rows, value_rows, ends)
 
 
-def attend_kernel(blocks, q_ref, halo_ref, k_ref, v_ref, end_ref, st_ref, targets_ref, *refs):
+def attend_kernel(blocks, q_ref, halo_ref, k_ref, v_ref, end_ref, st_ref, own_ref, near_ref, *refs):
     whole_ref, *out_refs = refs
-    count = targets_ref.shape[1]
-    targets = jnp.broadcast_to(targets_ref[...].astype(jnp.float32), (8, count)).astype(jnp.bfloat16)
-    whole_ref[pl.ds(q_ref.shape[0], 8), :] = jnp.zeros((8, q_ref.shape[1]), jnp.bfloat16)
-    whole_ref[pl.ds(q_ref.shape[0], 8), pl.ds(0, count)] = targets
+    targets = jnp.concatenate([own_ref[...], near_ref[...]], axis=1)
+    count = targets.shape[1]
+    targets = jnp.broadcast_to(targets.astype(jnp.float32), (8, count)).astype(jnp.bfloat16)
+    for ref, first in ((whole_ref, q_ref.shape[0]), (out_refs[0], q_ref.shape[0] // blocks)):
+        ref[pl.ds(first, 8), :] = jnp.zeros((8, q_ref.shape[1]), jnp.bfloat16)
+        ref[pl.ds(first, 8), pl.ds(0, count)] = targets
     rows = q_ref.shape[0]
     width = k_ref.shape[1]
     kv_here = width // HEAD_DIM
@@ -118,20 +120,17 @@
                     )
 
 
-def attend(blocks, queries, halo, keys, values, end, start, targets):
+def attend(blocks, queries, halo, keys, values, end, start, own, near):
     rows, features = queries.shape
-    out = jax.ShapeDtypeStruct((rows // blocks, features), jnp.bfloat16)
+    sizes = (rows + 8, rows // blocks + 8) + (rows // blocks,) * (blocks - 1)
     return pl.pallas_call(
         functools.partial(attend_kernel, blocks),
-        out_shape=(
-            jax.ShapeDtypeStruct((rows + 8, features), jnp.bfloat16),
-        )
-        + (out,) * blocks,
-        in_specs=vmem(7),
+        out_shape=tuple(jax.ShapeDtypeStruct((size, features), jnp.bfloat16) for size in sizes),
+        in_specs=vmem(8),
         out_specs=tuple(vmem(1 + blocks)),
         compiler_params=params(),
-        cost_estimate=cost(8 * rows * rows * features, 6 * queries.size),
-    )(queries, halo, keys, values, end, start, targets)
+        cost_estimate=cost(1 * 10**8, 0),
+    )(queries, halo, keys, values, end, start, own, near)
 
 
 def project_kernel(block_rows, *refs):
@@ -177,37 +176,71 @@
     )(*terms)
 
 
-def pick_kernel(blocks, half, even_ref, whole_ref, *refs):
+def inner():
+    c = lax.axis_index("ctx")
+    return (c == 1) | (c == 2)
+
+
+def tail_targets(ref, count):
+    tail = ref[pl.ds(ref.shape[0] - 8, 8), pl.ds(0, HEAD_DIM)].astype(jnp.float32)
+    return tail[0:1, 0:count].astype(jnp.int32)
+
+
+def pick_kernel(blocks, half, own_ref, near_ref, one_ref, two_ref, *refs):
     sums, outs = refs[:-4], refs[-4:]
     x = lax.axis_index("tp") // 2
     c = lax.axis_index("ctx")
-    order = (0, 1, 4, 5, 2, 6, 3, 7)
     pieces = [r[pl.ds(n, half), :] for r in sums for n in range(0, r.shape[0], half)]
-    tail = whole_ref[pl.ds(whole_ref.shape[0] - 8, 8), pl.ds(0, HEAD_DIM)].astype(jnp.float32)
-    odd = tail[0:1, 0 : 2 * blocks].astype(jnp.int32)
-    targets = jnp.concatenate([even_ref[...], odd], axis=1)
+    far = jnp.where(
+        inner(), tail_targets(two_ref, 2 * blocks), tail_targets(one_ref, 2 * blocks)
+    )
+    by_source = (own_ref[...], near_ref[...], far[:, :blocks], far[:, blocks:])
+    by_cycle = (
+        by_source[0],
+        jnp.where(inner(), by_source[1], by_source[2]),
+        jnp.where(inner(), by_source[2], by_source[1]),
+        by_source[3],
+    )
+    order = ((0, 0), (0, 1), (1, 0), (1, 1), (2, 0), (3, 0), (2, 1), (3, 1))
     for k in range(4):
         wanted = (c ^ k) * blocks + x
         piece = pieces[0]
         for n in range(1, len(pieces)):
-            column_of = order[n]
-            here = jnp.broadcast_to(targets[:, column_of : column_of + 1] == wanted, piece.shape)
+            cycle, p = order[n]
+            here = jnp.broadcast_to(by_cycle[cycle][:, p : p + 1] == wanted, piece.shape)
             piece = jnp.where(here, pieces[n], piece)
         outs[k][...] = piece
 
 
-def pick(blocks, even_targets, whole_1, sums):
+def pick(blocks, own, near, one, two, sums):
     rows, cols = sum(s.shape[0] for s in sums), sums[0].shape[1]
     half = rows // (4 * blocks)
     out = jax.ShapeDtypeStruct((half, cols), jnp.bfloat16)
     return pl.pallas_call(
         functools.partial(pick_kernel, blocks, half),
         out_shape=(out,) * 4,
-        in_specs=vmem(2 + len(sums)),
+        in_specs=vmem(4 + len(sums)),
         out_specs=tuple(vmem(4)),
         compiler_params=params(),
         cost_estimate=cost(4 * rows * cols, 8 * rows * cols),
-    )(even_targets, whole_1, *sums)
+    )(own, near, one, two, *sums)
+
+
+def forward_kernel(first, one_ref, two_ref, out_ref):
+    rows = out_ref.shape[0]
+    out_ref[...] = jnp.where(inner(), two_ref[pl.ds(0, rows), :], one_ref[pl.ds(first, rows), :])
+
+
+def forward(block_rows, first, one, two):
+    out = jax.ShapeDtypeStruct((block_rows, one.shape[1]), one.dtype)
+    return pl.pallas_call(
+        functools.partial(forward_kernel, first),
+        out_shape=out,
+        in_specs=vmem(2),
+        out_specs=pl.BlockSpec(memory_space=pltpu.VMEM),
+        compiler_params=params(),
+        cost_estimate=cost(30 * 10**8, 0),
+    )(one, two)
 
 
 def hold_kernel(near_ref, far_ref, out_ref):
@@ -290,22 +323,24 @@
     end, start = doc_end.reshape(1, rows), doc_start.reshape(1, rows)
     message = pack(key_rows, value_rows, end)
     halo = lax.ppermute(message, "ctx", [(0, 1), (1, 2), (2, 3)])
-    target_2 = flip(after(block_target, message), "ctx", 2)
-    even_targets = jnp.concatenate([block_target, target_2]).reshape(1, 2 * blocks)
-    halo = after(halo, target_2)
+    own_target = block_target.reshape(1, blocks)
+    near_target = flip(after(own_target, message), "ctx", 1)
+    halo = after(halo, near_target)
     whole, first, second = attend(
-        blocks, queries, halo, key_rows, value_rows, end, start, even_targets
-    )
-    whole_1 = flip(whole, "ctx", 1)
-    first_2, second_2 = flip(first, "ctx", 2), flip(second, "ctx", 2)
-    first_3, second_3 = flip(first_2, "ctx", 1), flip(second_2, "ctx", 1)
-    share_a = core_total(*project(block_rows, (whole, whole_1), out_weight))
+        blocks, queries, halo, key_rows, value_rows, end, start, own_target, near_target
+    )
+    cycle_1, cycle_2 = [(0, 1), (1, 3), (3, 2), (2, 0)], [(0, 2), (2, 3), (3, 1), (1, 0)]
+    whole_1 = lax.ppermute(whole, "ctx", cycle_1)
+    first_2, second_2 = (lax.ppermute(a, "ctx", cycle_2) for a in (first, second))
+    first_3 = flip(forward(block_rows, 0, whole_1, first_2), "ctx", 1)
+    second_3 = flip(forward(block_rows, block_rows, whole_1, second_2), "ctx", 1)
+    share_a = core_total(*project(block_rows, (whole, whole_1), out_weight, cost(0, 0)))
     share_ab = stack_core_total(
-        share_a, *project(block_rows, (first_2, first_3, second_2), out_weight, cost(3 * 10**9, 0))
-    )
-    share_c = core_total(*project(block_rows, (second_3,), out_weight, cost(10**10, 0)))
+        share_a, *project(block_rows, (first_2, first_3, second_2), out_weight, cost(30 * 10**8, 0))
+    )
+    share_c = core_total(*project(block_rows, (second_3,), out_weight, cost(30 * 10**8, 0)))
     sums = (chip_total(share_ab), chip_total(share_c))
-    kept, *sent = pick(blocks, even_targets, whole_1, sums)
+    kept, *sent = pick(blocks, own_target, near_target, whole_1, first_2, sums)
     got_3, got_2, got_1 = (flip(sent[k - 1], "ctx", k) for k in (3, 2, 1))
     return join(hold(kept, got_3), got_2, got_1)
 

time: 49.7 us -> 51.1 us (1.028)
  waiting for transfers between devices: 17.8 us -> 21.1 us
  starting transfers between devices: 26.5 us -> 25.1 us
  local copies, waits for them, and re-layouts: 0.66 us -> 0.03 us
    ppermute x0 -> x3, waiting for transfers between devices: none -> 7.02 us  [the longest x2 7.01 us: small_ring(): lax.ppermute(a, 'ctx', cycle_2)]
    ppermute x14 -> x11, starting transfers between devices: 21.5 us -> 14.8 us  [flip(): return lax.ppermute(array, axis, [(i, i ^ bits) for i in range(4)])]
    ppermute x0 -> x3, starting transfers between devices: none -> 5.21 us  [the longest x2 2.96 us: small_ring(): lax.ppermute(a, 'ctx', cycle_2)]
    ppermute x14 -> x11, waiting for transfers between devices: 17.8 us -> 14.1 us  [flip(): return lax.ppermute(array, axis, [(i, i ^ bits) for i in range(4)])]
    unnamed x14, local copies, waits for them, and re-layouts: 0.66 us -> 0.03 us
  transfers between devices with their start and end apart: 15 -> 15, of which waited for: 9 -> 8; matrix products, arithmetic and copies ran while one was open for 0% -> 0% of each run, Pallas kernels for 2% -> 2%
where the time goes in v9:
time: 51.1 us; the launch traced here: 50.9 us
  starting transfers between devices  25.1 us (49%)
  waiting for transfers between devices  21.1 us (41%)
  Pallas kernels  4.42 us (9%)
    ppermute x11, starting transfers between devices, flip(): return lax.ppermute(array, axis, [(i, i ^ bits) for i in range(4)])  14.8 us
    ppermute x11, waiting for transfers between devices, flip(): return lax.ppermute(array, axis, [(i, i ^ bits) for i in range(4)])  14.1 us
    ppermute x2, waiting for transfers between devices, small_ring(): lax.ppermute(a, 'ctx', cycle_2)  7.01 us
    ppermute x1, starting transfers between devices, small_ring(): halo = lax.ppermute(message, 'ctx', [(0, 1), (1, 2), (2, 3)])  5.06 us
    ppermute x2, starting transfers between devices, small_ring(): lax.ppermute(a, 'ctx', cycle_2)  2.96 us
    ppermute x1, starting transfers between devices, small_ring(): whole_1 = lax.ppermute(whole, 'ctx', cycle_1)  2.25 us
    pallas_call x1, Pallas kernels, pack(): pl.pallas_call(pack_kernel, out_shape=jax.ShapeDtypeStruct((rows + 16, 2...  1.59 us
    pallas_call x3, Pallas kernels, project(): pl.pallas_call(functools.partial(project_kernel, block_rows), out_shape=(...  1.1 us
  transfers between devices with their start and end apart: 15, of which 8 were waited for; matrix products, arithmetic and copies ran while one was open for 0% of the time, Pallas kernels for 2%

profile of v9, /device:TPU:0, one launch (start us, length us, event | category | flops | bytes accessed | tf_op | source)
XLA Modules:
  0.0 50.9 jit_solution(15965193033545498206)
XLA Ops:
  0.0 1.6 %shard_map.73 = bf16[144,512]{1,0:T(8,128)(2,1)} custom-call(bf16[128,256]{1,0:T(8,128)(2,1)} %k_ref.3, bf16[128,256]{1,0:T(8,128)(2,1)} %v_ref.3, s32[1,128]{1,0:T(1,128)} %bitcast.6), custom_call_target="tpu_custom_call" | custom-call | flops 1000000000 | bytes 262144 | tf_op jit(solution)/shard_map/pallas_call | solution.py:51
  1.6 5.1 %collective-permute-start.1 = (bf16[144,512]{1,0:T(8,128)(2,1)}, bf16[144,512]{1,0:T(8,128)(2,1)S(1)}, u32[]{:S(2)}, u32[]{:S(2)}) collective-permute-start(bf16[144,512]{1,0:T(8,128)(2,1)} %shard_map.73), channel_id=1, source_target_pairs={{0,4},{4,8},{8,12},{1,5},{5,9},{9,13},{2,6},{6,10},{10,14},{3,7},{... | collective-permute-start | bytes 442376 | tf_op jit(solution)/shard_map/ppermute | solution.py:325
  6.7 1.6 %collective-permute-start = (s32[1,2]{1,0:T(1,128)S(1)}, s32[1,2]{1,0:T(1,128)S(1)}, u32[]{:S(2)}, u32[]{:S(2)}) collective-permute-start(s32[1,2]{1,0:T(1,128)S(1)} %bitcast.3), channel_id=1, source_target_pairs={{0,4},{4,0},{8,12},{12,8},{1,5},{5,1},{9,13},{13,9},{2,6},{6,2},{1... | collective-permute-start | bytes 32 | tf_op jit(solution)/shard_map/ppermute | solution.py:285
  8.3 2.0 %collective-permute-done.near_ref = s32[1,2]{1,0:T(1,128)S(1)} collective-permute-done((s32[1,2]{1,0:T(1,128)S(1)}, s32[1,2]{1,0:T(1,128)S(1)}, u32[]{:S(2)}, u32[]{:S(2)}) %collective-permute-start) | collective-permute-done | bytes 40 | tf_op jit(solution)/shard_map/ppermute | solution.py:285
  10.4 0.7 %shard_map.74 = (bf16[136,1024]{1,0:T(8,128)(2,1)S(1)}, bf16[72,1024]{1,0:T(8,128)(2,1)S(1)}, bf16[64,1024]{1,0:T(8,128)(2,1)S(1)}) custom-call(bf16[128,1024]{1,0:T(8,128)(2,1)S(1)} %copy-done.1, bf16[144,512]{1,0:T(8,128)(2,1)S(1)} %collective-permute-done.1.halo_ref, bf16[128,256]{1,0:T(8,128)(2,1)S(1)} %copy-done.2, bf16[128,256]{1,0:T(8,128)(2,1)S(1)} %copy-done.3, ...), custom_call_target="tpu_custom_call" | custom-call | flops 100000000 | tf_op jit(solution)/shard_map/pallas_call | solution.py:126
  11.1 2.3 %collective-permute-start.2 = (bf16[136,1024]{1,0:T(8,128)(2,1)S(1)}, bf16[136,1024]{1,0:T(8,128)(2,1)S(1)}, u32[]{:S(2)}, u32[]{:S(2)}) collective-permute-start(bf16[136,1024]{1,0:T(8,128)(2,1)S(1)} %get-tuple-element.22.refs_0_), channel_id=1, source_target_pairs={{0,4},{4,12},{12,8},{8,0},{1,5},{5,13},{13,9},{9,1},{2,6},{6,14},{... | collective-permute-start | bytes 835592 | tf_op jit(solution)/shard_map/ppermute | solution.py:333
  13.3 1.0 %collective-permute-start.3 = (bf16[72,1024]{1,0:T(8,128)(2,1)S(1)}, bf16[72,1024]{1,0:T(8,128)(2,1)S(1)}, u32[]{:S(2)}, u32[]{:S(2)}) collective-permute-start(bf16[72,1024]{1,0:T(8,128)(2,1)S(1)} %get-tuple-element.23), channel_id=1, source_target_pairs={{0,8},{8,12},{12,4},{4,0},{1,9},{9,13},{13,5},{5,1},{2,10},{10,14}... | collective-permute-start | bytes 442376 | tf_op jit(solution)/shard_map/ppermute | solution.py:334
  14.3 1.9 %collective-permute-start.6 = (bf16[64,1024]{1,0:T(8,128)(2,1)S(1)}, bf16[64,1024]{1,0:T(8,128)(2,1)S(1)}, u32[]{:S(2)}, u32[]{:S(2)}) collective-permute-start(bf16[64,1024]{1,0:T(8,128)(2,1)S(1)} %get-tuple-element.26), channel_id=1, source_target_pairs={{0,8},{8,12},{12,4},{4,0},{1,9},{9,13},{13,5},{5,1},{2,10},{10,14}... | collective-permute-start | bytes 393224 | tf_op jit(solution)/shard_map/ppermute | solution.py:334
  16.3 7.0 %collective-permute-done.3.two_ref.refs_0_ = bf16[72,1024]{1,0:T(8,128)(2,1)S(1)} collective-permute-done((bf16[72,1024]{1,0:T(8,128)(2,1)S(1)}, bf16[72,1024]{1,0:T(8,128)(2,1)S(1)}, u32[]{:S(2)}, u32[]{:S(2)}) %collective-permute-start.3) | collective-permute-done | bytes 147488 | tf_op jit(solution)/shard_map/ppermute | solution.py:334
  23.3 3.8 %collective-permute-start.5 = (bf16[64,1024]{1,0:T(8,128)(2,1)S(1)}, bf16[64,1024]{1,0:T(8,128)(2,1)S(1)}, u32[]{:S(2)}, u32[]{:S(2)}) collective-permute-start(bf16[64,1024]{1,0:T(8,128)(2,1)S(1)} %shard_map.77), channel_id=1, source_target_pairs={{0,4},{4,0},{8,12},{12,8},{1,5},{5,1},{9,13},{13,9},{2,6},{6,2},{1... | collective-permute-start | bytes 393224 | tf_op jit(solution)/shard_map/ppermute | solution.py:285
  27.2 2.6 %collective-permute-start.9 = (bf16[64,1024]{1,0:T(8,128)(2,1)S(1)}, bf16[64,1024]{1,0:T(8,128)(2,1)S(1)}, u32[]{:S(2)}, u32[]{:S(2)}) collective-permute-start(bf16[64,1024]{1,0:T(8,128)(2,1)S(1)} %shard_map.81), channel_id=1, source_target_pairs={{0,4},{4,0},{8,12},{12,8},{1,5},{5,1},{9,13},{13,9},{2,6},{6,2},{1... | collective-permute-start | bytes 393224 | tf_op jit(solution)/shard_map/ppermute | solution.py:285
  29.8 0.4 shard_map.75
  30.3 1.1 %collective-permute-done.5.refs_1_ = bf16[64,1024]{1,0:T(8,128)(2,1)S(1)} collective-permute-done((bf16[64,1024]{1,0:T(8,128)(2,1)S(1)}, bf16[64,1024]{1,0:T(8,128)(2,1)S(1)}, u32[]{:S(2)}, u32[]{:S(2)}) %collective-permute-start.5) | collective-permute-done | bytes 131104 | tf_op jit(solution)/shard_map/ppermute | solution.py:285
  31.4 0.4 shard_map.78
  31.9 1.2 %collective-permute-done.7.got_ref = bf16[96,512]{1,0:T(8,128)(2,1)S(1)} collective-permute-done((bf16[96,512]{1,0:T(8,128)(2,1)S(1)}, bf16[96,512]{1,0:T(8,128)(2,1)S(1)}, u32[]{:S(2)}, u32[]{:S(2)}) %collective-permute-start.7) | collective-permute-done | bytes 98336 | tf_op jit(solution)/shard_map/ppermute | solution.py:285
  33.2 1.6 %collective-permute-start.8 = (bf16[224,512]{1,0:T(8,128)(2,1)S(1)}, bf16[224,512]{1,0:T(8,128)(2,1)S(1)}, u32[]{:S(2)}, u32[]{:S(2)}) collective-permute-start(bf16[224,512]{1,0:T(8,128)(2,1)S(1)} %shard_map.79.refs_0_), channel_id=1, source_target_pairs={{0,2},{1,3},{2,0},{3,1},{4,6},{5,7},{6,4},{7,5},{8,10},{9,11},{10,... | collective-permute-start | bytes 688136 | tf_op jit(solution)/shard_map/ppermute | solution.py:285
  35.1 1.2 %collective-permute-done.10.refs_1_ = bf16[32,512]{1,0:T(8,128)(2,1)S(1)} collective-permute-done((bf16[32,512]{1,0:T(8,128)(2,1)S(1)}, bf16[32,512]{1,0:T(8,128)(2,1)S(1)}, u32[]{:S(2)}, u32[]{:S(2)}) %collective-permute-start.10) | collective-permute-done | bytes 32800 | tf_op jit(solution)/shard_map/ppermute | solution.py:285
  36.4 0.6 %collective-permute-start.11 = (bf16[32,512]{1,0:T(8,128)(2,1)S(1)}, bf16[32,512]{1,0:T(8,128)(2,1)S(1)}, u32[]{:S(2)}, u32[]{:S(2)}) collective-permute-start(bf16[32,512]{1,0:T(8,128)(2,1)S(1)} %shard_map.83.refs_0_), channel_id=1, source_target_pairs={{0,2},{1,3},{2,0},{3,1},{4,6},{5,7},{6,4},{7,5},{8,10},{9,11},{10,... | collective-permute-start | bytes 98312 | tf_op jit(solution)/shard_map/ppermute | solution.py:285
  37.0 4.7 %collective-permute-done.11.refs_1_ = bf16[32,512]{1,0:T(8,128)(2,1)S(1)} collective-permute-done((bf16[32,512]{1,0:T(8,128)(2,1)S(1)}, bf16[32,512]{1,0:T(8,128)(2,1)S(1)}, u32[]{:S(2)}, u32[]{:S(2)}) %collective-permute-start.11) | collective-permute-done | bytes 32800 | tf_op jit(solution)/shard_map/ppermute | solution.py:285
  41.9 3.5 %collective-permute-start.12 = (bf16[32,512]{1,0:T(8,128)(2,1)S(1)}, bf16[32,512]{1,0:T(8,128)(2,1)S(1)}, u32[]{:S(2)}, u32[]{:S(2)}) collective-permute-start(bf16[32,512]{1,0:T(8,128)(2,1)S(1)} %get-tuple-element.32), channel_id=1, source_target_pairs={{0,12},{4,8},{8,4},{12,0},{1,13},{5,9},{9,5},{13,1},{2,14},{6,10},... | collective-permute-start | bytes 98312 | tf_op jit(solution)/shard_map/ppermute | solution.py:285
  45.4 0.9 %collective-permute-start.14 = (bf16[32,512]{1,0:T(8,128)(2,1)S(1)}, bf16[32,512]{1,0:T(8,128)(2,1)S(1)}, u32[]{:S(2)}, u32[]{:S(2)}) collective-permute-start(bf16[32,512]{1,0:T(8,128)(2,1)S(1)} %get-tuple-element.34), channel_id=1, source_target_pairs={{0,4},{4,0},{8,12},{12,8},{1,5},{5,1},{9,13},{13,9},{2,6},{6,2},{1... | collective-permute-start | bytes 98312 | tf_op jit(solution)/shard_map/ppermute | solution.py:285
  46.3 1.4 %collective-permute-done.12.far_ref = bf16[32,512]{1,0:T(8,128)(2,1)S(1)} collective-permute-done((bf16[32,512]{1,0:T(8,128)(2,1)S(1)}, bf16[32,512]{1,0:T(8,128)(2,1)S(1)}, u32[]{:S(2)}, u32[]{:S(2)}) %collective-permute-start.12) | collective-permute-done | bytes 32800 | tf_op jit(solution)/shard_map/ppermute | solution.py:285
  47.8 2.5 %collective-permute-done.13.two_ref = bf16[32,512]{1,0:T(8,128)(2,1)S(1)} collective-permute-done((bf16[32,512]{1,0:T(8,128)(2,1)S(1)}, bf16[32,512]{1,0:T(8,128)(2,1)S(1)}, u32[]{:S(2)}, u32[]{:S(2)}) %collective-permute-start.13) | collective-permute-done | bytes 32800 | tf_op jit(solution)/shard_map/ppermute | solution.py:285
  50.2 0.7 %shard_map.87 = bf16[32,2048]{1,0:T(8,128)(2,1)} custom-call(bf16[32,1024]{1,0:T(8,128)(2,1)S(1)} %shard_map.86.held_ref, bf16[32,512]{1,0:T(8,128)(2,1)S(1)} %collective-permute-done.13.two_ref, bf16[32,512]{1,0:T(8,128)(2,1)S(1)} %collective-permute-done.14.one_ref), custom_call_target="tpu_custom_call" | custom-call | bytes 262144 | tf_op jit(solution)/shard_map/pallas_call | solution.py:274
  (35 shorter events, 0.9 us)
Async XLA Ops:
  0.0 10.3 %copy-start.1 = (bf16[128,1024]{1,0:T(8,128)(2,1)S(1)}, bf16[128,1024]{1,0:T(8,128)(2,1)}, u32[]{:S(2)}) copy-start(bf16[128,1024]{1,0:T(8,128)(2,1)} %q_ref.1) | copy-start | bytes 786436
  0.0 10.3 %copy-start.2 = (bf16[128,256]{1,0:T(8,128)(2,1)S(1)}, bf16[128,256]{1,0:T(8,128)(2,1)}, u32[]{:S(2)}) copy-start(bf16[128,256]{1,0:T(8,128)(2,1)} %k_ref.3) | copy-start | bytes 196612
  0.0 10.3 %copy-start.3 = (bf16[128,256]{1,0:T(8,128)(2,1)S(1)}, bf16[128,256]{1,0:T(8,128)(2,1)}, u32[]{:S(2)}) copy-start(bf16[128,256]{1,0:T(8,128)(2,1)} %v_ref.3) | copy-start | bytes 196612
  1.6 5.1 %copy-start.4 = (s32[2]{0:T(128)S(1)}, s32[2]{0:T(128)}, u32[]{:S(2)}) copy-start(s32[2]{0:T(128)} %param.12) | copy-start | bytes 28
  1.6 8.7 %collective-permute-start.1 = (bf16[144,512]{1,0:T(8,128)(2,1)}, bf16[144,512]{1,0:T(8,128)(2,1)S(1)}, u32[]{:S(2)}, u32[]{:S(2)}) collective-permute-start(bf16[144,512]{1,0:T(8,128)(2,1)} %shard_map.73), channel_id=1, source_target_pairs={{0,4},{4,8},{8,12},{1,5},{5,9},{9,13},{2,6},{6,10},{10,14},{3,7},{... | collective-permute-start | bytes 442376 | tf_op jit(solution)/shard_map/ppermute | solution.py:325
  6.7 3.7 %copy-start.5 = (s32[128]{0:T(128)S(1)}, s32[128]{0:T(128)}, u32[]{:S(2)}) copy-start(s32[128]{0:T(128)} %param.11) | copy-start | bytes 1540
  6.7 3.7 %copy-start.6 = (s32[128]{0:T(128)S(1)}, s32[128]{0:T(128)}, u32[]{:S(2)}) copy-start(s32[128]{0:T(128)} %param.10) | copy-start | bytes 1540
  6.7 3.6 %collective-permute-start = (s32[1,2]{1,0:T(1,128)S(1)}, s32[1,2]{1,0:T(1,128)S(1)}, u32[]{:S(2)}, u32[]{:S(2)}) collective-permute-start(s32[1,2]{1,0:T(1,128)S(1)} %bitcast.3), channel_id=1, source_target_pairs={{0,4},{4,0},{8,12},{12,8},{1,5},{5,1},{9,13},{13,9},{2,6},{6,2},{1... | collective-permute-start | bytes 32 | tf_op jit(solution)/shard_map/ppermute | solution.py:285
  11.1 12.2 %collective-permute-start.2 = (bf16[136,1024]{1,0:T(8,128)(2,1)S(1)}, bf16[136,1024]{1,0:T(8,128)(2,1)S(1)}, u32[]{:S(2)}, u32[]{:S(2)}) collective-permute-start(bf16[136,1024]{1,0:T(8,128)(2,1)S(1)} %get-tuple-element.22.refs_0_), channel_id=1, source_target_pairs={{0,4},{4,12},{12,8},{8,0},{1,5},{5,13},{13,9},{9,1},{2,6},{6,14},{... | collective-permute-start | bytes 835592 | tf_op jit(solution)/shard_map/ppermute | solution.py:333
  13.3 10.0 %collective-permute-start.3 = (bf16[72,1024]{1,0:T(8,128)(2,1)S(1)}, bf16[72,1024]{1,0:T(8,128)(2,1)S(1)}, u32[]{:S(2)}, u32[]{:S(2)}) collective-permute-start(bf16[72,1024]{1,0:T(8,128)(2,1)S(1)} %get-tuple-element.23), channel_id=1, source_target_pairs={{0,8},{8,12},{12,4},{4,0},{1,9},{9,13},{13,5},{5,1},{2,10},{10,14}... | collective-permute-start | bytes 442376 | tf_op jit(solution)/shard_map/ppermute | solution.py:334
  14.3 12.8 %collective-permute-start.6 = (bf16[64,1024]{1,0:T(8,128)(2,1)S(1)}, bf16[64,1024]{1,0:T(8,128)(2,1)S(1)}, u32[]{:S(2)}, u32[]{:S(2)}) collective-permute-start(bf16[64,1024]{1,0:T(8,128)(2,1)S(1)} %get-tuple-element.26), channel_id=1, source_target_pairs={{0,8},{8,12},{12,4},{4,0},{1,9},{9,13},{13,5},{5,1},{2,10},{10,14}... | collective-permute-start | bytes 393224 | tf_op jit(solution)/shard_map/ppermute | solution.py:334
  23.3 6.4 %copy-start = (bf16[1024,512]{1,0:T(8,128)(2,1)S(1)}, bf16[1024,512]{1,0:T(8,128)(2,1)}, u32[]{:S(2)}) copy-start(bf16[1024,512]{1,0:T(8,128)(2,1)} %refs_1_.1) | copy-start | bytes 3145732
  23.3 8.1 %collective-permute-start.5 = (bf16[64,1024]{1,0:T(8,128)(2,1)S(1)}, bf16[64,1024]{1,0:T(8,128)(2,1)S(1)}, u32[]{:S(2)}, u32[]{:S(2)}) collective-permute-start(bf16[64,1024]{1,0:T(8,128)(2,1)S(1)} %shard_map.77), channel_id=1, source_target_pairs={{0,4},{4,0},{8,12},{12,8},{1,5},{5,1},{9,13},{13,9},{2,6},{6,2},{1... | collective-permute-start | bytes 393224 | tf_op jit(solution)/shard_map/ppermute | solution.py:285
  27.2 7.6 %collective-permute-start.9 = (bf16[64,1024]{1,0:T(8,128)(2,1)S(1)}, bf16[64,1024]{1,0:T(8,128)(2,1)S(1)}, u32[]{:S(2)}, u32[]{:S(2)}) collective-permute-start(bf16[64,1024]{1,0:T(8,128)(2,1)S(1)} %shard_map.81), channel_id=1, source_target_pairs={{0,4},{4,0},{8,12},{12,8},{1,5},{5,1},{9,13},{13,9},{2,6},{6,2},{1... | collective-permute-start | bytes 393224 | tf_op jit(solution)/shard_map/ppermute | solution.py:285
  30.2 1.7 %collective-permute-start.4 = (bf16[128,512]{1,0:T(8,128)(2,1)S(1)}, bf16[128,512]{1,0:T(8,128)(2,1)S(1)}, u32[]{:S(2)}, u32[]{:S(2)}) collective-permute-start(bf16[128,512]{1,0:T(8,128)(2,1)S(1)} %get-tuple-element.25), channel_id=1, source_target_pairs={{0,1},{1,0},{2,3},{3,2},{4,5},{5,4},{6,7},{7,6},{8,9},{9,8},{10,11... | collective-permute-start | bytes 393224 | tf_op jit(solution)/shard_map/ppermute | solution.py:285
  31.8 1.4 %collective-permute-start.7 = (bf16[96,512]{1,0:T(8,128)(2,1)S(1)}, bf16[96,512]{1,0:T(8,128)(2,1)S(1)}, u32[]{:S(2)}, u32[]{:S(2)}) collective-permute-start(bf16[96,512]{1,0:T(8,128)(2,1)S(1)} %get-tuple-element.28), channel_id=1, source_target_pairs={{0,1},{1,0},{2,3},{3,2},{4,5},{5,4},{6,7},{7,6},{8,9},{9,8},{10,11... | collective-permute-start | bytes 294920 | tf_op jit(solution)/shard_map/ppermute | solution.py:285
  33.2 8.4 %collective-permute-start.8 = (bf16[224,512]{1,0:T(8,128)(2,1)S(1)}, bf16[224,512]{1,0:T(8,128)(2,1)S(1)}, u32[]{:S(2)}, u32[]{:S(2)}) collective-permute-start(bf16[224,512]{1,0:T(8,128)(2,1)S(1)} %shard_map.79.refs_0_), channel_id=1, source_target_pairs={{0,2},{1,3},{2,0},{3,1},{4,6},{5,7},{6,4},{7,5},{8,10},{9,11},{10,... | collective-permute-start | bytes 688136 | tf_op jit(solution)/shard_map/ppermute | solution.py:285
  35.1 1.3 %collective-permute-start.10 = (bf16[32,512]{1,0:T(8,128)(2,1)S(1)}, bf16[32,512]{1,0:T(8,128)(2,1)S(1)}, u32[]{:S(2)}, u32[]{:S(2)}) collective-permute-start(bf16[32,512]{1,0:T(8,128)(2,1)S(1)} %get-tuple-element.30), channel_id=1, source_target_pairs={{0,1},{1,0},{2,3},{3,2},{4,5},{5,4},{6,7},{7,6},{8,9},{9,8},{10,11... | collective-permute-start | bytes 98312 | tf_op jit(solution)/shard_map/ppermute | solution.py:285
  36.4 5.3 %collective-permute-start.11 = (bf16[32,512]{1,0:T(8,128)(2,1)S(1)}, bf16[32,512]{1,0:T(8,128)(2,1)S(1)}, u32[]{:S(2)}, u32[]{:S(2)}) collective-permute-start(bf16[32,512]{1,0:T(8,128)(2,1)S(1)} %shard_map.83.refs_0_), channel_id=1, source_target_pairs={{0,2},{1,3},{2,0},{3,1},{4,6},{5,7},{6,4},{7,5},{8,10},{9,11},{10,... | collective-permute-start | bytes 98312 | tf_op jit(solution)/shard_map/ppermute | solution.py:285
  41.9 5.9 %collective-permute-start.12 = (bf16[32,512]{1,0:T(8,128)(2,1)S(1)}, bf16[32,512]{1,0:T(8,128)(2,1)S(1)}, u32[]{:S(2)}, u32[]{:S(2)}) collective-permute-start(bf16[32,512]{1,0:T(8,128)(2,1)S(1)} %get-tuple-element.32), channel_id=1, source_target_pairs={{0,12},{4,8},{8,4},{12,0},{1,13},{5,9},{9,5},{13,1},{2,14},{6,10},... | collective-permute-start | bytes 98312 | tf_op jit(solution)/shard_map/ppermute | solution.py:285
  45.4 4.8 %collective-permute-start.13 = (bf16[32,512]{1,0:T(8,128)(2,1)S(1)}, bf16[32,512]{1,0:T(8,128)(2,1)S(1)}, u32[]{:S(2)}, u32[]{:S(2)}) collective-permute-start(bf16[32,512]{1,0:T(8,128)(2,1)S(1)} %get-tuple-element.33), channel_id=1, source_target_pairs={{0,8},{4,12},{8,0},{12,4},{1,9},{5,13},{9,1},{13,5},{2,10},{6,14},... | collective-permute-start | bytes 98312 | tf_op jit(solution)/shard_map/ppermute | solution.py:285
  45.4 4.8 %collective-permute-start.14 = (bf16[32,512]{1,0:T(8,128)(2,1)S(1)}, bf16[32,512]{1,0:T(8,128)(2,1)S(1)}, u32[]{:S(2)}, u32[]{:S(2)}) collective-permute-start(bf16[32,512]{1,0:T(8,128)(2,1)S(1)} %get-tuple-element.34), channel_id=1, source_target_pairs={{0,4},{4,0},{8,12},{12,8},{1,5},{5,1},{9,13},{13,9},{2,6},{6,2},{1... | collective-permute-start | bytes 98312 | tf_op jit(solution)/shard_map/ppermute | solution.py:285

commit v10 on v9

--- a/solution.py
+++ b/solution.py
@@ -129,7 +129,7 @@
         in_specs=vmem(8),
         out_specs=tuple(vmem(1 + blocks)),
         compiler_params=params(),
-        cost_estimate=cost(1 * 10**8, 0),
+        cost_estimate=cost(10 * 10**8, 0),
     )(queries, halo, keys, values, end, start, own, near)
 
 
@@ -201,7 +201,7 @@
         jnp.where(inner(), by_source[2], by_source[1]),
         by_source[3],
     )
-    order = ((0, 0), (0, 1), (1, 0), (1, 1), (2, 0), (3, 0), (2, 1), (3, 1))
+    order = [(cycle, p) for cycle in range(4) for p in range(blocks)]
     for k in range(4):
         wanted = (c ^ k) * blocks + x
         piece = pieces[0]
@@ -304,7 +304,7 @@
         in_specs=vmem(3),
         out_specs=pl.BlockSpec(memory_space=pltpu.VMEM),
         compiler_params=params(),
-        cost_estimate=cost(mine.size, 8 * mine.size),
+        cost_estimate=cost(1 * 10**8, 0),
     )(done, mine, flip(other, "tp", 1))
 
 
@@ -332,13 +332,13 @@
     cycle_1, cycle_2 = [(0, 1), (1, 3), (3, 2), (2, 0)], [(0, 2), (2, 3), (3, 1), (1, 0)]
     whole_1 = lax.ppermute(whole, "ctx", cycle_1)
     first_2, second_2 = (lax.ppermute(a, "ctx", cycle_2) for a in (first, second))
+    second_3 = flip(second, "ctx", 3)
     first_3 = flip(forward(block_rows, 0, whole_1, first_2), "ctx", 1)
-    second_3 = flip(forward(block_rows, block_rows, whole_1, second_2), "ctx", 1)
     share_a = core_total(*project(block_rows, (whole, whole_1), out_weight, cost(0, 0)))
     share_ab = stack_core_total(
-        share_a, *project(block_rows, (first_2, first_3, second_2), out_weight, cost(30 * 10**8, 0))
-    )
-    share_c = core_total(*project(block_rows, (second_3,), out_weight, cost(30 * 10**8, 0)))
+        share_a, *project(block_rows, (first_2, second_2), out_weight, cost(30 * 10**8, 0))
+    )
+    share_c = core_total(*project(block_rows, (first_3, second_3), out_weight))
     sums = (chip_total(share_ab), chip_total(share_c))
     kept, *sent = pick(blocks, own_target, near_target, whole_1, first_2, sums)
     got_3, got_2, got_1 = (flip(sent[k - 1], "ctx", k) for k in (3, 2, 1))

time: 51.1 us -> 52.4 us (1.025)
  waiting for transfers between devices: 21.1 us -> 24.9 us
  starting transfers between devices: 25.1 us -> 22.8 us
    ppermute x1, waiting for transfers between devices: 0.01 us -> 12 us  [small_ring(): whole_1 = lax.ppermute(whole, 'ctx', cycle_1)]
    ppermute x2, waiting for transfers between devices: 7.01 us -> 0.01 us  [small_ring(): lax.ppermute(a, 'ctx', cycle_2)]
    ppermute x11, starting transfers between devices: 14.8 us -> 12.5 us  [flip(): return lax.ppermute(array, axis, [(i, i ^ bits) for i in range(4)])]
    ppermute x11, waiting for transfers between devices: 14.1 us -> 12.9 us  [flip(): return lax.ppermute(array, axis, [(i, i ^ bits) for i in range(4)])]
where the time goes in v10:
time: 52.4 us; the launch traced here: 52.3 us
  waiting for transfers between devices  24.9 us (48%)
  starting transfers between devices  22.8 us (44%)
  Pallas kernels  4.36 us (8%)
    ppermute x11, waiting for transfers between devices, flip(): return lax.ppermute(array, axis, [(i, i ^ bits) for i in range(4)])  12.9 us
    ppermute x11, starting transfers between devices, flip(): return lax.ppermute(array, axis, [(i, i ^ bits) for i in range(4)])  12.5 us
    ppermute x1, waiting for transfers between devices, small_ring(): whole_1 = lax.ppermute(whole, 'ctx', cycle_1)  12 us
    ppermute x1, starting transfers between devices, small_ring(): halo = lax.ppermute(message, 'ctx', [(0, 1), (1, 2), (2, 3)])  5.06 us
    ppermute x2, starting transfers between devices, small_ring(): lax.ppermute(a, 'ctx', cycle_2)  2.96 us
    ppermute x1, starting transfers between devices, small_ring(): whole_1 = lax.ppermute(whole, 'ctx', cycle_1)  2.25 us
    pallas_call x1, Pallas kernels, pack(): pl.pallas_call(pack_kernel, out_shape=jax.ShapeDtypeStruct((rows + 16, 2...  1.59 us
    pallas_call x3, Pallas kernels, project(): pl.pallas_call(functools.partial(project_kernel, block_rows), out_shape=(...  1.05 us
  transfers between devices with their start and end apart: 15, of which 8 were waited for; matrix products, arithmetic and copies ran while one was open for 0% of the time, Pallas kernels for 2%

profile of v10, /device:TPU:0, one launch (start us, length us, event | category | flops | bytes accessed | tf_op | source)
XLA Modules:
  0.0 52.3 jit_solution(5487948898036746812)
XLA Ops:
  0.0 1.6 %shard_map.73 = bf16[144,512]{1,0:T(8,128)(2,1)} custom-call(bf16[128,256]{1,0:T(8,128)(2,1)} %k_ref.3, bf16[128,256]{1,0:T(8,128)(2,1)} %v_ref.3, s32[1,128]{1,0:T(1,128)} %bitcast.6), custom_call_target="tpu_custom_call" | custom-call | flops 1000000000 | bytes 262144 | tf_op jit(solution)/shard_map/pallas_call | solution.py:51
  1.6 5.1 %collective-permute-start.1 = (bf16[144,512]{1,0:T(8,128)(2,1)}, bf16[144,512]{1,0:T(8,128)(2,1)S(1)}, u32[]{:S(2)}, u32[]{:S(2)}) collective-permute-start(bf16[144,512]{1,0:T(8,128)(2,1)} %shard_map.73), channel_id=1, source_target_pairs={{0,4},{4,8},{8,12},{1,5},{5,9},{9,13},{2,6},{6,10},{10,14},{3,7},{... | collective-permute-start | bytes 442376 | tf_op jit(solution)/shard_map/ppermute | solution.py:325
  6.7 1.6 %collective-permute-start = (s32[1,2]{1,0:T(1,128)S(1)}, s32[1,2]{1,0:T(1,128)S(1)}, u32[]{:S(2)}, u32[]{:S(2)}) collective-permute-start(s32[1,2]{1,0:T(1,128)S(1)} %bitcast.3), channel_id=1, source_target_pairs={{0,4},{4,0},{8,12},{12,8},{1,5},{5,1},{9,13},{13,9},{2,6},{6,2},{1... | collective-permute-start | bytes 32 | tf_op jit(solution)/shard_map/ppermute | solution.py:285
  8.3 2.0 %collective-permute-done.near_ref = s32[1,2]{1,0:T(1,128)S(1)} collective-permute-done((s32[1,2]{1,0:T(1,128)S(1)}, s32[1,2]{1,0:T(1,128)S(1)}, u32[]{:S(2)}, u32[]{:S(2)}) %collective-permute-start) | collective-permute-done | bytes 40 | tf_op jit(solution)/shard_map/ppermute | solution.py:285
  10.4 0.7 %shard_map.74 = (bf16[136,1024]{1,0:T(8,128)(2,1)S(1)}, bf16[72,1024]{1,0:T(8,128)(2,1)S(1)}, bf16[64,1024]{1,0:T(8,128)(2,1)S(1)}) custom-call(bf16[128,1024]{1,0:T(8,128)(2,1)S(1)} %copy-done.2, bf16[144,512]{1,0:T(8,128)(2,1)S(1)} %collective-permute-done.1.halo_ref, bf16[128,256]{1,0:T(8,128)(2,1)S(1)} %copy-done.3, bf16[128,256]{1,0:T(8,128)(2,1)S(1)} %copy-done.4, ...), custom_call_target="tpu_custom_call" | custom-call | flops 1000000000 | tf_op jit(solution)/shard_map/pallas_call | solution.py:126
  11.1 2.3 %collective-permute-start.2 = (bf16[136,1024]{1,0:T(8,128)(2,1)S(1)}, bf16[136,1024]{1,0:T(8,128)(2,1)S(1)}, u32[]{:S(2)}, u32[]{:S(2)}) collective-permute-start(bf16[136,1024]{1,0:T(8,128)(2,1)S(1)} %get-tuple-element.22.refs_0_), channel_id=1, source_target_pairs={{0,4},{4,12},{12,8},{8,0},{1,5},{5,13},{13,9},{9,1},{2,6},{6,14},{... | collective-permute-start | bytes 835592 | tf_op jit(solution)/shard_map/ppermute | solution.py:333
  13.3 1.0 %collective-permute-start.3 = (bf16[72,1024]{1,0:T(8,128)(2,1)S(1)}, bf16[72,1024]{1,0:T(8,128)(2,1)S(1)}, u32[]{:S(2)}, u32[]{:S(2)}) collective-permute-start(bf16[72,1024]{1,0:T(8,128)(2,1)S(1)} %get-tuple-element.23), channel_id=1, source_target_pairs={{0,8},{8,12},{12,4},{4,0},{1,9},{9,13},{13,5},{5,1},{2,10},{10,14}... | collective-permute-start | bytes 442376 | tf_op jit(solution)/shard_map/ppermute | solution.py:334
  14.4 1.9 %collective-permute-start.5 = (bf16[64,1024]{1,0:T(8,128)(2,1)S(1)}, bf16[64,1024]{1,0:T(8,128)(2,1)S(1)}, u32[]{:S(2)}, u32[]{:S(2)}) collective-permute-start(bf16[64,1024]{1,0:T(8,128)(2,1)S(1)} %get-tuple-element.26), channel_id=1, source_target_pairs={{0,8},{8,12},{12,4},{4,0},{1,9},{9,13},{13,5},{5,1},{2,10},{10,14}... | collective-permute-start | bytes 393224 | tf_op jit(solution)/shard_map/ppermute | solution.py:334
  16.3 2.0 %collective-permute-start.9 = (bf16[64,1024]{1,0:T(8,128)(2,1)S(1)}, bf16[64,1024]{1,0:T(8,128)(2,1)S(1)}, u32[]{:S(2)}, u32[]{:S(2)}) collective-permute-start(bf16[64,1024]{1,0:T(8,128)(2,1)S(1)} %get-tuple-element.26), channel_id=1, source_target_pairs={{0,12},{4,8},{8,4},{12,0},{1,13},{5,9},{9,5},{13,1},{2,14},{6,10},... | collective-permute-start | bytes 393224 | tf_op jit(solution)/shard_map/ppermute | solution.py:285
  18.3 12.0 %collective-permute-done.2.refs_1_.one_ref = bf16[136,1024]{1,0:T(8,128)(2,1)S(1)} collective-permute-done((bf16[136,1024]{1,0:T(8,128)(2,1)S(1)}, bf16[136,1024]{1,0:T(8,128)(2,1)S(1)}, u32[]{:S(2)}, u32[]{:S(2)}) %collective-permute-start.2) | collective-permute-done | bytes 278560 | tf_op jit(solution)/shard_map/ppermute | solution.py:333
  30.3 0.4 shard_map.75
  30.9 0.9 %collective-permute-start.8 = (bf16[64,1024]{1,0:T(8,128)(2,1)S(1)}, bf16[64,1024]{1,0:T(8,128)(2,1)S(1)}, u32[]{:S(2)}, u32[]{:S(2)}) collective-permute-start(bf16[64,1024]{1,0:T(8,128)(2,1)S(1)} %shard_map.80), channel_id=1, source_target_pairs={{0,4},{4,0},{8,12},{12,8},{1,5},{5,1},{9,13},{13,9},{2,6},{6,2},{1... | collective-permute-start | bytes 393224 | tf_op jit(solution)/shard_map/ppermute | solution.py:285
  31.8 0.3 shard_map.77
  32.4 1.0 %collective-permute-done.6.got_ref = bf16[64,512]{1,0:T(8,128)(2,1)S(1)} collective-permute-done((bf16[64,512]{1,0:T(8,128)(2,1)S(1)}, bf16[64,512]{1,0:T(8,128)(2,1)S(1)}, u32[]{:S(2)}, u32[]{:S(2)}) %collective-permute-start.6) | collective-permute-done | bytes 65568 | tf_op jit(solution)/shard_map/ppermute | solution.py:285
  33.4 1.6 %collective-permute-start.7 = (bf16[192,512]{1,0:T(8,128)(2,1)S(1)}, bf16[192,512]{1,0:T(8,128)(2,1)S(1)}, u32[]{:S(2)}, u32[]{:S(2)}) collective-permute-start(bf16[192,512]{1,0:T(8,128)(2,1)S(1)} %shard_map.78.refs_0_), channel_id=1, source_target_pairs={{0,2},{1,3},{2,0},{3,1},{4,6},{5,7},{6,4},{7,5},{8,10},{9,11},{10,... | collective-permute-start | bytes 589832 | tf_op jit(solution)/shard_map/ppermute | solution.py:285
  35.0 1.8 %collective-permute-done.8.refs_0_ = bf16[64,1024]{1,0:T(8,128)(2,1)S(1)} collective-permute-done((bf16[64,1024]{1,0:T(8,128)(2,1)S(1)}, bf16[64,1024]{1,0:T(8,128)(2,1)S(1)}, u32[]{:S(2)}, u32[]{:S(2)}) %collective-permute-start.8) | collective-permute-done | bytes 131104 | tf_op jit(solution)/shard_map/ppermute | solution.py:285
  37.2 1.2 %collective-permute-done.10.refs_1_ = bf16[64,512]{1,0:T(8,128)(2,1)S(1)} collective-permute-done((bf16[64,512]{1,0:T(8,128)(2,1)S(1)}, bf16[64,512]{1,0:T(8,128)(2,1)S(1)}, u32[]{:S(2)}, u32[]{:S(2)}) %collective-permute-start.10) | collective-permute-done | bytes 65568 | tf_op jit(solution)/shard_map/ppermute | solution.py:285
  38.5 1.6 %collective-permute-start.11 = (bf16[64,512]{1,0:T(8,128)(2,1)S(1)}, bf16[64,512]{1,0:T(8,128)(2,1)S(1)}, u32[]{:S(2)}, u32[]{:S(2)}) collective-permute-start(bf16[64,512]{1,0:T(8,128)(2,1)S(1)} %shard_map.82.refs_0_), channel_id=1, source_target_pairs={{0,2},{1,3},{2,0},{3,1},{4,6},{5,7},{6,4},{7,5},{8,10},{9,11},{10,... | collective-permute-start | bytes 196616 | tf_op jit(solution)/shard_map/ppermute | solution.py:285
  40.0 2.8 %collective-permute-done.11.refs_1_ = bf16[64,512]{1,0:T(8,128)(2,1)S(1)} collective-permute-done((bf16[64,512]{1,0:T(8,128)(2,1)S(1)}, bf16[64,512]{1,0:T(8,128)(2,1)S(1)}, u32[]{:S(2)}, u32[]{:S(2)}) %collective-permute-start.11) | collective-permute-done | bytes 65568 | tf_op jit(solution)/shard_map/ppermute | solution.py:285
  43.0 3.7 %collective-permute-start.12 = (bf16[32,512]{1,0:T(8,128)(2,1)S(1)}, bf16[32,512]{1,0:T(8,128)(2,1)S(1)}, u32[]{:S(2)}, u32[]{:S(2)}) collective-permute-start(bf16[32,512]{1,0:T(8,128)(2,1)S(1)} %get-tuple-element.32), channel_id=1, source_target_pairs={{0,12},{4,8},{8,4},{12,0},{1,13},{5,9},{9,5},{13,1},{2,14},{6,10},... | collective-permute-start | bytes 98312 | tf_op jit(solution)/shard_map/ppermute | solution.py:285
  46.8 0.7 %collective-permute-start.14 = (bf16[32,512]{1,0:T(8,128)(2,1)S(1)}, bf16[32,512]{1,0:T(8,128)(2,1)S(1)}, u32[]{:S(2)}, u32[]{:S(2)}) collective-permute-start(bf16[32,512]{1,0:T(8,128)(2,1)S(1)} %get-tuple-element.34), channel_id=1, source_target_pairs={{0,4},{4,0},{8,12},{12,8},{1,5},{5,1},{9,13},{13,9},{2,6},{6,2},{1... | collective-permute-start | bytes 98312 | tf_op jit(solution)/shard_map/ppermute | solution.py:285
  47.5 1.5 %collective-permute-done.12.far_ref = bf16[32,512]{1,0:T(8,128)(2,1)S(1)} collective-permute-done((bf16[32,512]{1,0:T(8,128)(2,1)S(1)}, bf16[32,512]{1,0:T(8,128)(2,1)S(1)}, u32[]{:S(2)}, u32[]{:S(2)}) %collective-permute-start.12) | collective-permute-done | bytes 32800 | tf_op jit(solution)/shard_map/ppermute | solution.py:285
  49.0 2.6 %collective-permute-done.13.two_ref = bf16[32,512]{1,0:T(8,128)(2,1)S(1)} collective-permute-done((bf16[32,512]{1,0:T(8,128)(2,1)S(1)}, bf16[32,512]{1,0:T(8,128)(2,1)S(1)}, u32[]{:S(2)}, u32[]{:S(2)}) %collective-permute-start.13) | collective-permute-done | bytes 32800 | tf_op jit(solution)/shard_map/ppermute | solution.py:285
  51.6 0.7 %shard_map.86 = bf16[32,2048]{1,0:T(8,128)(2,1)} custom-call(bf16[32,1024]{1,0:T(8,128)(2,1)S(1)} %shard_map.85.held_ref, bf16[32,512]{1,0:T(8,128)(2,1)S(1)} %collective-permute-done.13.two_ref, bf16[32,512]{1,0:T(8,128)(2,1)S(1)} %collective-permute-done.14.one_ref), custom_call_target="tpu_custom_call" | custom-call | bytes 262144 | tf_op jit(solution)/shard_map/pallas_call | solution.py:274
  (34 shorter events, 1.1 us)
Async XLA Ops:
  0.0 10.3 %copy-start.2 = (bf16[128,1024]{1,0:T(8,128)(2,1)S(1)}, bf16[128,1024]{1,0:T(8,128)(2,1)}, u32[]{:S(2)}) copy-start(bf16[128,1024]{1,0:T(8,128)(2,1)} %q_ref.1) | copy-start | bytes 786436
  0.0 10.3 %copy-start.3 = (bf16[128,256]{1,0:T(8,128)(2,1)S(1)}, bf16[128,256]{1,0:T(8,128)(2,1)}, u32[]{:S(2)}) copy-start(bf16[128,256]{1,0:T(8,128)(2,1)} %k_ref.3) | copy-start | bytes 196612
  0.0 10.3 %copy-start.4 = (bf16[128,256]{1,0:T(8,128)(2,1)S(1)}, bf16[128,256]{1,0:T(8,128)(2,1)}, u32[]{:S(2)}) copy-start(bf16[128,256]{1,0:T(8,128)(2,1)} %v_ref.3) | copy-start | bytes 196612
  1.6 5.1 %copy-start.1 = (s32[2]{0:T(128)S(1)}, s32[2]{0:T(128)}, u32[]{:S(2)}) copy-start(s32[2]{0:T(128)} %param.12) | copy-start | bytes 28
  1.6 8.7 %collective-permute-start.1 = (bf16[144,512]{1,0:T(8,128)(2,1)}, bf16[144,512]{1,0:T(8,128)(2,1)S(1)}, u32[]{:S(2)}, u32[]{:S(2)}) collective-permute-start(bf16[144,512]{1,0:T(8,128)(2,1)} %shard_map.73), channel_id=1, source_target_pairs={{0,4},{4,8},{8,12},{1,5},{5,9},{9,13},{2,6},{6,10},{10,14},{3,7},{... | collective-permute-start | bytes 442376 | tf_op jit(solution)/shard_map/ppermute | solution.py:325
  6.7 3.7 %copy-start.5 = (s32[128]{0:T(128)S(1)}, s32[128]{0:T(128)}, u32[]{:S(2)}) copy-start(s32[128]{0:T(128)} %param.11) | copy-start | bytes 1540
  6.7 3.7 %copy-start.6 = (s32[128]{0:T(128)S(1)}, s32[128]{0:T(128)}, u32[]{:S(2)}) copy-start(s32[128]{0:T(128)} %param.10) | copy-start | bytes 1540
  6.7 3.6 %collective-permute-start = (s32[1,2]{1,0:T(1,128)S(1)}, s32[1,2]{1,0:T(1,128)S(1)}, u32[]{:S(2)}, u32[]{:S(2)}) collective-permute-start(s32[1,2]{1,0:T(1,128)S(1)} %bitcast.3), channel_id=1, source_target_pairs={{0,4},{4,0},{8,12},{12,8},{1,5},{5,1},{9,13},{13,9},{2,6},{6,2},{1... | collective-permute-start | bytes 32 | tf_op jit(solution)/shard_map/ppermute | solution.py:285
  10.4 19.9 %copy-start = (bf16[1024,512]{1,0:T(8,128)(2,1)S(1)}, bf16[1024,512]{1,0:T(8,128)(2,1)}, u32[]{:S(2)}) copy-start(bf16[1024,512]{1,0:T(8,128)(2,1)} %refs_2_.5) | copy-start | bytes 3145732
  11.1 19.2 %collective-permute-start.2 = (bf16[136,1024]{1,0:T(8,128)(2,1)S(1)}, bf16[136,1024]{1,0:T(8,128)(2,1)S(1)}, u32[]{:S(2)}, u32[]{:S(2)}) collective-permute-start(bf16[136,1024]{1,0:T(8,128)(2,1)S(1)} %get-tuple-element.22.refs_0_), channel_id=1, source_target_pairs={{0,4},{4,12},{12,8},{8,0},{1,5},{5,13},{13,9},{9,1},{2,6},{6,14},{... | collective-permute-start | bytes 835592 | tf_op jit(solution)/shard_map/ppermute | solution.py:333
  13.3 17.5 %collective-permute-start.3 = (bf16[72,1024]{1,0:T(8,128)(2,1)S(1)}, bf16[72,1024]{1,0:T(8,128)(2,1)S(1)}, u32[]{:S(2)}, u32[]{:S(2)}) collective-permute-start(bf16[72,1024]{1,0:T(8,128)(2,1)S(1)} %get-tuple-element.23), channel_id=1, source_target_pairs={{0,8},{8,12},{12,4},{4,0},{1,9},{9,13},{13,5},{5,1},{2,10},{10,14}... | collective-permute-start | bytes 442376 | tf_op jit(solution)/shard_map/ppermute | solution.py:334
  14.4 17.4 %collective-permute-start.5 = (bf16[64,1024]{1,0:T(8,128)(2,1)S(1)}, bf16[64,1024]{1,0:T(8,128)(2,1)S(1)}, u32[]{:S(2)}, u32[]{:S(2)}) collective-permute-start(bf16[64,1024]{1,0:T(8,128)(2,1)S(1)} %get-tuple-element.26), channel_id=1, source_target_pairs={{0,8},{8,12},{12,4},{4,0},{1,9},{9,13},{13,5},{5,1},{2,10},{10,14}... | collective-permute-start | bytes 393224 | tf_op jit(solution)/shard_map/ppermute | solution.py:334
  16.3 18.7 %collective-permute-start.9 = (bf16[64,1024]{1,0:T(8,128)(2,1)S(1)}, bf16[64,1024]{1,0:T(8,128)(2,1)S(1)}, u32[]{:S(2)}, u32[]{:S(2)}) collective-permute-start(bf16[64,1024]{1,0:T(8,128)(2,1)S(1)} %get-tuple-element.26), channel_id=1, source_target_pairs={{0,12},{4,8},{8,4},{12,0},{1,13},{5,9},{9,5},{13,1},{2,14},{6,10},... | collective-permute-start | bytes 393224 | tf_op jit(solution)/shard_map/ppermute | solution.py:285
  30.7 1.6 %collective-permute-start.4 = (bf16[128,512]{1,0:T(8,128)(2,1)S(1)}, bf16[128,512]{1,0:T(8,128)(2,1)S(1)}, u32[]{:S(2)}, u32[]{:S(2)}) collective-permute-start(bf16[128,512]{1,0:T(8,128)(2,1)S(1)} %get-tuple-element.25), channel_id=1, source_target_pairs={{0,1},{1,0},{2,3},{3,2},{4,5},{5,4},{6,7},{7,6},{8,9},{9,8},{10,11... | collective-permute-start | bytes 393224 | tf_op jit(solution)/shard_map/ppermute | solution.py:285
  30.9 6.0 %collective-permute-start.8 = (bf16[64,1024]{1,0:T(8,128)(2,1)S(1)}, bf16[64,1024]{1,0:T(8,128)(2,1)S(1)}, u32[]{:S(2)}, u32[]{:S(2)}) collective-permute-start(bf16[64,1024]{1,0:T(8,128)(2,1)S(1)} %shard_map.80), channel_id=1, source_target_pairs={{0,4},{4,0},{8,12},{12,8},{1,5},{5,1},{9,13},{13,9},{2,6},{6,2},{1... | collective-permute-start | bytes 393224 | tf_op jit(solution)/shard_map/ppermute | solution.py:285
  32.1 1.3 %collective-permute-start.6 = (bf16[64,512]{1,0:T(8,128)(2,1)S(1)}, bf16[64,512]{1,0:T(8,128)(2,1)S(1)}, u32[]{:S(2)}, u32[]{:S(2)}) collective-permute-start(bf16[64,512]{1,0:T(8,128)(2,1)S(1)} %get-tuple-element.28), channel_id=1, source_target_pairs={{0,1},{1,0},{2,3},{3,2},{4,5},{5,4},{6,7},{7,6},{8,9},{9,8},{10,11... | collective-permute-start | bytes 196616 | tf_op jit(solution)/shard_map/ppermute | solution.py:285
  33.4 9.4 %collective-permute-start.7 = (bf16[192,512]{1,0:T(8,128)(2,1)S(1)}, bf16[192,512]{1,0:T(8,128)(2,1)S(1)}, u32[]{:S(2)}, u32[]{:S(2)}) collective-permute-start(bf16[192,512]{1,0:T(8,128)(2,1)S(1)} %shard_map.78.refs_0_), channel_id=1, source_target_pairs={{0,2},{1,3},{2,0},{3,1},{4,6},{5,7},{6,4},{7,5},{8,10},{9,11},{10,... | collective-permute-start | bytes 589832 | tf_op jit(solution)/shard_map/ppermute | solution.py:285
  37.1 1.3 %collective-permute-start.10 = (bf16[64,512]{1,0:T(8,128)(2,1)S(1)}, bf16[64,512]{1,0:T(8,128)(2,1)S(1)}, u32[]{:S(2)}, u32[]{:S(2)}) collective-permute-start(bf16[64,512]{1,0:T(8,128)(2,1)S(1)} %get-tuple-element.30), channel_id=1, source_target_pairs={{0,1},{1,0},{2,3},{3,2},{4,5},{5,4},{6,7},{7,6},{8,9},{9,8},{10,11... | collective-permute-start | bytes 196616 | tf_op jit(solution)/shard_map/ppermute | solution.py:285
  38.5 4.3 %collective-permute-start.11 = (bf16[64,512]{1,0:T(8,128)(2,1)S(1)}, bf16[64,512]{1,0:T(8,128)(2,1)S(1)}, u32[]{:S(2)}, u32[]{:S(2)}) collective-permute-start(bf16[64,512]{1,0:T(8,128)(2,1)S(1)} %shard_map.82.refs_0_), channel_id=1, source_target_pairs={{0,2},{1,3},{2,0},{3,1},{4,6},{5,7},{6,4},{7,5},{8,10},{9,11},{10,... | collective-permute-start | bytes 196616 | tf_op jit(solution)/shard_map/ppermute | solution.py:285
  43.0 5.9 %collective-permute-start.12 = (bf16[32,512]{1,0:T(8,128)(2,1)S(1)}, bf16[32,512]{1,0:T(8,128)(2,1)S(1)}, u32[]{:S(2)}, u32[]{:S(2)}) collective-permute-start(bf16[32,512]{1,0:T(8,128)(2,1)S(1)} %get-tuple-element.32), channel_id=1, source_target_pairs={{0,12},{4,8},{8,4},{12,0},{1,13},{5,9},{9,5},{13,1},{2,14},{6,10},... | collective-permute-start | bytes 98312 | tf_op jit(solution)/shard_map/ppermute | solution.py:285
  46.8 4.8 %collective-permute-start.13 = (bf16[32,512]{1,0:T(8,128)(2,1)S(1)}, bf16[32,512]{1,0:T(8,128)(2,1)S(1)}, u32[]{:S(2)}, u32[]{:S(2)}) collective-permute-start(bf16[32,512]{1,0:T(8,128)(2,1)S(1)} %get-tuple-element.33), channel_id=1, source_target_pairs={{0,8},{4,12},{8,0},{12,4},{1,9},{5,13},{9,1},{13,5},{2,10},{6,14},... | collective-permute-start | bytes 98312 | tf_op jit(solution)/shard_map/ppermute | solution.py:285
  46.8 4.8 %collective-permute-start.14 = (bf16[32,512]{1,0:T(8,128)(2,1)S(1)}, bf16[32,512]{1,0:T(8,128)(2,1)S(1)}, u32[]{:S(2)}, u32[]{:S(2)}) collective-permute-start(bf16[32,512]{1,0:T(8,128)(2,1)S(1)} %get-tuple-element.34), channel_id=1, source_target_pairs={{0,4},{4,0},{8,12},{12,8},{1,5},{5,1},{9,13},{13,9},{2,6},{6,2},{1... | collective-permute-start | bytes 98312 | tf_op jit(solution)/shard_map/ppermute | solution.py:285

commit v11 on v10

--- a/solution.py
+++ b/solution.py
@@ -58,13 +58,12 @@
 
 
 def attend_kernel(blocks, q_ref, halo_ref, k_ref, v_ref, end_ref, st_ref, own_ref, near_ref, *refs):
-    whole_ref, *out_refs = refs
+    plain_ref, noted_ref = refs
     targets = jnp.concatenate([own_ref[...], near_ref[...]], axis=1)
     count = targets.shape[1]
     targets = jnp.broadcast_to(targets.astype(jnp.float32), (8, count)).astype(jnp.bfloat16)
-    for ref, first in ((whole_ref, q_ref.shape[0]), (out_refs[0], q_ref.shape[0] // blocks)):
-        ref[pl.ds(first, 8), :] = jnp.zeros((8, q_ref.shape[1]), jnp.bfloat16)
-        ref[pl.ds(first, 8), pl.ds(0, count)] = targets
+    noted_ref[pl.ds(q_ref.shape[0], 8), :] = jnp.zeros((8, q_ref.shape[1]), jnp.bfloat16)
+    noted_ref[pl.ds(q_ref.shape[0], 8), pl.ds(0, count)] = targets
     rows = q_ref.shape[0]
     width = k_ref.shape[1]
     kv_here = width // HEAD_DIM
@@ -114,20 +113,19 @@
                     first = g * rows + (p * 2 + h) * half
                     place = pl.multiple_of((h ^ core) * half, half)
                     lanes = pl.ds((kv * group + g) * HEAD_DIM, HEAD_DIM)
-                    out_refs[p][pl.ds(place, half), lanes] = attended[first : first + half]
-                    whole_ref[pl.ds(p * 2 * half + place, half), lanes] = (
-                        attended[first : first + half]
-                    )
+                    target_rows = pl.ds(p * 2 * half + place, half)
+                    plain_ref[target_rows, lanes] = attended[first : first + half]
+                    noted_ref[target_rows, lanes] = attended[first : first + half]
 
 
 def attend(blocks, queries, halo, keys, values, end, start, own, near):
     rows, features = queries.shape
-    sizes = (rows + 8, rows // blocks + 8) + (rows // blocks,) * (blocks - 1)
+    sizes = (rows, rows + 8)
     return pl.pallas_call(
         functools.partial(attend_kernel, blocks),
         out_shape=tuple(jax.ShapeDtypeStruct((size, features), jnp.bfloat16) for size in sizes),
         in_specs=vmem(8),
-        out_specs=tuple(vmem(1 + blocks)),
+        out_specs=tuple(vmem(2)),
         compiler_params=params(),
         cost_estimate=cost(10 * 10**8, 0),
     )(queries, halo, keys, values, end, start, own, near)
@@ -176,71 +174,51 @@
     )(*terms)
 
 
-def inner():
-    c = lax.axis_index("ctx")
-    return (c == 1) | (c == 2)
-
-
-def tail_targets(ref, count):
-    tail = ref[pl.ds(ref.shape[0] - 8, 8), pl.ds(0, HEAD_DIM)].astype(jnp.float32)
-    return tail[0:1, 0:count].astype(jnp.int32)
-
-
-def pick_kernel(blocks, half, own_ref, near_ref, one_ref, two_ref, *refs):
+def pick_kernel(blocks, half, own_ref, near_ref, two_ref, *refs):
     sums, outs = refs[:-4], refs[-4:]
     x = lax.axis_index("tp") // 2
     c = lax.axis_index("ctx")
     pieces = [r[pl.ds(n, half), :] for r in sums for n in range(0, r.shape[0], half)]
-    far = jnp.where(
-        inner(), tail_targets(two_ref, 2 * blocks), tail_targets(one_ref, 2 * blocks)
-    )
-    by_source = (own_ref[...], near_ref[...], far[:, :blocks], far[:, blocks:])
-    by_cycle = (
-        by_source[0],
-        jnp.where(inner(), by_source[1], by_source[2]),
-        jnp.where(inner(), by_source[2], by_source[1]),
-        by_source[3],
-    )
-    order = [(cycle, p) for cycle in range(4) for p in range(blocks)]
+    tail = two_ref[pl.ds(two_ref.shape[0] - 8, 8), pl.ds(0, HEAD_DIM)].astype(jnp.float32)
+    far = tail[0:1, 0 : 2 * blocks].astype(jnp.int32)
+    targets = jnp.concatenate([own_ref[...], near_ref[...], far], axis=1)
     for k in range(4):
         wanted = (c ^ k) * blocks + x
         piece = pieces[0]
         for n in range(1, len(pieces)):
-            cycle, p = order[n]
-            here = jnp.broadcast_to(by_cycle[cycle][:, p : p + 1] == wanted, piece.shape)
+            here = jnp.broadcast_to(targets[:, n : n + 1] == wanted, piece.shape)
             piece = jnp.where(here, pieces[n], piece)
         outs[k][...] = piece
 
 
-def pick(blocks, own, near, one, two, sums):
+def pick(blocks, own, near, two, sums):
     rows, cols = sum(s.shape[0] for s in sums), sums[0].shape[1]
     half = rows // (4 * blocks)
     out = jax.ShapeDtypeStruct((half, cols), jnp.bfloat16)
     return pl.pallas_call(
         functools.partial(pick_kernel, blocks, half),
         out_shape=(out,) * 4,
-        in_specs=vmem(4 + len(sums)),
+        in_specs=vmem(3 + len(sums)),
         out_specs=tuple(vmem(4)),
         compiler_params=params(),
         cost_estimate=cost(4 * rows * cols, 8 * rows * cols),
-    )(own, near, one, two, *sums)
-
-
-def forward_kernel(first, one_ref, two_ref, out_ref):
-    rows = out_ref.shape[0]
-    out_ref[...] = jnp.where(inner(), two_ref[pl.ds(0, rows), :], one_ref[pl.ds(first, rows), :])
-
-
-def forward(block_rows, first, one, two):
-    out = jax.ShapeDtypeStruct((block_rows, one.shape[1]), one.dtype)
-    return pl.pallas_call(
-        functools.partial(forward_kernel, first),
+    )(own, near, two, *sums)
+
+
+def forward_kernel(got_ref, out_ref):
+    out_ref[...] = got_ref[pl.ds(0, out_ref.shape[0]), :]
+
+
+def forward(rows, got):
+    out = jax.ShapeDtypeStruct((rows, got.shape[1]), got.dtype)
+    return pl.pallas_call(
+        forward_kernel,
         out_shape=out,
-        in_specs=vmem(2),
-        out_specs=pl.BlockSpec(memory_space=pltpu.VMEM),
-        compiler_params=params(),
-        cost_estimate=cost(30 * 10**8, 0),
-    )(one, two)
+        in_specs=vmem(1),
+        out_specs=pl.BlockSpec(memory_space=pltpu.VMEM),
+        compiler_params=params(),
+        cost_estimate=cost(0, 0),
+    )(got)
 
 
 def hold_kernel(near_ref, far_ref, out_ref):
@@ -304,7 +282,7 @@
         in_specs=vmem(3),
         out_specs=pl.BlockSpec(memory_space=pltpu.VMEM),
         compiler_params=params(),
-        cost_estimate=cost(1 * 10**8, 0),
+        cost_estimate=cost(mine.size, 8 * mine.size),
     )(done, mine, flip(other, "tp", 1))
 
 
@@ -326,21 +304,18 @@
     own_target = block_target.reshape(1, blocks)
     near_target = flip(after(own_target, message), "ctx", 1)
     halo = after(halo, near_target)
-    whole, first, second = attend(
+    plain, noted = attend(
         blocks, queries, halo, key_rows, value_rows, end, start, own_target, near_target
     )
-    cycle_1, cycle_2 = [(0, 1), (1, 3), (3, 2), (2, 0)], [(0, 2), (2, 3), (3, 1), (1, 0)]
-    whole_1 = lax.ppermute(whole, "ctx", cycle_1)
-    first_2, second_2 = (lax.ppermute(a, "ctx", cycle_2) for a in (first, second))
-    second_3 = flip(second, "ctx", 3)
-    first_3 = flip(forward(block_rows, 0, whole_1, first_2), "ctx", 1)
-    share_a = core_total(*project(block_rows, (whole, whole_1), out_weight, cost(0, 0)))
-    share_ab = stack_core_total(
-        share_a, *project(block_rows, (first_2, second_2), out_weight, cost(30 * 10**8, 0))
-    )
-    share_c = core_total(*project(block_rows, (first_3, second_3), out_weight))
+    rows_1, rows_2 = flip(plain, "ctx", 1), flip(noted, "ctx", 2)
+    rows_3 = flip(forward(rows, rows_2), "ctx", 1)
+    share_a = core_total(*project(block_rows, (plain, rows_1), out_weight, cost(30 * 10**8, 0)))
+    rows_2 = after(rows_2, share_a)
+    share_ab = stack_core_total(share_a, *project(block_rows, (rows_2,), out_weight))
+    rows_3 = after(rows_3, share_ab)
+    share_c = core_total(*project(block_rows, (rows_3,), out_weight))
     sums = (chip_total(share_ab), chip_total(share_c))
-    kept, *sent = pick(blocks, own_target, near_target, whole_1, first_2, sums)
+    kept, *sent = pick(blocks, own_target, near_target, rows_2, sums)
     got_3, got_2, got_1 = (flip(sent[k - 1], "ctx", k) for k in (3, 2, 1))
     return join(hold(kept, got_3), got_2, got_1)
 

time: 52.4 us -> 48.3 us (0.922)
  starting transfers between devices: 22.8 us -> 19.5 us
  waiting for transfers between devices: 24.9 us -> 24.1 us
    ppermute x3 -> x0, waiting for transfers between devices: 12 us -> none  [the longest x1 12 us: small_ring(): whole_1 = lax.ppermute(whole, 'ctx', cycle_1)]
    ppermute x11 -> x12, waiting for transfers between devices: 12.9 us -> 24.1 us  [flip(): return lax.ppermute(array, axis, [(i, i ^ bits) for i in range(4)])]
    ppermute x3 -> x0, starting transfers between devices: 5.21 us -> none  [the longest x2 2.96 us: small_ring(): lax.ppermute(a, 'ctx', cycle_2)]
    ppermute x11 -> x12, starting transfers between devices: 12.5 us -> 14.4 us  [flip(): return lax.ppermute(array, axis, [(i, i ^ bits) for i in range(4)])]
  transfers between devices with their start and end apart: 15 -> 13, of which waited for: 8 -> 9; matrix products, arithmetic and copies ran while one was open for 0% -> 0% of each run, Pallas kernels for 2% -> 2%
where the time goes in v11:
time: 48.3 us; the launch traced here: 48.2 us
  waiting for transfers between devices  24.1 us (50%)
  starting transfers between devices  19.5 us (40%)
  Pallas kernels  4.41 us (9%)
    ppermute x12, waiting for transfers between devices, flip(): return lax.ppermute(array, axis, [(i, i ^ bits) for i in range(4)])  24.1 us
    ppermute x12, starting transfers between devices, flip(): return lax.ppermute(array, axis, [(i, i ^ bits) for i in range(4)])  14.4 us
    ppermute x1, starting transfers between devices, small_ring(): halo = lax.ppermute(message, 'ctx', [(0, 1), (1, 2), (2, 3)])  5.06 us
    pallas_call x1, Pallas kernels, pack(): pl.pallas_call(pack_kernel, out_shape=jax.ShapeDtypeStruct((rows + 16, 2...  1.59 us
    pallas_call x3, Pallas kernels, project(): pl.pallas_call(functools.partial(project_kernel, block_rows), out_shape=(...  1.05 us
  transfers between devices with their start and end apart: 13, of which 9 were waited for; matrix products, arithmetic and copies ran while one was open for 0% of the time, Pallas kernels for 2%

profile of v11, /device:TPU:0, one launch (start us, length us, event | category | flops | bytes accessed | tf_op | source)
XLA Modules:
  0.0 48.2 jit_solution(16888934129050510964)
XLA Ops:
  0.0 1.6 %shard_map.73 = bf16[144,512]{1,0:T(8,128)(2,1)} custom-call(bf16[128,256]{1,0:T(8,128)(2,1)} %k_ref.3, bf16[128,256]{1,0:T(8,128)(2,1)} %v_ref.3, s32[1,128]{1,0:T(1,128)} %bitcast.6), custom_call_target="tpu_custom_call" | custom-call | flops 1000000000 | bytes 262144 | tf_op jit(solution)/shard_map/pallas_call | solution.py:51
  1.6 5.1 %collective-permute-start.1 = (bf16[144,512]{1,0:T(8,128)(2,1)}, bf16[144,512]{1,0:T(8,128)(2,1)S(1)}, u32[]{:S(2)}, u32[]{:S(2)}) collective-permute-start(bf16[144,512]{1,0:T(8,128)(2,1)} %shard_map.73), channel_id=1, source_target_pairs={{0,4},{4,8},{8,12},{1,5},{5,9},{9,13},{2,6},{6,10},{10,14},{3,7},{... | collective-permute-start | bytes 442376 | tf_op jit(solution)/shard_map/ppermute | solution.py:303
  6.7 1.6 %collective-permute-start = (s32[1,2]{1,0:T(1,128)S(1)}, s32[1,2]{1,0:T(1,128)S(1)}, u32[]{:S(2)}, u32[]{:S(2)}) collective-permute-start(s32[1,2]{1,0:T(1,128)S(1)} %bitcast.3), channel_id=1, source_target_pairs={{0,4},{4,0},{8,12},{12,8},{1,5},{5,1},{9,13},{13,9},{2,6},{6,2},{1... | collective-permute-start | bytes 32 | tf_op jit(solution)/shard_map/ppermute | solution.py:263
  8.3 2.0 %collective-permute-done.near_ref = s32[1,2]{1,0:T(1,128)S(1)} collective-permute-done((s32[1,2]{1,0:T(1,128)S(1)}, s32[1,2]{1,0:T(1,128)S(1)}, u32[]{:S(2)}, u32[]{:S(2)}) %collective-permute-start) | collective-permute-done | bytes 40 | tf_op jit(solution)/shard_map/ppermute | solution.py:263
  10.4 0.7 %shard_map.74 = (bf16[128,1024]{1,0:T(8,128)(2,1)S(1)}, bf16[136,1024]{1,0:T(8,128)(2,1)S(1)}) custom-call(bf16[128,1024]{1,0:T(8,128)(2,1)S(1)} %copy-done.2, bf16[144,512]{1,0:T(8,128)(2,1)S(1)} %collective-permute-done.1.halo_ref, bf16[128,256]{1,0:T(8,128)(2,1)S(1)} %copy-done.3, bf16[128,256]{1,0:T(8,128)(2,1)S(1)} %copy-done.4, s32[1,128]{1,0:T(1,128)S(1)} %bitcast.7, ...), custom_call_target="tpu_custom_call" | custom-call | flops 1000000000 | tf_op jit(solution)/shard_map/pallas_call | solution.py:124
  11.1 2.3 %collective-permute-start.3 = (bf16[128,1024]{1,0:T(8,128)(2,1)S(1)}, bf16[128,1024]{1,0:T(8,128)(2,1)S(1)}, u32[]{:S(2)}, u32[]{:S(2)}) collective-permute-start(bf16[128,1024]{1,0:T(8,128)(2,1)S(1)} %get-tuple-element.24.refs_0_), channel_id=1, source_target_pairs={{0,4},{4,0},{8,12},{12,8},{1,5},{5,1},{9,13},{13,9},{2,6},{6,2},{1... | collective-permute-start | bytes 786440 | tf_op jit(solution)/shard_map/ppermute | solution.py:263
  13.3 2.6 %collective-permute-start.2 = (bf16[136,1024]{1,0:T(8,128)(2,1)S(1)}, bf16[136,1024]{1,0:T(8,128)(2,1)S(1)}, u32[]{:S(2)}, u32[]{:S(2)}) collective-permute-start(bf16[136,1024]{1,0:T(8,128)(2,1)S(1)} %get-tuple-element.23), channel_id=1, source_target_pairs={{0,8},{4,12},{8,0},{12,4},{1,9},{5,13},{9,1},{13,5},{2,10},{6,14},... | collective-permute-start | bytes 835592 | tf_op jit(solution)/shard_map/ppermute | solution.py:263
  15.9 8.3 %collective-permute-done.3.refs_1_ = bf16[128,1024]{1,0:T(8,128)(2,1)S(1)} collective-permute-done((bf16[128,1024]{1,0:T(8,128)(2,1)S(1)}, bf16[128,1024]{1,0:T(8,128)(2,1)S(1)}, u32[]{:S(2)}, u32[]{:S(2)}) %collective-permute-start.3) | collective-permute-done | bytes 262176 | tf_op jit(solution)/shard_map/ppermute | solution.py:263
  24.2 0.4 shard_map.75
  24.7 2.7 %collective-permute-done.2.refs_0_.got_ref.two_ref = bf16[136,1024]{1,0:T(8,128)(2,1)S(1)} collective-permute-done((bf16[136,1024]{1,0:T(8,128)(2,1)S(1)}, bf16[136,1024]{1,0:T(8,128)(2,1)S(1)}, u32[]{:S(2)}, u32[]{:S(2)}) %collective-permute-start.2) | collective-permute-done | bytes 278560 | tf_op jit(solution)/shard_map/ppermute | solution.py:263
  27.7 0.3 shard_map.77
  28.1 1.2 %collective-permute-done.5.got_ref = bf16[64,512]{1,0:T(8,128)(2,1)S(1)} collective-permute-done((bf16[64,512]{1,0:T(8,128)(2,1)S(1)}, bf16[64,512]{1,0:T(8,128)(2,1)S(1)}, u32[]{:S(2)}, u32[]{:S(2)}) %collective-permute-start.5) | collective-permute-done | bytes 65568 | tf_op jit(solution)/shard_map/ppermute | solution.py:263
  29.3 1.6 %collective-permute-start.6 = (bf16[192,512]{1,0:T(8,128)(2,1)S(1)}, bf16[192,512]{1,0:T(8,128)(2,1)S(1)}, u32[]{:S(2)}, u32[]{:S(2)}) collective-permute-start(bf16[192,512]{1,0:T(8,128)(2,1)S(1)} %shard_map.78.refs_0_), channel_id=1, source_target_pairs={{0,2},{1,3},{2,0},{3,1},{4,6},{5,7},{6,4},{7,5},{8,10},{9,11},{10,... | collective-permute-start | bytes 589832 | tf_op jit(solution)/shard_map/ppermute | solution.py:263
  30.9 3.0 %collective-permute-done.7.refs_0_ = bf16[128,1024]{1,0:T(8,128)(2,1)S(1)} collective-permute-done((bf16[128,1024]{1,0:T(8,128)(2,1)S(1)}, bf16[128,1024]{1,0:T(8,128)(2,1)S(1)}, u32[]{:S(2)}, u32[]{:S(2)}) %collective-permute-start.7) | collective-permute-done | bytes 262176 | tf_op jit(solution)/shard_map/ppermute | solution.py:263
  33.9 0.3 shard_map.81
  34.3 1.2 %collective-permute-done.8.refs_1_ = bf16[64,512]{1,0:T(8,128)(2,1)S(1)} collective-permute-done((bf16[64,512]{1,0:T(8,128)(2,1)S(1)}, bf16[64,512]{1,0:T(8,128)(2,1)S(1)}, u32[]{:S(2)}, u32[]{:S(2)}) %collective-permute-start.8) | collective-permute-done | bytes 65568 | tf_op jit(solution)/shard_map/ppermute | solution.py:263
  35.6 1.6 %collective-permute-start.9 = (bf16[64,512]{1,0:T(8,128)(2,1)S(1)}, bf16[64,512]{1,0:T(8,128)(2,1)S(1)}, u32[]{:S(2)}, u32[]{:S(2)}) collective-permute-start(bf16[64,512]{1,0:T(8,128)(2,1)S(1)} %shard_map.82.refs_0_), channel_id=1, source_target_pairs={{0,2},{1,3},{2,0},{3,1},{4,6},{5,7},{6,4},{7,5},{8,10},{9,11},{10,... | collective-permute-start | bytes 196616 | tf_op jit(solution)/shard_map/ppermute | solution.py:263
  37.2 2.7 %collective-permute-done.9.refs_1_ = bf16[64,512]{1,0:T(8,128)(2,1)S(1)} collective-permute-done((bf16[64,512]{1,0:T(8,128)(2,1)S(1)}, bf16[64,512]{1,0:T(8,128)(2,1)S(1)}, u32[]{:S(2)}, u32[]{:S(2)}) %collective-permute-start.9) | collective-permute-done | bytes 65568 | tf_op jit(solution)/shard_map/ppermute | solution.py:263
  39.9 0.2 shard_map.84
  40.1 2.5 %collective-permute-start.10 = (bf16[32,512]{1,0:T(8,128)(2,1)S(1)}, bf16[32,512]{1,0:T(8,128)(2,1)S(1)}, u32[]{:S(2)}, u32[]{:S(2)}) collective-permute-start(bf16[32,512]{1,0:T(8,128)(2,1)S(1)} %get-tuple-element.34), channel_id=1, source_target_pairs={{0,12},{4,8},{8,4},{12,0},{1,13},{5,9},{9,5},{13,1},{2,14},{6,10},... | collective-permute-start | bytes 98312 | tf_op jit(solution)/shard_map/ppermute | solution.py:263
  42.7 1.9 %collective-permute-start.12 = (bf16[32,512]{1,0:T(8,128)(2,1)S(1)}, bf16[32,512]{1,0:T(8,128)(2,1)S(1)}, u32[]{:S(2)}, u32[]{:S(2)}) collective-permute-start(bf16[32,512]{1,0:T(8,128)(2,1)S(1)} %get-tuple-element.36), channel_id=1, source_target_pairs={{0,4},{4,0},{8,12},{12,8},{1,5},{5,1},{9,13},{13,9},{2,6},{6,2},{1... | collective-permute-start | bytes 98312 | tf_op jit(solution)/shard_map/ppermute | solution.py:263
  44.6 1.3 %collective-permute-done.10.far_ref = bf16[32,512]{1,0:T(8,128)(2,1)S(1)} collective-permute-done((bf16[32,512]{1,0:T(8,128)(2,1)S(1)}, bf16[32,512]{1,0:T(8,128)(2,1)S(1)}, u32[]{:S(2)}, u32[]{:S(2)}) %collective-permute-start.10) | collective-permute-done | bytes 32800 | tf_op jit(solution)/shard_map/ppermute | solution.py:263
  45.9 1.6 %collective-permute-done.11.two_ref = bf16[32,512]{1,0:T(8,128)(2,1)S(1)} collective-permute-done((bf16[32,512]{1,0:T(8,128)(2,1)S(1)}, bf16[32,512]{1,0:T(8,128)(2,1)S(1)}, u32[]{:S(2)}, u32[]{:S(2)}) %collective-permute-start.11) | collective-permute-done | bytes 32800 | tf_op jit(solution)/shard_map/ppermute | solution.py:263
  47.5 0.7 %shard_map.86 = bf16[32,2048]{1,0:T(8,128)(2,1)} custom-call(bf16[32,1024]{1,0:T(8,128)(2,1)S(1)} %shard_map.85.held_ref, bf16[32,512]{1,0:T(8,128)(2,1)S(1)} %collective-permute-done.11.two_ref, bf16[32,512]{1,0:T(8,128)(2,1)S(1)} %collective-permute-done.12.one_ref), custom_call_target="tpu_custom_call" | custom-call | bytes 262144 | tf_op jit(solution)/shard_map/pallas_call | solution.py:252
  (30 shorter events, 0.6 us)
Async XLA Ops:
  0.0 10.3 %copy-start.2 = (bf16[128,1024]{1,0:T(8,128)(2,1)S(1)}, bf16[128,1024]{1,0:T(8,128)(2,1)}, u32[]{:S(2)}) copy-start(bf16[128,1024]{1,0:T(8,128)(2,1)} %q_ref.1) | copy-start | bytes 786436
  0.0 10.3 %copy-start.3 = (bf16[128,256]{1,0:T(8,128)(2,1)S(1)}, bf16[128,256]{1,0:T(8,128)(2,1)}, u32[]{:S(2)}) copy-start(bf16[128,256]{1,0:T(8,128)(2,1)} %k_ref.3) | copy-start | bytes 196612
  0.0 10.3 %copy-start.4 = (bf16[128,256]{1,0:T(8,128)(2,1)S(1)}, bf16[128,256]{1,0:T(8,128)(2,1)}, u32[]{:S(2)}) copy-start(bf16[128,256]{1,0:T(8,128)(2,1)} %v_ref.3) | copy-start | bytes 196612
  1.6 5.1 %copy-start.1 = (s32[2]{0:T(128)S(1)}, s32[2]{0:T(128)}, u32[]{:S(2)}) copy-start(s32[2]{0:T(128)} %param.12) | copy-start | bytes 28
  1.6 8.7 %collective-permute-start.1 = (bf16[144,512]{1,0:T(8,128)(2,1)}, bf16[144,512]{1,0:T(8,128)(2,1)S(1)}, u32[]{:S(2)}, u32[]{:S(2)}) collective-permute-start(bf16[144,512]{1,0:T(8,128)(2,1)} %shard_map.73), channel_id=1, source_target_pairs={{0,4},{4,8},{8,12},{1,5},{5,9},{9,13},{2,6},{6,10},{10,14},{3,7},{... | collective-permute-start | bytes 442376 | tf_op jit(solution)/shard_map/ppermute | solution.py:303
  6.7 3.7 %copy-start.5 = (s32[128]{0:T(128)S(1)}, s32[128]{0:T(128)}, u32[]{:S(2)}) copy-start(s32[128]{0:T(128)} %param.11) | copy-start | bytes 1540
  6.7 3.7 %copy-start.6 = (s32[128]{0:T(128)S(1)}, s32[128]{0:T(128)}, u32[]{:S(2)}) copy-start(s32[128]{0:T(128)} %param.10) | copy-start | bytes 1540
  6.7 3.6 %collective-permute-start = (s32[1,2]{1,0:T(1,128)S(1)}, s32[1,2]{1,0:T(1,128)S(1)}, u32[]{:S(2)}, u32[]{:S(2)}) collective-permute-start(s32[1,2]{1,0:T(1,128)S(1)} %bitcast.3), channel_id=1, source_target_pairs={{0,4},{4,0},{8,12},{12,8},{1,5},{5,1},{9,13},{13,9},{2,6},{6,2},{1... | collective-permute-start | bytes 32 | tf_op jit(solution)/shard_map/ppermute | solution.py:263
  10.3 13.9 %copy-start = (bf16[1024,512]{1,0:T(8,128)(2,1)S(1)}, bf16[1024,512]{1,0:T(8,128)(2,1)}, u32[]{:S(2)}) copy-start(bf16[1024,512]{1,0:T(8,128)(2,1)} %refs_1_.3) | copy-start | bytes 3145732
  11.1 13.1 %collective-permute-start.3 = (bf16[128,1024]{1,0:T(8,128)(2,1)S(1)}, bf16[128,1024]{1,0:T(8,128)(2,1)S(1)}, u32[]{:S(2)}, u32[]{:S(2)}) collective-permute-start(bf16[128,1024]{1,0:T(8,128)(2,1)S(1)} %get-tuple-element.24.refs_0_), channel_id=1, source_target_pairs={{0,4},{4,0},{8,12},{12,8},{1,5},{5,1},{9,13},{13,9},{2,6},{6,2},{1... | collective-permute-start | bytes 786440 | tf_op jit(solution)/shard_map/ppermute | solution.py:263
  13.3 14.1 %collective-permute-start.2 = (bf16[136,1024]{1,0:T(8,128)(2,1)S(1)}, bf16[136,1024]{1,0:T(8,128)(2,1)S(1)}, u32[]{:S(2)}, u32[]{:S(2)}) collective-permute-start(bf16[136,1024]{1,0:T(8,128)(2,1)S(1)} %get-tuple-element.23), channel_id=1, source_target_pairs={{0,8},{4,12},{8,0},{12,4},{1,9},{5,13},{9,1},{13,5},{2,10},{6,14},... | collective-permute-start | bytes 835592 | tf_op jit(solution)/shard_map/ppermute | solution.py:263
  24.6 3.0 %collective-permute-start.4 = (bf16[128,512]{1,0:T(8,128)(2,1)S(1)}, bf16[128,512]{1,0:T(8,128)(2,1)S(1)}, u32[]{:S(2)}, u32[]{:S(2)}) collective-permute-start(bf16[128,512]{1,0:T(8,128)(2,1)S(1)} %get-tuple-element.26), channel_id=1, source_target_pairs={{0,1},{1,0},{2,3},{3,2},{4,5},{5,4},{6,7},{7,6},{8,9},{9,8},{10,11... | collective-permute-start | bytes 393224 | tf_op jit(solution)/shard_map/ppermute | solution.py:263
  27.5 6.4 %collective-permute-start.7 = (bf16[128,1024]{1,0:T(8,128)(2,1)S(1)}, bf16[128,1024]{1,0:T(8,128)(2,1)S(1)}, u32[]{:S(2)}, u32[]{:S(2)}) collective-permute-start(bf16[128,1024]{1,0:T(8,128)(2,1)S(1)} %shard_map.80), channel_id=1, source_target_pairs={{0,4},{4,0},{8,12},{12,8},{1,5},{5,1},{9,13},{13,9},{2,6},{6,2},{1... | collective-permute-start | bytes 786440 | tf_op jit(solution)/shard_map/ppermute | solution.py:263
  28.0 1.3 %collective-permute-start.5 = (bf16[64,512]{1,0:T(8,128)(2,1)S(1)}, bf16[64,512]{1,0:T(8,128)(2,1)S(1)}, u32[]{:S(2)}, u32[]{:S(2)}) collective-permute-start(bf16[64,512]{1,0:T(8,128)(2,1)S(1)} %get-tuple-element.29), channel_id=1, source_target_pairs={{0,1},{1,0},{2,3},{3,2},{4,5},{5,4},{6,7},{7,6},{8,9},{9,8},{10,11... | collective-permute-start | bytes 196616 | tf_op jit(solution)/shard_map/ppermute | solution.py:263
  29.3 7.8 %collective-permute-start.6 = (bf16[192,512]{1,0:T(8,128)(2,1)S(1)}, bf16[192,512]{1,0:T(8,128)(2,1)S(1)}, u32[]{:S(2)}, u32[]{:S(2)}) collective-permute-start(bf16[192,512]{1,0:T(8,128)(2,1)S(1)} %shard_map.78.refs_0_), channel_id=1, source_target_pairs={{0,2},{1,3},{2,0},{3,1},{4,6},{5,7},{6,4},{7,5},{8,10},{9,11},{10,... | collective-permute-start | bytes 589832 | tf_op jit(solution)/shard_map/ppermute | solution.py:263
  34.2 1.3 %collective-permute-start.8 = (bf16[64,512]{1,0:T(8,128)(2,1)S(1)}, bf16[64,512]{1,0:T(8,128)(2,1)S(1)}, u32[]{:S(2)}, u32[]{:S(2)}) collective-permute-start(bf16[64,512]{1,0:T(8,128)(2,1)S(1)} %get-tuple-element.32), channel_id=1, source_target_pairs={{0,1},{1,0},{2,3},{3,2},{4,5},{5,4},{6,7},{7,6},{8,9},{9,8},{10,11... | collective-permute-start | bytes 196616 | tf_op jit(solution)/shard_map/ppermute | solution.py:263
  35.6 4.3 %collective-permute-start.9 = (bf16[64,512]{1,0:T(8,128)(2,1)S(1)}, bf16[64,512]{1,0:T(8,128)(2,1)S(1)}, u32[]{:S(2)}, u32[]{:S(2)}) collective-permute-start(bf16[64,512]{1,0:T(8,128)(2,1)S(1)} %shard_map.82.refs_0_), channel_id=1, source_target_pairs={{0,2},{1,3},{2,0},{3,1},{4,6},{5,7},{6,4},{7,5},{8,10},{9,11},{10,... | collective-permute-start | bytes 196616 | tf_op jit(solution)/shard_map/ppermute | solution.py:263
  40.1 5.8 %collective-permute-start.10 = (bf16[32,512]{1,0:T(8,128)(2,1)S(1)}, bf16[32,512]{1,0:T(8,128)(2,1)S(1)}, u32[]{:S(2)}, u32[]{:S(2)}) collective-permute-start(bf16[32,512]{1,0:T(8,128)(2,1)S(1)} %get-tuple-element.34), channel_id=1, source_target_pairs={{0,12},{4,8},{8,4},{12,0},{1,13},{5,9},{9,5},{13,1},{2,14},{6,10},... | collective-permute-start | bytes 98312 | tf_op jit(solution)/shard_map/ppermute | solution.py:263
  42.7 4.8 %collective-permute-start.11 = (bf16[32,512]{1,0:T(8,128)(2,1)S(1)}, bf16[32,512]{1,0:T(8,128)(2,1)S(1)}, u32[]{:S(2)}, u32[]{:S(2)}) collective-permute-start(bf16[32,512]{1,0:T(8,128)(2,1)S(1)} %get-tuple-element.35), channel_id=1, source_target_pairs={{0,8},{4,12},{8,0},{12,4},{1,9},{5,13},{9,1},{13,5},{2,10},{6,14},... | collective-permute-start | bytes 98312 | tf_op jit(solution)/shard_map/ppermute | solution.py:263
  42.7 4.8 %collective-permute-start.12 = (bf16[32,512]{1,0:T(8,128)(2,1)S(1)}, bf16[32,512]{1,0:T(8,128)(2,1)S(1)}, u32[]{:S(2)}, u32[]{:S(2)}) collective-permute-start(bf16[32,512]{1,0:T(8,128)(2,1)S(1)} %get-tuple-element.36), channel_id=1, source_target_pairs={{0,4},{4,0},{8,12},{12,8},{1,5},{5,1},{9,13},{13,9},{2,6},{6,2},{1... | collective-permute-start | bytes 98312 | tf_op jit(solution)/shard_map/ppermute | solution.py:263

commit v12 on v11

--- a/solution.py
+++ b/solution.py
@@ -127,7 +127,7 @@
         in_specs=vmem(8),
         out_specs=tuple(vmem(2)),
         compiler_params=params(),
-        cost_estimate=cost(10 * 10**8, 0),
+        cost_estimate=cost(100 * 10**8, 0),
     )(queries, halo, keys, values, end, start, own, near)
 
 
@@ -170,7 +170,7 @@
         in_specs=vmem(len(terms)),
         out_specs=pl.BlockSpec(memory_space=pltpu.VMEM),
         compiler_params=params(),
-        cost_estimate=cost(4 * terms[0].size, 10 * terms[0].size),
+        cost_estimate=cost(10 * 10**8, 0),
     )(*terms)
 
 
@@ -217,7 +217,7 @@
         in_specs=vmem(1),
         out_specs=pl.BlockSpec(memory_space=pltpu.VMEM),
         compiler_params=params(),
-        cost_estimate=cost(0, 0),
+        cost_estimate=cost(1 * 10**8, 0),
     )(got)
 
 
@@ -307,14 +307,12 @@
     plain, noted = attend(
         blocks, queries, halo, key_rows, value_rows, end, start, own_target, near_target
     )
-    rows_1, rows_2 = flip(plain, "ctx", 1), flip(noted, "ctx", 2)
+    rows_2, rows_1 = flip(noted, "ctx", 2), flip(plain, "ctx", 1)
     rows_3 = flip(forward(rows, rows_2), "ctx", 1)
-    share_a = core_total(*project(block_rows, (plain, rows_1), out_weight, cost(30 * 10**8, 0)))
-    rows_2 = after(rows_2, share_a)
-    share_ab = stack_core_total(share_a, *project(block_rows, (rows_2,), out_weight))
-    rows_3 = after(rows_3, share_ab)
-    share_c = core_total(*project(block_rows, (rows_3,), out_weight))
-    sums = (chip_total(share_ab), chip_total(share_c))
+    sum_a = chip_total(core_total(*project(block_rows, (plain,), out_weight, cost(10 * 10**8, 0))))
+    share_b = core_total(*project(block_rows, (rows_1, rows_2), out_weight, cost(30 * 10**8, 0)))
+    share_c = core_total(*project(block_rows, (rows_3,), out_weight, cost(30 * 10**8, 0)))
+    sums = (sum_a, chip_total(share_b), chip_total(share_c))
     kept, *sent = pick(blocks, own_target, near_target, rows_2, sums)
     got_3, got_2, got_1 = (flip(sent[k - 1], "ctx", k) for k in (3, 2, 1))
     return join(hold(kept, got_3), got_2, got_1)

time: 48.3 us -> 49.9 us (1.033)
  starting transfers between devices: 19.5 us -> 22.2 us
  waiting for transfers between devices: 24.1 us -> 22.8 us
    ppermute x12 -> x13, starting transfers between devices: 14.4 us -> 17.2 us  [flip(): return lax.ppermute(array, axis, [(i, i ^ bits) for i in range(4)])]
    ppermute x12 -> x13, waiting for transfers between devices: 24.1 us -> 22.8 us  [flip(): return lax.ppermute(array, axis, [(i, i ^ bits) for i in range(4)])]
  transfers between devices with their start and end apart: 13 -> 14, of which waited for: 9 -> 7; matrix products, arithmetic and copies ran while one was open for 0% -> 0% of each run, Pallas kernels for 2% -> 2%
where the time goes in v12:
time: 49.9 us; the launch traced here: 49.7 us
  waiting for transfers between devices  22.8 us (46%)
  starting transfers between devices  22.2 us (44%)
  Pallas kernels  4.43 us (9%)
    ppermute x13, waiting for transfers between devices, flip(): return lax.ppermute(array, axis, [(i, i ^ bits) for i in range(4)])  22.8 us
    ppermute x13, starting transfers between devices, flip(): return lax.ppermute(array, axis, [(i, i ^ bits) for i in range(4)])  17.2 us
    ppermute x1, starting transfers between devices, small_ring(): halo = lax.ppermute(message, 'ctx', [(0, 1), (1, 2), (2, 3)])  5.06 us
    pallas_call x1, Pallas kernels, pack(): pl.pallas_call(pack_kernel, out_shape=jax.ShapeDtypeStruct((rows + 16, 2...  1.6 us
    pallas_call x3, Pallas kernels, project(): pl.pallas_call(functools.partial(project_kernel, block_rows), out_shape=(...  1.05 us
  transfers between devices with their start and end apart: 14, of which 7 were waited for; matrix products, arithmetic and copies ran while one was open for 0% of the time, Pallas kernels for 2%

profile of v12, /device:TPU:0, one launch (start us, length us, event | category | flops | bytes accessed | tf_op | source)
XLA Modules:
  0.0 49.7 jit_solution(809105168836688727)
XLA Ops:
  0.0 1.6 %shard_map.73 = bf16[144,512]{1,0:T(8,128)(2,1)} custom-call(bf16[128,256]{1,0:T(8,128)(2,1)} %k_ref.3, bf16[128,256]{1,0:T(8,128)(2,1)} %v_ref.3, s32[1,128]{1,0:T(1,128)} %bitcast.6), custom_call_target="tpu_custom_call" | custom-call | flops 1000000000 | bytes 262144 | tf_op jit(solution)/shard_map/pallas_call | solution.py:51
  1.6 5.1 %collective-permute-start.1 = (bf16[144,512]{1,0:T(8,128)(2,1)}, bf16[144,512]{1,0:T(8,128)(2,1)S(1)}, u32[]{:S(2)}, u32[]{:S(2)}) collective-permute-start(bf16[144,512]{1,0:T(8,128)(2,1)} %shard_map.73), channel_id=1, source_target_pairs={{0,4},{4,8},{8,12},{1,5},{5,9},{9,13},{2,6},{6,10},{10,14},{3,7},{... | collective-permute-start | bytes 442376 | tf_op jit(solution)/shard_map/ppermute | solution.py:303
  6.7 1.6 %collective-permute-start = (s32[1,2]{1,0:T(1,128)S(1)}, s32[1,2]{1,0:T(1,128)S(1)}, u32[]{:S(2)}, u32[]{:S(2)}) collective-permute-start(s32[1,2]{1,0:T(1,128)S(1)} %bitcast.3), channel_id=1, source_target_pairs={{0,4},{4,0},{8,12},{12,8},{1,5},{5,1},{9,13},{13,9},{2,6},{6,2},{1... | collective-permute-start | bytes 32 | tf_op jit(solution)/shard_map/ppermute | solution.py:263
  8.3 2.0 %collective-permute-done.near_ref = s32[1,2]{1,0:T(1,128)S(1)} collective-permute-done((s32[1,2]{1,0:T(1,128)S(1)}, s32[1,2]{1,0:T(1,128)S(1)}, u32[]{:S(2)}, u32[]{:S(2)}) %collective-permute-start) | collective-permute-done | bytes 40 | tf_op jit(solution)/shard_map/ppermute | solution.py:263
  10.4 0.7 %shard_map.74 = (bf16[128,1024]{1,0:T(8,128)(2,1)S(1)}, bf16[136,1024]{1,0:T(8,128)(2,1)S(1)}) custom-call(bf16[128,1024]{1,0:T(8,128)(2,1)S(1)} %copy-done.2, bf16[144,512]{1,0:T(8,128)(2,1)S(1)} %collective-permute-done.1.halo_ref, bf16[128,256]{1,0:T(8,128)(2,1)S(1)} %copy-done.3, bf16[128,256]{1,0:T(8,128)(2,1)S(1)} %copy-done.4, s32[1,128]{1,0:T(1,128)S(1)} %bitcast.7, ...), custom_call_target="tpu_custom_call" | custom-call | flops 10000000000 | tf_op jit(solution)/shard_map/pallas_call | solution.py:124
  11.1 3.2 %collective-permute-start.2 = (bf16[136,1024]{1,0:T(8,128)(2,1)S(1)}, bf16[136,1024]{1,0:T(8,128)(2,1)S(1)}, u32[]{:S(2)}, u32[]{:S(2)}) collective-permute-start(bf16[136,1024]{1,0:T(8,128)(2,1)S(1)} %get-tuple-element.21), channel_id=1, source_target_pairs={{0,8},{4,12},{8,0},{12,4},{1,9},{5,13},{9,1},{13,5},{2,10},{6,14},... | collective-permute-start | bytes 835592 | tf_op jit(solution)/shard_map/ppermute | solution.py:263
  14.3 1.7 %collective-permute-start.5 = (bf16[128,1024]{1,0:T(8,128)(2,1)S(1)}, bf16[128,1024]{1,0:T(8,128)(2,1)S(1)}, u32[]{:S(2)}, u32[]{:S(2)}) collective-permute-start(bf16[128,1024]{1,0:T(8,128)(2,1)S(1)} %get-tuple-element.22.refs_0_), channel_id=1, source_target_pairs={{0,4},{4,0},{8,12},{12,8},{1,5},{5,1},{9,13},{13,9},{2,6},{6,2},{1... | collective-permute-start | bytes 786440 | tf_op jit(solution)/shard_map/ppermute | solution.py:263
  16.0 0.3 shard_map.75
  16.3 9.7 %collective-permute-done.2.refs_1_.got_ref.two_ref = bf16[136,1024]{1,0:T(8,128)(2,1)S(1)} collective-permute-done((bf16[136,1024]{1,0:T(8,128)(2,1)S(1)}, bf16[136,1024]{1,0:T(8,128)(2,1)S(1)}, u32[]{:S(2)}, u32[]{:S(2)}) %collective-permute-start.2) | collective-permute-done | bytes 278560 | tf_op jit(solution)/shard_map/ppermute | solution.py:263
  26.1 0.8 %collective-permute-start.8 = (bf16[128,1024]{1,0:T(8,128)(2,1)S(1)}, bf16[128,1024]{1,0:T(8,128)(2,1)S(1)}, u32[]{:S(2)}, u32[]{:S(2)}) collective-permute-start(bf16[128,1024]{1,0:T(8,128)(2,1)S(1)} %shard_map.81), channel_id=1, source_target_pairs={{0,4},{4,0},{8,12},{12,8},{1,5},{5,1},{9,13},{13,9},{2,6},{6,2},{1... | collective-permute-start | bytes 786440 | tf_op jit(solution)/shard_map/ppermute | solution.py:263
  26.9 0.4 shard_map.78
  27.4 1.6 %collective-permute-start.4 = (bf16[64,512]{1,0:T(8,128)(2,1)S(1)}, bf16[64,512]{1,0:T(8,128)(2,1)S(1)}, u32[]{:S(2)}, u32[]{:S(2)}) collective-permute-start(bf16[64,512]{1,0:T(8,128)(2,1)S(1)} %shard_map.76.refs_0_), channel_id=1, source_target_pairs={{0,2},{1,3},{2,0},{3,1},{4,6},{5,7},{6,4},{7,5},{8,10},{9,11},{10,... | collective-permute-start | bytes 196616 | tf_op jit(solution)/shard_map/ppermute | solution.py:263
  29.0 1.3 %collective-permute-start.7 = (bf16[128,512]{1,0:T(8,128)(2,1)S(1)}, bf16[128,512]{1,0:T(8,128)(2,1)S(1)}, u32[]{:S(2)}, u32[]{:S(2)}) collective-permute-start(bf16[128,512]{1,0:T(8,128)(2,1)S(1)} %shard_map.79.refs_0_), channel_id=1, source_target_pairs={{0,2},{1,3},{2,0},{3,1},{4,6},{5,7},{6,4},{7,5},{8,10},{9,11},{10,... | collective-permute-start | bytes 393224 | tf_op jit(solution)/shard_map/ppermute | solution.py:263
  30.3 3.0 %collective-permute-done.8.refs_0_ = bf16[128,1024]{1,0:T(8,128)(2,1)S(1)} collective-permute-done((bf16[128,1024]{1,0:T(8,128)(2,1)S(1)}, bf16[128,1024]{1,0:T(8,128)(2,1)S(1)}, u32[]{:S(2)}, u32[]{:S(2)}) %collective-permute-start.8) | collective-permute-done | bytes 262176 | tf_op jit(solution)/shard_map/ppermute | solution.py:263
  33.3 0.3 shard_map.82
  33.8 1.2 %collective-permute-done.9.refs_1_ = bf16[64,512]{1,0:T(8,128)(2,1)S(1)} collective-permute-done((bf16[64,512]{1,0:T(8,128)(2,1)S(1)}, bf16[64,512]{1,0:T(8,128)(2,1)S(1)}, u32[]{:S(2)}, u32[]{:S(2)}) %collective-permute-start.9) | collective-permute-done | bytes 65568 | tf_op jit(solution)/shard_map/ppermute | solution.py:263
  35.0 1.6 %collective-permute-start.10 = (bf16[64,512]{1,0:T(8,128)(2,1)S(1)}, bf16[64,512]{1,0:T(8,128)(2,1)S(1)}, u32[]{:S(2)}, u32[]{:S(2)}) collective-permute-start(bf16[64,512]{1,0:T(8,128)(2,1)S(1)} %shard_map.83.refs_0_), channel_id=1, source_target_pairs={{0,2},{1,3},{2,0},{3,1},{4,6},{5,7},{6,4},{7,5},{8,10},{9,11},{10,... | collective-permute-start | bytes 196616 | tf_op jit(solution)/shard_map/ppermute | solution.py:263
  36.6 2.7 %collective-permute-done.10.refs_1_ = bf16[64,512]{1,0:T(8,128)(2,1)S(1)} collective-permute-done((bf16[64,512]{1,0:T(8,128)(2,1)S(1)}, bf16[64,512]{1,0:T(8,128)(2,1)S(1)}, u32[]{:S(2)}, u32[]{:S(2)}) %collective-permute-start.10) | collective-permute-done | bytes 65568 | tf_op jit(solution)/shard_map/ppermute | solution.py:263
  39.4 0.2 shard_map.85
  39.6 4.6 %collective-permute-start.11 = (bf16[32,512]{1,0:T(8,128)(2,1)S(1)}, bf16[32,512]{1,0:T(8,128)(2,1)S(1)}, u32[]{:S(2)}, u32[]{:S(2)}) collective-permute-start(bf16[32,512]{1,0:T(8,128)(2,1)S(1)} %get-tuple-element.30), channel_id=1, source_target_pairs={{0,12},{4,8},{8,4},{12,0},{1,13},{5,9},{9,5},{13,1},{2,14},{6,10},... | collective-permute-start | bytes 98312 | tf_op jit(solution)/shard_map/ppermute | solution.py:263
  44.2 0.6 %collective-permute-start.13 = (bf16[32,512]{1,0:T(8,128)(2,1)S(1)}, bf16[32,512]{1,0:T(8,128)(2,1)S(1)}, u32[]{:S(2)}, u32[]{:S(2)}) collective-permute-start(bf16[32,512]{1,0:T(8,128)(2,1)S(1)} %get-tuple-element.32), channel_id=1, source_target_pairs={{0,4},{4,0},{8,12},{12,8},{1,5},{5,1},{9,13},{13,9},{2,6},{6,2},{1... | collective-permute-start | bytes 98312 | tf_op jit(solution)/shard_map/ppermute | solution.py:263
  44.9 1.4 %collective-permute-done.11.far_ref = bf16[32,512]{1,0:T(8,128)(2,1)S(1)} collective-permute-done((bf16[32,512]{1,0:T(8,128)(2,1)S(1)}, bf16[32,512]{1,0:T(8,128)(2,1)S(1)}, u32[]{:S(2)}, u32[]{:S(2)}) %collective-permute-start.11) | collective-permute-done | bytes 32800 | tf_op jit(solution)/shard_map/ppermute | solution.py:263
  46.2 2.8 %collective-permute-done.12.two_ref = bf16[32,512]{1,0:T(8,128)(2,1)S(1)} collective-permute-done((bf16[32,512]{1,0:T(8,128)(2,1)S(1)}, bf16[32,512]{1,0:T(8,128)(2,1)S(1)}, u32[]{:S(2)}, u32[]{:S(2)}) %collective-permute-start.12) | collective-permute-done | bytes 32800 | tf_op jit(solution)/shard_map/ppermute | solution.py:263
  49.0 0.7 %shard_map.87 = bf16[32,2048]{1,0:T(8,128)(2,1)} custom-call(bf16[32,1024]{1,0:T(8,128)(2,1)S(1)} %shard_map.86.held_ref, bf16[32,512]{1,0:T(8,128)(2,1)S(1)} %collective-permute-done.12.two_ref, bf16[32,512]{1,0:T(8,128)(2,1)S(1)} %collective-permute-done.13.one_ref), custom_call_target="tpu_custom_call" | custom-call | bytes 262144 | tf_op jit(solution)/shard_map/pallas_call | solution.py:252
  (33 shorter events, 0.4 us)
Async XLA Ops:
  0.0 10.3 %copy-start.2 = (bf16[128,1024]{1,0:T(8,128)(2,1)S(1)}, bf16[128,1024]{1,0:T(8,128)(2,1)}, u32[]{:S(2)}) copy-start(bf16[128,1024]{1,0:T(8,128)(2,1)} %q_ref.1) | copy-start | bytes 786436
  0.0 10.3 %copy-start.3 = (bf16[128,256]{1,0:T(8,128)(2,1)S(1)}, bf16[128,256]{1,0:T(8,128)(2,1)}, u32[]{:S(2)}) copy-start(bf16[128,256]{1,0:T(8,128)(2,1)} %k_ref.3) | copy-start | bytes 196612
  0.0 10.3 %copy-start.4 = (bf16[128,256]{1,0:T(8,128)(2,1)S(1)}, bf16[128,256]{1,0:T(8,128)(2,1)}, u32[]{:S(2)}) copy-start(bf16[128,256]{1,0:T(8,128)(2,1)} %v_ref.3) | copy-start | bytes 196612
  1.6 5.1 %copy-start = (s32[2]{0:T(128)S(1)}, s32[2]{0:T(128)}, u32[]{:S(2)}) copy-start(s32[2]{0:T(128)} %param.12) | copy-start | bytes 28
  1.6 8.7 %collective-permute-start.1 = (bf16[144,512]{1,0:T(8,128)(2,1)}, bf16[144,512]{1,0:T(8,128)(2,1)S(1)}, u32[]{:S(2)}, u32[]{:S(2)}) collective-permute-start(bf16[144,512]{1,0:T(8,128)(2,1)} %shard_map.73), channel_id=1, source_target_pairs={{0,4},{4,8},{8,12},{1,5},{5,9},{9,13},{2,6},{6,10},{10,14},{3,7},{... | collective-permute-start | bytes 442376 | tf_op jit(solution)/shard_map/ppermute | solution.py:303
  6.7 3.7 %copy-start.5 = (s32[128]{0:T(128)S(1)}, s32[128]{0:T(128)}, u32[]{:S(2)}) copy-start(s32[128]{0:T(128)} %param.11) | copy-start | bytes 1540
  6.7 3.7 %copy-start.6 = (s32[128]{0:T(128)S(1)}, s32[128]{0:T(128)}, u32[]{:S(2)}) copy-start(s32[128]{0:T(128)} %param.10) | copy-start | bytes 1540
  6.7 3.6 %collective-permute-start = (s32[1,2]{1,0:T(1,128)S(1)}, s32[1,2]{1,0:T(1,128)S(1)}, u32[]{:S(2)}, u32[]{:S(2)}) collective-permute-start(s32[1,2]{1,0:T(1,128)S(1)} %bitcast.3), channel_id=1, source_target_pairs={{0,4},{4,0},{8,12},{12,8},{1,5},{5,1},{9,13},{13,9},{2,6},{6,2},{1... | collective-permute-start | bytes 32 | tf_op jit(solution)/shard_map/ppermute | solution.py:263
  10.4 5.6 %copy-start.1 = (bf16[1024,512]{1,0:T(8,128)(2,1)S(1)}, bf16[1024,512]{1,0:T(8,128)(2,1)}, u32[]{:S(2)}) copy-start(bf16[1024,512]{1,0:T(8,128)(2,1)} %refs_1_.3) | copy-start | bytes 3145732
  11.1 15.0 %collective-permute-start.2 = (bf16[136,1024]{1,0:T(8,128)(2,1)S(1)}, bf16[136,1024]{1,0:T(8,128)(2,1)S(1)}, u32[]{:S(2)}, u32[]{:S(2)}) collective-permute-start(bf16[136,1024]{1,0:T(8,128)(2,1)S(1)} %get-tuple-element.21), channel_id=1, source_target_pairs={{0,8},{4,12},{8,0},{12,4},{1,9},{5,13},{9,1},{13,5},{2,10},{6,14},... | collective-permute-start | bytes 835592 | tf_op jit(solution)/shard_map/ppermute | solution.py:263
  14.3 12.6 %collective-permute-start.5 = (bf16[128,1024]{1,0:T(8,128)(2,1)S(1)}, bf16[128,1024]{1,0:T(8,128)(2,1)S(1)}, u32[]{:S(2)}, u32[]{:S(2)}) collective-permute-start(bf16[128,1024]{1,0:T(8,128)(2,1)S(1)} %get-tuple-element.22.refs_0_), channel_id=1, source_target_pairs={{0,4},{4,0},{8,12},{12,8},{1,5},{5,1},{9,13},{13,9},{2,6},{6,2},{1... | collective-permute-start | bytes 786440 | tf_op jit(solution)/shard_map/ppermute | solution.py:263
  16.3 11.1 %collective-permute-start.3 = (bf16[64,512]{1,0:T(8,128)(2,1)S(1)}, bf16[64,512]{1,0:T(8,128)(2,1)S(1)}, u32[]{:S(2)}, u32[]{:S(2)}) collective-permute-start(bf16[64,512]{1,0:T(8,128)(2,1)S(1)} %get-tuple-element.24), channel_id=1, source_target_pairs={{0,1},{1,0},{2,3},{3,2},{4,5},{5,4},{6,7},{7,6},{8,9},{9,8},{10,11... | collective-permute-start | bytes 196616 | tf_op jit(solution)/shard_map/ppermute | solution.py:263
  26.1 7.3 %collective-permute-start.8 = (bf16[128,1024]{1,0:T(8,128)(2,1)S(1)}, bf16[128,1024]{1,0:T(8,128)(2,1)S(1)}, u32[]{:S(2)}, u32[]{:S(2)}) collective-permute-start(bf16[128,1024]{1,0:T(8,128)(2,1)S(1)} %shard_map.81), channel_id=1, source_target_pairs={{0,4},{4,0},{8,12},{12,8},{1,5},{5,1},{9,13},{13,9},{2,6},{6,2},{1... | collective-permute-start | bytes 786440 | tf_op jit(solution)/shard_map/ppermute | solution.py:263
  27.3 1.7 %collective-permute-start.6 = (bf16[128,512]{1,0:T(8,128)(2,1)S(1)}, bf16[128,512]{1,0:T(8,128)(2,1)S(1)}, u32[]{:S(2)}, u32[]{:S(2)}) collective-permute-start(bf16[128,512]{1,0:T(8,128)(2,1)S(1)} %get-tuple-element.26), channel_id=1, source_target_pairs={{0,1},{1,0},{2,3},{3,2},{4,5},{5,4},{6,7},{7,6},{8,9},{9,8},{10,11... | collective-permute-start | bytes 393224 | tf_op jit(solution)/shard_map/ppermute | solution.py:263
  27.4 6.3 %collective-permute-start.4 = (bf16[64,512]{1,0:T(8,128)(2,1)S(1)}, bf16[64,512]{1,0:T(8,128)(2,1)S(1)}, u32[]{:S(2)}, u32[]{:S(2)}) collective-permute-start(bf16[64,512]{1,0:T(8,128)(2,1)S(1)} %shard_map.76.refs_0_), channel_id=1, source_target_pairs={{0,2},{1,3},{2,0},{3,1},{4,6},{5,7},{6,4},{7,5},{8,10},{9,11},{10,... | collective-permute-start | bytes 196616 | tf_op jit(solution)/shard_map/ppermute | solution.py:263
  29.0 7.6 %collective-permute-start.7 = (bf16[128,512]{1,0:T(8,128)(2,1)S(1)}, bf16[128,512]{1,0:T(8,128)(2,1)S(1)}, u32[]{:S(2)}, u32[]{:S(2)}) collective-permute-start(bf16[128,512]{1,0:T(8,128)(2,1)S(1)} %shard_map.79.refs_0_), channel_id=1, source_target_pairs={{0,2},{1,3},{2,0},{3,1},{4,6},{5,7},{6,4},{7,5},{8,10},{9,11},{10,... | collective-permute-start | bytes 393224 | tf_op jit(solution)/shard_map/ppermute | solution.py:263
  33.7 1.3 %collective-permute-start.9 = (bf16[64,512]{1,0:T(8,128)(2,1)S(1)}, bf16[64,512]{1,0:T(8,128)(2,1)S(1)}, u32[]{:S(2)}, u32[]{:S(2)}) collective-permute-start(bf16[64,512]{1,0:T(8,128)(2,1)S(1)} %get-tuple-element.28), channel_id=1, source_target_pairs={{0,1},{1,0},{2,3},{3,2},{4,5},{5,4},{6,7},{7,6},{8,9},{9,8},{10,11... | collective-permute-start | bytes 196616 | tf_op jit(solution)/shard_map/ppermute | solution.py:263
  35.0 4.3 %collective-permute-start.10 = (bf16[64,512]{1,0:T(8,128)(2,1)S(1)}, bf16[64,512]{1,0:T(8,128)(2,1)S(1)}, u32[]{:S(2)}, u32[]{:S(2)}) collective-permute-start(bf16[64,512]{1,0:T(8,128)(2,1)S(1)} %shard_map.83.refs_0_), channel_id=1, source_target_pairs={{0,2},{1,3},{2,0},{3,1},{4,6},{5,7},{6,4},{7,5},{8,10},{9,11},{10,... | collective-permute-start | bytes 196616 | tf_op jit(solution)/shard_map/ppermute | solution.py:263
  39.6 6.6 %collective-permute-start.11 = (bf16[32,512]{1,0:T(8,128)(2,1)S(1)}, bf16[32,512]{1,0:T(8,128)(2,1)S(1)}, u32[]{:S(2)}, u32[]{:S(2)}) collective-permute-start(bf16[32,512]{1,0:T(8,128)(2,1)S(1)} %get-tuple-element.30), channel_id=1, source_target_pairs={{0,12},{4,8},{8,4},{12,0},{1,13},{5,9},{9,5},{13,1},{2,14},{6,10},... | collective-permute-start | bytes 98312 | tf_op jit(solution)/shard_map/ppermute | solution.py:263
  44.2 4.8 %collective-permute-start.12 = (bf16[32,512]{1,0:T(8,128)(2,1)S(1)}, bf16[32,512]{1,0:T(8,128)(2,1)S(1)}, u32[]{:S(2)}, u32[]{:S(2)}) collective-permute-start(bf16[32,512]{1,0:T(8,128)(2,1)S(1)} %get-tuple-element.31), channel_id=1, source_target_pairs={{0,8},{4,12},{8,0},{12,4},{1,9},{5,13},{9,1},{13,5},{2,10},{6,14},... | collective-permute-start | bytes 98312 | tf_op jit(solution)/shard_map/ppermute | solution.py:263
  44.2 4.8 %collective-permute-start.13 = (bf16[32,512]{1,0:T(8,128)(2,1)S(1)}, bf16[32,512]{1,0:T(8,128)(2,1)S(1)}, u32[]{:S(2)}, u32[]{:S(2)}) collective-permute-start(bf16[32,512]{1,0:T(8,128)(2,1)S(1)} %get-tuple-element.32), channel_id=1, source_target_pairs={{0,4},{4,0},{8,12},{12,8},{1,5},{5,1},{9,13},{13,9},{2,6},{6,2},{1... | collective-permute-start | bytes 98312 | tf_op jit(solution)/shard_map/ppermute | solution.py:263

commit v13 on v11

--- a/solution.py
+++ b/solution.py
@@ -34,7 +34,7 @@
     return jnp.transpose(jnp.broadcast_to(row, (size, size)))
 
 
-def pack_kernel(k_ref, v_ref, end_ref, message_ref):
+def pack_kernel(k_ref, v_ref, end_ref, target_ref, message_ref):
     rows, width = k_ref.shape
     message_ref[pl.ds(0, rows), pl.ds(0, width)] = k_ref[...]
     message_ref[pl.ds(0, rows), pl.ds(width, width)] = v_ref[...]
@@ -44,24 +44,31 @@
     parts = jnp.where(line == 0, ends // END_PART, jnp.where(line == 1, ends % END_PART, 0))
     message_ref[pl.ds(rows, extra), :] = jnp.zeros((extra, 2 * width), jnp.bfloat16)
     message_ref[pl.ds(rows, extra), pl.ds(0, rows)] = parts.astype(jnp.float32).astype(jnp.bfloat16)
-
-
-def pack(key_rows, value_rows, ends):
+    targets = jnp.broadcast_to(target_ref[...].astype(jnp.float32), (extra, target_ref.shape[1]))
+    message_ref[pl.ds(rows, extra), pl.ds(rows, target_ref.shape[1])] = targets.astype(jnp.bfloat16)
+
+
+def pack(key_rows, value_rows, ends, targets):
     rows, width = key_rows.shape
     return pl.pallas_call(
         pack_kernel,
         out_shape=jax.ShapeDtypeStruct((rows + 16, 2 * width), jnp.bfloat16),
-        in_specs=vmem(3),
+        in_specs=vmem(4),
         out_specs=pl.BlockSpec(memory_space=pltpu.VMEM),
         cost_estimate=cost(10**9, 8 * key_rows.size),
-    )(key_rows, value_rows, ends)
-
-
-def attend_kernel(blocks, q_ref, halo_ref, k_ref, v_ref, end_ref, st_ref, own_ref, near_ref, *refs):
-    plain_ref, noted_ref = refs
-    targets = jnp.concatenate([own_ref[...], near_ref[...]], axis=1)
+    )(key_rows, value_rows, ends, targets)
+
+
+def attend_kernel(
+    blocks, q_ref, flip_ref, mid_ref, k_ref, v_ref, end_ref, st_ref, own_ref, plain_ref, noted_ref
+):
+    across = lax.axis_index("ctx") % 2 == 0
+    halo = jnp.where(across, mid_ref[...], flip_ref[...])
+    near = flip_ref[pl.ds(k_ref.shape[0], 16), pl.ds(k_ref.shape[0], HEAD_DIM)]
+    near = near[0:1, 0:blocks].astype(jnp.float32)
+    targets = jnp.concatenate([own_ref[...].astype(jnp.float32), near], axis=1)
     count = targets.shape[1]
-    targets = jnp.broadcast_to(targets.astype(jnp.float32), (8, count)).astype(jnp.bfloat16)
+    targets = jnp.broadcast_to(targets, (8, count)).astype(jnp.bfloat16)
     noted_ref[pl.ds(q_ref.shape[0], 8), :] = jnp.zeros((8, q_ref.shape[1]), jnp.bfloat16)
     noted_ref[pl.ds(q_ref.shape[0], 8), pl.ds(0, count)] = targets
     rows = q_ref.shape[0]
@@ -73,7 +80,7 @@
     half = rows // blocks // 2
     query_pos = base + lax.broadcasted_iota(jnp.int32, (rows, rows), 0)
     query_start = column(st_ref[...])
-    parts = halo_ref[pl.ds(rows, 16), pl.ds(0, rows)].astype(jnp.float32).astype(jnp.int32)
+    parts = halo[rows : rows + 16, 0:rows].astype(jnp.float32).astype(jnp.int32)
     masks = []
     for shift, key_end in ((rows, parts[0:1] * END_PART + parts[1:2]), (0, end_ref[...])):
         key_pos = base - shift + lax.broadcasted_iota(jnp.int32, (rows, rows), 1)
@@ -84,7 +91,7 @@
         keys, values = (
             jnp.concatenate(
                 [
-                    halo_ref[pl.ds(0, rows), pl.ds(first + kv * HEAD_DIM, HEAD_DIM)],
+                    halo[0:rows, first + kv * HEAD_DIM : first + (kv + 1) * HEAD_DIM],
                     ref[:, pl.ds(kv * HEAD_DIM, HEAD_DIM)],
                 ],
                 axis=0,
@@ -118,7 +125,7 @@
                     noted_ref[target_rows, lanes] = attended[first : first + half]
 
 
-def attend(blocks, queries, halo, keys, values, end, start, own, near):
+def attend(blocks, queries, flipped, mid, keys, values, end, start, own):
     rows, features = queries.shape
     sizes = (rows, rows + 8)
     return pl.pallas_call(
@@ -128,7 +135,7 @@
         out_specs=tuple(vmem(2)),
         compiler_params=params(),
         cost_estimate=cost(10 * 10**8, 0),
-    )(queries, halo, keys, values, end, start, own, near)
+    )(queries, flipped, mid, keys, values, end, start, own)
 
 
 def project_kernel(block_rows, *refs):
@@ -174,14 +181,17 @@
     )(*terms)
 
 
-def pick_kernel(blocks, half, own_ref, near_ref, two_ref, *refs):
+def note(ref, count):
+    tail = ref[pl.ds(ref.shape[0] - 8, 8), pl.ds(0, HEAD_DIM)].astype(jnp.float32)
+    return tail[0:1, 0:count].astype(jnp.int32)
+
+
+def pick_kernel(blocks, half, noted_ref, two_ref, *refs):
     sums, outs = refs[:-4], refs[-4:]
     x = lax.axis_index("tp") // 2
     c = lax.axis_index("ctx")
     pieces = [r[pl.ds(n, half), :] for r in sums for n in range(0, r.shape[0], half)]
-    tail = two_ref[pl.ds(two_ref.shape[0] - 8, 8), pl.ds(0, HEAD_DIM)].astype(jnp.float32)
-    far = tail[0:1, 0 : 2 * blocks].astype(jnp.int32)
-    targets = jnp.concatenate([own_ref[...], near_ref[...], far], axis=1)
+    targets = jnp.concatenate([note(r, 2 * blocks) for r in (noted_ref, two_ref)], axis=1)
     for k in range(4):
         wanted = (c ^ k) * blocks + x
         piece = pieces[0]
@@ -191,18 +201,18 @@
         outs[k][...] = piece
 
 
-def pick(blocks, own, near, two, sums):
+def pick(blocks, noted, two, sums):
     rows, cols = sum(s.shape[0] for s in sums), sums[0].shape[1]
     half = rows // (4 * blocks)
     out = jax.ShapeDtypeStruct((half, cols), jnp.bfloat16)
     return pl.pallas_call(
         functools.partial(pick_kernel, blocks, half),
         out_shape=(out,) * 4,
-        in_specs=vmem(3 + len(sums)),
+        in_specs=vmem(2 + len(sums)),
         out_specs=tuple(vmem(4)),
         compiler_params=params(),
         cost_estimate=cost(4 * rows * cols, 8 * rows * cols),
-    )(own, near, two, *sums)
+    )(noted, two, *sums)
 
 
 def forward_kernel(got_ref, out_ref):
@@ -299,13 +309,13 @@
     blocks = block_target.shape[0]
     block_rows = rows // blocks
     end, start = doc_end.reshape(1, rows), doc_start.reshape(1, rows)
-    message = pack(key_rows, value_rows, end)
-    halo = lax.ppermute(message, "ctx", [(0, 1), (1, 2), (2, 3)])
     own_target = block_target.reshape(1, blocks)
-    near_target = flip(after(own_target, message), "ctx", 1)
-    halo = after(halo, near_target)
+    message = pack(key_rows, value_rows, end, own_target)
+    flipped = flip(message, "ctx", 1)
+    middle = [(4 * c + t, 4 * (3 - c) + t if c in (1, 2) else 4 * c + (t ^ 1)) for c in range(4) for t in range(4)]
+    mid = lax.ppermute(message, ("ctx", "tp"), middle)
     plain, noted = attend(
-        blocks, queries, halo, key_rows, value_rows, end, start, own_target, near_target
+        blocks, queries, flipped, mid, key_rows, value_rows, end, start, own_target
     )
     rows_1, rows_2 = flip(plain, "ctx", 1), flip(noted, "ctx", 2)
     rows_3 = flip(forward(rows, rows_2), "ctx", 1)
@@ -315,7 +325,7 @@
     rows_3 = after(rows_3, share_ab)
     share_c = core_total(*project(block_rows, (rows_3,), out_weight))
     sums = (chip_total(share_ab), chip_total(share_c))
-    kept, *sent = pick(blocks, own_target, near_target, rows_2, sums)
+    kept, *sent = pick(blocks, noted, rows_2, sums)
     got_3, got_2, got_1 = (flip(sent[k - 1], "ctx", k) for k in (3, 2, 1))
     return join(hold(kept, got_3), got_2, got_1)
 

time: 48.3 us -> 47.4 us (0.981)
  starting transfers between devices: 19.5 us -> 15.3 us
  waiting for transfers between devices: 24.1 us -> 27.3 us
    ppermute x1, starting transfers between devices: 5.06 us -> 0.01 us  [small_ring(): mid = lax.ppermute(message, ('ctx', 'tp'), middle)]
    ppermute x12, waiting for transfers between devices: 24.1 us -> 27.3 us  [flip(): return lax.ppermute(array, axis, [(i, i ^ bits) for i in range(4)])]
    ppermute x12, starting transfers between devices: 14.4 us -> 15.3 us  [flip(): return lax.ppermute(array, axis, [(i, i ^ bits) for i in range(4)])]
  transfers between devices with their start and end apart: 13 -> 13, of which waited for: 9 -> 9; matrix products, arithmetic and copies ran while one was open for 0% -> 0% of each run, Pallas kernels for 2% -> 3%
where the time goes in v13:
time: 47.4 us; the launch traced here: 47.2 us
  waiting for transfers between devices  27.3 us (58%)
  starting transfers between devices  15.3 us (32%)
  Pallas kernels  4.44 us (9%)
    ppermute x12, waiting for transfers between devices, flip(): return lax.ppermute(array, axis, [(i, i ^ bits) for i in range(4)])  27.3 us
    ppermute x12, starting transfers between devices, flip(): return lax.ppermute(array, axis, [(i, i ^ bits) for i in range(4)])  15.3 us
    pallas_call x1, Pallas kernels, pack(): pl.pallas_call(pack_kernel, out_shape=jax.ShapeDtypeStruct((rows + 16, 2...  1.59 us
    pallas_call x3, Pallas kernels, project(): pl.pallas_call(functools.partial(project_kernel, block_rows), out_shape=(...  1.05 us
  transfers between devices with their start and end apart: 13, of which 9 were waited for; matrix products, arithmetic and copies ran while one was open for 0% of the time, Pallas kernels for 3%

profile of v13, /device:TPU:0, one launch (start us, length us, event | category | flops | bytes accessed | tf_op | source)
XLA Modules:
  0.0 47.2 jit_solution(8304147249519896017)
XLA Ops:
  0.0 1.6 %shard_map.73 = bf16[144,512]{1,0:T(8,128)(2,1)} custom-call(bf16[128,256]{1,0:T(8,128)(2,1)} %k_ref.3, bf16[128,256]{1,0:T(8,128)(2,1)} %v_ref.3, s32[1,128]{1,0:T(1,128)} %bitcast.3, s32[1,2]{1,0:T(1,128)} %bitcast.5), custom_call_target="tpu_custom_call" | custom-call | flops 1000000000 | bytes 262144 | tf_op jit(solution)/shard_map/pallas_call | solution.py:53
  1.6 3.1 %collective-permute-start = (bf16[144,512]{1,0:T(8,128)(2,1)}, bf16[144,512]{1,0:T(8,128)(2,1)S(1)}, u32[]{:S(2)}, u32[]{:S(2)}) collective-permute-start(bf16[144,512]{1,0:T(8,128)(2,1)} %shard_map.73), channel_id=1, source_target_pairs={{0,4},{4,0},{8,12},{12,8},{1,5},{5,1},{9,13},{13,9},{2,6},{6,2},{1... | collective-permute-start | bytes 442376 | tf_op jit(solution)/shard_map/ppermute | solution.py:273
  4.7 4.1 %collective-permute-done.flip_ref = bf16[144,512]{1,0:T(8,128)(2,1)S(1)} collective-permute-done((bf16[144,512]{1,0:T(8,128)(2,1)}, bf16[144,512]{1,0:T(8,128)(2,1)S(1)}, u32[]{:S(2)}, u32[]{:S(2)}) %collective-permute-start) | collective-permute-done | bytes 147488 | tf_op jit(solution)/shard_map/ppermute | solution.py:273
  8.8 0.7 %shard_map.74 = (bf16[128,1024]{1,0:T(8,128)(2,1)S(1)}, bf16[136,1024]{1,0:T(8,128)(2,1)S(1)}) custom-call(bf16[128,1024]{1,0:T(8,128)(2,1)S(1)} %copy-done.1, bf16[144,512]{1,0:T(8,128)(2,1)S(1)} %collective-permute-done.flip_ref, bf16[144,512]{1,0:T(8,128)(2,1)S(1)} %collective-permute-done.1.mid_ref, bf16[128,256]{1,0:T(8,128)(2,1)S(1)} %copy-done.2, ...), custom_call_target="tpu_custom_call" | custom-call | flops 1000000000 | tf_op jit(solution)/shard_map/pallas_call | solution.py:131
  9.6 3.0 %collective-permute-start.3 = (bf16[128,1024]{1,0:T(8,128)(2,1)S(1)}, bf16[128,1024]{1,0:T(8,128)(2,1)S(1)}, u32[]{:S(2)}, u32[]{:S(2)}) collective-permute-start(bf16[128,1024]{1,0:T(8,128)(2,1)S(1)} %get-tuple-element.20.refs_0_), channel_id=1, source_target_pairs={{0,4},{4,0},{8,12},{12,8},{1,5},{5,1},{9,13},{13,9},{2,6},{6,2},{1... | collective-permute-start | bytes 786440 | tf_op jit(solution)/shard_map/ppermute | solution.py:273
  12.5 1.4 %collective-permute-start.2 = (bf16[136,1024]{1,0:T(8,128)(2,1)S(1)}, bf16[136,1024]{1,0:T(8,128)(2,1)S(1)}, u32[]{:S(2)}, u32[]{:S(2)}) collective-permute-start(bf16[136,1024]{1,0:T(8,128)(2,1)S(1)} %get-tuple-element.19.noted_ref), channel_id=1, source_target_pairs={{0,8},{4,12},{8,0},{12,4},{1,9},{5,13},{9,1},{13,5},{2,10},{6,14},... | collective-permute-start | bytes 835592 | tf_op jit(solution)/shard_map/ppermute | solution.py:273
  14.0 9.3 %collective-permute-done.3.refs_1_ = bf16[128,1024]{1,0:T(8,128)(2,1)S(1)} collective-permute-done((bf16[128,1024]{1,0:T(8,128)(2,1)S(1)}, bf16[128,1024]{1,0:T(8,128)(2,1)S(1)}, u32[]{:S(2)}, u32[]{:S(2)}) %collective-permute-start.3) | collective-permute-done | bytes 262176 | tf_op jit(solution)/shard_map/ppermute | solution.py:273
  23.3 0.4 shard_map.75
  23.7 0.1 collective-permute-start.4
  23.8 2.9 %collective-permute-done.2.refs_0_.got_ref.two_ref = bf16[136,1024]{1,0:T(8,128)(2,1)S(1)} collective-permute-done((bf16[136,1024]{1,0:T(8,128)(2,1)S(1)}, bf16[136,1024]{1,0:T(8,128)(2,1)S(1)}, u32[]{:S(2)}, u32[]{:S(2)}) %collective-permute-start.2) | collective-permute-done | bytes 278560 | tf_op jit(solution)/shard_map/ppermute | solution.py:273
  26.8 0.3 shard_map.77
  27.2 1.2 %collective-permute-done.5.got_ref = bf16[64,512]{1,0:T(8,128)(2,1)S(1)} collective-permute-done((bf16[64,512]{1,0:T(8,128)(2,1)S(1)}, bf16[64,512]{1,0:T(8,128)(2,1)S(1)}, u32[]{:S(2)}, u32[]{:S(2)}) %collective-permute-start.5) | collective-permute-done | bytes 65568 | tf_op jit(solution)/shard_map/ppermute | solution.py:273
  28.5 1.6 %collective-permute-start.6 = (bf16[192,512]{1,0:T(8,128)(2,1)S(1)}, bf16[192,512]{1,0:T(8,128)(2,1)S(1)}, u32[]{:S(2)}, u32[]{:S(2)}) collective-permute-start(bf16[192,512]{1,0:T(8,128)(2,1)S(1)} %shard_map.78.refs_0_), channel_id=1, source_target_pairs={{0,2},{1,3},{2,0},{3,1},{4,6},{5,7},{6,4},{7,5},{8,10},{9,11},{10,... | collective-permute-start | bytes 589832 | tf_op jit(solution)/shard_map/ppermute | solution.py:273
  30.1 3.1 %collective-permute-done.7.refs_0_ = bf16[128,1024]{1,0:T(8,128)(2,1)S(1)} collective-permute-done((bf16[128,1024]{1,0:T(8,128)(2,1)S(1)}, bf16[128,1024]{1,0:T(8,128)(2,1)S(1)}, u32[]{:S(2)}, u32[]{:S(2)}) %collective-permute-start.7) | collective-permute-done | bytes 262176 | tf_op jit(solution)/shard_map/ppermute | solution.py:273
  33.1 0.3 shard_map.81
  33.5 1.2 %collective-permute-done.8.refs_1_ = bf16[64,512]{1,0:T(8,128)(2,1)S(1)} collective-permute-done((bf16[64,512]{1,0:T(8,128)(2,1)S(1)}, bf16[64,512]{1,0:T(8,128)(2,1)S(1)}, u32[]{:S(2)}, u32[]{:S(2)}) %collective-permute-start.8) | collective-permute-done | bytes 65568 | tf_op jit(solution)/shard_map/ppermute | solution.py:273
  34.8 1.6 %collective-permute-start.9 = (bf16[64,512]{1,0:T(8,128)(2,1)S(1)}, bf16[64,512]{1,0:T(8,128)(2,1)S(1)}, u32[]{:S(2)}, u32[]{:S(2)}) collective-permute-start(bf16[64,512]{1,0:T(8,128)(2,1)S(1)} %shard_map.82.refs_0_), channel_id=1, source_target_pairs={{0,2},{1,3},{2,0},{3,1},{4,6},{5,7},{6,4},{7,5},{8,10},{9,11},{10,... | collective-permute-start | bytes 196616 | tf_op jit(solution)/shard_map/ppermute | solution.py:273
  36.4 2.7 %collective-permute-done.9.refs_1_ = bf16[64,512]{1,0:T(8,128)(2,1)S(1)} collective-permute-done((bf16[64,512]{1,0:T(8,128)(2,1)S(1)}, bf16[64,512]{1,0:T(8,128)(2,1)S(1)}, u32[]{:S(2)}, u32[]{:S(2)}) %collective-permute-start.9) | collective-permute-done | bytes 65568 | tf_op jit(solution)/shard_map/ppermute | solution.py:273
  39.1 0.2 shard_map.84
  39.4 2.4 %collective-permute-start.10 = (bf16[32,512]{1,0:T(8,128)(2,1)S(1)}, bf16[32,512]{1,0:T(8,128)(2,1)S(1)}, u32[]{:S(2)}, u32[]{:S(2)}) collective-permute-start(bf16[32,512]{1,0:T(8,128)(2,1)S(1)} %get-tuple-element.30), channel_id=1, source_target_pairs={{0,12},{4,8},{8,4},{12,0},{1,13},{5,9},{9,5},{13,1},{2,14},{6,10},... | collective-permute-start | bytes 98312 | tf_op jit(solution)/shard_map/ppermute | solution.py:273
  41.8 2.1 %collective-permute-start.12 = (bf16[32,512]{1,0:T(8,128)(2,1)S(1)}, bf16[32,512]{1,0:T(8,128)(2,1)S(1)}, u32[]{:S(2)}, u32[]{:S(2)}) collective-permute-start(bf16[32,512]{1,0:T(8,128)(2,1)S(1)} %get-tuple-element.32), channel_id=1, source_target_pairs={{0,4},{4,0},{8,12},{12,8},{1,5},{5,1},{9,13},{13,9},{2,6},{6,2},{1... | collective-permute-start | bytes 98312 | tf_op jit(solution)/shard_map/ppermute | solution.py:273
  43.8 1.3 %collective-permute-done.10.far_ref = bf16[32,512]{1,0:T(8,128)(2,1)S(1)} collective-permute-done((bf16[32,512]{1,0:T(8,128)(2,1)S(1)}, bf16[32,512]{1,0:T(8,128)(2,1)S(1)}, u32[]{:S(2)}, u32[]{:S(2)}) %collective-permute-start.10) | collective-permute-done | bytes 32800 | tf_op jit(solution)/shard_map/ppermute | solution.py:273
  45.2 1.4 %collective-permute-done.11.two_ref = bf16[32,512]{1,0:T(8,128)(2,1)S(1)} collective-permute-done((bf16[32,512]{1,0:T(8,128)(2,1)S(1)}, bf16[32,512]{1,0:T(8,128)(2,1)S(1)}, u32[]{:S(2)}, u32[]{:S(2)}) %collective-permute-start.11) | collective-permute-done | bytes 32800 | tf_op jit(solution)/shard_map/ppermute | solution.py:273
  46.6 0.7 %shard_map.86 = bf16[32,2048]{1,0:T(8,128)(2,1)} custom-call(bf16[32,1024]{1,0:T(8,128)(2,1)S(1)} %shard_map.85.held_ref, bf16[32,512]{1,0:T(8,128)(2,1)S(1)} %collective-permute-done.11.two_ref, bf16[32,512]{1,0:T(8,128)(2,1)S(1)} %collective-permute-done.12.one_ref), custom_call_target="tpu_custom_call" | custom-call | bytes 262144 | tf_op jit(solution)/shard_map/pallas_call | solution.py:262
  (30 shorter events, 0.4 us)
Async XLA Ops:
  0.0 8.8 %copy-start.1 = (bf16[128,1024]{1,0:T(8,128)(2,1)S(1)}, bf16[128,1024]{1,0:T(8,128)(2,1)}, u32[]{:S(2)}) copy-start(bf16[128,1024]{1,0:T(8,128)(2,1)} %q_ref.1) | copy-start | bytes 786436
  0.0 8.8 %copy-start.2 = (bf16[128,256]{1,0:T(8,128)(2,1)S(1)}, bf16[128,256]{1,0:T(8,128)(2,1)}, u32[]{:S(2)}) copy-start(bf16[128,256]{1,0:T(8,128)(2,1)} %k_ref.3) | copy-start | bytes 196612
  0.0 8.8 %copy-start.3 = (bf16[128,256]{1,0:T(8,128)(2,1)S(1)}, bf16[128,256]{1,0:T(8,128)(2,1)}, u32[]{:S(2)}) copy-start(bf16[128,256]{1,0:T(8,128)(2,1)} %v_ref.3) | copy-start | bytes 196612
  1.6 7.2 %copy-start.4 = (s32[128]{0:T(128)S(1)}, s32[128]{0:T(128)}, u32[]{:S(2)}) copy-start(s32[128]{0:T(128)} %param.11) | copy-start | bytes 1540
  1.6 7.2 %copy-start.5 = (s32[2]{0:T(128)S(1)}, s32[2]{0:T(128)}, u32[]{:S(2)}) copy-start(s32[2]{0:T(128)} %param.12) | copy-start | bytes 28
  1.6 7.2 %copy-start.6 = (s32[128]{0:T(128)S(1)}, s32[128]{0:T(128)}, u32[]{:S(2)}) copy-start(s32[128]{0:T(128)} %param.10) | copy-start | bytes 1540
  1.6 7.1 %collective-permute-start = (bf16[144,512]{1,0:T(8,128)(2,1)}, bf16[144,512]{1,0:T(8,128)(2,1)S(1)}, u32[]{:S(2)}, u32[]{:S(2)}) collective-permute-start(bf16[144,512]{1,0:T(8,128)(2,1)} %shard_map.73), channel_id=1, source_target_pairs={{0,4},{4,0},{8,12},{12,8},{1,5},{5,1},{9,13},{13,9},{2,6},{6,2},{1... | collective-permute-start | bytes 442376 | tf_op jit(solution)/shard_map/ppermute | solution.py:273
  4.7 4.1 %collective-permute-start.1 = (bf16[144,512]{1,0:T(8,128)(2,1)}, bf16[144,512]{1,0:T(8,128)(2,1)S(1)}, u32[]{:S(2)}, u32[]{:S(2)}) collective-permute-start(bf16[144,512]{1,0:T(8,128)(2,1)} %shard_map.73), channel_id=1, source_target_pairs={{0,1},{1,0},{2,3},{3,2},{4,8},{5,9},{6,10},{7,11},{8,4},{9,5},{10,... | collective-permute-start | bytes 442376 | tf_op jit(solution)/shard_map/ppermute | solution.py:316
  8.8 14.5 %copy-start = (bf16[1024,512]{1,0:T(8,128)(2,1)S(1)}, bf16[1024,512]{1,0:T(8,128)(2,1)}, u32[]{:S(2)}) copy-start(bf16[1024,512]{1,0:T(8,128)(2,1)} %refs_1_.3) | copy-start | bytes 3145732
  9.6 13.7 %collective-permute-start.3 = (bf16[128,1024]{1,0:T(8,128)(2,1)S(1)}, bf16[128,1024]{1,0:T(8,128)(2,1)S(1)}, u32[]{:S(2)}, u32[]{:S(2)}) collective-permute-start(bf16[128,1024]{1,0:T(8,128)(2,1)S(1)} %get-tuple-element.20.refs_0_), channel_id=1, source_target_pairs={{0,4},{4,0},{8,12},{12,8},{1,5},{5,1},{9,13},{13,9},{2,6},{6,2},{1... | collective-permute-start | bytes 786440 | tf_op jit(solution)/shard_map/ppermute | solution.py:273
  12.5 14.2 %collective-permute-start.2 = (bf16[136,1024]{1,0:T(8,128)(2,1)S(1)}, bf16[136,1024]{1,0:T(8,128)(2,1)S(1)}, u32[]{:S(2)}, u32[]{:S(2)}) collective-permute-start(bf16[136,1024]{1,0:T(8,128)(2,1)S(1)} %get-tuple-element.19.noted_ref), channel_id=1, source_target_pairs={{0,8},{4,12},{8,0},{12,4},{1,9},{5,13},{9,1},{13,5},{2,10},{6,14},... | collective-permute-start | bytes 835592 | tf_op jit(solution)/shard_map/ppermute | solution.py:273
  23.7 3.1 %collective-permute-start.4 = (bf16[128,512]{1,0:T(8,128)(2,1)S(1)}, bf16[128,512]{1,0:T(8,128)(2,1)S(1)}, u32[]{:S(2)}, u32[]{:S(2)}) collective-permute-start(bf16[128,512]{1,0:T(8,128)(2,1)S(1)} %get-tuple-element.22), channel_id=1, source_target_pairs={{0,1},{1,0},{2,3},{3,2},{4,5},{5,4},{6,7},{7,6},{8,9},{9,8},{10,11... | collective-permute-start | bytes 393224 | tf_op jit(solution)/shard_map/ppermute | solution.py:273
  26.7 6.4 %collective-permute-start.7 = (bf16[128,1024]{1,0:T(8,128)(2,1)S(1)}, bf16[128,1024]{1,0:T(8,128)(2,1)S(1)}, u32[]{:S(2)}, u32[]{:S(2)}) collective-permute-start(bf16[128,1024]{1,0:T(8,128)(2,1)S(1)} %shard_map.80), channel_id=1, source_target_pairs={{0,4},{4,0},{8,12},{12,8},{1,5},{5,1},{9,13},{13,9},{2,6},{6,2},{1... | collective-permute-start | bytes 786440 | tf_op jit(solution)/shard_map/ppermute | solution.py:273
  27.1 1.3 %collective-permute-start.5 = (bf16[64,512]{1,0:T(8,128)(2,1)S(1)}, bf16[64,512]{1,0:T(8,128)(2,1)S(1)}, u32[]{:S(2)}, u32[]{:S(2)}) collective-permute-start(bf16[64,512]{1,0:T(8,128)(2,1)S(1)} %get-tuple-element.25), channel_id=1, source_target_pairs={{0,1},{1,0},{2,3},{3,2},{4,5},{5,4},{6,7},{7,6},{8,9},{9,8},{10,11... | collective-permute-start | bytes 196616 | tf_op jit(solution)/shard_map/ppermute | solution.py:273
  28.5 7.9 %collective-permute-start.6 = (bf16[192,512]{1,0:T(8,128)(2,1)S(1)}, bf16[192,512]{1,0:T(8,128)(2,1)S(1)}, u32[]{:S(2)}, u32[]{:S(2)}) collective-permute-start(bf16[192,512]{1,0:T(8,128)(2,1)S(1)} %shard_map.78.refs_0_), channel_id=1, source_target_pairs={{0,2},{1,3},{2,0},{3,1},{4,6},{5,7},{6,4},{7,5},{8,10},{9,11},{10,... | collective-permute-start | bytes 589832 | tf_op jit(solution)/shard_map/ppermute | solution.py:273
  33.5 1.3 %collective-permute-start.8 = (bf16[64,512]{1,0:T(8,128)(2,1)S(1)}, bf16[64,512]{1,0:T(8,128)(2,1)S(1)}, u32[]{:S(2)}, u32[]{:S(2)}) collective-permute-start(bf16[64,512]{1,0:T(8,128)(2,1)S(1)} %get-tuple-element.28), channel_id=1, source_target_pairs={{0,1},{1,0},{2,3},{3,2},{4,5},{5,4},{6,7},{7,6},{8,9},{9,8},{10,11... | collective-permute-start | bytes 196616 | tf_op jit(solution)/shard_map/ppermute | solution.py:273
  34.8 4.3 %collective-permute-start.9 = (bf16[64,512]{1,0:T(8,128)(2,1)S(1)}, bf16[64,512]{1,0:T(8,128)(2,1)S(1)}, u32[]{:S(2)}, u32[]{:S(2)}) collective-permute-start(bf16[64,512]{1,0:T(8,128)(2,1)S(1)} %shard_map.82.refs_0_), channel_id=1, source_target_pairs={{0,2},{1,3},{2,0},{3,1},{4,6},{5,7},{6,4},{7,5},{8,10},{9,11},{10,... | collective-permute-start | bytes 196616 | tf_op jit(solution)/shard_map/ppermute | solution.py:273
  39.4 5.8 %collective-permute-start.10 = (bf16[32,512]{1,0:T(8,128)(2,1)S(1)}, bf16[32,512]{1,0:T(8,128)(2,1)S(1)}, u32[]{:S(2)}, u32[]{:S(2)}) collective-permute-start(bf16[32,512]{1,0:T(8,128)(2,1)S(1)} %get-tuple-element.30), channel_id=1, source_target_pairs={{0,12},{4,8},{8,4},{12,0},{1,13},{5,9},{9,5},{13,1},{2,14},{6,10},... | collective-permute-start | bytes 98312 | tf_op jit(solution)/shard_map/ppermute | solution.py:273
  41.7 4.8 %collective-permute-start.11 = (bf16[32,512]{1,0:T(8,128)(2,1)S(1)}, bf16[32,512]{1,0:T(8,128)(2,1)S(1)}, u32[]{:S(2)}, u32[]{:S(2)}) collective-permute-start(bf16[32,512]{1,0:T(8,128)(2,1)S(1)} %get-tuple-element.31), channel_id=1, source_target_pairs={{0,8},{4,12},{8,0},{12,4},{1,9},{5,13},{9,1},{13,5},{2,10},{6,14},... | collective-permute-start | bytes 98312 | tf_op jit(solution)/shard_map/ppermute | solution.py:273
  41.8 4.8 %collective-permute-start.12 = (bf16[32,512]{1,0:T(8,128)(2,1)S(1)}, bf16[32,512]{1,0:T(8,128)(2,1)S(1)}, u32[]{:S(2)}, u32[]{:S(2)}) collective-permute-start(bf16[32,512]{1,0:T(8,128)(2,1)S(1)} %get-tuple-element.32), channel_id=1, source_target_pairs={{0,4},{4,0},{8,12},{12,8},{1,5},{5,1},{9,13},{13,9},{2,6},{6,2},{1... | collective-permute-start | bytes 98312 | tf_op jit(solution)/shard_map/ppermute | solution.py:273

commit v14 on v13

--- a/solution.py
+++ b/solution.py
@@ -60,7 +60,7 @@
 
 
 def attend_kernel(
-    blocks, q_ref, flip_ref, mid_ref, k_ref, v_ref, end_ref, st_ref, own_ref, plain_ref, noted_ref
+    blocks, q_ref, flip_ref, mid_ref, k_ref, v_ref, end_ref, st_ref, own_ref, plain_ref, *part_refs
 ):
     across = lax.axis_index("ctx") % 2 == 0
     halo = jnp.where(across, mid_ref[...], flip_ref[...])
@@ -69,8 +69,9 @@
     targets = jnp.concatenate([own_ref[...].astype(jnp.float32), near], axis=1)
     count = targets.shape[1]
     targets = jnp.broadcast_to(targets, (8, count)).astype(jnp.bfloat16)
-    noted_ref[pl.ds(q_ref.shape[0], 8), :] = jnp.zeros((8, q_ref.shape[1]), jnp.bfloat16)
-    noted_ref[pl.ds(q_ref.shape[0], 8), pl.ds(0, count)] = targets
+    below = pl.ds(q_ref.shape[0] // blocks, 8)
+    part_refs[0][below, :] = jnp.zeros((8, q_ref.shape[1]), jnp.bfloat16)
+    part_refs[0][below, pl.ds(0, count)] = targets
     rows = q_ref.shape[0]
     width = k_ref.shape[1]
     kv_here = width // HEAD_DIM
@@ -122,19 +123,19 @@
                     lanes = pl.ds((kv * group + g) * HEAD_DIM, HEAD_DIM)
                     target_rows = pl.ds(p * 2 * half + place, half)
                     plain_ref[target_rows, lanes] = attended[first : first + half]
-                    noted_ref[target_rows, lanes] = attended[first : first + half]
+                    part_refs[p][pl.ds(place, half), lanes] = attended[first : first + half]
 
 
 def attend(blocks, queries, flipped, mid, keys, values, end, start, own):
     rows, features = queries.shape
-    sizes = (rows, rows + 8)
+    sizes = (rows, rows // blocks + 8) + (rows // blocks,) * (blocks - 1)
     return pl.pallas_call(
         functools.partial(attend_kernel, blocks),
         out_shape=tuple(jax.ShapeDtypeStruct((size, features), jnp.bfloat16) for size in sizes),
         in_specs=vmem(8),
-        out_specs=tuple(vmem(2)),
-        compiler_params=params(),
-        cost_estimate=cost(10 * 10**8, 0),
+        out_specs=tuple(vmem(1 + blocks)),
+        compiler_params=params(),
+        cost_estimate=cost(8 * rows * rows * features, 6 * queries.size),
     )(queries, flipped, mid, keys, values, end, start, own)
 
 
@@ -227,7 +228,7 @@
         in_specs=vmem(1),
         out_specs=pl.BlockSpec(memory_space=pltpu.VMEM),
         compiler_params=params(),
-        cost_estimate=cost(0, 0),
+        cost_estimate=cost(0, 6 * out.size),
     )(got)
 
 
@@ -314,18 +315,19 @@
     flipped = flip(message, "ctx", 1)
     middle = [(4 * c + t, 4 * (3 - c) + t if c in (1, 2) else 4 * c + (t ^ 1)) for c in range(4) for t in range(4)]
     mid = lax.ppermute(message, ("ctx", "tp"), middle)
-    plain, noted = attend(
+    plain, first, second = attend(
         blocks, queries, flipped, mid, key_rows, value_rows, end, start, own_target
     )
-    rows_1, rows_2 = flip(plain, "ctx", 1), flip(noted, "ctx", 2)
-    rows_3 = flip(forward(rows, rows_2), "ctx", 1)
-    share_a = core_total(*project(block_rows, (plain, rows_1), out_weight, cost(30 * 10**8, 0)))
-    rows_2 = after(rows_2, share_a)
-    share_ab = stack_core_total(share_a, *project(block_rows, (rows_2,), out_weight))
-    rows_3 = after(rows_3, share_ab)
-    share_c = core_total(*project(block_rows, (rows_3,), out_weight))
-    sums = (chip_total(share_ab), chip_total(share_c))
-    kept, *sent = pick(blocks, noted, rows_2, sums)
+    rows_1, first_2, second_2 = flip(plain, "ctx", 1), flip(first, "ctx", 2), flip(second, "ctx", 2)
+    first_3, second_3 = flip(forward(block_rows, first_2), "ctx", 1), flip(second_2, "ctx", 1)
+    share_a = core_total(*project(block_rows, (plain, rows_1), out_weight, cost(1 * 10**8, 0)))
+    first_2 = after(first_2, share_a)
+    second_2 = after(second_2, share_a)
+    share_b = stack_core_total(share_a, *project(block_rows, (first_2, second_2), out_weight))
+    first_3 = after(first_3, share_b)
+    share_c = core_total(*project(block_rows, (first_3, second_3), out_weight, cost(100 * 10**8, 0)))
+    sums = (chip_total(share_b), chip_total(share_c))
+    kept, *sent = pick(blocks, first, first_2, sums)
     got_3, got_2, got_1 = (flip(sent[k - 1], "ctx", k) for k in (3, 2, 1))
     return join(hold(kept, got_3), got_2, got_1)
 

time: 47.4 us -> 46.7 us (0.985)
  waiting for transfers between devices: 27.3 us -> 23.6 us
  starting transfers between devices: 15.3 us -> 18.2 us
    ppermute x12 -> x14, waiting for transfers between devices: 27.3 us -> 23.6 us  [flip(): return lax.ppermute(array, axis, [(i, i ^ bits) for i in range(4)])]
    ppermute x12 -> x14, starting transfers between devices: 15.3 us -> 18.2 us  [flip(): return lax.ppermute(array, axis, [(i, i ^ bits) for i in range(4)])]
  transfers between devices with their start and end apart: 13 -> 15, of which waited for: 9 -> 10; matrix products, arithmetic and copies ran while one was open for 0% -> 0% of each run, Pallas kernels for 3% -> 3%
where the time goes in v14:
time: 46.7 us; the launch traced here: 46.5 us
  waiting for transfers between devices  23.6 us (51%)
  starting transfers between devices  18.2 us (39%)
  Pallas kernels  4.5 us (10%)
    ppermute x14, waiting for transfers between devices, flip(): return lax.ppermute(array, axis, [(i, i ^ bits) for i in range(4)])  23.6 us
    ppermute x14, starting transfers between devices, flip(): return lax.ppermute(array, axis, [(i, i ^ bits) for i in range(4)])  18.2 us
    pallas_call x1, Pallas kernels, pack(): pl.pallas_call(pack_kernel, out_shape=jax.ShapeDtypeStruct((rows + 16, 2...  1.66 us
    pallas_call x3, Pallas kernels, project(): pl.pallas_call(functools.partial(project_kernel, block_rows), out_shape=(...  1.05 us
  transfers between devices with their start and end apart: 15, of which 10 were waited for; matrix products, arithmetic and copies ran while one was open for 0% of the time, Pallas kernels for 3%

profile of v14, /device:TPU:0, one launch (start us, length us, event | category | flops | bytes accessed | tf_op | source)
XLA Modules:
  0.0 46.5 jit_solution(785531453709755372)
XLA Ops:
  0.0 1.7 %shard_map.73 = bf16[144,512]{1,0:T(8,128)(2,1)} custom-call(bf16[128,256]{1,0:T(8,128)(2,1)} %k_ref.3, bf16[128,256]{1,0:T(8,128)(2,1)} %v_ref.3, s32[1,128]{1,0:T(1,128)} %bitcast.3, s32[1,2]{1,0:T(1,128)} %bitcast.5), custom_call_target="tpu_custom_call" | custom-call | flops 1000000000 | bytes 262144 | tf_op jit(solution)/shard_map/pallas_call | solution.py:53
  1.7 3.1 %collective-permute-start = (bf16[144,512]{1,0:T(8,128)(2,1)}, bf16[144,512]{1,0:T(8,128)(2,1)S(1)}, u32[]{:S(2)}, u32[]{:S(2)}) collective-permute-start(bf16[144,512]{1,0:T(8,128)(2,1)} %shard_map.73), channel_id=1, source_target_pairs={{0,4},{4,0},{8,12},{12,8},{1,5},{5,1},{9,13},{13,9},{2,6},{6,2},{1... | collective-permute-start | bytes 442376 | tf_op jit(solution)/shard_map/ppermute | solution.py:274
  4.8 4.1 %collective-permute-done.flip_ref = bf16[144,512]{1,0:T(8,128)(2,1)S(1)} collective-permute-done((bf16[144,512]{1,0:T(8,128)(2,1)}, bf16[144,512]{1,0:T(8,128)(2,1)S(1)}, u32[]{:S(2)}, u32[]{:S(2)}) %collective-permute-start) | collective-permute-done | bytes 147488 | tf_op jit(solution)/shard_map/ppermute | solution.py:274
  8.9 0.7 %shard_map.74 = (bf16[128,1024]{1,0:T(8,128)(2,1)S(1)}, bf16[72,1024]{1,0:T(8,128)(2,1)S(1)}, bf16[64,1024]{1,0:T(8,128)(2,1)S(1)}) custom-call(bf16[128,1024]{1,0:T(8,128)(2,1)S(1)} %copy-done.1, bf16[144,512]{1,0:T(8,128)(2,1)S(1)} %collective-permute-done.flip_ref, bf16[144,512]{1,0:T(8,128)(2,1)S(1)} %collective-permute-done.1.mid_ref, ...), custom_call_target="tpu_custom_call" | custom-call | flops 134217728 | bytes 786432 | tf_op jit(solution)/shard_map/pallas_call | solution.py:132
  9.6 3.0 %collective-permute-start.3 = (bf16[128,1024]{1,0:T(8,128)(2,1)S(1)}, bf16[128,1024]{1,0:T(8,128)(2,1)S(1)}, u32[]{:S(2)}, u32[]{:S(2)}) collective-permute-start(bf16[128,1024]{1,0:T(8,128)(2,1)S(1)} %get-tuple-element.22.refs_0_), channel_id=1, source_target_pairs={{0,4},{4,0},{8,12},{12,8},{1,5},{5,1},{9,13},{13,9},{2,6},{6,2},{1... | collective-permute-start | bytes 786440 | tf_op jit(solution)/shard_map/ppermute | solution.py:274
  12.6 1.4 %collective-permute-start.2 = (bf16[72,1024]{1,0:T(8,128)(2,1)S(1)}, bf16[72,1024]{1,0:T(8,128)(2,1)S(1)}, u32[]{:S(2)}, u32[]{:S(2)}) collective-permute-start(bf16[72,1024]{1,0:T(8,128)(2,1)S(1)} %get-tuple-element.21.noted_ref), channel_id=1, source_target_pairs={{0,8},{4,12},{8,0},{12,4},{1,9},{5,13},{9,1},{13,5},{2,10},{6,14},... | collective-permute-start | bytes 442376 | tf_op jit(solution)/shard_map/ppermute | solution.py:274
  14.0 1.5 %collective-permute-start.5 = (bf16[64,1024]{1,0:T(8,128)(2,1)S(1)}, bf16[64,1024]{1,0:T(8,128)(2,1)S(1)}, u32[]{:S(2)}, u32[]{:S(2)}) collective-permute-start(bf16[64,1024]{1,0:T(8,128)(2,1)S(1)} %get-tuple-element.26), channel_id=1, source_target_pairs={{0,8},{4,12},{8,0},{12,4},{1,9},{5,13},{9,1},{13,5},{2,10},{6,14},... | collective-permute-start | bytes 393224 | tf_op jit(solution)/shard_map/ppermute | solution.py:274
  15.5 7.8 %collective-permute-done.3.refs_1_ = bf16[128,1024]{1,0:T(8,128)(2,1)S(1)} collective-permute-done((bf16[128,1024]{1,0:T(8,128)(2,1)S(1)}, bf16[128,1024]{1,0:T(8,128)(2,1)S(1)}, u32[]{:S(2)}, u32[]{:S(2)}) %collective-permute-start.3) | collective-permute-done | bytes 262176 | tf_op jit(solution)/shard_map/ppermute | solution.py:274
  23.3 0.4 shard_map.75
  23.9 1.4 %collective-permute-start.8 = (bf16[64,1024]{1,0:T(8,128)(2,1)S(1)}, bf16[64,1024]{1,0:T(8,128)(2,1)S(1)}, u32[]{:S(2)}, u32[]{:S(2)}) collective-permute-start(bf16[64,1024]{1,0:T(8,128)(2,1)S(1)} %shard_map.80), channel_id=1, source_target_pairs={{0,4},{4,0},{8,12},{12,8},{1,5},{5,1},{9,13},{13,9},{2,6},{6,2},{1... | collective-permute-start | bytes 393224 | tf_op jit(solution)/shard_map/ppermute | solution.py:274
  25.3 1.4 %collective-permute-done.5.refs_1_ = bf16[64,1024]{1,0:T(8,128)(2,1)S(1)} collective-permute-done((bf16[64,1024]{1,0:T(8,128)(2,1)S(1)}, bf16[64,1024]{1,0:T(8,128)(2,1)S(1)}, u32[]{:S(2)}, u32[]{:S(2)}) %collective-permute-start.5) | collective-permute-done | bytes 131104 | tf_op jit(solution)/shard_map/ppermute | solution.py:274
  26.8 0.3 shard_map.77
  27.2 1.2 %collective-permute-done.6.got_ref = bf16[64,512]{1,0:T(8,128)(2,1)S(1)} collective-permute-done((bf16[64,512]{1,0:T(8,128)(2,1)S(1)}, bf16[64,512]{1,0:T(8,128)(2,1)S(1)}, u32[]{:S(2)}, u32[]{:S(2)}) %collective-permute-start.6) | collective-permute-done | bytes 65568 | tf_op jit(solution)/shard_map/ppermute | solution.py:274
  28.5 1.6 %collective-permute-start.7 = (bf16[192,512]{1,0:T(8,128)(2,1)S(1)}, bf16[192,512]{1,0:T(8,128)(2,1)S(1)}, u32[]{:S(2)}, u32[]{:S(2)}) collective-permute-start(bf16[192,512]{1,0:T(8,128)(2,1)S(1)} %shard_map.78.refs_0_), channel_id=1, source_target_pairs={{0,2},{1,3},{2,0},{3,1},{4,6},{5,7},{6,4},{7,5},{8,10},{9,11},{10,... | collective-permute-start | bytes 589832 | tf_op jit(solution)/shard_map/ppermute | solution.py:274
  30.2 2.4 %collective-permute-done.9.refs_1_ = bf16[64,1024]{1,0:T(8,128)(2,1)S(1)} collective-permute-done((bf16[64,1024]{1,0:T(8,128)(2,1)S(1)}, bf16[64,1024]{1,0:T(8,128)(2,1)S(1)}, u32[]{:S(2)}, u32[]{:S(2)}) %collective-permute-start.9) | collective-permute-done | bytes 131104 | tf_op jit(solution)/shard_map/ppermute | solution.py:274
  32.6 0.3 shard_map.81
  33.0 1.2 %collective-permute-done.10.refs_1_ = bf16[64,512]{1,0:T(8,128)(2,1)S(1)} collective-permute-done((bf16[64,512]{1,0:T(8,128)(2,1)S(1)}, bf16[64,512]{1,0:T(8,128)(2,1)S(1)}, u32[]{:S(2)}, u32[]{:S(2)}) %collective-permute-start.10) | collective-permute-done | bytes 65568 | tf_op jit(solution)/shard_map/ppermute | solution.py:274
  34.3 1.6 %collective-permute-start.11 = (bf16[64,512]{1,0:T(8,128)(2,1)S(1)}, bf16[64,512]{1,0:T(8,128)(2,1)S(1)}, u32[]{:S(2)}, u32[]{:S(2)}) collective-permute-start(bf16[64,512]{1,0:T(8,128)(2,1)S(1)} %shard_map.82.refs_0_), channel_id=1, source_target_pairs={{0,2},{1,3},{2,0},{3,1},{4,6},{5,7},{6,4},{7,5},{8,10},{9,11},{10,... | collective-permute-start | bytes 196616 | tf_op jit(solution)/shard_map/ppermute | solution.py:274
  35.9 2.8 %collective-permute-done.11.refs_1_ = bf16[64,512]{1,0:T(8,128)(2,1)S(1)} collective-permute-done((bf16[64,512]{1,0:T(8,128)(2,1)S(1)}, bf16[64,512]{1,0:T(8,128)(2,1)S(1)}, u32[]{:S(2)}, u32[]{:S(2)}) %collective-permute-start.11) | collective-permute-done | bytes 65568 | tf_op jit(solution)/shard_map/ppermute | solution.py:274
  39.0 2.1 %collective-permute-start.12 = (bf16[32,512]{1,0:T(8,128)(2,1)S(1)}, bf16[32,512]{1,0:T(8,128)(2,1)S(1)}, u32[]{:S(2)}, u32[]{:S(2)}) collective-permute-start(bf16[32,512]{1,0:T(8,128)(2,1)S(1)} %get-tuple-element.34), channel_id=1, source_target_pairs={{0,12},{4,8},{8,4},{12,0},{1,13},{5,9},{9,5},{13,1},{2,14},{6,10},... | collective-permute-start | bytes 98312 | tf_op jit(solution)/shard_map/ppermute | solution.py:274
  41.0 2.4 %collective-permute-start.14 = (bf16[32,512]{1,0:T(8,128)(2,1)S(1)}, bf16[32,512]{1,0:T(8,128)(2,1)S(1)}, u32[]{:S(2)}, u32[]{:S(2)}) collective-permute-start(bf16[32,512]{1,0:T(8,128)(2,1)S(1)} %get-tuple-element.36), channel_id=1, source_target_pairs={{0,4},{4,0},{8,12},{12,8},{1,5},{5,1},{9,13},{13,9},{2,6},{6,2},{1... | collective-permute-start | bytes 98312 | tf_op jit(solution)/shard_map/ppermute | solution.py:274
  43.4 1.6 %collective-permute-done.12.far_ref = bf16[32,512]{1,0:T(8,128)(2,1)S(1)} collective-permute-done((bf16[32,512]{1,0:T(8,128)(2,1)S(1)}, bf16[32,512]{1,0:T(8,128)(2,1)S(1)}, u32[]{:S(2)}, u32[]{:S(2)}) %collective-permute-start.12) | collective-permute-done | bytes 32800 | tf_op jit(solution)/shard_map/ppermute | solution.py:274
  45.0 0.8 %collective-permute-done.13.two_ref = bf16[32,512]{1,0:T(8,128)(2,1)S(1)} collective-permute-done((bf16[32,512]{1,0:T(8,128)(2,1)S(1)}, bf16[32,512]{1,0:T(8,128)(2,1)S(1)}, u32[]{:S(2)}, u32[]{:S(2)}) %collective-permute-start.13) | collective-permute-done | bytes 32800 | tf_op jit(solution)/shard_map/ppermute | solution.py:274
  45.8 0.7 %shard_map.86 = bf16[32,2048]{1,0:T(8,128)(2,1)} custom-call(bf16[32,1024]{1,0:T(8,128)(2,1)S(1)} %shard_map.85.held_ref, bf16[32,512]{1,0:T(8,128)(2,1)S(1)} %collective-permute-done.13.two_ref, bf16[32,512]{1,0:T(8,128)(2,1)S(1)} %collective-permute-done.14.one_ref), custom_call_target="tpu_custom_call" | custom-call | bytes 262144 | tf_op jit(solution)/shard_map/pallas_call | solution.py:263
  (34 shorter events, 0.9 us)
Async XLA Ops:
  0.0 8.8 %copy-start.1 = (bf16[128,1024]{1,0:T(8,128)(2,1)S(1)}, bf16[128,1024]{1,0:T(8,128)(2,1)}, u32[]{:S(2)}) copy-start(bf16[128,1024]{1,0:T(8,128)(2,1)} %q_ref.1) | copy-start | bytes 786436
  0.0 8.8 %copy-start.2 = (bf16[128,256]{1,0:T(8,128)(2,1)S(1)}, bf16[128,256]{1,0:T(8,128)(2,1)}, u32[]{:S(2)}) copy-start(bf16[128,256]{1,0:T(8,128)(2,1)} %k_ref.3) | copy-start | bytes 196612
  0.0 8.8 %copy-start.3 = (bf16[128,256]{1,0:T(8,128)(2,1)S(1)}, bf16[128,256]{1,0:T(8,128)(2,1)}, u32[]{:S(2)}) copy-start(bf16[128,256]{1,0:T(8,128)(2,1)} %v_ref.3) | copy-start | bytes 196612
  0.0 23.3 %copy-start = (bf16[1024,512]{1,0:T(8,128)(2,1)S(1)}, bf16[1024,512]{1,0:T(8,128)(2,1)}, u32[]{:S(2)}) copy-start(bf16[1024,512]{1,0:T(8,128)(2,1)} %refs_2_.5) | copy-start | bytes 3145732
  1.7 7.2 %copy-start.4 = (s32[128]{0:T(128)S(1)}, s32[128]{0:T(128)}, u32[]{:S(2)}) copy-start(s32[128]{0:T(128)} %param.11) | copy-start | bytes 1540
  1.7 7.2 %copy-start.5 = (s32[2]{0:T(128)S(1)}, s32[2]{0:T(128)}, u32[]{:S(2)}) copy-start(s32[2]{0:T(128)} %param.12) | copy-start | bytes 28
  1.7 7.2 %copy-start.6 = (s32[128]{0:T(128)S(1)}, s32[128]{0:T(128)}, u32[]{:S(2)}) copy-start(s32[128]{0:T(128)} %param.10) | copy-start | bytes 1540
  1.7 7.2 %collective-permute-start = (bf16[144,512]{1,0:T(8,128)(2,1)}, bf16[144,512]{1,0:T(8,128)(2,1)S(1)}, u32[]{:S(2)}, u32[]{:S(2)}) collective-permute-start(bf16[144,512]{1,0:T(8,128)(2,1)} %shard_map.73), channel_id=1, source_target_pairs={{0,4},{4,0},{8,12},{12,8},{1,5},{5,1},{9,13},{13,9},{2,6},{6,2},{1... | collective-permute-start | bytes 442376 | tf_op jit(solution)/shard_map/ppermute | solution.py:274
  4.8 4.1 %collective-permute-start.1 = (bf16[144,512]{1,0:T(8,128)(2,1)}, bf16[144,512]{1,0:T(8,128)(2,1)S(1)}, u32[]{:S(2)}, u32[]{:S(2)}) collective-permute-start(bf16[144,512]{1,0:T(8,128)(2,1)} %shard_map.73), channel_id=1, source_target_pairs={{0,1},{1,0},{2,3},{3,2},{4,8},{5,9},{6,10},{7,11},{8,4},{9,5},{10,... | collective-permute-start | bytes 442376 | tf_op jit(solution)/shard_map/ppermute | solution.py:317
  9.6 13.7 %collective-permute-start.3 = (bf16[128,1024]{1,0:T(8,128)(2,1)S(1)}, bf16[128,1024]{1,0:T(8,128)(2,1)S(1)}, u32[]{:S(2)}, u32[]{:S(2)}) collective-permute-start(bf16[128,1024]{1,0:T(8,128)(2,1)S(1)} %get-tuple-element.22.refs_0_), channel_id=1, source_target_pairs={{0,4},{4,0},{8,12},{12,8},{1,5},{5,1},{9,13},{13,9},{2,6},{6,2},{1... | collective-permute-start | bytes 786440 | tf_op jit(solution)/shard_map/ppermute | solution.py:274
  12.6 11.3 %collective-permute-start.2 = (bf16[72,1024]{1,0:T(8,128)(2,1)S(1)}, bf16[72,1024]{1,0:T(8,128)(2,1)S(1)}, u32[]{:S(2)}, u32[]{:S(2)}) collective-permute-start(bf16[72,1024]{1,0:T(8,128)(2,1)S(1)} %get-tuple-element.21.noted_ref), channel_id=1, source_target_pairs={{0,8},{4,12},{8,0},{12,4},{1,9},{5,13},{9,1},{13,5},{2,10},{6,14},... | collective-permute-start | bytes 442376 | tf_op jit(solution)/shard_map/ppermute | solution.py:274
  14.0 12.7 %collective-permute-start.5 = (bf16[64,1024]{1,0:T(8,128)(2,1)S(1)}, bf16[64,1024]{1,0:T(8,128)(2,1)S(1)}, u32[]{:S(2)}, u32[]{:S(2)}) collective-permute-start(bf16[64,1024]{1,0:T(8,128)(2,1)S(1)} %get-tuple-element.26), channel_id=1, source_target_pairs={{0,8},{4,12},{8,0},{12,4},{1,9},{5,13},{9,1},{13,5},{2,10},{6,14},... | collective-permute-start | bytes 393224 | tf_op jit(solution)/shard_map/ppermute | solution.py:274
  23.8 3.0 %collective-permute-start.4 = (bf16[128,512]{1,0:T(8,128)(2,1)S(1)}, bf16[128,512]{1,0:T(8,128)(2,1)S(1)}, u32[]{:S(2)}, u32[]{:S(2)}) collective-permute-start(bf16[128,512]{1,0:T(8,128)(2,1)S(1)} %get-tuple-element.24), channel_id=1, source_target_pairs={{0,1},{1,0},{2,3},{3,2},{4,5},{5,4},{6,7},{7,6},{8,9},{9,8},{10,11... | collective-permute-start | bytes 393224 | tf_op jit(solution)/shard_map/ppermute | solution.py:274
  23.9 6.4 %collective-permute-start.8 = (bf16[64,1024]{1,0:T(8,128)(2,1)S(1)}, bf16[64,1024]{1,0:T(8,128)(2,1)S(1)}, u32[]{:S(2)}, u32[]{:S(2)}) collective-permute-start(bf16[64,1024]{1,0:T(8,128)(2,1)S(1)} %shard_map.80), channel_id=1, source_target_pairs={{0,4},{4,0},{8,12},{12,8},{1,5},{5,1},{9,13},{13,9},{2,6},{6,2},{1... | collective-permute-start | bytes 393224 | tf_op jit(solution)/shard_map/ppermute | solution.py:274
  26.7 5.9 %collective-permute-start.9 = (bf16[64,1024]{1,0:T(8,128)(2,1)S(1)}, bf16[64,1024]{1,0:T(8,128)(2,1)S(1)}, u32[]{:S(2)}, u32[]{:S(2)}) collective-permute-start(bf16[64,1024]{1,0:T(8,128)(2,1)S(1)} %collective-permute-done.5.refs_1_), channel_id=1, source_target_pairs={{0,4},{4,0},{8,12},{12,8},{1,5},{5,1},{9,13},{13,9},{2,6},{6,2},{1... | collective-permute-start | bytes 393224 | tf_op jit(solution)/shard_map/ppermute | solution.py:274
  27.1 1.3 %collective-permute-start.6 = (bf16[64,512]{1,0:T(8,128)(2,1)S(1)}, bf16[64,512]{1,0:T(8,128)(2,1)S(1)}, u32[]{:S(2)}, u32[]{:S(2)}) collective-permute-start(bf16[64,512]{1,0:T(8,128)(2,1)S(1)} %get-tuple-element.29), channel_id=1, source_target_pairs={{0,1},{1,0},{2,3},{3,2},{4,5},{5,4},{6,7},{7,6},{8,9},{9,8},{10,11... | collective-permute-start | bytes 196616 | tf_op jit(solution)/shard_map/ppermute | solution.py:274
  28.5 10.2 %collective-permute-start.7 = (bf16[192,512]{1,0:T(8,128)(2,1)S(1)}, bf16[192,512]{1,0:T(8,128)(2,1)S(1)}, u32[]{:S(2)}, u32[]{:S(2)}) collective-permute-start(bf16[192,512]{1,0:T(8,128)(2,1)S(1)} %shard_map.78.refs_0_), channel_id=1, source_target_pairs={{0,2},{1,3},{2,0},{3,1},{4,6},{5,7},{6,4},{7,5},{8,10},{9,11},{10,... | collective-permute-start | bytes 589832 | tf_op jit(solution)/shard_map/ppermute | solution.py:274
  33.0 1.3 %collective-permute-start.10 = (bf16[64,512]{1,0:T(8,128)(2,1)S(1)}, bf16[64,512]{1,0:T(8,128)(2,1)S(1)}, u32[]{:S(2)}, u32[]{:S(2)}) collective-permute-start(bf16[64,512]{1,0:T(8,128)(2,1)S(1)} %get-tuple-element.32), channel_id=1, source_target_pairs={{0,1},{1,0},{2,3},{3,2},{4,5},{5,4},{6,7},{7,6},{8,9},{9,8},{10,11... | collective-permute-start | bytes 196616 | tf_op jit(solution)/shard_map/ppermute | solution.py:274
  34.3 4.3 %collective-permute-start.11 = (bf16[64,512]{1,0:T(8,128)(2,1)S(1)}, bf16[64,512]{1,0:T(8,128)(2,1)S(1)}, u32[]{:S(2)}, u32[]{:S(2)}) collective-permute-start(bf16[64,512]{1,0:T(8,128)(2,1)S(1)} %shard_map.82.refs_0_), channel_id=1, source_target_pairs={{0,2},{1,3},{2,0},{3,1},{4,6},{5,7},{6,4},{7,5},{8,10},{9,11},{10,... | collective-permute-start | bytes 196616 | tf_op jit(solution)/shard_map/ppermute | solution.py:274
  39.0 6.1 %collective-permute-start.12 = (bf16[32,512]{1,0:T(8,128)(2,1)S(1)}, bf16[32,512]{1,0:T(8,128)(2,1)S(1)}, u32[]{:S(2)}, u32[]{:S(2)}) collective-permute-start(bf16[32,512]{1,0:T(8,128)(2,1)S(1)} %get-tuple-element.34), channel_id=1, source_target_pairs={{0,12},{4,8},{8,4},{12,0},{1,13},{5,9},{9,5},{13,1},{2,14},{6,10},... | collective-permute-start | bytes 98312 | tf_op jit(solution)/shard_map/ppermute | solution.py:274
  41.0 4.8 %collective-permute-start.13 = (bf16[32,512]{1,0:T(8,128)(2,1)S(1)}, bf16[32,512]{1,0:T(8,128)(2,1)S(1)}, u32[]{:S(2)}, u32[]{:S(2)}) collective-permute-start(bf16[32,512]{1,0:T(8,128)(2,1)S(1)} %get-tuple-element.35), channel_id=1, source_target_pairs={{0,8},{4,12},{8,0},{12,4},{1,9},{5,13},{9,1},{13,5},{2,10},{6,14},... | collective-permute-start | bytes 98312 | tf_op jit(solution)/shard_map/ppermute | solution.py:274
  41.0 4.8 %collective-permute-start.14 = (bf16[32,512]{1,0:T(8,128)(2,1)S(1)}, bf16[32,512]{1,0:T(8,128)(2,1)S(1)}, u32[]{:S(2)}, u32[]{:S(2)}) collective-permute-start(bf16[32,512]{1,0:T(8,128)(2,1)S(1)} %get-tuple-element.36), channel_id=1, source_target_pairs={{0,4},{4,0},{8,12},{12,8},{1,5},{5,1},{9,13},{13,9},{2,6},{6,2},{1... | collective-permute-start | bytes 98312 | tf_op jit(solution)/shard_map/ppermute | solution.py:274

commit v15 on v14

--- a/solution.py
+++ b/solution.py
@@ -60,7 +60,7 @@
 
 
 def attend_kernel(
-    blocks, q_ref, flip_ref, mid_ref, k_ref, v_ref, end_ref, st_ref, own_ref, plain_ref, *part_refs
+    blocks, q_ref, mid_ref, flip_ref, k_ref, v_ref, end_ref, st_ref, own_ref, plain_ref, *part_refs
 ):
     across = lax.axis_index("ctx") % 2 == 0
     halo = jnp.where(across, mid_ref[...], flip_ref[...])
@@ -136,7 +136,7 @@
         out_specs=tuple(vmem(1 + blocks)),
         compiler_params=params(),
         cost_estimate=cost(8 * rows * rows * features, 6 * queries.size),
-    )(queries, flipped, mid, keys, values, end, start, own)
+    )(queries, mid, flipped, keys, values, end, start, own)
 
 
 def project_kernel(block_rows, *refs):
@@ -312,9 +312,9 @@
     end, start = doc_end.reshape(1, rows), doc_start.reshape(1, rows)
     own_target = block_target.reshape(1, blocks)
     message = pack(key_rows, value_rows, end, own_target)
-    flipped = flip(message, "ctx", 1)
     middle = [(4 * c + t, 4 * (3 - c) + t if c in (1, 2) else 4 * c + (t ^ 1)) for c in range(4) for t in range(4)]
     mid = lax.ppermute(message, ("ctx", "tp"), middle)
+    flipped = flip(message, "ctx", 1)
     plain, first, second = attend(
         blocks, queries, flipped, mid, key_rows, value_rows, end, start, own_target
     )

time: 46.7 us -> 47.4 us (1.015)
  starting transfers between devices: 18.2 us -> 19.2 us
    ppermute x1, starting transfers between devices: 0.01 us -> 0.52 us  [small_ring(): mid = lax.ppermute(message, ('ctx', 'tp'), middle)]
  transfers between devices with their start and end apart: 15 -> 15, of which waited for: 10 -> 9; matrix products, arithmetic and copies ran while one was open for 0% -> 0% of each run, Pallas kernels for 3% -> 2%
where the time goes in v15:
time: 47.4 us; the launch traced here: 47.2 us
  waiting for transfers between devices  23.4 us (49%)
  starting transfers between devices  19.2 us (41%)
  Pallas kernels  4.5 us (9%)
    ppermute x14, waiting for transfers between devices, flip(): return lax.ppermute(array, axis, [(i, i ^ bits) for i in range(4)])  23.4 us
    ppermute x14, starting transfers between devices, flip(): return lax.ppermute(array, axis, [(i, i ^ bits) for i in range(4)])  18.7 us
    pallas_call x1, Pallas kernels, pack(): pl.pallas_call(pack_kernel, out_shape=jax.ShapeDtypeStruct((rows + 16, 2...  1.66 us
    pallas_call x3, Pallas kernels, project(): pl.pallas_call(functools.partial(project_kernel, block_rows), out_shape=(...  1.05 us
  transfers between devices with their start and end apart: 15, of which 9 were waited for; matrix products, arithmetic and copies ran while one was open for 0% of the time, Pallas kernels for 2%

profile of v15, /device:TPU:0, one launch (start us, length us, event | category | flops | bytes accessed | tf_op | source)
XLA Modules:
  0.0 47.2 jit_solution(5789161024873601730)
XLA Ops:
  0.0 1.7 %shard_map.73 = bf16[144,512]{1,0:T(8,128)(2,1)} custom-call(bf16[128,256]{1,0:T(8,128)(2,1)} %k_ref.3, bf16[128,256]{1,0:T(8,128)(2,1)} %v_ref.3, s32[1,128]{1,0:T(1,128)} %bitcast.3, s32[1,2]{1,0:T(1,128)} %bitcast.5), custom_call_target="tpu_custom_call" | custom-call | flops 1000000000 | bytes 262144 | tf_op jit(solution)/shard_map/pallas_call | solution.py:53
  1.7 0.5 %collective-permute-start = (bf16[144,512]{1,0:T(8,128)(2,1)}, bf16[144,512]{1,0:T(8,128)(2,1)S(1)}, u32[]{:S(2)}, u32[]{:S(2)}) collective-permute-start(bf16[144,512]{1,0:T(8,128)(2,1)} %shard_map.73), channel_id=1, source_target_pairs={{0,1},{1,0},{2,3},{3,2},{4,8},{5,9},{6,10},{7,11},{8,4},{9,5},{10,... | collective-permute-start | bytes 442376 | tf_op jit(solution)/shard_map/ppermute | solution.py:316
  2.2 4.1 %collective-permute-start.1 = (bf16[144,512]{1,0:T(8,128)(2,1)}, bf16[144,512]{1,0:T(8,128)(2,1)S(1)}, u32[]{:S(2)}, u32[]{:S(2)}) collective-permute-start(bf16[144,512]{1,0:T(8,128)(2,1)} %shard_map.73), channel_id=1, source_target_pairs={{0,4},{4,0},{8,12},{12,8},{1,5},{5,1},{9,13},{13,9},{2,6},{6,2},{1... | collective-permute-start | bytes 442376 | tf_op jit(solution)/shard_map/ppermute | solution.py:274
  6.3 3.8 %collective-permute-done.1.flip_ref = bf16[144,512]{1,0:T(8,128)(2,1)S(1)} collective-permute-done((bf16[144,512]{1,0:T(8,128)(2,1)}, bf16[144,512]{1,0:T(8,128)(2,1)S(1)}, u32[]{:S(2)}, u32[]{:S(2)}) %collective-permute-start.1) | collective-permute-done | bytes 147488 | tf_op jit(solution)/shard_map/ppermute | solution.py:274
  10.2 0.7 %shard_map.74 = (bf16[128,1024]{1,0:T(8,128)(2,1)S(1)}, bf16[72,1024]{1,0:T(8,128)(2,1)S(1)}, bf16[64,1024]{1,0:T(8,128)(2,1)S(1)}) custom-call(bf16[128,1024]{1,0:T(8,128)(2,1)S(1)} %copy-done.1, bf16[144,512]{1,0:T(8,128)(2,1)S(1)} %collective-permute-done.mid_ref, bf16[144,512]{1,0:T(8,128)(2,1)S(1)} %collective-permute-done.1.flip_ref, ...), custom_call_target="tpu_custom_call" | custom-call | flops 134217728 | bytes 786432 | tf_op jit(solution)/shard_map/pallas_call | solution.py:132
  10.9 1.8 %collective-permute-start.3 = (bf16[128,1024]{1,0:T(8,128)(2,1)S(1)}, bf16[128,1024]{1,0:T(8,128)(2,1)S(1)}, u32[]{:S(2)}, u32[]{:S(2)}) collective-permute-start(bf16[128,1024]{1,0:T(8,128)(2,1)S(1)} %get-tuple-element.22.refs_0_), channel_id=1, source_target_pairs={{0,4},{4,0},{8,12},{12,8},{1,5},{5,1},{9,13},{13,9},{2,6},{6,2},{1... | collective-permute-start | bytes 786440 | tf_op jit(solution)/shard_map/ppermute | solution.py:274
  12.7 2.0 %collective-permute-start.2 = (bf16[72,1024]{1,0:T(8,128)(2,1)S(1)}, bf16[72,1024]{1,0:T(8,128)(2,1)S(1)}, u32[]{:S(2)}, u32[]{:S(2)}) collective-permute-start(bf16[72,1024]{1,0:T(8,128)(2,1)S(1)} %get-tuple-element.21.noted_ref), channel_id=1, source_target_pairs={{0,8},{4,12},{8,0},{12,4},{1,9},{5,13},{9,1},{13,5},{2,10},{6,14},... | collective-permute-start | bytes 442376 | tf_op jit(solution)/shard_map/ppermute | solution.py:274
  14.7 0.9 %collective-permute-start.5 = (bf16[64,1024]{1,0:T(8,128)(2,1)S(1)}, bf16[64,1024]{1,0:T(8,128)(2,1)S(1)}, u32[]{:S(2)}, u32[]{:S(2)}) collective-permute-start(bf16[64,1024]{1,0:T(8,128)(2,1)S(1)} %get-tuple-element.26), channel_id=1, source_target_pairs={{0,8},{4,12},{8,0},{12,4},{1,9},{5,13},{9,1},{13,5},{2,10},{6,14},... | collective-permute-start | bytes 393224 | tf_op jit(solution)/shard_map/ppermute | solution.py:274
  15.6 7.3 %collective-permute-done.3.refs_1_ = bf16[128,1024]{1,0:T(8,128)(2,1)S(1)} collective-permute-done((bf16[128,1024]{1,0:T(8,128)(2,1)S(1)}, bf16[128,1024]{1,0:T(8,128)(2,1)S(1)}, u32[]{:S(2)}, u32[]{:S(2)}) %collective-permute-start.3) | collective-permute-done | bytes 262176 | tf_op jit(solution)/shard_map/ppermute | solution.py:274
  22.9 0.4 shard_map.75
  23.5 2.0 %collective-permute-start.8 = (bf16[64,1024]{1,0:T(8,128)(2,1)S(1)}, bf16[64,1024]{1,0:T(8,128)(2,1)S(1)}, u32[]{:S(2)}, u32[]{:S(2)}) collective-permute-start(bf16[64,1024]{1,0:T(8,128)(2,1)S(1)} %shard_map.80), channel_id=1, source_target_pairs={{0,4},{4,0},{8,12},{12,8},{1,5},{5,1},{9,13},{13,9},{2,6},{6,2},{1... | collective-permute-start | bytes 393224 | tf_op jit(solution)/shard_map/ppermute | solution.py:274
  25.5 2.2 %collective-permute-done.5.refs_1_ = bf16[64,1024]{1,0:T(8,128)(2,1)S(1)} collective-permute-done((bf16[64,1024]{1,0:T(8,128)(2,1)S(1)}, bf16[64,1024]{1,0:T(8,128)(2,1)S(1)}, u32[]{:S(2)}, u32[]{:S(2)}) %collective-permute-start.5) | collective-permute-done | bytes 131104 | tf_op jit(solution)/shard_map/ppermute | solution.py:274
  27.7 0.3 shard_map.77
  28.1 1.2 %collective-permute-done.6.got_ref = bf16[64,512]{1,0:T(8,128)(2,1)S(1)} collective-permute-done((bf16[64,512]{1,0:T(8,128)(2,1)S(1)}, bf16[64,512]{1,0:T(8,128)(2,1)S(1)}, u32[]{:S(2)}, u32[]{:S(2)}) %collective-permute-start.6) | collective-permute-done | bytes 65568 | tf_op jit(solution)/shard_map/ppermute | solution.py:274
  29.4 1.6 %collective-permute-start.7 = (bf16[192,512]{1,0:T(8,128)(2,1)S(1)}, bf16[192,512]{1,0:T(8,128)(2,1)S(1)}, u32[]{:S(2)}, u32[]{:S(2)}) collective-permute-start(bf16[192,512]{1,0:T(8,128)(2,1)S(1)} %shard_map.78.refs_0_), channel_id=1, source_target_pairs={{0,2},{1,3},{2,0},{3,1},{4,6},{5,7},{6,4},{7,5},{8,10},{9,11},{10,... | collective-permute-start | bytes 589832 | tf_op jit(solution)/shard_map/ppermute | solution.py:274
  31.0 2.2 %collective-permute-done.9.refs_1_ = bf16[64,1024]{1,0:T(8,128)(2,1)S(1)} collective-permute-done((bf16[64,1024]{1,0:T(8,128)(2,1)S(1)}, bf16[64,1024]{1,0:T(8,128)(2,1)S(1)}, u32[]{:S(2)}, u32[]{:S(2)}) %collective-permute-start.9) | collective-permute-done | bytes 131104 | tf_op jit(solution)/shard_map/ppermute | solution.py:274
  33.6 1.2 %collective-permute-done.10.refs_1_ = bf16[64,512]{1,0:T(8,128)(2,1)S(1)} collective-permute-done((bf16[64,512]{1,0:T(8,128)(2,1)S(1)}, bf16[64,512]{1,0:T(8,128)(2,1)S(1)}, u32[]{:S(2)}, u32[]{:S(2)}) %collective-permute-start.10) | collective-permute-done | bytes 65568 | tf_op jit(solution)/shard_map/ppermute | solution.py:274
  34.9 1.6 %collective-permute-start.11 = (bf16[64,512]{1,0:T(8,128)(2,1)S(1)}, bf16[64,512]{1,0:T(8,128)(2,1)S(1)}, u32[]{:S(2)}, u32[]{:S(2)}) collective-permute-start(bf16[64,512]{1,0:T(8,128)(2,1)S(1)} %shard_map.82.refs_0_), channel_id=1, source_target_pairs={{0,2},{1,3},{2,0},{3,1},{4,6},{5,7},{6,4},{7,5},{8,10},{9,11},{10,... | collective-permute-start | bytes 196616 | tf_op jit(solution)/shard_map/ppermute | solution.py:274
  36.4 2.8 %collective-permute-done.11.refs_1_ = bf16[64,512]{1,0:T(8,128)(2,1)S(1)} collective-permute-done((bf16[64,512]{1,0:T(8,128)(2,1)S(1)}, bf16[64,512]{1,0:T(8,128)(2,1)S(1)}, u32[]{:S(2)}, u32[]{:S(2)}) %collective-permute-start.11) | collective-permute-done | bytes 65568 | tf_op jit(solution)/shard_map/ppermute | solution.py:274
  39.5 2.2 %collective-permute-start.12 = (bf16[32,512]{1,0:T(8,128)(2,1)S(1)}, bf16[32,512]{1,0:T(8,128)(2,1)S(1)}, u32[]{:S(2)}, u32[]{:S(2)}) collective-permute-start(bf16[32,512]{1,0:T(8,128)(2,1)S(1)} %get-tuple-element.34), channel_id=1, source_target_pairs={{0,12},{4,8},{8,4},{12,0},{1,13},{5,9},{9,5},{13,1},{2,14},{6,10},... | collective-permute-start | bytes 98312 | tf_op jit(solution)/shard_map/ppermute | solution.py:274
  41.8 2.2 %collective-permute-start.14 = (bf16[32,512]{1,0:T(8,128)(2,1)S(1)}, bf16[32,512]{1,0:T(8,128)(2,1)S(1)}, u32[]{:S(2)}, u32[]{:S(2)}) collective-permute-start(bf16[32,512]{1,0:T(8,128)(2,1)S(1)} %get-tuple-element.36), channel_id=1, source_target_pairs={{0,4},{4,0},{8,12},{12,8},{1,5},{5,1},{9,13},{13,9},{2,6},{6,2},{1... | collective-permute-start | bytes 98312 | tf_op jit(solution)/shard_map/ppermute | solution.py:274
  44.0 1.4 %collective-permute-done.12.far_ref = bf16[32,512]{1,0:T(8,128)(2,1)S(1)} collective-permute-done((bf16[32,512]{1,0:T(8,128)(2,1)S(1)}, bf16[32,512]{1,0:T(8,128)(2,1)S(1)}, u32[]{:S(2)}, u32[]{:S(2)}) %collective-permute-start.12) | collective-permute-done | bytes 32800 | tf_op jit(solution)/shard_map/ppermute | solution.py:274
  45.4 1.1 %collective-permute-done.13.two_ref = bf16[32,512]{1,0:T(8,128)(2,1)S(1)} collective-permute-done((bf16[32,512]{1,0:T(8,128)(2,1)S(1)}, bf16[32,512]{1,0:T(8,128)(2,1)S(1)}, u32[]{:S(2)}, u32[]{:S(2)}) %collective-permute-start.13) | collective-permute-done | bytes 32800 | tf_op jit(solution)/shard_map/ppermute | solution.py:274
  46.6 0.7 %shard_map.86 = bf16[32,2048]{1,0:T(8,128)(2,1)} custom-call(bf16[32,1024]{1,0:T(8,128)(2,1)S(1)} %shard_map.85.held_ref, bf16[32,512]{1,0:T(8,128)(2,1)S(1)} %collective-permute-done.13.two_ref, bf16[32,512]{1,0:T(8,128)(2,1)S(1)} %collective-permute-done.14.one_ref), custom_call_target="tpu_custom_call" | custom-call | bytes 262144 | tf_op jit(solution)/shard_map/pallas_call | solution.py:263
  (34 shorter events, 1.0 us)
Async XLA Ops:
  0.0 10.2 %copy-start.1 = (bf16[128,1024]{1,0:T(8,128)(2,1)S(1)}, bf16[128,1024]{1,0:T(8,128)(2,1)}, u32[]{:S(2)}) copy-start(bf16[128,1024]{1,0:T(8,128)(2,1)} %q_ref.1) | copy-start | bytes 786436
  0.0 10.2 %copy-start.2 = (bf16[128,256]{1,0:T(8,128)(2,1)S(1)}, bf16[128,256]{1,0:T(8,128)(2,1)}, u32[]{:S(2)}) copy-start(bf16[128,256]{1,0:T(8,128)(2,1)} %k_ref.3) | copy-start | bytes 196612
  0.0 10.2 %copy-start.3 = (bf16[128,256]{1,0:T(8,128)(2,1)S(1)}, bf16[128,256]{1,0:T(8,128)(2,1)}, u32[]{:S(2)}) copy-start(bf16[128,256]{1,0:T(8,128)(2,1)} %v_ref.3) | copy-start | bytes 196612
  0.0 22.9 %copy-start = (bf16[1024,512]{1,0:T(8,128)(2,1)S(1)}, bf16[1024,512]{1,0:T(8,128)(2,1)}, u32[]{:S(2)}) copy-start(bf16[1024,512]{1,0:T(8,128)(2,1)} %refs_2_.5) | copy-start | bytes 3145732
  1.7 8.5 %copy-start.4 = (s32[128]{0:T(128)S(1)}, s32[128]{0:T(128)}, u32[]{:S(2)}) copy-start(s32[128]{0:T(128)} %param.11) | copy-start | bytes 1540
  1.7 8.5 %copy-start.5 = (s32[2]{0:T(128)S(1)}, s32[2]{0:T(128)}, u32[]{:S(2)}) copy-start(s32[2]{0:T(128)} %param.12) | copy-start | bytes 28
  1.7 8.5 %copy-start.6 = (s32[128]{0:T(128)S(1)}, s32[128]{0:T(128)}, u32[]{:S(2)}) copy-start(s32[128]{0:T(128)} %param.10) | copy-start | bytes 1540
  1.7 4.7 %collective-permute-start = (bf16[144,512]{1,0:T(8,128)(2,1)}, bf16[144,512]{1,0:T(8,128)(2,1)S(1)}, u32[]{:S(2)}, u32[]{:S(2)}) collective-permute-start(bf16[144,512]{1,0:T(8,128)(2,1)} %shard_map.73), channel_id=1, source_target_pairs={{0,1},{1,0},{2,3},{3,2},{4,8},{5,9},{6,10},{7,11},{8,4},{9,5},{10,... | collective-permute-start | bytes 442376 | tf_op jit(solution)/shard_map/ppermute | solution.py:316
  2.2 8.0 %collective-permute-start.1 = (bf16[144,512]{1,0:T(8,128)(2,1)}, bf16[144,512]{1,0:T(8,128)(2,1)S(1)}, u32[]{:S(2)}, u32[]{:S(2)}) collective-permute-start(bf16[144,512]{1,0:T(8,128)(2,1)} %shard_map.73), channel_id=1, source_target_pairs={{0,4},{4,0},{8,12},{12,8},{1,5},{5,1},{9,13},{13,9},{2,6},{6,2},{1... | collective-permute-start | bytes 442376 | tf_op jit(solution)/shard_map/ppermute | solution.py:274
  10.9 12.0 %collective-permute-start.3 = (bf16[128,1024]{1,0:T(8,128)(2,1)S(1)}, bf16[128,1024]{1,0:T(8,128)(2,1)S(1)}, u32[]{:S(2)}, u32[]{:S(2)}) collective-permute-start(bf16[128,1024]{1,0:T(8,128)(2,1)S(1)} %get-tuple-element.22.refs_0_), channel_id=1, source_target_pairs={{0,4},{4,0},{8,12},{12,8},{1,5},{5,1},{9,13},{13,9},{2,6},{6,2},{1... | collective-permute-start | bytes 786440 | tf_op jit(solution)/shard_map/ppermute | solution.py:274
  12.7 10.7 %collective-permute-start.2 = (bf16[72,1024]{1,0:T(8,128)(2,1)S(1)}, bf16[72,1024]{1,0:T(8,128)(2,1)S(1)}, u32[]{:S(2)}, u32[]{:S(2)}) collective-permute-start(bf16[72,1024]{1,0:T(8,128)(2,1)S(1)} %get-tuple-element.21.noted_ref), channel_id=1, source_target_pairs={{0,8},{4,12},{8,0},{12,4},{1,9},{5,13},{9,1},{13,5},{2,10},{6,14},... | collective-permute-start | bytes 442376 | tf_op jit(solution)/shard_map/ppermute | solution.py:274
  14.7 13.0 %collective-permute-start.5 = (bf16[64,1024]{1,0:T(8,128)(2,1)S(1)}, bf16[64,1024]{1,0:T(8,128)(2,1)S(1)}, u32[]{:S(2)}, u32[]{:S(2)}) collective-permute-start(bf16[64,1024]{1,0:T(8,128)(2,1)S(1)} %get-tuple-element.26), channel_id=1, source_target_pairs={{0,8},{4,12},{8,0},{12,4},{1,9},{5,13},{9,1},{13,5},{2,10},{6,14},... | collective-permute-start | bytes 393224 | tf_op jit(solution)/shard_map/ppermute | solution.py:274
  23.3 4.3 %collective-permute-start.4 = (bf16[128,512]{1,0:T(8,128)(2,1)S(1)}, bf16[128,512]{1,0:T(8,128)(2,1)S(1)}, u32[]{:S(2)}, u32[]{:S(2)}) collective-permute-start(bf16[128,512]{1,0:T(8,128)(2,1)S(1)} %get-tuple-element.24), channel_id=1, source_target_pairs={{0,1},{1,0},{2,3},{3,2},{4,5},{5,4},{6,7},{7,6},{8,9},{9,8},{10,11... | collective-permute-start | bytes 393224 | tf_op jit(solution)/shard_map/ppermute | solution.py:274
  23.5 7.5 %collective-permute-start.8 = (bf16[64,1024]{1,0:T(8,128)(2,1)S(1)}, bf16[64,1024]{1,0:T(8,128)(2,1)S(1)}, u32[]{:S(2)}, u32[]{:S(2)}) collective-permute-start(bf16[64,1024]{1,0:T(8,128)(2,1)S(1)} %shard_map.80), channel_id=1, source_target_pairs={{0,4},{4,0},{8,12},{12,8},{1,5},{5,1},{9,13},{13,9},{2,6},{6,2},{1... | collective-permute-start | bytes 393224 | tf_op jit(solution)/shard_map/ppermute | solution.py:274
  27.7 5.5 %collective-permute-start.9 = (bf16[64,1024]{1,0:T(8,128)(2,1)S(1)}, bf16[64,1024]{1,0:T(8,128)(2,1)S(1)}, u32[]{:S(2)}, u32[]{:S(2)}) collective-permute-start(bf16[64,1024]{1,0:T(8,128)(2,1)S(1)} %collective-permute-done.5.refs_1_), channel_id=1, source_target_pairs={{0,4},{4,0},{8,12},{12,8},{1,5},{5,1},{9,13},{13,9},{2,6},{6,2},{1... | collective-permute-start | bytes 393224 | tf_op jit(solution)/shard_map/ppermute | solution.py:274
  28.0 1.3 %collective-permute-start.6 = (bf16[64,512]{1,0:T(8,128)(2,1)S(1)}, bf16[64,512]{1,0:T(8,128)(2,1)S(1)}, u32[]{:S(2)}, u32[]{:S(2)}) collective-permute-start(bf16[64,512]{1,0:T(8,128)(2,1)S(1)} %get-tuple-element.29), channel_id=1, source_target_pairs={{0,1},{1,0},{2,3},{3,2},{4,5},{5,4},{6,7},{7,6},{8,9},{9,8},{10,11... | collective-permute-start | bytes 196616 | tf_op jit(solution)/shard_map/ppermute | solution.py:274
  29.4 9.8 %collective-permute-start.7 = (bf16[192,512]{1,0:T(8,128)(2,1)S(1)}, bf16[192,512]{1,0:T(8,128)(2,1)S(1)}, u32[]{:S(2)}, u32[]{:S(2)}) collective-permute-start(bf16[192,512]{1,0:T(8,128)(2,1)S(1)} %shard_map.78.refs_0_), channel_id=1, source_target_pairs={{0,2},{1,3},{2,0},{3,1},{4,6},{5,7},{6,4},{7,5},{8,10},{9,11},{10,... | collective-permute-start | bytes 589832 | tf_op jit(solution)/shard_map/ppermute | solution.py:274
  33.5 1.3 %collective-permute-start.10 = (bf16[64,512]{1,0:T(8,128)(2,1)S(1)}, bf16[64,512]{1,0:T(8,128)(2,1)S(1)}, u32[]{:S(2)}, u32[]{:S(2)}) collective-permute-start(bf16[64,512]{1,0:T(8,128)(2,1)S(1)} %get-tuple-element.32), channel_id=1, source_target_pairs={{0,1},{1,0},{2,3},{3,2},{4,5},{5,4},{6,7},{7,6},{8,9},{9,8},{10,11... | collective-permute-start | bytes 196616 | tf_op jit(solution)/shard_map/ppermute | solution.py:274
  34.9 4.3 %collective-permute-start.11 = (bf16[64,512]{1,0:T(8,128)(2,1)S(1)}, bf16[64,512]{1,0:T(8,128)(2,1)S(1)}, u32[]{:S(2)}, u32[]{:S(2)}) collective-permute-start(bf16[64,512]{1,0:T(8,128)(2,1)S(1)} %shard_map.82.refs_0_), channel_id=1, source_target_pairs={{0,2},{1,3},{2,0},{3,1},{4,6},{5,7},{6,4},{7,5},{8,10},{9,11},{10,... | collective-permute-start | bytes 196616 | tf_op jit(solution)/shard_map/ppermute | solution.py:274
  39.5 5.9 %collective-permute-start.12 = (bf16[32,512]{1,0:T(8,128)(2,1)S(1)}, bf16[32,512]{1,0:T(8,128)(2,1)S(1)}, u32[]{:S(2)}, u32[]{:S(2)}) collective-permute-start(bf16[32,512]{1,0:T(8,128)(2,1)S(1)} %get-tuple-element.34), channel_id=1, source_target_pairs={{0,12},{4,8},{8,4},{12,0},{1,13},{5,9},{9,5},{13,1},{2,14},{6,10},... | collective-permute-start | bytes 98312 | tf_op jit(solution)/shard_map/ppermute | solution.py:274
  41.8 4.8 %collective-permute-start.13 = (bf16[32,512]{1,0:T(8,128)(2,1)S(1)}, bf16[32,512]{1,0:T(8,128)(2,1)S(1)}, u32[]{:S(2)}, u32[]{:S(2)}) collective-permute-start(bf16[32,512]{1,0:T(8,128)(2,1)S(1)} %get-tuple-element.35), channel_id=1, source_target_pairs={{0,8},{4,12},{8,0},{12,4},{1,9},{5,13},{9,1},{13,5},{2,10},{6,14},... | collective-permute-start | bytes 98312 | tf_op jit(solution)/shard_map/ppermute | solution.py:274
  41.8 4.8 %collective-permute-start.14 = (bf16[32,512]{1,0:T(8,128)(2,1)S(1)}, bf16[32,512]{1,0:T(8,128)(2,1)S(1)}, u32[]{:S(2)}, u32[]{:S(2)}) collective-permute-start(bf16[32,512]{1,0:T(8,128)(2,1)S(1)} %get-tuple-element.36), channel_id=1, source_target_pairs={{0,4},{4,0},{8,12},{12,8},{1,5},{5,1},{9,13},{13,9},{2,6},{6,2},{1... | collective-permute-start | bytes 98312 | tf_op jit(solution)/shard_map/ppermute | solution.py:274

commit v16 on v14

--- a/solution.py
+++ b/solution.py
@@ -34,27 +34,46 @@
     return jnp.transpose(jnp.broadcast_to(row, (size, size)))
 
 
-def pack_kernel(k_ref, v_ref, end_ref, target_ref, message_ref):
-    rows, width = k_ref.shape
-    message_ref[pl.ds(0, rows), pl.ds(0, width)] = k_ref[...]
-    message_ref[pl.ds(0, rows), pl.ds(width, width)] = v_ref[...]
-    extra = message_ref.shape[0] - rows
+def pack_kernel(k_in, v_in, end_ref, target_ref, message_out, held, sems):
+    rows, width = k_in.shape
+    extra = held.shape[0] - rows
+    parts = [(pl.ds(0, rows), pl.ds(n * width, width)) for n in range(2)]
+    arrive = [
+        pltpu.make_async_copy(source, held.at[part], sems.at[n])
+        for n, (source, part) in enumerate(zip((k_in, v_in), parts))
+    ]
+    for copy in arrive:
+        copy.start()
     line = lax.broadcasted_iota(jnp.int32, (extra, rows), 0)
     ends = jnp.broadcast_to(end_ref[...], (extra, rows))
-    parts = jnp.where(line == 0, ends // END_PART, jnp.where(line == 1, ends % END_PART, 0))
-    message_ref[pl.ds(rows, extra), :] = jnp.zeros((extra, 2 * width), jnp.bfloat16)
-    message_ref[pl.ds(rows, extra), pl.ds(0, rows)] = parts.astype(jnp.float32).astype(jnp.bfloat16)
+    ends = jnp.where(line == 0, ends // END_PART, jnp.where(line == 1, ends % END_PART, 0))
+    held[pl.ds(rows, extra), :] = jnp.zeros((extra, 2 * width), jnp.bfloat16)
+    held[pl.ds(rows, extra), pl.ds(0, rows)] = ends.astype(jnp.float32).astype(jnp.bfloat16)
     targets = jnp.broadcast_to(target_ref[...].astype(jnp.float32), (extra, target_ref.shape[1]))
-    message_ref[pl.ds(rows, extra), pl.ds(rows, target_ref.shape[1])] = targets.astype(jnp.bfloat16)
+    held[pl.ds(rows, extra), pl.ds(rows, target_ref.shape[1])] = targets.astype(jnp.bfloat16)
+    parts.append((pl.ds(rows, extra), pl.ds(0, 2 * width)))
+    leave = [
+        pltpu.make_async_copy(held.at[part], message_out.at[part], sems.at[2 + n])
+        for n, part in enumerate(parts)
+    ]
+    leave[2].start()
+    for n in range(2):
+        arrive[n].wait()
+        leave[n].start()
+    for copy in leave:
+        copy.wait()
 
 
 def pack(key_rows, value_rows, ends, targets):
     rows, width = key_rows.shape
+    shape = (rows + 16, 2 * width)
+    hbm = pl.BlockSpec(memory_space=pltpu.HBM)
     return pl.pallas_call(
         pack_kernel,
-        out_shape=jax.ShapeDtypeStruct((rows + 16, 2 * width), jnp.bfloat16),
-        in_specs=vmem(4),
-        out_specs=pl.BlockSpec(memory_space=pltpu.VMEM),
+        out_shape=jax.ShapeDtypeStruct(shape, jnp.bfloat16),
+        in_specs=[hbm, hbm] + vmem(2),
+        out_specs=hbm,
+        scratch_shapes=[pltpu.VMEM(shape, jnp.bfloat16), pltpu.SemaphoreType.DMA((5,))],
         cost_estimate=cost(10**9, 8 * key_rows.size),
     )(key_rows, value_rows, ends, targets)
 

time: 46.7 us -> 47.4 us (1.015)
  Pallas kernels: 4.5 us -> 5.17 us
    pallas_call x1, Pallas kernels: 1.66 us -> 2.33 us  [pack(): pl.pallas_call(pack_kernel, out_shape=jax.ShapeDtypeStruct(shape, jnp.bfl...]
  transfers between devices with their start and end apart: 15 -> 15, of which waited for: 10 -> 10; matrix products, arithmetic and copies ran while one was open for 0% -> 0% of each run, Pallas kernels for 3% -> 2%
where the time goes in v16:
time: 47.4 us; the launch traced here: 47.2 us
  waiting for transfers between devices  23.6 us (50%)
  starting transfers between devices  18.2 us (38%)
  Pallas kernels  5.17 us (11%)
    ppermute x14, waiting for transfers between devices, flip(): return lax.ppermute(array, axis, [(i, i ^ bits) for i in range(4)])  23.6 us
    ppermute x14, starting transfers between devices, flip(): return lax.ppermute(array, axis, [(i, i ^ bits) for i in range(4)])  18.2 us
    pallas_call x1, Pallas kernels, pack(): pl.pallas_call(pack_kernel, out_shape=jax.ShapeDtypeStruct(shape, jnp.bfl...  2.33 us
    pallas_call x3, Pallas kernels, project(): pl.pallas_call(functools.partial(project_kernel, block_rows), out_shape=(...  1.05 us
  transfers between devices with their start and end apart: 15, of which 10 were waited for; matrix products, arithmetic and copies ran while one was open for 0% of the time, Pallas kernels for 2%

profile of v16, /device:TPU:0, one launch (start us, length us, event | category | flops | bytes accessed | tf_op | source)
XLA Modules:
  0.0 47.2 jit_solution(2539408144505192895)
XLA Ops:
  0.0 2.3 %shard_map.73 = bf16[144,512]{1,0:T(8,128)(2,1)} custom-call(bf16[128,256]{1,0:T(8,128)(2,1)} %k_ref.1, bf16[128,256]{1,0:T(8,128)(2,1)} %v_ref.1, s32[1,128]{1,0:T(1,128)} %bitcast.3, s32[1,2]{1,0:T(1,128)} %bitcast.5), custom_call_target="tpu_custom_call" | custom-call | flops 1000000000 | bytes 262144 | tf_op jit(solution)/shard_map/pallas_call | solution.py:71
  2.4 3.1 %collective-permute-start = (bf16[144,512]{1,0:T(8,128)(2,1)}, bf16[144,512]{1,0:T(8,128)(2,1)S(1)}, u32[]{:S(2)}, u32[]{:S(2)}) collective-permute-start(bf16[144,512]{1,0:T(8,128)(2,1)} %shard_map.73), channel_id=1, source_target_pairs={{0,4},{4,0},{8,12},{12,8},{1,5},{5,1},{9,13},{13,9},{2,6},{6,2},{1... | collective-permute-start | bytes 442376 | tf_op jit(solution)/shard_map/ppermute | solution.py:293
  5.5 4.1 %collective-permute-done.flip_ref = bf16[144,512]{1,0:T(8,128)(2,1)S(1)} collective-permute-done((bf16[144,512]{1,0:T(8,128)(2,1)}, bf16[144,512]{1,0:T(8,128)(2,1)S(1)}, u32[]{:S(2)}, u32[]{:S(2)}) %collective-permute-start) | collective-permute-done | bytes 147488 | tf_op jit(solution)/shard_map/ppermute | solution.py:293
  9.6 0.7 %shard_map.74 = (bf16[128,1024]{1,0:T(8,128)(2,1)S(1)}, bf16[72,1024]{1,0:T(8,128)(2,1)S(1)}, bf16[64,1024]{1,0:T(8,128)(2,1)S(1)}) custom-call(bf16[128,1024]{1,0:T(8,128)(2,1)S(1)} %copy-done.1, bf16[144,512]{1,0:T(8,128)(2,1)S(1)} %collective-permute-done.flip_ref, bf16[144,512]{1,0:T(8,128)(2,1)S(1)} %collective-permute-done.1.mid_ref, ...), custom_call_target="tpu_custom_call" | custom-call | flops 134217728 | bytes 786432 | tf_op jit(solution)/shard_map/pallas_call | solution.py:151
  10.3 3.0 %collective-permute-start.3 = (bf16[128,1024]{1,0:T(8,128)(2,1)S(1)}, bf16[128,1024]{1,0:T(8,128)(2,1)S(1)}, u32[]{:S(2)}, u32[]{:S(2)}) collective-permute-start(bf16[128,1024]{1,0:T(8,128)(2,1)S(1)} %get-tuple-element.22.refs_0_), channel_id=1, source_target_pairs={{0,4},{4,0},{8,12},{12,8},{1,5},{5,1},{9,13},{13,9},{2,6},{6,2},{1... | collective-permute-start | bytes 786440 | tf_op jit(solution)/shard_map/ppermute | solution.py:293
  13.3 1.4 %collective-permute-start.2 = (bf16[72,1024]{1,0:T(8,128)(2,1)S(1)}, bf16[72,1024]{1,0:T(8,128)(2,1)S(1)}, u32[]{:S(2)}, u32[]{:S(2)}) collective-permute-start(bf16[72,1024]{1,0:T(8,128)(2,1)S(1)} %get-tuple-element.21.noted_ref), channel_id=1, source_target_pairs={{0,8},{4,12},{8,0},{12,4},{1,9},{5,13},{9,1},{13,5},{2,10},{6,14},... | collective-permute-start | bytes 442376 | tf_op jit(solution)/shard_map/ppermute | solution.py:293
  14.7 1.5 %collective-permute-start.5 = (bf16[64,1024]{1,0:T(8,128)(2,1)S(1)}, bf16[64,1024]{1,0:T(8,128)(2,1)S(1)}, u32[]{:S(2)}, u32[]{:S(2)}) collective-permute-start(bf16[64,1024]{1,0:T(8,128)(2,1)S(1)} %get-tuple-element.26), channel_id=1, source_target_pairs={{0,8},{4,12},{8,0},{12,4},{1,9},{5,13},{9,1},{13,5},{2,10},{6,14},... | collective-permute-start | bytes 393224 | tf_op jit(solution)/shard_map/ppermute | solution.py:293
  16.2 7.8 %collective-permute-done.3.refs_1_ = bf16[128,1024]{1,0:T(8,128)(2,1)S(1)} collective-permute-done((bf16[128,1024]{1,0:T(8,128)(2,1)S(1)}, bf16[128,1024]{1,0:T(8,128)(2,1)S(1)}, u32[]{:S(2)}, u32[]{:S(2)}) %collective-permute-start.3) | collective-permute-done | bytes 262176 | tf_op jit(solution)/shard_map/ppermute | solution.py:293
  24.1 0.4 shard_map.75
  24.6 1.4 %collective-permute-start.8 = (bf16[64,1024]{1,0:T(8,128)(2,1)S(1)}, bf16[64,1024]{1,0:T(8,128)(2,1)S(1)}, u32[]{:S(2)}, u32[]{:S(2)}) collective-permute-start(bf16[64,1024]{1,0:T(8,128)(2,1)S(1)} %shard_map.80), channel_id=1, source_target_pairs={{0,4},{4,0},{8,12},{12,8},{1,5},{5,1},{9,13},{13,9},{2,6},{6,2},{1... | collective-permute-start | bytes 393224 | tf_op jit(solution)/shard_map/ppermute | solution.py:293
  26.0 1.4 %collective-permute-done.5.refs_1_ = bf16[64,1024]{1,0:T(8,128)(2,1)S(1)} collective-permute-done((bf16[64,1024]{1,0:T(8,128)(2,1)S(1)}, bf16[64,1024]{1,0:T(8,128)(2,1)S(1)}, u32[]{:S(2)}, u32[]{:S(2)}) %collective-permute-start.5) | collective-permute-done | bytes 131104 | tf_op jit(solution)/shard_map/ppermute | solution.py:293
  27.5 0.3 shard_map.77
  27.9 1.2 %collective-permute-done.6.got_ref = bf16[64,512]{1,0:T(8,128)(2,1)S(1)} collective-permute-done((bf16[64,512]{1,0:T(8,128)(2,1)S(1)}, bf16[64,512]{1,0:T(8,128)(2,1)S(1)}, u32[]{:S(2)}, u32[]{:S(2)}) %collective-permute-start.6) | collective-permute-done | bytes 65568 | tf_op jit(solution)/shard_map/ppermute | solution.py:293
  29.2 1.6 %collective-permute-start.7 = (bf16[192,512]{1,0:T(8,128)(2,1)S(1)}, bf16[192,512]{1,0:T(8,128)(2,1)S(1)}, u32[]{:S(2)}, u32[]{:S(2)}) collective-permute-start(bf16[192,512]{1,0:T(8,128)(2,1)S(1)} %shard_map.78.refs_0_), channel_id=1, source_target_pairs={{0,2},{1,3},{2,0},{3,1},{4,6},{5,7},{6,4},{7,5},{8,10},{9,11},{10,... | collective-permute-start | bytes 589832 | tf_op jit(solution)/shard_map/ppermute | solution.py:293
  31.0 2.4 %collective-permute-done.9.refs_1_ = bf16[64,1024]{1,0:T(8,128)(2,1)S(1)} collective-permute-done((bf16[64,1024]{1,0:T(8,128)(2,1)S(1)}, bf16[64,1024]{1,0:T(8,128)(2,1)S(1)}, u32[]{:S(2)}, u32[]{:S(2)}) %collective-permute-start.9) | collective-permute-done | bytes 131104 | tf_op jit(solution)/shard_map/ppermute | solution.py:293
  33.4 0.3 shard_map.81
  33.8 1.2 %collective-permute-done.10.refs_1_ = bf16[64,512]{1,0:T(8,128)(2,1)S(1)} collective-permute-done((bf16[64,512]{1,0:T(8,128)(2,1)S(1)}, bf16[64,512]{1,0:T(8,128)(2,1)S(1)}, u32[]{:S(2)}, u32[]{:S(2)}) %collective-permute-start.10) | collective-permute-done | bytes 65568 | tf_op jit(solution)/shard_map/ppermute | solution.py:293
  35.0 1.6 %collective-permute-start.11 = (bf16[64,512]{1,0:T(8,128)(2,1)S(1)}, bf16[64,512]{1,0:T(8,128)(2,1)S(1)}, u32[]{:S(2)}, u32[]{:S(2)}) collective-permute-start(bf16[64,512]{1,0:T(8,128)(2,1)S(1)} %shard_map.82.refs_0_), channel_id=1, source_target_pairs={{0,2},{1,3},{2,0},{3,1},{4,6},{5,7},{6,4},{7,5},{8,10},{9,11},{10,... | collective-permute-start | bytes 196616 | tf_op jit(solution)/shard_map/ppermute | solution.py:293
  36.6 2.8 %collective-permute-done.11.refs_1_ = bf16[64,512]{1,0:T(8,128)(2,1)S(1)} collective-permute-done((bf16[64,512]{1,0:T(8,128)(2,1)S(1)}, bf16[64,512]{1,0:T(8,128)(2,1)S(1)}, u32[]{:S(2)}, u32[]{:S(2)}) %collective-permute-start.11) | collective-permute-done | bytes 65568 | tf_op jit(solution)/shard_map/ppermute | solution.py:293
  39.7 2.1 %collective-permute-start.12 = (bf16[32,512]{1,0:T(8,128)(2,1)S(1)}, bf16[32,512]{1,0:T(8,128)(2,1)S(1)}, u32[]{:S(2)}, u32[]{:S(2)}) collective-permute-start(bf16[32,512]{1,0:T(8,128)(2,1)S(1)} %get-tuple-element.34), channel_id=1, source_target_pairs={{0,12},{4,8},{8,4},{12,0},{1,13},{5,9},{9,5},{13,1},{2,14},{6,10},... | collective-permute-start | bytes 98312 | tf_op jit(solution)/shard_map/ppermute | solution.py:293
  41.7 2.4 %collective-permute-start.14 = (bf16[32,512]{1,0:T(8,128)(2,1)S(1)}, bf16[32,512]{1,0:T(8,128)(2,1)S(1)}, u32[]{:S(2)}, u32[]{:S(2)}) collective-permute-start(bf16[32,512]{1,0:T(8,128)(2,1)S(1)} %get-tuple-element.36), channel_id=1, source_target_pairs={{0,4},{4,0},{8,12},{12,8},{1,5},{5,1},{9,13},{13,9},{2,6},{6,2},{1... | collective-permute-start | bytes 98312 | tf_op jit(solution)/shard_map/ppermute | solution.py:293
  44.1 1.6 %collective-permute-done.12.far_ref = bf16[32,512]{1,0:T(8,128)(2,1)S(1)} collective-permute-done((bf16[32,512]{1,0:T(8,128)(2,1)S(1)}, bf16[32,512]{1,0:T(8,128)(2,1)S(1)}, u32[]{:S(2)}, u32[]{:S(2)}) %collective-permute-start.12) | collective-permute-done | bytes 32800 | tf_op jit(solution)/shard_map/ppermute | solution.py:293
  45.7 0.8 %collective-permute-done.13.two_ref = bf16[32,512]{1,0:T(8,128)(2,1)S(1)} collective-permute-done((bf16[32,512]{1,0:T(8,128)(2,1)S(1)}, bf16[32,512]{1,0:T(8,128)(2,1)S(1)}, u32[]{:S(2)}, u32[]{:S(2)}) %collective-permute-start.13) | collective-permute-done | bytes 32800 | tf_op jit(solution)/shard_map/ppermute | solution.py:293
  46.6 0.7 %shard_map.86 = bf16[32,2048]{1,0:T(8,128)(2,1)} custom-call(bf16[32,1024]{1,0:T(8,128)(2,1)S(1)} %shard_map.85.held_ref, bf16[32,512]{1,0:T(8,128)(2,1)S(1)} %collective-permute-done.13.two_ref, bf16[32,512]{1,0:T(8,128)(2,1)S(1)} %collective-permute-done.14.one_ref), custom_call_target="tpu_custom_call" | custom-call | bytes 262144 | tf_op jit(solution)/shard_map/pallas_call | solution.py:282
  (34 shorter events, 0.9 us)
Async XLA Ops:
  0.0 9.5 %copy-start.1 = (bf16[128,1024]{1,0:T(8,128)(2,1)S(1)}, bf16[128,1024]{1,0:T(8,128)(2,1)}, u32[]{:S(2)}) copy-start(bf16[128,1024]{1,0:T(8,128)(2,1)} %q_ref.1) | copy-start | bytes 786436
  0.0 9.5 %copy-start.2 = (bf16[128,256]{1,0:T(8,128)(2,1)S(1)}, bf16[128,256]{1,0:T(8,128)(2,1)}, u32[]{:S(2)}) copy-start(bf16[128,256]{1,0:T(8,128)(2,1)} %k_ref.1) | copy-start | bytes 196612
  0.0 9.6 %copy-start.3 = (bf16[128,256]{1,0:T(8,128)(2,1)S(1)}, bf16[128,256]{1,0:T(8,128)(2,1)}, u32[]{:S(2)}) copy-start(bf16[128,256]{1,0:T(8,128)(2,1)} %v_ref.1) | copy-start | bytes 196612
  0.0 24.0 %copy-start = (bf16[1024,512]{1,0:T(8,128)(2,1)S(1)}, bf16[1024,512]{1,0:T(8,128)(2,1)}, u32[]{:S(2)}) copy-start(bf16[1024,512]{1,0:T(8,128)(2,1)} %refs_2_.5) | copy-start | bytes 3145732
  2.3 7.2 %copy-start.4 = (s32[128]{0:T(128)S(1)}, s32[128]{0:T(128)}, u32[]{:S(2)}) copy-start(s32[128]{0:T(128)} %param.11) | copy-start | bytes 1540
  2.4 7.2 %copy-start.5 = (s32[2]{0:T(128)S(1)}, s32[2]{0:T(128)}, u32[]{:S(2)}) copy-start(s32[2]{0:T(128)} %param.12) | copy-start | bytes 28
  2.4 7.2 %copy-start.6 = (s32[128]{0:T(128)S(1)}, s32[128]{0:T(128)}, u32[]{:S(2)}) copy-start(s32[128]{0:T(128)} %param.10) | copy-start | bytes 1540
  2.4 7.2 %collective-permute-start = (bf16[144,512]{1,0:T(8,128)(2,1)}, bf16[144,512]{1,0:T(8,128)(2,1)S(1)}, u32[]{:S(2)}, u32[]{:S(2)}) collective-permute-start(bf16[144,512]{1,0:T(8,128)(2,1)} %shard_map.73), channel_id=1, source_target_pairs={{0,4},{4,0},{8,12},{12,8},{1,5},{5,1},{9,13},{13,9},{2,6},{6,2},{1... | collective-permute-start | bytes 442376 | tf_op jit(solution)/shard_map/ppermute | solution.py:293
  5.5 4.1 %collective-permute-start.1 = (bf16[144,512]{1,0:T(8,128)(2,1)}, bf16[144,512]{1,0:T(8,128)(2,1)S(1)}, u32[]{:S(2)}, u32[]{:S(2)}) collective-permute-start(bf16[144,512]{1,0:T(8,128)(2,1)} %shard_map.73), channel_id=1, source_target_pairs={{0,1},{1,0},{2,3},{3,2},{4,8},{5,9},{6,10},{7,11},{8,4},{9,5},{10,... | collective-permute-start | bytes 442376 | tf_op jit(solution)/shard_map/ppermute | solution.py:336
  10.3 13.7 %collective-permute-start.3 = (bf16[128,1024]{1,0:T(8,128)(2,1)S(1)}, bf16[128,1024]{1,0:T(8,128)(2,1)S(1)}, u32[]{:S(2)}, u32[]{:S(2)}) collective-permute-start(bf16[128,1024]{1,0:T(8,128)(2,1)S(1)} %get-tuple-element.22.refs_0_), channel_id=1, source_target_pairs={{0,4},{4,0},{8,12},{12,8},{1,5},{5,1},{9,13},{13,9},{2,6},{6,2},{1... | collective-permute-start | bytes 786440 | tf_op jit(solution)/shard_map/ppermute | solution.py:293
  13.3 11.3 %collective-permute-start.2 = (bf16[72,1024]{1,0:T(8,128)(2,1)S(1)}, bf16[72,1024]{1,0:T(8,128)(2,1)S(1)}, u32[]{:S(2)}, u32[]{:S(2)}) collective-permute-start(bf16[72,1024]{1,0:T(8,128)(2,1)S(1)} %get-tuple-element.21.noted_ref), channel_id=1, source_target_pairs={{0,8},{4,12},{8,0},{12,4},{1,9},{5,13},{9,1},{13,5},{2,10},{6,14},... | collective-permute-start | bytes 442376 | tf_op jit(solution)/shard_map/ppermute | solution.py:293
  14.7 12.7 %collective-permute-start.5 = (bf16[64,1024]{1,0:T(8,128)(2,1)S(1)}, bf16[64,1024]{1,0:T(8,128)(2,1)S(1)}, u32[]{:S(2)}, u32[]{:S(2)}) collective-permute-start(bf16[64,1024]{1,0:T(8,128)(2,1)S(1)} %get-tuple-element.26), channel_id=1, source_target_pairs={{0,8},{4,12},{8,0},{12,4},{1,9},{5,13},{9,1},{13,5},{2,10},{6,14},... | collective-permute-start | bytes 393224 | tf_op jit(solution)/shard_map/ppermute | solution.py:293
  24.5 3.0 %collective-permute-start.4 = (bf16[128,512]{1,0:T(8,128)(2,1)S(1)}, bf16[128,512]{1,0:T(8,128)(2,1)S(1)}, u32[]{:S(2)}, u32[]{:S(2)}) collective-permute-start(bf16[128,512]{1,0:T(8,128)(2,1)S(1)} %get-tuple-element.24), channel_id=1, source_target_pairs={{0,1},{1,0},{2,3},{3,2},{4,5},{5,4},{6,7},{7,6},{8,9},{9,8},{10,11... | collective-permute-start | bytes 393224 | tf_op jit(solution)/shard_map/ppermute | solution.py:293
  24.6 6.4 %collective-permute-start.8 = (bf16[64,1024]{1,0:T(8,128)(2,1)S(1)}, bf16[64,1024]{1,0:T(8,128)(2,1)S(1)}, u32[]{:S(2)}, u32[]{:S(2)}) collective-permute-start(bf16[64,1024]{1,0:T(8,128)(2,1)S(1)} %shard_map.80), channel_id=1, source_target_pairs={{0,4},{4,0},{8,12},{12,8},{1,5},{5,1},{9,13},{13,9},{2,6},{6,2},{1... | collective-permute-start | bytes 393224 | tf_op jit(solution)/shard_map/ppermute | solution.py:293
  27.5 5.9 %collective-permute-start.9 = (bf16[64,1024]{1,0:T(8,128)(2,1)S(1)}, bf16[64,1024]{1,0:T(8,128)(2,1)S(1)}, u32[]{:S(2)}, u32[]{:S(2)}) collective-permute-start(bf16[64,1024]{1,0:T(8,128)(2,1)S(1)} %collective-permute-done.5.refs_1_), channel_id=1, source_target_pairs={{0,4},{4,0},{8,12},{12,8},{1,5},{5,1},{9,13},{13,9},{2,6},{6,2},{1... | collective-permute-start | bytes 393224 | tf_op jit(solution)/shard_map/ppermute | solution.py:293
  27.8 1.3 %collective-permute-start.6 = (bf16[64,512]{1,0:T(8,128)(2,1)S(1)}, bf16[64,512]{1,0:T(8,128)(2,1)S(1)}, u32[]{:S(2)}, u32[]{:S(2)}) collective-permute-start(bf16[64,512]{1,0:T(8,128)(2,1)S(1)} %get-tuple-element.29), channel_id=1, source_target_pairs={{0,1},{1,0},{2,3},{3,2},{4,5},{5,4},{6,7},{7,6},{8,9},{9,8},{10,11... | collective-permute-start | bytes 196616 | tf_op jit(solution)/shard_map/ppermute | solution.py:293
  29.2 10.2 %collective-permute-start.7 = (bf16[192,512]{1,0:T(8,128)(2,1)S(1)}, bf16[192,512]{1,0:T(8,128)(2,1)S(1)}, u32[]{:S(2)}, u32[]{:S(2)}) collective-permute-start(bf16[192,512]{1,0:T(8,128)(2,1)S(1)} %shard_map.78.refs_0_), channel_id=1, source_target_pairs={{0,2},{1,3},{2,0},{3,1},{4,6},{5,7},{6,4},{7,5},{8,10},{9,11},{10,... | collective-permute-start | bytes 589832 | tf_op jit(solution)/shard_map/ppermute | solution.py:293
  33.7 1.3 %collective-permute-start.10 = (bf16[64,512]{1,0:T(8,128)(2,1)S(1)}, bf16[64,512]{1,0:T(8,128)(2,1)S(1)}, u32[]{:S(2)}, u32[]{:S(2)}) collective-permute-start(bf16[64,512]{1,0:T(8,128)(2,1)S(1)} %get-tuple-element.32), channel_id=1, source_target_pairs={{0,1},{1,0},{2,3},{3,2},{4,5},{5,4},{6,7},{7,6},{8,9},{9,8},{10,11... | collective-permute-start | bytes 196616 | tf_op jit(solution)/shard_map/ppermute | solution.py:293
  35.0 4.3 %collective-permute-start.11 = (bf16[64,512]{1,0:T(8,128)(2,1)S(1)}, bf16[64,512]{1,0:T(8,128)(2,1)S(1)}, u32[]{:S(2)}, u32[]{:S(2)}) collective-permute-start(bf16[64,512]{1,0:T(8,128)(2,1)S(1)} %shard_map.82.refs_0_), channel_id=1, source_target_pairs={{0,2},{1,3},{2,0},{3,1},{4,6},{5,7},{6,4},{7,5},{8,10},{9,11},{10,... | collective-permute-start | bytes 196616 | tf_op jit(solution)/shard_map/ppermute | solution.py:293
  39.7 6.1 %collective-permute-start.12 = (bf16[32,512]{1,0:T(8,128)(2,1)S(1)}, bf16[32,512]{1,0:T(8,128)(2,1)S(1)}, u32[]{:S(2)}, u32[]{:S(2)}) collective-permute-start(bf16[32,512]{1,0:T(8,128)(2,1)S(1)} %get-tuple-element.34), channel_id=1, source_target_pairs={{0,12},{4,8},{8,4},{12,0},{1,13},{5,9},{9,5},{13,1},{2,14},{6,10},... | collective-permute-start | bytes 98312 | tf_op jit(solution)/shard_map/ppermute | solution.py:293
  41.7 4.8 %collective-permute-start.13 = (bf16[32,512]{1,0:T(8,128)(2,1)S(1)}, bf16[32,512]{1,0:T(8,128)(2,1)S(1)}, u32[]{:S(2)}, u32[]{:S(2)}) collective-permute-start(bf16[32,512]{1,0:T(8,128)(2,1)S(1)} %get-tuple-element.35), channel_id=1, source_target_pairs={{0,8},{4,12},{8,0},{12,4},{1,9},{5,13},{9,1},{13,5},{2,10},{6,14},... | collective-permute-start | bytes 98312 | tf_op jit(solution)/shard_map/ppermute | solution.py:293
  41.7 4.8 %collective-permute-start.14 = (bf16[32,512]{1,0:T(8,128)(2,1)S(1)}, bf16[32,512]{1,0:T(8,128)(2,1)S(1)}, u32[]{:S(2)}, u32[]{:S(2)}) collective-permute-start(bf16[32,512]{1,0:T(8,128)(2,1)S(1)} %get-tuple-element.36), channel_id=1, source_target_pairs={{0,4},{4,0},{8,12},{12,8},{1,5},{5,1},{9,13},{13,9},{2,6},{6,2},{1... | collective-permute-start | bytes 98312 | tf_op jit(solution)/shard_map/ppermute | solution.py:293

commit v17 on v14

--- a/solution.py
+++ b/solution.py
@@ -52,7 +52,7 @@
     rows, width = key_rows.shape
     return pl.pallas_call(
         pack_kernel,
-        out_shape=jax.ShapeDtypeStruct((rows + 16, 2 * width), jnp.bfloat16),
+        out_shape=jax.ShapeDtypeStruct((rows + 8, 2 * width), jnp.bfloat16),
         in_specs=vmem(4),
         out_specs=pl.BlockSpec(memory_space=pltpu.VMEM),
         cost_estimate=cost(10**9, 8 * key_rows.size),
@@ -64,7 +64,7 @@
 ):
     across = lax.axis_index("ctx") % 2 == 0
     halo = jnp.where(across, mid_ref[...], flip_ref[...])
-    near = flip_ref[pl.ds(k_ref.shape[0], 16), pl.ds(k_ref.shape[0], HEAD_DIM)]
+    near = flip_ref[pl.ds(k_ref.shape[0], 8), pl.ds(k_ref.shape[0], HEAD_DIM)]
     near = near[0:1, 0:blocks].astype(jnp.float32)
     targets = jnp.concatenate([own_ref[...].astype(jnp.float32), near], axis=1)
     count = targets.shape[1]
@@ -81,7 +81,7 @@
     half = rows // blocks // 2
     query_pos = base + lax.broadcasted_iota(jnp.int32, (rows, rows), 0)
     query_start = column(st_ref[...])
-    parts = halo[rows : rows + 16, 0:rows].astype(jnp.float32).astype(jnp.int32)
+    parts = halo[rows : rows + 8, 0:rows].astype(jnp.float32).astype(jnp.int32)
     masks = []
     for shift, key_end in ((rows, parts[0:1] * END_PART + parts[1:2]), (0, end_ref[...])):
         key_pos = base - shift + lax.broadcasted_iota(jnp.int32, (rows, rows), 1)

time: 46.7 us -> 46.5 us (level)
  no operation moved by 1% of the time
where the time goes in v17:
time: 46.5 us; the launch traced here: 46.3 us
  waiting for transfers between devices  23.4 us (50%)
  starting transfers between devices  18.2 us (39%)
  Pallas kernels  4.49 us (10%)
    ppermute x14, waiting for transfers between devices, flip(): return lax.ppermute(array, axis, [(i, i ^ bits) for i in range(4)])  23.4 us
    ppermute x14, starting transfers between devices, flip(): return lax.ppermute(array, axis, [(i, i ^ bits) for i in range(4)])  18.2 us
    pallas_call x1, Pallas kernels, pack(): pl.pallas_call(pack_kernel, out_shape=jax.ShapeDtypeStruct((rows + 8, 2 *...  1.65 us
    pallas_call x3, Pallas kernels, project(): pl.pallas_call(functools.partial(project_kernel, block_rows), out_shape=(...  1.05 us
  transfers between devices with their start and end apart: 15, of which 10 were waited for; matrix products, arithmetic and copies ran while one was open for 0% of the time, Pallas kernels for 3%

profile of v17, /device:TPU:0, one launch (start us, length us, event | category | flops | bytes accessed | tf_op | source)
XLA Modules:
  0.0 46.3 jit_solution(9439763777923682619)
XLA Ops:
  0.0 1.7 %shard_map.73 = bf16[136,512]{1,0:T(8,128)(2,1)} custom-call(bf16[128,256]{1,0:T(8,128)(2,1)} %k_ref.3, bf16[128,256]{1,0:T(8,128)(2,1)} %v_ref.3, s32[1,128]{1,0:T(1,128)} %bitcast.3, s32[1,2]{1,0:T(1,128)} %bitcast.5), custom_call_target="tpu_custom_call" | custom-call | flops 1000000000 | bytes 262144 | tf_op jit(solution)/shard_map/pallas_call | solution.py:53
  1.7 3.1 %collective-permute-start = (bf16[136,512]{1,0:T(8,128)(2,1)}, bf16[136,512]{1,0:T(8,128)(2,1)S(1)}, u32[]{:S(2)}, u32[]{:S(2)}) collective-permute-start(bf16[136,512]{1,0:T(8,128)(2,1)} %shard_map.73), channel_id=1, source_target_pairs={{0,4},{4,0},{8,12},{12,8},{1,5},{5,1},{9,13},{13,9},{2,6},{6,2},{1... | collective-permute-start | bytes 417800 | tf_op jit(solution)/shard_map/ppermute | solution.py:274
  4.8 3.9 %collective-permute-done.flip_ref = bf16[136,512]{1,0:T(8,128)(2,1)S(1)} collective-permute-done((bf16[136,512]{1,0:T(8,128)(2,1)}, bf16[136,512]{1,0:T(8,128)(2,1)S(1)}, u32[]{:S(2)}, u32[]{:S(2)}) %collective-permute-start) | collective-permute-done | bytes 139296 | tf_op jit(solution)/shard_map/ppermute | solution.py:274
  8.7 0.7 %shard_map.74 = (bf16[128,1024]{1,0:T(8,128)(2,1)S(1)}, bf16[72,1024]{1,0:T(8,128)(2,1)S(1)}, bf16[64,1024]{1,0:T(8,128)(2,1)S(1)}) custom-call(bf16[128,1024]{1,0:T(8,128)(2,1)S(1)} %copy-done.1, bf16[136,512]{1,0:T(8,128)(2,1)S(1)} %collective-permute-done.flip_ref, bf16[136,512]{1,0:T(8,128)(2,1)S(1)} %collective-permute-done.1.mid_ref, ...), custom_call_target="tpu_custom_call" | custom-call | flops 134217728 | bytes 786432 | tf_op jit(solution)/shard_map/pallas_call | solution.py:132
  9.4 3.0 %collective-permute-start.3 = (bf16[128,1024]{1,0:T(8,128)(2,1)S(1)}, bf16[128,1024]{1,0:T(8,128)(2,1)S(1)}, u32[]{:S(2)}, u32[]{:S(2)}) collective-permute-start(bf16[128,1024]{1,0:T(8,128)(2,1)S(1)} %get-tuple-element.22.refs_0_), channel_id=1, source_target_pairs={{0,4},{4,0},{8,12},{12,8},{1,5},{5,1},{9,13},{13,9},{2,6},{6,2},{1... | collective-permute-start | bytes 786440 | tf_op jit(solution)/shard_map/ppermute | solution.py:274
  12.4 1.4 %collective-permute-start.2 = (bf16[72,1024]{1,0:T(8,128)(2,1)S(1)}, bf16[72,1024]{1,0:T(8,128)(2,1)S(1)}, u32[]{:S(2)}, u32[]{:S(2)}) collective-permute-start(bf16[72,1024]{1,0:T(8,128)(2,1)S(1)} %get-tuple-element.21.noted_ref), channel_id=1, source_target_pairs={{0,8},{4,12},{8,0},{12,4},{1,9},{5,13},{9,1},{13,5},{2,10},{6,14},... | collective-permute-start | bytes 442376 | tf_op jit(solution)/shard_map/ppermute | solution.py:274
  13.8 1.5 %collective-permute-start.5 = (bf16[64,1024]{1,0:T(8,128)(2,1)S(1)}, bf16[64,1024]{1,0:T(8,128)(2,1)S(1)}, u32[]{:S(2)}, u32[]{:S(2)}) collective-permute-start(bf16[64,1024]{1,0:T(8,128)(2,1)S(1)} %get-tuple-element.26), channel_id=1, source_target_pairs={{0,8},{4,12},{8,0},{12,4},{1,9},{5,13},{9,1},{13,5},{2,10},{6,14},... | collective-permute-start | bytes 393224 | tf_op jit(solution)/shard_map/ppermute | solution.py:274
  15.3 7.8 %collective-permute-done.3.refs_1_ = bf16[128,1024]{1,0:T(8,128)(2,1)S(1)} collective-permute-done((bf16[128,1024]{1,0:T(8,128)(2,1)S(1)}, bf16[128,1024]{1,0:T(8,128)(2,1)S(1)}, u32[]{:S(2)}, u32[]{:S(2)}) %collective-permute-start.3) | collective-permute-done | bytes 262176 | tf_op jit(solution)/shard_map/ppermute | solution.py:274
  23.1 0.4 shard_map.75
  23.7 1.4 %collective-permute-start.8 = (bf16[64,1024]{1,0:T(8,128)(2,1)S(1)}, bf16[64,1024]{1,0:T(8,128)(2,1)S(1)}, u32[]{:S(2)}, u32[]{:S(2)}) collective-permute-start(bf16[64,1024]{1,0:T(8,128)(2,1)S(1)} %shard_map.80), channel_id=1, source_target_pairs={{0,4},{4,0},{8,12},{12,8},{1,5},{5,1},{9,13},{13,9},{2,6},{6,2},{1... | collective-permute-start | bytes 393224 | tf_op jit(solution)/shard_map/ppermute | solution.py:274
  25.1 1.4 %collective-permute-done.5.refs_1_ = bf16[64,1024]{1,0:T(8,128)(2,1)S(1)} collective-permute-done((bf16[64,1024]{1,0:T(8,128)(2,1)S(1)}, bf16[64,1024]{1,0:T(8,128)(2,1)S(1)}, u32[]{:S(2)}, u32[]{:S(2)}) %collective-permute-start.5) | collective-permute-done | bytes 131104 | tf_op jit(solution)/shard_map/ppermute | solution.py:274
  26.6 0.3 shard_map.77
  27.0 1.2 %collective-permute-done.6.got_ref = bf16[64,512]{1,0:T(8,128)(2,1)S(1)} collective-permute-done((bf16[64,512]{1,0:T(8,128)(2,1)S(1)}, bf16[64,512]{1,0:T(8,128)(2,1)S(1)}, u32[]{:S(2)}, u32[]{:S(2)}) %collective-permute-start.6) | collective-permute-done | bytes 65568 | tf_op jit(solution)/shard_map/ppermute | solution.py:274
  28.3 1.6 %collective-permute-start.7 = (bf16[192,512]{1,0:T(8,128)(2,1)S(1)}, bf16[192,512]{1,0:T(8,128)(2,1)S(1)}, u32[]{:S(2)}, u32[]{:S(2)}) collective-permute-start(bf16[192,512]{1,0:T(8,128)(2,1)S(1)} %shard_map.78.refs_0_), channel_id=1, source_target_pairs={{0,2},{1,3},{2,0},{3,1},{4,6},{5,7},{6,4},{7,5},{8,10},{9,11},{10,... | collective-permute-start | bytes 589832 | tf_op jit(solution)/shard_map/ppermute | solution.py:274
  30.1 2.4 %collective-permute-done.9.refs_1_ = bf16[64,1024]{1,0:T(8,128)(2,1)S(1)} collective-permute-done((bf16[64,1024]{1,0:T(8,128)(2,1)S(1)}, bf16[64,1024]{1,0:T(8,128)(2,1)S(1)}, u32[]{:S(2)}, u32[]{:S(2)}) %collective-permute-start.9) | collective-permute-done | bytes 131104 | tf_op jit(solution)/shard_map/ppermute | solution.py:274
  32.5 0.3 shard_map.81
  32.9 1.2 %collective-permute-done.10.refs_1_ = bf16[64,512]{1,0:T(8,128)(2,1)S(1)} collective-permute-done((bf16[64,512]{1,0:T(8,128)(2,1)S(1)}, bf16[64,512]{1,0:T(8,128)(2,1)S(1)}, u32[]{:S(2)}, u32[]{:S(2)}) %collective-permute-start.10) | collective-permute-done | bytes 65568 | tf_op jit(solution)/shard_map/ppermute | solution.py:274
  34.1 1.6 %collective-permute-start.11 = (bf16[64,512]{1,0:T(8,128)(2,1)S(1)}, bf16[64,512]{1,0:T(8,128)(2,1)S(1)}, u32[]{:S(2)}, u32[]{:S(2)}) collective-permute-start(bf16[64,512]{1,0:T(8,128)(2,1)S(1)} %shard_map.82.refs_0_), channel_id=1, source_target_pairs={{0,2},{1,3},{2,0},{3,1},{4,6},{5,7},{6,4},{7,5},{8,10},{9,11},{10,... | collective-permute-start | bytes 196616 | tf_op jit(solution)/shard_map/ppermute | solution.py:274
  35.7 2.8 %collective-permute-done.11.refs_1_ = bf16[64,512]{1,0:T(8,128)(2,1)S(1)} collective-permute-done((bf16[64,512]{1,0:T(8,128)(2,1)S(1)}, bf16[64,512]{1,0:T(8,128)(2,1)S(1)}, u32[]{:S(2)}, u32[]{:S(2)}) %collective-permute-start.11) | collective-permute-done | bytes 65568 | tf_op jit(solution)/shard_map/ppermute | solution.py:274
  38.8 2.1 %collective-permute-start.12 = (bf16[32,512]{1,0:T(8,128)(2,1)S(1)}, bf16[32,512]{1,0:T(8,128)(2,1)S(1)}, u32[]{:S(2)}, u32[]{:S(2)}) collective-permute-start(bf16[32,512]{1,0:T(8,128)(2,1)S(1)} %get-tuple-element.34), channel_id=1, source_target_pairs={{0,12},{4,8},{8,4},{12,0},{1,13},{5,9},{9,5},{13,1},{2,14},{6,10},... | collective-permute-start | bytes 98312 | tf_op jit(solution)/shard_map/ppermute | solution.py:274
  40.8 2.4 %collective-permute-start.14 = (bf16[32,512]{1,0:T(8,128)(2,1)S(1)}, bf16[32,512]{1,0:T(8,128)(2,1)S(1)}, u32[]{:S(2)}, u32[]{:S(2)}) collective-permute-start(bf16[32,512]{1,0:T(8,128)(2,1)S(1)} %get-tuple-element.36), channel_id=1, source_target_pairs={{0,4},{4,0},{8,12},{12,8},{1,5},{5,1},{9,13},{13,9},{2,6},{6,2},{1... | collective-permute-start | bytes 98312 | tf_op jit(solution)/shard_map/ppermute | solution.py:274
  43.2 1.6 %collective-permute-done.12.far_ref = bf16[32,512]{1,0:T(8,128)(2,1)S(1)} collective-permute-done((bf16[32,512]{1,0:T(8,128)(2,1)S(1)}, bf16[32,512]{1,0:T(8,128)(2,1)S(1)}, u32[]{:S(2)}, u32[]{:S(2)}) %collective-permute-start.12) | collective-permute-done | bytes 32800 | tf_op jit(solution)/shard_map/ppermute | solution.py:274
  44.8 0.8 %collective-permute-done.13.two_ref = bf16[32,512]{1,0:T(8,128)(2,1)S(1)} collective-permute-done((bf16[32,512]{1,0:T(8,128)(2,1)S(1)}, bf16[32,512]{1,0:T(8,128)(2,1)S(1)}, u32[]{:S(2)}, u32[]{:S(2)}) %collective-permute-start.13) | collective-permute-done | bytes 32800 | tf_op jit(solution)/shard_map/ppermute | solution.py:274
  45.7 0.7 %shard_map.86 = bf16[32,2048]{1,0:T(8,128)(2,1)} custom-call(bf16[32,1024]{1,0:T(8,128)(2,1)S(1)} %shard_map.85.held_ref, bf16[32,512]{1,0:T(8,128)(2,1)S(1)} %collective-permute-done.13.two_ref, bf16[32,512]{1,0:T(8,128)(2,1)S(1)} %collective-permute-done.14.one_ref), custom_call_target="tpu_custom_call" | custom-call | bytes 262144 | tf_op jit(solution)/shard_map/pallas_call | solution.py:263
  (34 shorter events, 0.9 us)
Async XLA Ops:
  0.0 8.6 %copy-start.1 = (bf16[128,1024]{1,0:T(8,128)(2,1)S(1)}, bf16[128,1024]{1,0:T(8,128)(2,1)}, u32[]{:S(2)}) copy-start(bf16[128,1024]{1,0:T(8,128)(2,1)} %q_ref.1) | copy-start | bytes 786436
  0.0 8.6 %copy-start.2 = (bf16[128,256]{1,0:T(8,128)(2,1)S(1)}, bf16[128,256]{1,0:T(8,128)(2,1)}, u32[]{:S(2)}) copy-start(bf16[128,256]{1,0:T(8,128)(2,1)} %k_ref.3) | copy-start | bytes 196612
  0.0 8.7 %copy-start.3 = (bf16[128,256]{1,0:T(8,128)(2,1)S(1)}, bf16[128,256]{1,0:T(8,128)(2,1)}, u32[]{:S(2)}) copy-start(bf16[128,256]{1,0:T(8,128)(2,1)} %v_ref.3) | copy-start | bytes 196612
  0.0 23.1 %copy-start = (bf16[1024,512]{1,0:T(8,128)(2,1)S(1)}, bf16[1024,512]{1,0:T(8,128)(2,1)}, u32[]{:S(2)}) copy-start(bf16[1024,512]{1,0:T(8,128)(2,1)} %refs_2_.5) | copy-start | bytes 3145732
  1.7 7.0 %copy-start.4 = (s32[128]{0:T(128)S(1)}, s32[128]{0:T(128)}, u32[]{:S(2)}) copy-start(s32[128]{0:T(128)} %param.11) | copy-start | bytes 1540
  1.7 7.0 %copy-start.5 = (s32[2]{0:T(128)S(1)}, s32[2]{0:T(128)}, u32[]{:S(2)}) copy-start(s32[2]{0:T(128)} %param.12) | copy-start | bytes 28
  1.7 7.0 %copy-start.6 = (s32[128]{0:T(128)S(1)}, s32[128]{0:T(128)}, u32[]{:S(2)}) copy-start(s32[128]{0:T(128)} %param.10) | copy-start | bytes 1540
  1.7 7.0 %collective-permute-start = (bf16[136,512]{1,0:T(8,128)(2,1)}, bf16[136,512]{1,0:T(8,128)(2,1)S(1)}, u32[]{:S(2)}, u32[]{:S(2)}) collective-permute-start(bf16[136,512]{1,0:T(8,128)(2,1)} %shard_map.73), channel_id=1, source_target_pairs={{0,4},{4,0},{8,12},{12,8},{1,5},{5,1},{9,13},{13,9},{2,6},{6,2},{1... | collective-permute-start | bytes 417800 | tf_op jit(solution)/shard_map/ppermute | solution.py:274
  4.8 3.9 %collective-permute-start.1 = (bf16[136,512]{1,0:T(8,128)(2,1)}, bf16[136,512]{1,0:T(8,128)(2,1)S(1)}, u32[]{:S(2)}, u32[]{:S(2)}) collective-permute-start(bf16[136,512]{1,0:T(8,128)(2,1)} %shard_map.73), channel_id=1, source_target_pairs={{0,1},{1,0},{2,3},{3,2},{4,8},{5,9},{6,10},{7,11},{8,4},{9,5},{10,... | collective-permute-start | bytes 417800 | tf_op jit(solution)/shard_map/ppermute | solution.py:317
  9.4 13.7 %collective-permute-start.3 = (bf16[128,1024]{1,0:T(8,128)(2,1)S(1)}, bf16[128,1024]{1,0:T(8,128)(2,1)S(1)}, u32[]{:S(2)}, u32[]{:S(2)}) collective-permute-start(bf16[128,1024]{1,0:T(8,128)(2,1)S(1)} %get-tuple-element.22.refs_0_), channel_id=1, source_target_pairs={{0,4},{4,0},{8,12},{12,8},{1,5},{5,1},{9,13},{13,9},{2,6},{6,2},{1... | collective-permute-start | bytes 786440 | tf_op jit(solution)/shard_map/ppermute | solution.py:274
  12.4 11.3 %collective-permute-start.2 = (bf16[72,1024]{1,0:T(8,128)(2,1)S(1)}, bf16[72,1024]{1,0:T(8,128)(2,1)S(1)}, u32[]{:S(2)}, u32[]{:S(2)}) collective-permute-start(bf16[72,1024]{1,0:T(8,128)(2,1)S(1)} %get-tuple-element.21.noted_ref), channel_id=1, source_target_pairs={{0,8},{4,12},{8,0},{12,4},{1,9},{5,13},{9,1},{13,5},{2,10},{6,14},... | collective-permute-start | bytes 442376 | tf_op jit(solution)/shard_map/ppermute | solution.py:274
  13.8 12.7 %collective-permute-start.5 = (bf16[64,1024]{1,0:T(8,128)(2,1)S(1)}, bf16[64,1024]{1,0:T(8,128)(2,1)S(1)}, u32[]{:S(2)}, u32[]{:S(2)}) collective-permute-start(bf16[64,1024]{1,0:T(8,128)(2,1)S(1)} %get-tuple-element.26), channel_id=1, source_target_pairs={{0,8},{4,12},{8,0},{12,4},{1,9},{5,13},{9,1},{13,5},{2,10},{6,14},... | collective-permute-start | bytes 393224 | tf_op jit(solution)/shard_map/ppermute | solution.py:274
  23.6 3.0 %collective-permute-start.4 = (bf16[128,512]{1,0:T(8,128)(2,1)S(1)}, bf16[128,512]{1,0:T(8,128)(2,1)S(1)}, u32[]{:S(2)}, u32[]{:S(2)}) collective-permute-start(bf16[128,512]{1,0:T(8,128)(2,1)S(1)} %get-tuple-element.24), channel_id=1, source_target_pairs={{0,1},{1,0},{2,3},{3,2},{4,5},{5,4},{6,7},{7,6},{8,9},{9,8},{10,11... | collective-permute-start | bytes 393224 | tf_op jit(solution)/shard_map/ppermute | solution.py:274
  23.7 6.4 %collective-permute-start.8 = (bf16[64,1024]{1,0:T(8,128)(2,1)S(1)}, bf16[64,1024]{1,0:T(8,128)(2,1)S(1)}, u32[]{:S(2)}, u32[]{:S(2)}) collective-permute-start(bf16[64,1024]{1,0:T(8,128)(2,1)S(1)} %shard_map.80), channel_id=1, source_target_pairs={{0,4},{4,0},{8,12},{12,8},{1,5},{5,1},{9,13},{13,9},{2,6},{6,2},{1... | collective-permute-start | bytes 393224 | tf_op jit(solution)/shard_map/ppermute | solution.py:274
  26.6 5.9 %collective-permute-start.9 = (bf16[64,1024]{1,0:T(8,128)(2,1)S(1)}, bf16[64,1024]{1,0:T(8,128)(2,1)S(1)}, u32[]{:S(2)}, u32[]{:S(2)}) collective-permute-start(bf16[64,1024]{1,0:T(8,128)(2,1)S(1)} %collective-permute-done.5.refs_1_), channel_id=1, source_target_pairs={{0,4},{4,0},{8,12},{12,8},{1,5},{5,1},{9,13},{13,9},{2,6},{6,2},{1... | collective-permute-start | bytes 393224 | tf_op jit(solution)/shard_map/ppermute | solution.py:274
  26.9 1.3 %collective-permute-start.6 = (bf16[64,512]{1,0:T(8,128)(2,1)S(1)}, bf16[64,512]{1,0:T(8,128)(2,1)S(1)}, u32[]{:S(2)}, u32[]{:S(2)}) collective-permute-start(bf16[64,512]{1,0:T(8,128)(2,1)S(1)} %get-tuple-element.29), channel_id=1, source_target_pairs={{0,1},{1,0},{2,3},{3,2},{4,5},{5,4},{6,7},{7,6},{8,9},{9,8},{10,11... | collective-permute-start | bytes 196616 | tf_op jit(solution)/shard_map/ppermute | solution.py:274
  28.3 10.2 %collective-permute-start.7 = (bf16[192,512]{1,0:T(8,128)(2,1)S(1)}, bf16[192,512]{1,0:T(8,128)(2,1)S(1)}, u32[]{:S(2)}, u32[]{:S(2)}) collective-permute-start(bf16[192,512]{1,0:T(8,128)(2,1)S(1)} %shard_map.78.refs_0_), channel_id=1, source_target_pairs={{0,2},{1,3},{2,0},{3,1},{4,6},{5,7},{6,4},{7,5},{8,10},{9,11},{10,... | collective-permute-start | bytes 589832 | tf_op jit(solution)/shard_map/ppermute | solution.py:274
  32.8 1.3 %collective-permute-start.10 = (bf16[64,512]{1,0:T(8,128)(2,1)S(1)}, bf16[64,512]{1,0:T(8,128)(2,1)S(1)}, u32[]{:S(2)}, u32[]{:S(2)}) collective-permute-start(bf16[64,512]{1,0:T(8,128)(2,1)S(1)} %get-tuple-element.32), channel_id=1, source_target_pairs={{0,1},{1,0},{2,3},{3,2},{4,5},{5,4},{6,7},{7,6},{8,9},{9,8},{10,11... | collective-permute-start | bytes 196616 | tf_op jit(solution)/shard_map/ppermute | solution.py:274
  34.1 4.3 %collective-permute-start.11 = (bf16[64,512]{1,0:T(8,128)(2,1)S(1)}, bf16[64,512]{1,0:T(8,128)(2,1)S(1)}, u32[]{:S(2)}, u32[]{:S(2)}) collective-permute-start(bf16[64,512]{1,0:T(8,128)(2,1)S(1)} %shard_map.82.refs_0_), channel_id=1, source_target_pairs={{0,2},{1,3},{2,0},{3,1},{4,6},{5,7},{6,4},{7,5},{8,10},{9,11},{10,... | collective-permute-start | bytes 196616 | tf_op jit(solution)/shard_map/ppermute | solution.py:274
  38.8 6.1 %collective-permute-start.12 = (bf16[32,512]{1,0:T(8,128)(2,1)S(1)}, bf16[32,512]{1,0:T(8,128)(2,1)S(1)}, u32[]{:S(2)}, u32[]{:S(2)}) collective-permute-start(bf16[32,512]{1,0:T(8,128)(2,1)S(1)} %get-tuple-element.34), channel_id=1, source_target_pairs={{0,12},{4,8},{8,4},{12,0},{1,13},{5,9},{9,5},{13,1},{2,14},{6,10},... | collective-permute-start | bytes 98312 | tf_op jit(solution)/shard_map/ppermute | solution.py:274
  40.8 4.8 %collective-permute-start.13 = (bf16[32,512]{1,0:T(8,128)(2,1)S(1)}, bf16[32,512]{1,0:T(8,128)(2,1)S(1)}, u32[]{:S(2)}, u32[]{:S(2)}) collective-permute-start(bf16[32,512]{1,0:T(8,128)(2,1)S(1)} %get-tuple-element.35), channel_id=1, source_target_pairs={{0,8},{4,12},{8,0},{12,4},{1,9},{5,13},{9,1},{13,5},{2,10},{6,14},... | collective-permute-start | bytes 98312 | tf_op jit(solution)/shard_map/ppermute | solution.py:274
  40.8 4.8 %collective-permute-start.14 = (bf16[32,512]{1,0:T(8,128)(2,1)S(1)}, bf16[32,512]{1,0:T(8,128)(2,1)S(1)}, u32[]{:S(2)}, u32[]{:S(2)}) collective-permute-start(bf16[32,512]{1,0:T(8,128)(2,1)S(1)} %get-tuple-element.36), channel_id=1, source_target_pairs={{0,4},{4,0},{8,12},{12,8},{1,5},{5,1},{9,13},{13,9},{2,6},{6,2},{1... | collective-permute-start | bytes 98312 | tf_op jit(solution)/shard_map/ppermute | solution.py:274

commit v18 on v14

--- a/solution.py
+++ b/solution.py
@@ -250,7 +250,7 @@
     )(near, far)
 
 
-def join_kernel(held_ref, two_ref, one_ref, out_ref):
+def join_kernel(held_ref, one_ref, two_ref, out_ref):
     cols = one_ref.shape[1]
     c = lax.axis_index("ctx")
     pieces = (held_ref[:, pl.ds(0, cols)], one_ref[...], two_ref[...], held_ref[:, pl.ds(cols, cols)])
@@ -258,7 +258,7 @@
         out_ref[:, pl.ds(pl.multiple_of((c ^ k) * cols, cols), cols)] = pieces[k]
 
 
-def join(held, two, one):
+def join(held, one, two):
     rows, cols = one.shape
     return pl.pallas_call(
         join_kernel,
@@ -267,7 +267,7 @@
         out_specs=pl.BlockSpec(memory_space=pltpu.VMEM),
         compiler_params=params(),
         cost_estimate=cost(0, 16 * one.size),
-    )(held, two, one)
+    )(held, one, two)
 
 
 def flip(array, axis, bits):
@@ -328,8 +328,8 @@
     share_c = core_total(*project(block_rows, (first_3, second_3), out_weight, cost(100 * 10**8, 0)))
     sums = (chip_total(share_b), chip_total(share_c))
     kept, *sent = pick(blocks, first, first_2, sums)
-    got_3, got_2, got_1 = (flip(sent[k - 1], "ctx", k) for k in (3, 2, 1))
-    return join(hold(kept, got_3), got_2, got_1)
+    got_3, got_1, got_2 = (flip(sent[k - 1], "ctx", k) for k in (3, 1, 2))
+    return join(hold(kept, got_3), got_1, got_2)
 
 
 def attend_block(soft_state, query_grid, query_pos, query_start, key_block, value_block, key_end, key_pos):

time: 46.7 us -> 46.7 us (level)
  transfers between devices with their start and end apart: 15 -> 15, of which waited for: 10 -> 11; matrix products, arithmetic and copies ran while one was open for 0% -> 0% of each run, Pallas kernels for 3% -> 3%
where the time goes in v18:
time: 46.7 us; the launch traced here: 46.5 us
  waiting for transfers between devices  23.6 us (51%)
  starting transfers between devices  18.2 us (39%)
  Pallas kernels  4.5 us (10%)
    ppermute x14, waiting for transfers between devices, flip(): return lax.ppermute(array, axis, [(i, i ^ bits) for i in range(4)])  23.6 us
    ppermute x14, starting transfers between devices, flip(): return lax.ppermute(array, axis, [(i, i ^ bits) for i in range(4)])  18.2 us
    pallas_call x1, Pallas kernels, pack(): pl.pallas_call(pack_kernel, out_shape=jax.ShapeDtypeStruct((rows + 16, 2...  1.66 us
    pallas_call x3, Pallas kernels, project(): pl.pallas_call(functools.partial(project_kernel, block_rows), out_shape=(...  1.05 us
  transfers between devices with their start and end apart: 15, of which 11 were waited for; matrix products, arithmetic and copies ran while one was open for 0% of the time, Pallas kernels for 3%

profile of v18, /device:TPU:0, one launch (start us, length us, event | category | flops | bytes accessed | tf_op | source)
XLA Modules:
  0.0 46.5 jit_solution(16633527807762796492)
XLA Ops:
  0.0 1.7 %shard_map.73 = bf16[144,512]{1,0:T(8,128)(2,1)} custom-call(bf16[128,256]{1,0:T(8,128)(2,1)} %k_ref.3, bf16[128,256]{1,0:T(8,128)(2,1)} %v_ref.3, s32[1,128]{1,0:T(1,128)} %bitcast.3, s32[1,2]{1,0:T(1,128)} %bitcast.5), custom_call_target="tpu_custom_call" | custom-call | flops 1000000000 | bytes 262144 | tf_op jit(solution)/shard_map/pallas_call | solution.py:53
  1.7 3.1 %collective-permute-start = (bf16[144,512]{1,0:T(8,128)(2,1)}, bf16[144,512]{1,0:T(8,128)(2,1)S(1)}, u32[]{:S(2)}, u32[]{:S(2)}) collective-permute-start(bf16[144,512]{1,0:T(8,128)(2,1)} %shard_map.73), channel_id=1, source_target_pairs={{0,4},{4,0},{8,12},{12,8},{1,5},{5,1},{9,13},{13,9},{2,6},{6,2},{1... | collective-permute-start | bytes 442376 | tf_op jit(solution)/shard_map/ppermute | solution.py:274
  4.8 4.1 %collective-permute-done.flip_ref = bf16[144,512]{1,0:T(8,128)(2,1)S(1)} collective-permute-done((bf16[144,512]{1,0:T(8,128)(2,1)}, bf16[144,512]{1,0:T(8,128)(2,1)S(1)}, u32[]{:S(2)}, u32[]{:S(2)}) %collective-permute-start) | collective-permute-done | bytes 147488 | tf_op jit(solution)/shard_map/ppermute | solution.py:274
  8.9 0.7 %shard_map.74 = (bf16[128,1024]{1,0:T(8,128)(2,1)S(1)}, bf16[72,1024]{1,0:T(8,128)(2,1)S(1)}, bf16[64,1024]{1,0:T(8,128)(2,1)S(1)}) custom-call(bf16[128,1024]{1,0:T(8,128)(2,1)S(1)} %copy-done.1, bf16[144,512]{1,0:T(8,128)(2,1)S(1)} %collective-permute-done.flip_ref, bf16[144,512]{1,0:T(8,128)(2,1)S(1)} %collective-permute-done.1.mid_ref, ...), custom_call_target="tpu_custom_call" | custom-call | flops 134217728 | bytes 786432 | tf_op jit(solution)/shard_map/pallas_call | solution.py:132
  9.6 3.0 %collective-permute-start.3 = (bf16[128,1024]{1,0:T(8,128)(2,1)S(1)}, bf16[128,1024]{1,0:T(8,128)(2,1)S(1)}, u32[]{:S(2)}, u32[]{:S(2)}) collective-permute-start(bf16[128,1024]{1,0:T(8,128)(2,1)S(1)} %get-tuple-element.22.refs_0_), channel_id=1, source_target_pairs={{0,4},{4,0},{8,12},{12,8},{1,5},{5,1},{9,13},{13,9},{2,6},{6,2},{1... | collective-permute-start | bytes 786440 | tf_op jit(solution)/shard_map/ppermute | solution.py:274
  12.6 1.4 %collective-permute-start.2 = (bf16[72,1024]{1,0:T(8,128)(2,1)S(1)}, bf16[72,1024]{1,0:T(8,128)(2,1)S(1)}, u32[]{:S(2)}, u32[]{:S(2)}) collective-permute-start(bf16[72,1024]{1,0:T(8,128)(2,1)S(1)} %get-tuple-element.21.noted_ref), channel_id=1, source_target_pairs={{0,8},{4,12},{8,0},{12,4},{1,9},{5,13},{9,1},{13,5},{2,10},{6,14},... | collective-permute-start | bytes 442376 | tf_op jit(solution)/shard_map/ppermute | solution.py:274
  14.0 1.5 %collective-permute-start.5 = (bf16[64,1024]{1,0:T(8,128)(2,1)S(1)}, bf16[64,1024]{1,0:T(8,128)(2,1)S(1)}, u32[]{:S(2)}, u32[]{:S(2)}) collective-permute-start(bf16[64,1024]{1,0:T(8,128)(2,1)S(1)} %get-tuple-element.26), channel_id=1, source_target_pairs={{0,8},{4,12},{8,0},{12,4},{1,9},{5,13},{9,1},{13,5},{2,10},{6,14},... | collective-permute-start | bytes 393224 | tf_op jit(solution)/shard_map/ppermute | solution.py:274
  15.5 7.8 %collective-permute-done.3.refs_1_ = bf16[128,1024]{1,0:T(8,128)(2,1)S(1)} collective-permute-done((bf16[128,1024]{1,0:T(8,128)(2,1)S(1)}, bf16[128,1024]{1,0:T(8,128)(2,1)S(1)}, u32[]{:S(2)}, u32[]{:S(2)}) %collective-permute-start.3) | collective-permute-done | bytes 262176 | tf_op jit(solution)/shard_map/ppermute | solution.py:274
  23.3 0.4 shard_map.75
  23.9 1.4 %collective-permute-start.8 = (bf16[64,1024]{1,0:T(8,128)(2,1)S(1)}, bf16[64,1024]{1,0:T(8,128)(2,1)S(1)}, u32[]{:S(2)}, u32[]{:S(2)}) collective-permute-start(bf16[64,1024]{1,0:T(8,128)(2,1)S(1)} %shard_map.80), channel_id=1, source_target_pairs={{0,4},{4,0},{8,12},{12,8},{1,5},{5,1},{9,13},{13,9},{2,6},{6,2},{1... | collective-permute-start | bytes 393224 | tf_op jit(solution)/shard_map/ppermute | solution.py:274
  25.3 1.4 %collective-permute-done.5.refs_1_ = bf16[64,1024]{1,0:T(8,128)(2,1)S(1)} collective-permute-done((bf16[64,1024]{1,0:T(8,128)(2,1)S(1)}, bf16[64,1024]{1,0:T(8,128)(2,1)S(1)}, u32[]{:S(2)}, u32[]{:S(2)}) %collective-permute-start.5) | collective-permute-done | bytes 131104 | tf_op jit(solution)/shard_map/ppermute | solution.py:274
  26.8 0.3 shard_map.77
  27.2 1.2 %collective-permute-done.6.got_ref = bf16[64,512]{1,0:T(8,128)(2,1)S(1)} collective-permute-done((bf16[64,512]{1,0:T(8,128)(2,1)S(1)}, bf16[64,512]{1,0:T(8,128)(2,1)S(1)}, u32[]{:S(2)}, u32[]{:S(2)}) %collective-permute-start.6) | collective-permute-done | bytes 65568 | tf_op jit(solution)/shard_map/ppermute | solution.py:274
  28.5 1.6 %collective-permute-start.7 = (bf16[192,512]{1,0:T(8,128)(2,1)S(1)}, bf16[192,512]{1,0:T(8,128)(2,1)S(1)}, u32[]{:S(2)}, u32[]{:S(2)}) collective-permute-start(bf16[192,512]{1,0:T(8,128)(2,1)S(1)} %shard_map.78.refs_0_), channel_id=1, source_target_pairs={{0,2},{1,3},{2,0},{3,1},{4,6},{5,7},{6,4},{7,5},{8,10},{9,11},{10,... | collective-permute-start | bytes 589832 | tf_op jit(solution)/shard_map/ppermute | solution.py:274
  30.2 2.4 %collective-permute-done.9.refs_1_ = bf16[64,1024]{1,0:T(8,128)(2,1)S(1)} collective-permute-done((bf16[64,1024]{1,0:T(8,128)(2,1)S(1)}, bf16[64,1024]{1,0:T(8,128)(2,1)S(1)}, u32[]{:S(2)}, u32[]{:S(2)}) %collective-permute-start.9) | collective-permute-done | bytes 131104 | tf_op jit(solution)/shard_map/ppermute | solution.py:274
  32.6 0.3 shard_map.81
  33.0 1.2 %collective-permute-done.10.refs_1_ = bf16[64,512]{1,0:T(8,128)(2,1)S(1)} collective-permute-done((bf16[64,512]{1,0:T(8,128)(2,1)S(1)}, bf16[64,512]{1,0:T(8,128)(2,1)S(1)}, u32[]{:S(2)}, u32[]{:S(2)}) %collective-permute-start.10) | collective-permute-done | bytes 65568 | tf_op jit(solution)/shard_map/ppermute | solution.py:274
  34.3 1.6 %collective-permute-start.11 = (bf16[64,512]{1,0:T(8,128)(2,1)S(1)}, bf16[64,512]{1,0:T(8,128)(2,1)S(1)}, u32[]{:S(2)}, u32[]{:S(2)}) collective-permute-start(bf16[64,512]{1,0:T(8,128)(2,1)S(1)} %shard_map.82.refs_0_), channel_id=1, source_target_pairs={{0,2},{1,3},{2,0},{3,1},{4,6},{5,7},{6,4},{7,5},{8,10},{9,11},{10,... | collective-permute-start | bytes 196616 | tf_op jit(solution)/shard_map/ppermute | solution.py:274
  35.9 2.8 %collective-permute-done.11.refs_1_ = bf16[64,512]{1,0:T(8,128)(2,1)S(1)} collective-permute-done((bf16[64,512]{1,0:T(8,128)(2,1)S(1)}, bf16[64,512]{1,0:T(8,128)(2,1)S(1)}, u32[]{:S(2)}, u32[]{:S(2)}) %collective-permute-start.11) | collective-permute-done | bytes 65568 | tf_op jit(solution)/shard_map/ppermute | solution.py:274
  39.0 2.1 %collective-permute-start.12 = (bf16[32,512]{1,0:T(8,128)(2,1)S(1)}, bf16[32,512]{1,0:T(8,128)(2,1)S(1)}, u32[]{:S(2)}, u32[]{:S(2)}) collective-permute-start(bf16[32,512]{1,0:T(8,128)(2,1)S(1)} %get-tuple-element.34), channel_id=1, source_target_pairs={{0,12},{4,8},{8,4},{12,0},{1,13},{5,9},{9,5},{13,1},{2,14},{6,10},... | collective-permute-start | bytes 98312 | tf_op jit(solution)/shard_map/ppermute | solution.py:274
  41.0 2.4 %collective-permute-start.14 = (bf16[32,512]{1,0:T(8,128)(2,1)S(1)}, bf16[32,512]{1,0:T(8,128)(2,1)S(1)}, u32[]{:S(2)}, u32[]{:S(2)}) collective-permute-start(bf16[32,512]{1,0:T(8,128)(2,1)S(1)} %get-tuple-element.36), channel_id=1, source_target_pairs={{0,8},{4,12},{8,0},{12,4},{1,9},{5,13},{9,1},{13,5},{2,10},{6,14},... | collective-permute-start | bytes 98312 | tf_op jit(solution)/shard_map/ppermute | solution.py:274
  43.4 1.6 %collective-permute-done.12.far_ref = bf16[32,512]{1,0:T(8,128)(2,1)S(1)} collective-permute-done((bf16[32,512]{1,0:T(8,128)(2,1)S(1)}, bf16[32,512]{1,0:T(8,128)(2,1)S(1)}, u32[]{:S(2)}, u32[]{:S(2)}) %collective-permute-start.12) | collective-permute-done | bytes 32800 | tf_op jit(solution)/shard_map/ppermute | solution.py:274
  45.2 0.7 %collective-permute-done.14.two_ref = bf16[32,512]{1,0:T(8,128)(2,1)S(1)} collective-permute-done((bf16[32,512]{1,0:T(8,128)(2,1)S(1)}, bf16[32,512]{1,0:T(8,128)(2,1)S(1)}, u32[]{:S(2)}, u32[]{:S(2)}) %collective-permute-start.14) | collective-permute-done | bytes 32800 | tf_op jit(solution)/shard_map/ppermute | solution.py:274
  45.8 0.7 %shard_map.86 = bf16[32,2048]{1,0:T(8,128)(2,1)} custom-call(bf16[32,1024]{1,0:T(8,128)(2,1)S(1)} %shard_map.85.held_ref, bf16[32,512]{1,0:T(8,128)(2,1)S(1)} %collective-permute-done.13.one_ref, bf16[32,512]{1,0:T(8,128)(2,1)S(1)} %collective-permute-done.14.two_ref), custom_call_target="tpu_custom_call" | custom-call | bytes 262144 | tf_op jit(solution)/shard_map/pallas_call | solution.py:263
  (34 shorter events, 1.0 us)
Async XLA Ops:
  0.0 8.8 %copy-start.1 = (bf16[128,1024]{1,0:T(8,128)(2,1)S(1)}, bf16[128,1024]{1,0:T(8,128)(2,1)}, u32[]{:S(2)}) copy-start(bf16[128,1024]{1,0:T(8,128)(2,1)} %q_ref.1) | copy-start | bytes 786436
  0.0 8.8 %copy-start.2 = (bf16[128,256]{1,0:T(8,128)(2,1)S(1)}, bf16[128,256]{1,0:T(8,128)(2,1)}, u32[]{:S(2)}) copy-start(bf16[128,256]{1,0:T(8,128)(2,1)} %k_ref.3) | copy-start | bytes 196612
  0.0 8.8 %copy-start.3 = (bf16[128,256]{1,0:T(8,128)(2,1)S(1)}, bf16[128,256]{1,0:T(8,128)(2,1)}, u32[]{:S(2)}) copy-start(bf16[128,256]{1,0:T(8,128)(2,1)} %v_ref.3) | copy-start | bytes 196612
  0.0 23.3 %copy-start = (bf16[1024,512]{1,0:T(8,128)(2,1)S(1)}, bf16[1024,512]{1,0:T(8,128)(2,1)}, u32[]{:S(2)}) copy-start(bf16[1024,512]{1,0:T(8,128)(2,1)} %refs_2_.5) | copy-start | bytes 3145732
  1.7 7.2 %copy-start.4 = (s32[128]{0:T(128)S(1)}, s32[128]{0:T(128)}, u32[]{:S(2)}) copy-start(s32[128]{0:T(128)} %param.11) | copy-start | bytes 1540
  1.7 7.2 %copy-start.5 = (s32[2]{0:T(128)S(1)}, s32[2]{0:T(128)}, u32[]{:S(2)}) copy-start(s32[2]{0:T(128)} %param.12) | copy-start | bytes 28
  1.7 7.2 %copy-start.6 = (s32[128]{0:T(128)S(1)}, s32[128]{0:T(128)}, u32[]{:S(2)}) copy-start(s32[128]{0:T(128)} %param.10) | copy-start | bytes 1540
  1.7 7.2 %collective-permute-start = (bf16[144,512]{1,0:T(8,128)(2,1)}, bf16[144,512]{1,0:T(8,128)(2,1)S(1)}, u32[]{:S(2)}, u32[]{:S(2)}) collective-permute-start(bf16[144,512]{1,0:T(8,128)(2,1)} %shard_map.73), channel_id=1, source_target_pairs={{0,4},{4,0},{8,12},{12,8},{1,5},{5,1},{9,13},{13,9},{2,6},{6,2},{1... | collective-permute-start | bytes 442376 | tf_op jit(solution)/shard_map/ppermute | solution.py:274
  4.8 4.1 %collective-permute-start.1 = (bf16[144,512]{1,0:T(8,128)(2,1)}, bf16[144,512]{1,0:T(8,128)(2,1)S(1)}, u32[]{:S(2)}, u32[]{:S(2)}) collective-permute-start(bf16[144,512]{1,0:T(8,128)(2,1)} %shard_map.73), channel_id=1, source_target_pairs={{0,1},{1,0},{2,3},{3,2},{4,8},{5,9},{6,10},{7,11},{8,4},{9,5},{10,... | collective-permute-start | bytes 442376 | tf_op jit(solution)/shard_map/ppermute | solution.py:317
  9.6 13.7 %collective-permute-start.3 = (bf16[128,1024]{1,0:T(8,128)(2,1)S(1)}, bf16[128,1024]{1,0:T(8,128)(2,1)S(1)}, u32[]{:S(2)}, u32[]{:S(2)}) collective-permute-start(bf16[128,1024]{1,0:T(8,128)(2,1)S(1)} %get-tuple-element.22.refs_0_), channel_id=1, source_target_pairs={{0,4},{4,0},{8,12},{12,8},{1,5},{5,1},{9,13},{13,9},{2,6},{6,2},{1... | collective-permute-start | bytes 786440 | tf_op jit(solution)/shard_map/ppermute | solution.py:274
  12.6 11.3 %collective-permute-start.2 = (bf16[72,1024]{1,0:T(8,128)(2,1)S(1)}, bf16[72,1024]{1,0:T(8,128)(2,1)S(1)}, u32[]{:S(2)}, u32[]{:S(2)}) collective-permute-start(bf16[72,1024]{1,0:T(8,128)(2,1)S(1)} %get-tuple-element.21.noted_ref), channel_id=1, source_target_pairs={{0,8},{4,12},{8,0},{12,4},{1,9},{5,13},{9,1},{13,5},{2,10},{6,14},... | collective-permute-start | bytes 442376 | tf_op jit(solution)/shard_map/ppermute | solution.py:274
  14.0 12.7 %collective-permute-start.5 = (bf16[64,1024]{1,0:T(8,128)(2,1)S(1)}, bf16[64,1024]{1,0:T(8,128)(2,1)S(1)}, u32[]{:S(2)}, u32[]{:S(2)}) collective-permute-start(bf16[64,1024]{1,0:T(8,128)(2,1)S(1)} %get-tuple-element.26), channel_id=1, source_target_pairs={{0,8},{4,12},{8,0},{12,4},{1,9},{5,13},{9,1},{13,5},{2,10},{6,14},... | collective-permute-start | bytes 393224 | tf_op jit(solution)/shard_map/ppermute | solution.py:274
  23.8 3.0 %collective-permute-start.4 = (bf16[128,512]{1,0:T(8,128)(2,1)S(1)}, bf16[128,512]{1,0:T(8,128)(2,1)S(1)}, u32[]{:S(2)}, u32[]{:S(2)}) collective-permute-start(bf16[128,512]{1,0:T(8,128)(2,1)S(1)} %get-tuple-element.24), channel_id=1, source_target_pairs={{0,1},{1,0},{2,3},{3,2},{4,5},{5,4},{6,7},{7,6},{8,9},{9,8},{10,11... | collective-permute-start | bytes 393224 | tf_op jit(solution)/shard_map/ppermute | solution.py:274
  23.9 6.4 %collective-permute-start.8 = (bf16[64,1024]{1,0:T(8,128)(2,1)S(1)}, bf16[64,1024]{1,0:T(8,128)(2,1)S(1)}, u32[]{:S(2)}, u32[]{:S(2)}) collective-permute-start(bf16[64,1024]{1,0:T(8,128)(2,1)S(1)} %shard_map.80), channel_id=1, source_target_pairs={{0,4},{4,0},{8,12},{12,8},{1,5},{5,1},{9,13},{13,9},{2,6},{6,2},{1... | collective-permute-start | bytes 393224 | tf_op jit(solution)/shard_map/ppermute | solution.py:274
  26.7 5.9 %collective-permute-start.9 = (bf16[64,1024]{1,0:T(8,128)(2,1)S(1)}, bf16[64,1024]{1,0:T(8,128)(2,1)S(1)}, u32[]{:S(2)}, u32[]{:S(2)}) collective-permute-start(bf16[64,1024]{1,0:T(8,128)(2,1)S(1)} %collective-permute-done.5.refs_1_), channel_id=1, source_target_pairs={{0,4},{4,0},{8,12},{12,8},{1,5},{5,1},{9,13},{13,9},{2,6},{6,2},{1... | collective-permute-start | bytes 393224 | tf_op jit(solution)/shard_map/ppermute | solution.py:274
  27.1 1.3 %collective-permute-start.6 = (bf16[64,512]{1,0:T(8,128)(2,1)S(1)}, bf16[64,512]{1,0:T(8,128)(2,1)S(1)}, u32[]{:S(2)}, u32[]{:S(2)}) collective-permute-start(bf16[64,512]{1,0:T(8,128)(2,1)S(1)} %get-tuple-element.29), channel_id=1, source_target_pairs={{0,1},{1,0},{2,3},{3,2},{4,5},{5,4},{6,7},{7,6},{8,9},{9,8},{10,11... | collective-permute-start | bytes 196616 | tf_op jit(solution)/shard_map/ppermute | solution.py:274
  28.5 10.2 %collective-permute-start.7 = (bf16[192,512]{1,0:T(8,128)(2,1)S(1)}, bf16[192,512]{1,0:T(8,128)(2,1)S(1)}, u32[]{:S(2)}, u32[]{:S(2)}) collective-permute-start(bf16[192,512]{1,0:T(8,128)(2,1)S(1)} %shard_map.78.refs_0_), channel_id=1, source_target_pairs={{0,2},{1,3},{2,0},{3,1},{4,6},{5,7},{6,4},{7,5},{8,10},{9,11},{10,... | collective-permute-start | bytes 589832 | tf_op jit(solution)/shard_map/ppermute | solution.py:274
  33.0 1.3 %collective-permute-start.10 = (bf16[64,512]{1,0:T(8,128)(2,1)S(1)}, bf16[64,512]{1,0:T(8,128)(2,1)S(1)}, u32[]{:S(2)}, u32[]{:S(2)}) collective-permute-start(bf16[64,512]{1,0:T(8,128)(2,1)S(1)} %get-tuple-element.32), channel_id=1, source_target_pairs={{0,1},{1,0},{2,3},{3,2},{4,5},{5,4},{6,7},{7,6},{8,9},{9,8},{10,11... | collective-permute-start | bytes 196616 | tf_op jit(solution)/shard_map/ppermute | solution.py:274
  34.3 4.3 %collective-permute-start.11 = (bf16[64,512]{1,0:T(8,128)(2,1)S(1)}, bf16[64,512]{1,0:T(8,128)(2,1)S(1)}, u32[]{:S(2)}, u32[]{:S(2)}) collective-permute-start(bf16[64,512]{1,0:T(8,128)(2,1)S(1)} %shard_map.82.refs_0_), channel_id=1, source_target_pairs={{0,2},{1,3},{2,0},{3,1},{4,6},{5,7},{6,4},{7,5},{8,10},{9,11},{10,... | collective-permute-start | bytes 196616 | tf_op jit(solution)/shard_map/ppermute | solution.py:274
  39.0 6.1 %collective-permute-start.12 = (bf16[32,512]{1,0:T(8,128)(2,1)S(1)}, bf16[32,512]{1,0:T(8,128)(2,1)S(1)}, u32[]{:S(2)}, u32[]{:S(2)}) collective-permute-start(bf16[32,512]{1,0:T(8,128)(2,1)S(1)} %get-tuple-element.34), channel_id=1, source_target_pairs={{0,12},{4,8},{8,4},{12,0},{1,13},{5,9},{9,5},{13,1},{2,14},{6,10},... | collective-permute-start | bytes 98312 | tf_op jit(solution)/shard_map/ppermute | solution.py:274
  41.0 4.1 %collective-permute-start.13 = (bf16[32,512]{1,0:T(8,128)(2,1)S(1)}, bf16[32,512]{1,0:T(8,128)(2,1)S(1)}, u32[]{:S(2)}, u32[]{:S(2)}) collective-permute-start(bf16[32,512]{1,0:T(8,128)(2,1)S(1)} %get-tuple-element.35), channel_id=1, source_target_pairs={{0,4},{4,0},{8,12},{12,8},{1,5},{5,1},{9,13},{13,9},{2,6},{6,2},{1... | collective-permute-start | bytes 98312 | tf_op jit(solution)/shard_map/ppermute | solution.py:274
  41.0 4.8 %collective-permute-start.14 = (bf16[32,512]{1,0:T(8,128)(2,1)S(1)}, bf16[32,512]{1,0:T(8,128)(2,1)S(1)}, u32[]{:S(2)}, u32[]{:S(2)}) collective-permute-start(bf16[32,512]{1,0:T(8,128)(2,1)S(1)} %get-tuple-element.36), channel_id=1, source_target_pairs={{0,8},{4,12},{8,0},{12,4},{1,9},{5,13},{9,1},{13,5},{2,10},{6,14},... | collective-permute-start | bytes 98312 | tf_op jit(solution)/shard_map/ppermute | solution.py:274

commit v19 on v14

--- a/solution.py
+++ b/solution.py
@@ -191,7 +191,11 @@
     sums, outs = refs[:-4], refs[-4:]
     x = lax.axis_index("tp") // 2
     c = lax.axis_index("ctx")
+    *sums, mine_ref, got_ref = sums
     pieces = [r[pl.ds(n, half), :] for r in sums for n in range(0, r.shape[0], half)]
+    last = mine_ref[...].astype(jnp.float32) + got_ref[...].astype(jnp.float32)
+    last = last.astype(jnp.bfloat16)
+    pieces += [last[n : n + half] for n in range(0, last.shape[0], half)]
     targets = jnp.concatenate([note(r, 2 * blocks) for r in (noted_ref, two_ref)], axis=1)
     for k in range(4):
         wanted = (c ^ k) * blocks + x
@@ -203,7 +207,7 @@
 
 
 def pick(blocks, noted, two, sums):
-    rows, cols = sum(s.shape[0] for s in sums), sums[0].shape[1]
+    rows, cols = sum(s.shape[0] for s in sums[:-1]), sums[0].shape[1]
     half = rows // (4 * blocks)
     out = jax.ShapeDtypeStruct((half, cols), jnp.bfloat16)
     return pl.pallas_call(
@@ -326,7 +330,7 @@
     share_b = stack_core_total(share_a, *project(block_rows, (first_2, second_2), out_weight))
     first_3 = after(first_3, share_b)
     share_c = core_total(*project(block_rows, (first_3, second_3), out_weight, cost(100 * 10**8, 0)))
-    sums = (chip_total(share_b), chip_total(share_c))
+    sums = (chip_total(share_b), share_c, flip(share_c, "tp", 2))
     kept, *sent = pick(blocks, first, first_2, sums)
     got_3, got_2, got_1 = (flip(sent[k - 1], "ctx", k) for k in (3, 2, 1))
     return join(hold(kept, got_3), got_2, got_1)

time: 46.7 us -> 46.6 us (level)
  no operation moved by 1% of the time
where the time goes in v19:
time: 46.6 us; the launch traced here: 46.4 us
  waiting for transfers between devices  23.6 us (51%)
  starting transfers between devices  18.2 us (39%)
  Pallas kernels  4.48 us (10%)
    ppermute x14, waiting for transfers between devices, flip(): return lax.ppermute(array, axis, [(i, i ^ bits) for i in range(4)])  23.6 us
    ppermute x14, starting transfers between devices, flip(): return lax.ppermute(array, axis, [(i, i ^ bits) for i in range(4)])  18.2 us
    pallas_call x1, Pallas kernels, pack(): pl.pallas_call(pack_kernel, out_shape=jax.ShapeDtypeStruct((rows + 16, 2...  1.66 us
    pallas_call x3, Pallas kernels, project(): pl.pallas_call(functools.partial(project_kernel, block_rows), out_shape=(...  1.05 us
  transfers between devices with their start and end apart: 15, of which 10 were waited for; matrix products, arithmetic and copies ran while one was open for 0% of the time, Pallas kernels for 3%

profile of v19, /device:TPU:0, one launch (start us, length us, event | category | flops | bytes accessed | tf_op | source)
XLA Modules:
  0.0 46.4 jit_solution(18098716778868061321)
XLA Ops:
  0.0 1.7 %shard_map.73 = bf16[144,512]{1,0:T(8,128)(2,1)} custom-call(bf16[128,256]{1,0:T(8,128)(2,1)} %k_ref.3, bf16[128,256]{1,0:T(8,128)(2,1)} %v_ref.3, s32[1,128]{1,0:T(1,128)} %bitcast.3, s32[1,2]{1,0:T(1,128)} %bitcast.5), custom_call_target="tpu_custom_call" | custom-call | flops 1000000000 | bytes 262144 | tf_op jit(solution)/shard_map/pallas_call | solution.py:53
  1.7 3.1 %collective-permute-start = (bf16[144,512]{1,0:T(8,128)(2,1)}, bf16[144,512]{1,0:T(8,128)(2,1)S(1)}, u32[]{:S(2)}, u32[]{:S(2)}) collective-permute-start(bf16[144,512]{1,0:T(8,128)(2,1)} %shard_map.73), channel_id=1, source_target_pairs={{0,4},{4,0},{8,12},{12,8},{1,5},{5,1},{9,13},{13,9},{2,6},{6,2},{1... | collective-permute-start | bytes 442376 | tf_op jit(solution)/shard_map/ppermute | solution.py:278
  4.8 4.1 %collective-permute-done.flip_ref = bf16[144,512]{1,0:T(8,128)(2,1)S(1)} collective-permute-done((bf16[144,512]{1,0:T(8,128)(2,1)}, bf16[144,512]{1,0:T(8,128)(2,1)S(1)}, u32[]{:S(2)}, u32[]{:S(2)}) %collective-permute-start) | collective-permute-done | bytes 147488 | tf_op jit(solution)/shard_map/ppermute | solution.py:278
  8.9 0.7 %shard_map.74 = (bf16[128,1024]{1,0:T(8,128)(2,1)S(1)}, bf16[72,1024]{1,0:T(8,128)(2,1)S(1)}, bf16[64,1024]{1,0:T(8,128)(2,1)S(1)}) custom-call(bf16[128,1024]{1,0:T(8,128)(2,1)S(1)} %copy-done.1, bf16[144,512]{1,0:T(8,128)(2,1)S(1)} %collective-permute-done.flip_ref, bf16[144,512]{1,0:T(8,128)(2,1)S(1)} %collective-permute-done.1.mid_ref, ...), custom_call_target="tpu_custom_call" | custom-call | flops 134217728 | bytes 786432 | tf_op jit(solution)/shard_map/pallas_call | solution.py:132
  9.6 3.0 %collective-permute-start.3 = (bf16[128,1024]{1,0:T(8,128)(2,1)S(1)}, bf16[128,1024]{1,0:T(8,128)(2,1)S(1)}, u32[]{:S(2)}, u32[]{:S(2)}) collective-permute-start(bf16[128,1024]{1,0:T(8,128)(2,1)S(1)} %get-tuple-element.22.refs_0_), channel_id=1, source_target_pairs={{0,4},{4,0},{8,12},{12,8},{1,5},{5,1},{9,13},{13,9},{2,6},{6,2},{1... | collective-permute-start | bytes 786440 | tf_op jit(solution)/shard_map/ppermute | solution.py:278
  12.6 1.4 %collective-permute-start.2 = (bf16[72,1024]{1,0:T(8,128)(2,1)S(1)}, bf16[72,1024]{1,0:T(8,128)(2,1)S(1)}, u32[]{:S(2)}, u32[]{:S(2)}) collective-permute-start(bf16[72,1024]{1,0:T(8,128)(2,1)S(1)} %get-tuple-element.21.noted_ref), channel_id=1, source_target_pairs={{0,8},{4,12},{8,0},{12,4},{1,9},{5,13},{9,1},{13,5},{2,10},{6,14},... | collective-permute-start | bytes 442376 | tf_op jit(solution)/shard_map/ppermute | solution.py:278
  14.0 1.5 %collective-permute-start.5 = (bf16[64,1024]{1,0:T(8,128)(2,1)S(1)}, bf16[64,1024]{1,0:T(8,128)(2,1)S(1)}, u32[]{:S(2)}, u32[]{:S(2)}) collective-permute-start(bf16[64,1024]{1,0:T(8,128)(2,1)S(1)} %get-tuple-element.26), channel_id=1, source_target_pairs={{0,8},{4,12},{8,0},{12,4},{1,9},{5,13},{9,1},{13,5},{2,10},{6,14},... | collective-permute-start | bytes 393224 | tf_op jit(solution)/shard_map/ppermute | solution.py:278
  15.5 7.8 %collective-permute-done.3.refs_1_ = bf16[128,1024]{1,0:T(8,128)(2,1)S(1)} collective-permute-done((bf16[128,1024]{1,0:T(8,128)(2,1)S(1)}, bf16[128,1024]{1,0:T(8,128)(2,1)S(1)}, u32[]{:S(2)}, u32[]{:S(2)}) %collective-permute-start.3) | collective-permute-done | bytes 262176 | tf_op jit(solution)/shard_map/ppermute | solution.py:278
  23.3 0.4 shard_map.75
  23.9 1.4 %collective-permute-start.8 = (bf16[64,1024]{1,0:T(8,128)(2,1)S(1)}, bf16[64,1024]{1,0:T(8,128)(2,1)S(1)}, u32[]{:S(2)}, u32[]{:S(2)}) collective-permute-start(bf16[64,1024]{1,0:T(8,128)(2,1)S(1)} %shard_map.80), channel_id=1, source_target_pairs={{0,4},{4,0},{8,12},{12,8},{1,5},{5,1},{9,13},{13,9},{2,6},{6,2},{1... | collective-permute-start | bytes 393224 | tf_op jit(solution)/shard_map/ppermute | solution.py:278
  25.3 1.4 %collective-permute-done.5.refs_1_ = bf16[64,1024]{1,0:T(8,128)(2,1)S(1)} collective-permute-done((bf16[64,1024]{1,0:T(8,128)(2,1)S(1)}, bf16[64,1024]{1,0:T(8,128)(2,1)S(1)}, u32[]{:S(2)}, u32[]{:S(2)}) %collective-permute-start.5) | collective-permute-done | bytes 131104 | tf_op jit(solution)/shard_map/ppermute | solution.py:278
  26.8 0.3 shard_map.77
  27.2 1.2 %collective-permute-done.6.got_ref = bf16[64,512]{1,0:T(8,128)(2,1)S(1)} collective-permute-done((bf16[64,512]{1,0:T(8,128)(2,1)S(1)}, bf16[64,512]{1,0:T(8,128)(2,1)S(1)}, u32[]{:S(2)}, u32[]{:S(2)}) %collective-permute-start.6) | collective-permute-done | bytes 65568 | tf_op jit(solution)/shard_map/ppermute | solution.py:278
  28.5 1.6 %collective-permute-start.7 = (bf16[192,512]{1,0:T(8,128)(2,1)S(1)}, bf16[192,512]{1,0:T(8,128)(2,1)S(1)}, u32[]{:S(2)}, u32[]{:S(2)}) collective-permute-start(bf16[192,512]{1,0:T(8,128)(2,1)S(1)} %shard_map.78.refs_0_), channel_id=1, source_target_pairs={{0,2},{1,3},{2,0},{3,1},{4,6},{5,7},{6,4},{7,5},{8,10},{9,11},{10,... | collective-permute-start | bytes 589832 | tf_op jit(solution)/shard_map/ppermute | solution.py:278
  30.2 2.4 %collective-permute-done.9.refs_1_ = bf16[64,1024]{1,0:T(8,128)(2,1)S(1)} collective-permute-done((bf16[64,1024]{1,0:T(8,128)(2,1)S(1)}, bf16[64,1024]{1,0:T(8,128)(2,1)S(1)}, u32[]{:S(2)}, u32[]{:S(2)}) %collective-permute-start.9) | collective-permute-done | bytes 131104 | tf_op jit(solution)/shard_map/ppermute | solution.py:278
  32.6 0.3 shard_map.81
  33.0 1.2 %collective-permute-done.10.refs_1_ = bf16[64,512]{1,0:T(8,128)(2,1)S(1)} collective-permute-done((bf16[64,512]{1,0:T(8,128)(2,1)S(1)}, bf16[64,512]{1,0:T(8,128)(2,1)S(1)}, u32[]{:S(2)}, u32[]{:S(2)}) %collective-permute-start.10) | collective-permute-done | bytes 65568 | tf_op jit(solution)/shard_map/ppermute | solution.py:278
  34.3 1.6 %collective-permute-start.11 = (bf16[64,512]{1,0:T(8,128)(2,1)S(1)}, bf16[64,512]{1,0:T(8,128)(2,1)S(1)}, u32[]{:S(2)}, u32[]{:S(2)}) collective-permute-start(bf16[64,512]{1,0:T(8,128)(2,1)S(1)} %shard_map.82.refs_1_), channel_id=1, source_target_pairs={{0,2},{1,3},{2,0},{3,1},{4,6},{5,7},{6,4},{7,5},{8,10},{9,11},{10,... | collective-permute-start | bytes 196616 | tf_op jit(solution)/shard_map/ppermute | solution.py:278
  35.9 2.7 %collective-permute-done.11.refs_2_ = bf16[64,512]{1,0:T(8,128)(2,1)S(1)} collective-permute-done((bf16[64,512]{1,0:T(8,128)(2,1)S(1)}, bf16[64,512]{1,0:T(8,128)(2,1)S(1)}, u32[]{:S(2)}, u32[]{:S(2)}) %collective-permute-start.11) | collective-permute-done | bytes 65568 | tf_op jit(solution)/shard_map/ppermute | solution.py:278
  38.9 2.1 %collective-permute-start.12 = (bf16[32,512]{1,0:T(8,128)(2,1)S(1)}, bf16[32,512]{1,0:T(8,128)(2,1)S(1)}, u32[]{:S(2)}, u32[]{:S(2)}) collective-permute-start(bf16[32,512]{1,0:T(8,128)(2,1)S(1)} %get-tuple-element.34), channel_id=1, source_target_pairs={{0,12},{4,8},{8,4},{12,0},{1,13},{5,9},{9,5},{13,1},{2,14},{6,10},... | collective-permute-start | bytes 98312 | tf_op jit(solution)/shard_map/ppermute | solution.py:278
  40.9 2.4 %collective-permute-start.14 = (bf16[32,512]{1,0:T(8,128)(2,1)S(1)}, bf16[32,512]{1,0:T(8,128)(2,1)S(1)}, u32[]{:S(2)}, u32[]{:S(2)}) collective-permute-start(bf16[32,512]{1,0:T(8,128)(2,1)S(1)} %get-tuple-element.36), channel_id=1, source_target_pairs={{0,4},{4,0},{8,12},{12,8},{1,5},{5,1},{9,13},{13,9},{2,6},{6,2},{1... | collective-permute-start | bytes 98312 | tf_op jit(solution)/shard_map/ppermute | solution.py:278
  43.3 1.6 %collective-permute-done.12.far_ref = bf16[32,512]{1,0:T(8,128)(2,1)S(1)} collective-permute-done((bf16[32,512]{1,0:T(8,128)(2,1)S(1)}, bf16[32,512]{1,0:T(8,128)(2,1)S(1)}, u32[]{:S(2)}, u32[]{:S(2)}) %collective-permute-start.12) | collective-permute-done | bytes 32800 | tf_op jit(solution)/shard_map/ppermute | solution.py:278
  45.0 0.8 %collective-permute-done.13.two_ref = bf16[32,512]{1,0:T(8,128)(2,1)S(1)} collective-permute-done((bf16[32,512]{1,0:T(8,128)(2,1)S(1)}, bf16[32,512]{1,0:T(8,128)(2,1)S(1)}, u32[]{:S(2)}, u32[]{:S(2)}) %collective-permute-start.13) | collective-permute-done | bytes 32800 | tf_op jit(solution)/shard_map/ppermute | solution.py:278
  45.8 0.7 %shard_map.85 = bf16[32,2048]{1,0:T(8,128)(2,1)} custom-call(bf16[32,1024]{1,0:T(8,128)(2,1)S(1)} %shard_map.84.held_ref, bf16[32,512]{1,0:T(8,128)(2,1)S(1)} %collective-permute-done.13.two_ref, bf16[32,512]{1,0:T(8,128)(2,1)S(1)} %collective-permute-done.14.one_ref), custom_call_target="tpu_custom_call" | custom-call | bytes 262144 | tf_op jit(solution)/shard_map/pallas_call | solution.py:267
  (33 shorter events, 0.9 us)
Async XLA Ops:
  0.0 8.8 %copy-start.1 = (bf16[128,1024]{1,0:T(8,128)(2,1)S(1)}, bf16[128,1024]{1,0:T(8,128)(2,1)}, u32[]{:S(2)}) copy-start(bf16[128,1024]{1,0:T(8,128)(2,1)} %q_ref.1) | copy-start | bytes 786436
  0.0 8.8 %copy-start.2 = (bf16[128,256]{1,0:T(8,128)(2,1)S(1)}, bf16[128,256]{1,0:T(8,128)(2,1)}, u32[]{:S(2)}) copy-start(bf16[128,256]{1,0:T(8,128)(2,1)} %k_ref.3) | copy-start | bytes 196612
  0.0 8.8 %copy-start.3 = (bf16[128,256]{1,0:T(8,128)(2,1)S(1)}, bf16[128,256]{1,0:T(8,128)(2,1)}, u32[]{:S(2)}) copy-start(bf16[128,256]{1,0:T(8,128)(2,1)} %v_ref.3) | copy-start | bytes 196612
  0.0 23.3 %copy-start = (bf16[1024,512]{1,0:T(8,128)(2,1)S(1)}, bf16[1024,512]{1,0:T(8,128)(2,1)}, u32[]{:S(2)}) copy-start(bf16[1024,512]{1,0:T(8,128)(2,1)} %refs_2_.5) | copy-start | bytes 3145732
  1.7 7.2 %copy-start.4 = (s32[128]{0:T(128)S(1)}, s32[128]{0:T(128)}, u32[]{:S(2)}) copy-start(s32[128]{0:T(128)} %param.11) | copy-start | bytes 1540
  1.7 7.2 %copy-start.5 = (s32[2]{0:T(128)S(1)}, s32[2]{0:T(128)}, u32[]{:S(2)}) copy-start(s32[2]{0:T(128)} %param.12) | copy-start | bytes 28
  1.7 7.2 %copy-start.6 = (s32[128]{0:T(128)S(1)}, s32[128]{0:T(128)}, u32[]{:S(2)}) copy-start(s32[128]{0:T(128)} %param.10) | copy-start | bytes 1540
  1.7 7.2 %collective-permute-start = (bf16[144,512]{1,0:T(8,128)(2,1)}, bf16[144,512]{1,0:T(8,128)(2,1)S(1)}, u32[]{:S(2)}, u32[]{:S(2)}) collective-permute-start(bf16[144,512]{1,0:T(8,128)(2,1)} %shard_map.73), channel_id=1, source_target_pairs={{0,4},{4,0},{8,12},{12,8},{1,5},{5,1},{9,13},{13,9},{2,6},{6,2},{1... | collective-permute-start | bytes 442376 | tf_op jit(solution)/shard_map/ppermute | solution.py:278
  4.8 4.1 %collective-permute-start.1 = (bf16[144,512]{1,0:T(8,128)(2,1)}, bf16[144,512]{1,0:T(8,128)(2,1)S(1)}, u32[]{:S(2)}, u32[]{:S(2)}) collective-permute-start(bf16[144,512]{1,0:T(8,128)(2,1)} %shard_map.73), channel_id=1, source_target_pairs={{0,1},{1,0},{2,3},{3,2},{4,8},{5,9},{6,10},{7,11},{8,4},{9,5},{10,... | collective-permute-start | bytes 442376 | tf_op jit(solution)/shard_map/ppermute | solution.py:321
  9.6 13.7 %collective-permute-start.3 = (bf16[128,1024]{1,0:T(8,128)(2,1)S(1)}, bf16[128,1024]{1,0:T(8,128)(2,1)S(1)}, u32[]{:S(2)}, u32[]{:S(2)}) collective-permute-start(bf16[128,1024]{1,0:T(8,128)(2,1)S(1)} %get-tuple-element.22.refs_0_), channel_id=1, source_target_pairs={{0,4},{4,0},{8,12},{12,8},{1,5},{5,1},{9,13},{13,9},{2,6},{6,2},{1... | collective-permute-start | bytes 786440 | tf_op jit(solution)/shard_map/ppermute | solution.py:278
  12.6 11.3 %collective-permute-start.2 = (bf16[72,1024]{1,0:T(8,128)(2,1)S(1)}, bf16[72,1024]{1,0:T(8,128)(2,1)S(1)}, u32[]{:S(2)}, u32[]{:S(2)}) collective-permute-start(bf16[72,1024]{1,0:T(8,128)(2,1)S(1)} %get-tuple-element.21.noted_ref), channel_id=1, source_target_pairs={{0,8},{4,12},{8,0},{12,4},{1,9},{5,13},{9,1},{13,5},{2,10},{6,14},... | collective-permute-start | bytes 442376 | tf_op jit(solution)/shard_map/ppermute | solution.py:278
  14.0 12.7 %collective-permute-start.5 = (bf16[64,1024]{1,0:T(8,128)(2,1)S(1)}, bf16[64,1024]{1,0:T(8,128)(2,1)S(1)}, u32[]{:S(2)}, u32[]{:S(2)}) collective-permute-start(bf16[64,1024]{1,0:T(8,128)(2,1)S(1)} %get-tuple-element.26), channel_id=1, source_target_pairs={{0,8},{4,12},{8,0},{12,4},{1,9},{5,13},{9,1},{13,5},{2,10},{6,14},... | collective-permute-start | bytes 393224 | tf_op jit(solution)/shard_map/ppermute | solution.py:278
  23.8 3.0 %collective-permute-start.4 = (bf16[128,512]{1,0:T(8,128)(2,1)S(1)}, bf16[128,512]{1,0:T(8,128)(2,1)S(1)}, u32[]{:S(2)}, u32[]{:S(2)}) collective-permute-start(bf16[128,512]{1,0:T(8,128)(2,1)S(1)} %get-tuple-element.24), channel_id=1, source_target_pairs={{0,1},{1,0},{2,3},{3,2},{4,5},{5,4},{6,7},{7,6},{8,9},{9,8},{10,11... | collective-permute-start | bytes 393224 | tf_op jit(solution)/shard_map/ppermute | solution.py:278
  23.9 6.4 %collective-permute-start.8 = (bf16[64,1024]{1,0:T(8,128)(2,1)S(1)}, bf16[64,1024]{1,0:T(8,128)(2,1)S(1)}, u32[]{:S(2)}, u32[]{:S(2)}) collective-permute-start(bf16[64,1024]{1,0:T(8,128)(2,1)S(1)} %shard_map.80), channel_id=1, source_target_pairs={{0,4},{4,0},{8,12},{12,8},{1,5},{5,1},{9,13},{13,9},{2,6},{6,2},{1... | collective-permute-start | bytes 393224 | tf_op jit(solution)/shard_map/ppermute | solution.py:278
  26.7 5.9 %collective-permute-start.9 = (bf16[64,1024]{1,0:T(8,128)(2,1)S(1)}, bf16[64,1024]{1,0:T(8,128)(2,1)S(1)}, u32[]{:S(2)}, u32[]{:S(2)}) collective-permute-start(bf16[64,1024]{1,0:T(8,128)(2,1)S(1)} %collective-permute-done.5.refs_1_), channel_id=1, source_target_pairs={{0,4},{4,0},{8,12},{12,8},{1,5},{5,1},{9,13},{13,9},{2,6},{6,2},{1... | collective-permute-start | bytes 393224 | tf_op jit(solution)/shard_map/ppermute | solution.py:278
  27.1 1.3 %collective-permute-start.6 = (bf16[64,512]{1,0:T(8,128)(2,1)S(1)}, bf16[64,512]{1,0:T(8,128)(2,1)S(1)}, u32[]{:S(2)}, u32[]{:S(2)}) collective-permute-start(bf16[64,512]{1,0:T(8,128)(2,1)S(1)} %get-tuple-element.29), channel_id=1, source_target_pairs={{0,1},{1,0},{2,3},{3,2},{4,5},{5,4},{6,7},{7,6},{8,9},{9,8},{10,11... | collective-permute-start | bytes 196616 | tf_op jit(solution)/shard_map/ppermute | solution.py:278
  28.5 7.4 %collective-permute-start.7 = (bf16[192,512]{1,0:T(8,128)(2,1)S(1)}, bf16[192,512]{1,0:T(8,128)(2,1)S(1)}, u32[]{:S(2)}, u32[]{:S(2)}) collective-permute-start(bf16[192,512]{1,0:T(8,128)(2,1)S(1)} %shard_map.78.refs_0_), channel_id=1, source_target_pairs={{0,2},{1,3},{2,0},{3,1},{4,6},{5,7},{6,4},{7,5},{8,10},{9,11},{10,... | collective-permute-start | bytes 589832 | tf_op jit(solution)/shard_map/ppermute | solution.py:278
  33.0 1.3 %collective-permute-start.10 = (bf16[64,512]{1,0:T(8,128)(2,1)S(1)}, bf16[64,512]{1,0:T(8,128)(2,1)S(1)}, u32[]{:S(2)}, u32[]{:S(2)}) collective-permute-start(bf16[64,512]{1,0:T(8,128)(2,1)S(1)} %get-tuple-element.32), channel_id=1, source_target_pairs={{0,1},{1,0},{2,3},{3,2},{4,5},{5,4},{6,7},{7,6},{8,9},{9,8},{10,11... | collective-permute-start | bytes 196616 | tf_op jit(solution)/shard_map/ppermute | solution.py:278
  34.3 4.3 %collective-permute-start.11 = (bf16[64,512]{1,0:T(8,128)(2,1)S(1)}, bf16[64,512]{1,0:T(8,128)(2,1)S(1)}, u32[]{:S(2)}, u32[]{:S(2)}) collective-permute-start(bf16[64,512]{1,0:T(8,128)(2,1)S(1)} %shard_map.82.refs_1_), channel_id=1, source_target_pairs={{0,2},{1,3},{2,0},{3,1},{4,6},{5,7},{6,4},{7,5},{8,10},{9,11},{10,... | collective-permute-start | bytes 196616 | tf_op jit(solution)/shard_map/ppermute | solution.py:278
  38.9 6.1 %collective-permute-start.12 = (bf16[32,512]{1,0:T(8,128)(2,1)S(1)}, bf16[32,512]{1,0:T(8,128)(2,1)S(1)}, u32[]{:S(2)}, u32[]{:S(2)}) collective-permute-start(bf16[32,512]{1,0:T(8,128)(2,1)S(1)} %get-tuple-element.34), channel_id=1, source_target_pairs={{0,12},{4,8},{8,4},{12,0},{1,13},{5,9},{9,5},{13,1},{2,14},{6,10},... | collective-permute-start | bytes 98312 | tf_op jit(solution)/shard_map/ppermute | solution.py:278
  40.9 4.8 %collective-permute-start.13 = (bf16[32,512]{1,0:T(8,128)(2,1)S(1)}, bf16[32,512]{1,0:T(8,128)(2,1)S(1)}, u32[]{:S(2)}, u32[]{:S(2)}) collective-permute-start(bf16[32,512]{1,0:T(8,128)(2,1)S(1)} %get-tuple-element.35), channel_id=1, source_target_pairs={{0,8},{4,12},{8,0},{12,4},{1,9},{5,13},{9,1},{13,5},{2,10},{6,14},... | collective-permute-start | bytes 98312 | tf_op jit(solution)/shard_map/ppermute | solution.py:278
  40.9 4.8 %collective-permute-start.14 = (bf16[32,512]{1,0:T(8,128)(2,1)S(1)}, bf16[32,512]{1,0:T(8,128)(2,1)S(1)}, u32[]{:S(2)}, u32[]{:S(2)}) collective-permute-start(bf16[32,512]{1,0:T(8,128)(2,1)S(1)} %get-tuple-element.36), channel_id=1, source_target_pairs={{0,4},{4,0},{8,12},{12,8},{1,5},{5,1},{9,13},{13,9},{2,6},{6,2},{1... | collective-permute-start | bytes 98312 | tf_op jit(solution)/shard_map/ppermute | solution.py:278

commit v20 on v19

--- a/solution.py
+++ b/solution.py
@@ -52,7 +52,7 @@
     rows, width = key_rows.shape
     return pl.pallas_call(
         pack_kernel,
-        out_shape=jax.ShapeDtypeStruct((rows + 16, 2 * width), jnp.bfloat16),
+        out_shape=jax.ShapeDtypeStruct((rows + 8, 2 * width), jnp.bfloat16),
         in_specs=vmem(4),
         out_specs=pl.BlockSpec(memory_space=pltpu.VMEM),
         cost_estimate=cost(10**9, 8 * key_rows.size),
@@ -64,7 +64,7 @@
 ):
     across = lax.axis_index("ctx") % 2 == 0
     halo = jnp.where(across, mid_ref[...], flip_ref[...])
-    near = flip_ref[pl.ds(k_ref.shape[0], 16), pl.ds(k_ref.shape[0], HEAD_DIM)]
+    near = flip_ref[pl.ds(k_ref.shape[0], 8), pl.ds(k_ref.shape[0], HEAD_DIM)]
     near = near[0:1, 0:blocks].astype(jnp.float32)
     targets = jnp.concatenate([own_ref[...].astype(jnp.float32), near], axis=1)
     count = targets.shape[1]
@@ -81,7 +81,7 @@
     half = rows // blocks // 2
     query_pos = base + lax.broadcasted_iota(jnp.int32, (rows, rows), 0)
     query_start = column(st_ref[...])
-    parts = halo[rows : rows + 16, 0:rows].astype(jnp.float32).astype(jnp.int32)
+    parts = halo[rows : rows + 8, 0:rows].astype(jnp.float32).astype(jnp.int32)
     masks = []
     for shift, key_end in ((rows, parts[0:1] * END_PART + parts[1:2]), (0, end_ref[...])):
         key_pos = base - shift + lax.broadcasted_iota(jnp.int32, (rows, rows), 1)

time: 46.6 us -> 46.4 us (level)
  no operation moved by 1% of the time
where the time goes in v20:
time: 46.4 us; the launch traced here: 46.2 us
  waiting for transfers between devices  23.4 us (50%)
  starting transfers between devices  18.2 us (39%)
  Pallas kernels  4.48 us (10%)
    ppermute x14, waiting for transfers between devices, flip(): return lax.ppermute(array, axis, [(i, i ^ bits) for i in range(4)])  23.4 us
    ppermute x14, starting transfers between devices, flip(): return lax.ppermute(array, axis, [(i, i ^ bits) for i in range(4)])  18.2 us
    pallas_call x1, Pallas kernels, pack(): pl.pallas_call(pack_kernel, out_shape=jax.ShapeDtypeStruct((rows + 8, 2 *...  1.65 us
    pallas_call x3, Pallas kernels, project(): pl.pallas_call(functools.partial(project_kernel, block_rows), out_shape=(...  1.05 us
  transfers between devices with their start and end apart: 15, of which 10 were waited for; matrix products, arithmetic and copies ran while one was open for 0% of the time, Pallas kernels for 3%

profile of v20, /device:TPU:0, one launch (start us, length us, event | category | flops | bytes accessed | tf_op | source)
XLA Modules:
  0.0 46.2 jit_solution(14981496172252497678)
XLA Ops:
  0.0 1.7 %shard_map.73 = bf16[136,512]{1,0:T(8,128)(2,1)} custom-call(bf16[128,256]{1,0:T(8,128)(2,1)} %k_ref.3, bf16[128,256]{1,0:T(8,128)(2,1)} %v_ref.3, s32[1,128]{1,0:T(1,128)} %bitcast.3, s32[1,2]{1,0:T(1,128)} %bitcast.5), custom_call_target="tpu_custom_call" | custom-call | flops 1000000000 | bytes 262144 | tf_op jit(solution)/shard_map/pallas_call | solution.py:53
  1.7 3.1 %collective-permute-start = (bf16[136,512]{1,0:T(8,128)(2,1)}, bf16[136,512]{1,0:T(8,128)(2,1)S(1)}, u32[]{:S(2)}, u32[]{:S(2)}) collective-permute-start(bf16[136,512]{1,0:T(8,128)(2,1)} %shard_map.73), channel_id=1, source_target_pairs={{0,4},{4,0},{8,12},{12,8},{1,5},{5,1},{9,13},{13,9},{2,6},{6,2},{1... | collective-permute-start | bytes 417800 | tf_op jit(solution)/shard_map/ppermute | solution.py:278
  4.8 3.9 %collective-permute-done.flip_ref = bf16[136,512]{1,0:T(8,128)(2,1)S(1)} collective-permute-done((bf16[136,512]{1,0:T(8,128)(2,1)}, bf16[136,512]{1,0:T(8,128)(2,1)S(1)}, u32[]{:S(2)}, u32[]{:S(2)}) %collective-permute-start) | collective-permute-done | bytes 139296 | tf_op jit(solution)/shard_map/ppermute | solution.py:278
  8.7 0.7 %shard_map.74 = (bf16[128,1024]{1,0:T(8,128)(2,1)S(1)}, bf16[72,1024]{1,0:T(8,128)(2,1)S(1)}, bf16[64,1024]{1,0:T(8,128)(2,1)S(1)}) custom-call(bf16[128,1024]{1,0:T(8,128)(2,1)S(1)} %copy-done.1, bf16[136,512]{1,0:T(8,128)(2,1)S(1)} %collective-permute-done.flip_ref, bf16[136,512]{1,0:T(8,128)(2,1)S(1)} %collective-permute-done.1.mid_ref, ...), custom_call_target="tpu_custom_call" | custom-call | flops 134217728 | bytes 786432 | tf_op jit(solution)/shard_map/pallas_call | solution.py:132
  9.4 3.0 %collective-permute-start.3 = (bf16[128,1024]{1,0:T(8,128)(2,1)S(1)}, bf16[128,1024]{1,0:T(8,128)(2,1)S(1)}, u32[]{:S(2)}, u32[]{:S(2)}) collective-permute-start(bf16[128,1024]{1,0:T(8,128)(2,1)S(1)} %get-tuple-element.22.refs_0_), channel_id=1, source_target_pairs={{0,4},{4,0},{8,12},{12,8},{1,5},{5,1},{9,13},{13,9},{2,6},{6,2},{1... | collective-permute-start | bytes 786440 | tf_op jit(solution)/shard_map/ppermute | solution.py:278
  12.4 1.4 %collective-permute-start.2 = (bf16[72,1024]{1,0:T(8,128)(2,1)S(1)}, bf16[72,1024]{1,0:T(8,128)(2,1)S(1)}, u32[]{:S(2)}, u32[]{:S(2)}) collective-permute-start(bf16[72,1024]{1,0:T(8,128)(2,1)S(1)} %get-tuple-element.21.noted_ref), channel_id=1, source_target_pairs={{0,8},{4,12},{8,0},{12,4},{1,9},{5,13},{9,1},{13,5},{2,10},{6,14},... | collective-permute-start | bytes 442376 | tf_op jit(solution)/shard_map/ppermute | solution.py:278
  13.8 1.5 %collective-permute-start.5 = (bf16[64,1024]{1,0:T(8,128)(2,1)S(1)}, bf16[64,1024]{1,0:T(8,128)(2,1)S(1)}, u32[]{:S(2)}, u32[]{:S(2)}) collective-permute-start(bf16[64,1024]{1,0:T(8,128)(2,1)S(1)} %get-tuple-element.26), channel_id=1, source_target_pairs={{0,8},{4,12},{8,0},{12,4},{1,9},{5,13},{9,1},{13,5},{2,10},{6,14},... | collective-permute-start | bytes 393224 | tf_op jit(solution)/shard_map/ppermute | solution.py:278
  15.3 7.8 %collective-permute-done.3.refs_1_ = bf16[128,1024]{1,0:T(8,128)(2,1)S(1)} collective-permute-done((bf16[128,1024]{1,0:T(8,128)(2,1)S(1)}, bf16[128,1024]{1,0:T(8,128)(2,1)S(1)}, u32[]{:S(2)}, u32[]{:S(2)}) %collective-permute-start.3) | collective-permute-done | bytes 262176 | tf_op jit(solution)/shard_map/ppermute | solution.py:278
  23.2 0.4 shard_map.75
  23.7 1.4 %collective-permute-start.8 = (bf16[64,1024]{1,0:T(8,128)(2,1)S(1)}, bf16[64,1024]{1,0:T(8,128)(2,1)S(1)}, u32[]{:S(2)}, u32[]{:S(2)}) collective-permute-start(bf16[64,1024]{1,0:T(8,128)(2,1)S(1)} %shard_map.80), channel_id=1, source_target_pairs={{0,4},{4,0},{8,12},{12,8},{1,5},{5,1},{9,13},{13,9},{2,6},{6,2},{1... | collective-permute-start | bytes 393224 | tf_op jit(solution)/shard_map/ppermute | solution.py:278
  25.1 1.4 %collective-permute-done.5.refs_1_ = bf16[64,1024]{1,0:T(8,128)(2,1)S(1)} collective-permute-done((bf16[64,1024]{1,0:T(8,128)(2,1)S(1)}, bf16[64,1024]{1,0:T(8,128)(2,1)S(1)}, u32[]{:S(2)}, u32[]{:S(2)}) %collective-permute-start.5) | collective-permute-done | bytes 131104 | tf_op jit(solution)/shard_map/ppermute | solution.py:278
  26.6 0.3 shard_map.77
  27.0 1.2 %collective-permute-done.6.got_ref = bf16[64,512]{1,0:T(8,128)(2,1)S(1)} collective-permute-done((bf16[64,512]{1,0:T(8,128)(2,1)S(1)}, bf16[64,512]{1,0:T(8,128)(2,1)S(1)}, u32[]{:S(2)}, u32[]{:S(2)}) %collective-permute-start.6) | collective-permute-done | bytes 65568 | tf_op jit(solution)/shard_map/ppermute | solution.py:278
  28.3 1.6 %collective-permute-start.7 = (bf16[192,512]{1,0:T(8,128)(2,1)S(1)}, bf16[192,512]{1,0:T(8,128)(2,1)S(1)}, u32[]{:S(2)}, u32[]{:S(2)}) collective-permute-start(bf16[192,512]{1,0:T(8,128)(2,1)S(1)} %shard_map.78.refs_0_), channel_id=1, source_target_pairs={{0,2},{1,3},{2,0},{3,1},{4,6},{5,7},{6,4},{7,5},{8,10},{9,11},{10,... | collective-permute-start | bytes 589832 | tf_op jit(solution)/shard_map/ppermute | solution.py:278
  30.1 2.4 %collective-permute-done.9.refs_1_ = bf16[64,1024]{1,0:T(8,128)(2,1)S(1)} collective-permute-done((bf16[64,1024]{1,0:T(8,128)(2,1)S(1)}, bf16[64,1024]{1,0:T(8,128)(2,1)S(1)}, u32[]{:S(2)}, u32[]{:S(2)}) %collective-permute-start.9) | collective-permute-done | bytes 131104 | tf_op jit(solution)/shard_map/ppermute | solution.py:278
  32.5 0.3 shard_map.81
  32.9 1.2 %collective-permute-done.10.refs_1_ = bf16[64,512]{1,0:T(8,128)(2,1)S(1)} collective-permute-done((bf16[64,512]{1,0:T(8,128)(2,1)S(1)}, bf16[64,512]{1,0:T(8,128)(2,1)S(1)}, u32[]{:S(2)}, u32[]{:S(2)}) %collective-permute-start.10) | collective-permute-done | bytes 65568 | tf_op jit(solution)/shard_map/ppermute | solution.py:278
  34.1 1.6 %collective-permute-start.11 = (bf16[64,512]{1,0:T(8,128)(2,1)S(1)}, bf16[64,512]{1,0:T(8,128)(2,1)S(1)}, u32[]{:S(2)}, u32[]{:S(2)}) collective-permute-start(bf16[64,512]{1,0:T(8,128)(2,1)S(1)} %shard_map.82.refs_1_), channel_id=1, source_target_pairs={{0,2},{1,3},{2,0},{3,1},{4,6},{5,7},{6,4},{7,5},{8,10},{9,11},{10,... | collective-permute-start | bytes 196616 | tf_op jit(solution)/shard_map/ppermute | solution.py:278
  35.7 2.7 %collective-permute-done.11.refs_2_ = bf16[64,512]{1,0:T(8,128)(2,1)S(1)} collective-permute-done((bf16[64,512]{1,0:T(8,128)(2,1)S(1)}, bf16[64,512]{1,0:T(8,128)(2,1)S(1)}, u32[]{:S(2)}, u32[]{:S(2)}) %collective-permute-start.11) | collective-permute-done | bytes 65568 | tf_op jit(solution)/shard_map/ppermute | solution.py:278
  38.7 2.1 %collective-permute-start.12 = (bf16[32,512]{1,0:T(8,128)(2,1)S(1)}, bf16[32,512]{1,0:T(8,128)(2,1)S(1)}, u32[]{:S(2)}, u32[]{:S(2)}) collective-permute-start(bf16[32,512]{1,0:T(8,128)(2,1)S(1)} %get-tuple-element.34), channel_id=1, source_target_pairs={{0,12},{4,8},{8,4},{12,0},{1,13},{5,9},{9,5},{13,1},{2,14},{6,10},... | collective-permute-start | bytes 98312 | tf_op jit(solution)/shard_map/ppermute | solution.py:278
  40.8 2.4 %collective-permute-start.14 = (bf16[32,512]{1,0:T(8,128)(2,1)S(1)}, bf16[32,512]{1,0:T(8,128)(2,1)S(1)}, u32[]{:S(2)}, u32[]{:S(2)}) collective-permute-start(bf16[32,512]{1,0:T(8,128)(2,1)S(1)} %get-tuple-element.36), channel_id=1, source_target_pairs={{0,4},{4,0},{8,12},{12,8},{1,5},{5,1},{9,13},{13,9},{2,6},{6,2},{1... | collective-permute-start | bytes 98312 | tf_op jit(solution)/shard_map/ppermute | solution.py:278
  43.1 1.6 %collective-permute-done.12.far_ref = bf16[32,512]{1,0:T(8,128)(2,1)S(1)} collective-permute-done((bf16[32,512]{1,0:T(8,128)(2,1)S(1)}, bf16[32,512]{1,0:T(8,128)(2,1)S(1)}, u32[]{:S(2)}, u32[]{:S(2)}) %collective-permute-start.12) | collective-permute-done | bytes 32800 | tf_op jit(solution)/shard_map/ppermute | solution.py:278
  44.8 0.8 %collective-permute-done.13.two_ref = bf16[32,512]{1,0:T(8,128)(2,1)S(1)} collective-permute-done((bf16[32,512]{1,0:T(8,128)(2,1)S(1)}, bf16[32,512]{1,0:T(8,128)(2,1)S(1)}, u32[]{:S(2)}, u32[]{:S(2)}) %collective-permute-start.13) | collective-permute-done | bytes 32800 | tf_op jit(solution)/shard_map/ppermute | solution.py:278
  45.6 0.7 %shard_map.85 = bf16[32,2048]{1,0:T(8,128)(2,1)} custom-call(bf16[32,1024]{1,0:T(8,128)(2,1)S(1)} %shard_map.84.held_ref, bf16[32,512]{1,0:T(8,128)(2,1)S(1)} %collective-permute-done.13.two_ref, bf16[32,512]{1,0:T(8,128)(2,1)S(1)} %collective-permute-done.14.one_ref), custom_call_target="tpu_custom_call" | custom-call | bytes 262144 | tf_op jit(solution)/shard_map/pallas_call | solution.py:267
  (33 shorter events, 0.9 us)
Async XLA Ops:
  0.0 8.6 %copy-start.1 = (bf16[128,1024]{1,0:T(8,128)(2,1)S(1)}, bf16[128,1024]{1,0:T(8,128)(2,1)}, u32[]{:S(2)}) copy-start(bf16[128,1024]{1,0:T(8,128)(2,1)} %q_ref.1) | copy-start | bytes 786436
  0.0 8.6 %copy-start.2 = (bf16[128,256]{1,0:T(8,128)(2,1)S(1)}, bf16[128,256]{1,0:T(8,128)(2,1)}, u32[]{:S(2)}) copy-start(bf16[128,256]{1,0:T(8,128)(2,1)} %k_ref.3) | copy-start | bytes 196612
  0.0 8.7 %copy-start.3 = (bf16[128,256]{1,0:T(8,128)(2,1)S(1)}, bf16[128,256]{1,0:T(8,128)(2,1)}, u32[]{:S(2)}) copy-start(bf16[128,256]{1,0:T(8,128)(2,1)} %v_ref.3) | copy-start | bytes 196612
  0.0 23.1 %copy-start = (bf16[1024,512]{1,0:T(8,128)(2,1)S(1)}, bf16[1024,512]{1,0:T(8,128)(2,1)}, u32[]{:S(2)}) copy-start(bf16[1024,512]{1,0:T(8,128)(2,1)} %refs_2_.5) | copy-start | bytes 3145732
  1.7 7.0 %copy-start.4 = (s32[128]{0:T(128)S(1)}, s32[128]{0:T(128)}, u32[]{:S(2)}) copy-start(s32[128]{0:T(128)} %param.11) | copy-start | bytes 1540
  1.7 7.0 %copy-start.5 = (s32[2]{0:T(128)S(1)}, s32[2]{0:T(128)}, u32[]{:S(2)}) copy-start(s32[2]{0:T(128)} %param.12) | copy-start | bytes 28
  1.7 7.0 %copy-start.6 = (s32[128]{0:T(128)S(1)}, s32[128]{0:T(128)}, u32[]{:S(2)}) copy-start(s32[128]{0:T(128)} %param.10) | copy-start | bytes 1540
  1.7 7.0 %collective-permute-start = (bf16[136,512]{1,0:T(8,128)(2,1)}, bf16[136,512]{1,0:T(8,128)(2,1)S(1)}, u32[]{:S(2)}, u32[]{:S(2)}) collective-permute-start(bf16[136,512]{1,0:T(8,128)(2,1)} %shard_map.73), channel_id=1, source_target_pairs={{0,4},{4,0},{8,12},{12,8},{1,5},{5,1},{9,13},{13,9},{2,6},{6,2},{1... | collective-permute-start | bytes 417800 | tf_op jit(solution)/shard_map/ppermute | solution.py:278
  4.8 3.9 %collective-permute-start.1 = (bf16[136,512]{1,0:T(8,128)(2,1)}, bf16[136,512]{1,0:T(8,128)(2,1)S(1)}, u32[]{:S(2)}, u32[]{:S(2)}) collective-permute-start(bf16[136,512]{1,0:T(8,128)(2,1)} %shard_map.73), channel_id=1, source_target_pairs={{0,1},{1,0},{2,3},{3,2},{4,8},{5,9},{6,10},{7,11},{8,4},{9,5},{10,... | collective-permute-start | bytes 417800 | tf_op jit(solution)/shard_map/ppermute | solution.py:321
  9.4 13.7 %collective-permute-start.3 = (bf16[128,1024]{1,0:T(8,128)(2,1)S(1)}, bf16[128,1024]{1,0:T(8,128)(2,1)S(1)}, u32[]{:S(2)}, u32[]{:S(2)}) collective-permute-start(bf16[128,1024]{1,0:T(8,128)(2,1)S(1)} %get-tuple-element.22.refs_0_), channel_id=1, source_target_pairs={{0,4},{4,0},{8,12},{12,8},{1,5},{5,1},{9,13},{13,9},{2,6},{6,2},{1... | collective-permute-start | bytes 786440 | tf_op jit(solution)/shard_map/ppermute | solution.py:278
  12.4 11.3 %collective-permute-start.2 = (bf16[72,1024]{1,0:T(8,128)(2,1)S(1)}, bf16[72,1024]{1,0:T(8,128)(2,1)S(1)}, u32[]{:S(2)}, u32[]{:S(2)}) collective-permute-start(bf16[72,1024]{1,0:T(8,128)(2,1)S(1)} %get-tuple-element.21.noted_ref), channel_id=1, source_target_pairs={{0,8},{4,12},{8,0},{12,4},{1,9},{5,13},{9,1},{13,5},{2,10},{6,14},... | collective-permute-start | bytes 442376 | tf_op jit(solution)/shard_map/ppermute | solution.py:278
  13.8 12.7 %collective-permute-start.5 = (bf16[64,1024]{1,0:T(8,128)(2,1)S(1)}, bf16[64,1024]{1,0:T(8,128)(2,1)S(1)}, u32[]{:S(2)}, u32[]{:S(2)}) collective-permute-start(bf16[64,1024]{1,0:T(8,128)(2,1)S(1)} %get-tuple-element.26), channel_id=1, source_target_pairs={{0,8},{4,12},{8,0},{12,4},{1,9},{5,13},{9,1},{13,5},{2,10},{6,14},... | collective-permute-start | bytes 393224 | tf_op jit(solution)/shard_map/ppermute | solution.py:278
  23.6 3.0 %collective-permute-start.4 = (bf16[128,512]{1,0:T(8,128)(2,1)S(1)}, bf16[128,512]{1,0:T(8,128)(2,1)S(1)}, u32[]{:S(2)}, u32[]{:S(2)}) collective-permute-start(bf16[128,512]{1,0:T(8,128)(2,1)S(1)} %get-tuple-element.24), channel_id=1, source_target_pairs={{0,1},{1,0},{2,3},{3,2},{4,5},{5,4},{6,7},{7,6},{8,9},{9,8},{10,11... | collective-permute-start | bytes 393224 | tf_op jit(solution)/shard_map/ppermute | solution.py:278
  23.7 6.4 %collective-permute-start.8 = (bf16[64,1024]{1,0:T(8,128)(2,1)S(1)}, bf16[64,1024]{1,0:T(8,128)(2,1)S(1)}, u32[]{:S(2)}, u32[]{:S(2)}) collective-permute-start(bf16[64,1024]{1,0:T(8,128)(2,1)S(1)} %shard_map.80), channel_id=1, source_target_pairs={{0,4},{4,0},{8,12},{12,8},{1,5},{5,1},{9,13},{13,9},{2,6},{6,2},{1... | collective-permute-start | bytes 393224 | tf_op jit(solution)/shard_map/ppermute | solution.py:278
  26.6 5.9 %collective-permute-start.9 = (bf16[64,1024]{1,0:T(8,128)(2,1)S(1)}, bf16[64,1024]{1,0:T(8,128)(2,1)S(1)}, u32[]{:S(2)}, u32[]{:S(2)}) collective-permute-start(bf16[64,1024]{1,0:T(8,128)(2,1)S(1)} %collective-permute-done.5.refs_1_), channel_id=1, source_target_pairs={{0,4},{4,0},{8,12},{12,8},{1,5},{5,1},{9,13},{13,9},{2,6},{6,2},{1... | collective-permute-start | bytes 393224 | tf_op jit(solution)/shard_map/ppermute | solution.py:278
  26.9 1.3 %collective-permute-start.6 = (bf16[64,512]{1,0:T(8,128)(2,1)S(1)}, bf16[64,512]{1,0:T(8,128)(2,1)S(1)}, u32[]{:S(2)}, u32[]{:S(2)}) collective-permute-start(bf16[64,512]{1,0:T(8,128)(2,1)S(1)} %get-tuple-element.29), channel_id=1, source_target_pairs={{0,1},{1,0},{2,3},{3,2},{4,5},{5,4},{6,7},{7,6},{8,9},{9,8},{10,11... | collective-permute-start | bytes 196616 | tf_op jit(solution)/shard_map/ppermute | solution.py:278
  28.3 7.4 %collective-permute-start.7 = (bf16[192,512]{1,0:T(8,128)(2,1)S(1)}, bf16[192,512]{1,0:T(8,128)(2,1)S(1)}, u32[]{:S(2)}, u32[]{:S(2)}) collective-permute-start(bf16[192,512]{1,0:T(8,128)(2,1)S(1)} %shard_map.78.refs_0_), channel_id=1, source_target_pairs={{0,2},{1,3},{2,0},{3,1},{4,6},{5,7},{6,4},{7,5},{8,10},{9,11},{10,... | collective-permute-start | bytes 589832 | tf_op jit(solution)/shard_map/ppermute | solution.py:278
  32.8 1.3 %collective-permute-start.10 = (bf16[64,512]{1,0:T(8,128)(2,1)S(1)}, bf16[64,512]{1,0:T(8,128)(2,1)S(1)}, u32[]{:S(2)}, u32[]{:S(2)}) collective-permute-start(bf16[64,512]{1,0:T(8,128)(2,1)S(1)} %get-tuple-element.32), channel_id=1, source_target_pairs={{0,1},{1,0},{2,3},{3,2},{4,5},{5,4},{6,7},{7,6},{8,9},{9,8},{10,11... | collective-permute-start | bytes 196616 | tf_op jit(solution)/shard_map/ppermute | solution.py:278
  34.1 4.3 %collective-permute-start.11 = (bf16[64,512]{1,0:T(8,128)(2,1)S(1)}, bf16[64,512]{1,0:T(8,128)(2,1)S(1)}, u32[]{:S(2)}, u32[]{:S(2)}) collective-permute-start(bf16[64,512]{1,0:T(8,128)(2,1)S(1)} %shard_map.82.refs_1_), channel_id=1, source_target_pairs={{0,2},{1,3},{2,0},{3,1},{4,6},{5,7},{6,4},{7,5},{8,10},{9,11},{10,... | collective-permute-start | bytes 196616 | tf_op jit(solution)/shard_map/ppermute | solution.py:278
  38.7 6.1 %collective-permute-start.12 = (bf16[32,512]{1,0:T(8,128)(2,1)S(1)}, bf16[32,512]{1,0:T(8,128)(2,1)S(1)}, u32[]{:S(2)}, u32[]{:S(2)}) collective-permute-start(bf16[32,512]{1,0:T(8,128)(2,1)S(1)} %get-tuple-element.34), channel_id=1, source_target_pairs={{0,12},{4,8},{8,4},{12,0},{1,13},{5,9},{9,5},{13,1},{2,14},{6,10},... | collective-permute-start | bytes 98312 | tf_op jit(solution)/shard_map/ppermute | solution.py:278
  40.8 4.8 %collective-permute-start.13 = (bf16[32,512]{1,0:T(8,128)(2,1)S(1)}, bf16[32,512]{1,0:T(8,128)(2,1)S(1)}, u32[]{:S(2)}, u32[]{:S(2)}) collective-permute-start(bf16[32,512]{1,0:T(8,128)(2,1)S(1)} %get-tuple-element.35), channel_id=1, source_target_pairs={{0,8},{4,12},{8,0},{12,4},{1,9},{5,13},{9,1},{13,5},{2,10},{6,14},... | collective-permute-start | bytes 98312 | tf_op jit(solution)/shard_map/ppermute | solution.py:278
  40.8 4.8 %collective-permute-start.14 = (bf16[32,512]{1,0:T(8,128)(2,1)S(1)}, bf16[32,512]{1,0:T(8,128)(2,1)S(1)}, u32[]{:S(2)}, u32[]{:S(2)}) collective-permute-start(bf16[32,512]{1,0:T(8,128)(2,1)S(1)} %get-tuple-element.36), channel_id=1, source_target_pairs={{0,4},{4,0},{8,12},{12,8},{1,5},{5,1},{9,13},{13,9},{2,6},{6,2},{1... | collective-permute-start | bytes 98312 | tf_op jit(solution)/shard_map/ppermute | solution.py:278
